TPU v7x, 128 devices: a whole 4x4x4 slice. The times are simulated.
128 devices in a mesh: head: 8 (over y_lo, z), ctx: 16 (over x, y_hi, core).
Axes of the slice: x: 4, y: 4 (y_hi: 2, y_lo: 2; y = y_hi * 2 + y_lo), z: 4, core: 2. Of those that a mesh axis runs over, the one named last changes fastest.
Arguments:
- keys: bfloat16 [8192, 5120], P('ctx', 'head'), may hold values from -6 to 6
- queries: bfloat16 [8192, 5120], P('ctx', 'head'), may hold values from -6 to 6
- values: bfloat16 [8192, 5120], P('ctx', 'head'), may hold values from -6 to 6
- rates: float32 [8192, 16], P('ctx', 'head'), may hold values from 0.02 to 1
- gate_fast: float32 [16, 320, 640], P('head'), may hold values from -0.3125 to 0.3125
- up_fast: float32 [16, 320, 640], P('head'), may hold values from -0.3125 to 0.3125
- down_fast: float32 [16, 320, 640], P('head'), may hold values from -0.25 to 0.25
- out_weight: bfloat16 [5120, 5120], P('head'), may hold values from -0.078125 to 0.078125
Outputs:
- layer_out: bfloat16 [8192, 5120], P(('ctx', 'head'))
All inputs are finite; a program needn't handle non-finite values.
Results may differ from a plain program's by a relative error of at most 0.011.
Values sent between devices are 32-bit elements; how exact they have to be, the bound alone decides.
No kernel may reach another device: no remote copies, remote signals or barrier semaphores. Data moves between devices by JAX's collectives and lax.ppermute only.
A program may use at most 128 MiB of HBM per device.

v0:
```python
import jax
import jax.numpy as jnp
from jax import lax
from jax.experimental import pallas as pl
from jax.experimental.pallas import tpu as pltpu
from jax.sharding import Mesh, PartitionSpec as P

NS_STEPS = 5
ns_a = 3.4445
ns_b = -4.775
ns_c = 2.0315
eps_value = 1e-06

AXES = ("yl", "z", "x", "yh", "core")
PLANE = ("x", "yh")
SHARDS = 8
TILE = 256
F32 = jnp.float32
BF16 = jnp.bfloat16


def mm(a, b):
    return jnp.dot(a, b, preferred_element_type=F32)


def mm_nt(a, b):
    return lax.dot_general(a, b, (((1,), (1,)), ((), ())), preferred_element_type=F32)


def grads_kernel(head_ref, k_ref, v_ref, r_ref, g_ref, u_ref, d_ref, o_ref, k_s, v_s, hk_s, dg_s, du_s):
    head = head_ref[0]
    rows, width = k_s.shape
    for h in range(2):

        @pl.when(head == h)
        def _():
            k_s[...] = k_ref[:, h * width : (h + 1) * width]
            rate = r_ref[h : h + 1, :].T
            v = v_ref[:, h * width : (h + 1) * width].astype(F32)
            v_s[...] = (-rate * v).astype(BF16)

    wg = g_ref[0].astype(BF16)
    wu = u_ref[0].astype(BF16)
    wd = d_ref[0].astype(BF16)
    step = 128
    for t in range(0, rows, step):
        at = slice(t, t + step)
        k = k_s[at, :]
        gate = mm(k, wg)
        upper = mm(k, wu)
        dhid = mm(v_s[at, :], wd)
        sig = jax.nn.sigmoid(gate)
        act = gate * sig
        hk_s[at, :] = (act * upper).astype(BF16)
        dg_s[at, :] = (dhid * upper * sig * (1.0 + gate * (1.0 - sig))).astype(BF16)
        du_s[at, :] = (dhid * act).astype(BF16)
    kt = k_s[...].T
    vt = v_s[...].T
    part = width // SHARDS
    for m, (left, right) in enumerate(((kt, dg_s), (kt, du_s), (vt, hk_s))):
        grad = mm(left, right[...])
        for j in range(SHARDS):
            o_ref[j, m] = grad[j * part : (j + 1) * part, :]


def head_grads(head, keys, values, rates, gate, up, down):
    rows = keys.shape[0]
    heads, width, hidden = gate.shape
    whole = lambda a: pl.BlockSpec(a.shape, lambda i, h: (0,) * a.ndim)
    one = pl.BlockSpec((1, width, hidden), lambda i, h: (h[0], 0, 0))
    shape = (SHARDS, 3, width // SHARDS, hidden)
    return pl.pallas_call(
        grads_kernel,
        out_shape=jax.ShapeDtypeStruct(shape, F32),
        grid_spec=pltpu.PrefetchScalarGridSpec(
            num_scalar_prefetch=1,
            grid=(1,),
            in_specs=[whole(keys), whole(values), whole(rates), one, one, one],
            out_specs=pl.BlockSpec(shape, lambda i, h: (0, 0, 0, 0)),
            scratch_shapes=[
                pltpu.VMEM((rows, width), BF16),
                pltpu.VMEM((rows, width), BF16),
                pltpu.VMEM((rows, hidden), BF16),
                pltpu.VMEM((rows, hidden), BF16),
                pltpu.VMEM((rows, hidden), BF16),
            ],
        ),
        compiler_params=pltpu.CompilerParams(vmem_limit_bytes=56 << 20),
        name="head_grads",
    )(head, keys, values, rates, gate, up, down)


def split(x):
    high = x.astype(BF16)
    return high, (x - high.astype(F32)).astype(BF16)


def packed(high, low):
    return jnp.concatenate([high, high, low], axis=1)


def mirrored(left, corner):
    at = left.shape[1]
    return jnp.concatenate([left, jnp.concatenate([left[at:].T, corner], axis=0)], axis=1)


def gram_of(xh, xl):
    a, b = packed(xh, xl), jnp.concatenate([xh, xl, xh], axis=1)
    return mirrored(mm_nt(a, b[:TILE]), mm_nt(a[TILE:], b[TILE:]))


def square_of(ah, al):
    a, b = packed(ah, al), jnp.concatenate([ah, al, ah], axis=0)
    return mirrored(mm(a, b[:, :TILE]), mm(a[TILE:], b[:, TILE:]))


def newton_kernel(g_ref, o_ref):
    matrices, width, hidden = o_ref.shape
    every = range(matrices)
    for m in every:
        grad = g_ref[:, m].reshape(width, hidden)
        total = jnp.sum(jnp.sum(grad * grad, axis=1, keepdims=True), axis=0, keepdims=True)
        o_ref[m] = grad * lax.rsqrt(total + eps_value)

    def sweep(_, carry):
        xs = [o_ref[m] for m in every]
        parts = [split(x) for x in xs]
        grams = [gram_of(*p) for p in parts]
        squares = [square_of(*split(g)) for g in grams]
        mixers = [split(ns_b * g + ns_c * q) for g, q in zip(grams, squares)]
        for m, x, (xh, xl), mixer in zip(every, xs, parts, mixers):
            o_ref[m] = ns_a * x + mm(packed(*mixer), jnp.concatenate([xh, xl, xh], axis=0))
        return carry

    lax.fori_loop(0, NS_STEPS, sweep, 0)


def newton(grads):
    shape = (grads.shape[1], grads.shape[0] * grads.shape[2], grads.shape[3])
    return pl.pallas_call(
        newton_kernel,
        out_shape=jax.ShapeDtypeStruct(shape, F32),
        compiler_params=pltpu.CompilerParams(vmem_limit_bytes=56 << 20),
        name="newton",
    )(grads)


def query_rows(at_ref, q_ref, q_s):
    rows, width = q_s.shape
    block = rows // 8
    for h in range(2):

        @pl.when(at_ref[0] == h)
        def _():
            for r in range(8):
                row = ((at_ref[1] + r // 4) % 2) * 4 + (at_ref[2] + r % 4) % 4
                source = pl.ds(pl.multiple_of(row * block, block), block)
                q_s[r * block : (r + 1) * block, :] = q_ref[source, h * width : (h + 1) * width]


def query_chunks(q_s, x_ref, g_ref, u_ref, d_ref):
    vg = (g_ref[0] - x_ref[0]).astype(BF16)
    vu = (u_ref[0] - x_ref[1]).astype(BF16)
    vd = (d_ref[0] - x_ref[2]).astype(BF16)
    step = 128
    for t in range(0, q_s.shape[0], step):
        q = q_s[t : t + step, :]
        gate = mm(q, vg)
        hidden = (gate * jax.nn.sigmoid(gate) * mm(q, vu)).astype(BF16)
        yield slice(t, t + step), mm_nt(hidden, vd).astype(BF16)


def first_kernel(at_ref, q_ref, x_ref, g_ref, u_ref, d_ref, o_ref, q_s):
    query_rows(at_ref, q_ref, q_s)
    for rows, o in query_chunks(q_s, x_ref, g_ref, u_ref, d_ref):
        o_ref[rows, :] = o


def second_kernel(at_ref, q_ref, x_ref, g_ref, u_ref, d_ref, p_ref, o_ref, q_s, o_s):
    width = q_s.shape[1]
    query_rows(at_ref, q_ref, q_s)
    for rows, o in query_chunks(q_s, x_ref, g_ref, u_ref, d_ref):
        o_s[rows, :] = o
    for h in range(2):

        @pl.when(at_ref[0] == h)
        def _():
            o_ref[:, h * width : (h + 1) * width] = o_s[...]
            o_ref[:, (1 - h) * width : (2 - h) * width] = p_ref[...]


def head_query(kernel, at, queries, x, gate, up, down, *first):
    rows = queries.shape[0]
    heads, width, hidden = gate.shape
    whole = lambda a: pl.BlockSpec(a.shape, lambda i, at: (0,) * a.ndim)
    one = pl.BlockSpec((1, width, hidden), lambda i, at: (at[0], 0, 0))
    scratch = [pltpu.VMEM((rows, width), BF16)] * (1 + len(first))
    columns = width * (1 + len(first))
    return pl.pallas_call(
        kernel,
        out_shape=jax.ShapeDtypeStruct((rows, columns), BF16),
        grid_spec=pltpu.PrefetchScalarGridSpec(
            num_scalar_prefetch=1,
            grid=(1,),
            in_specs=[whole(queries), whole(x), one, one, one] + [whole(a) for a in first],
            out_specs=pl.BlockSpec((rows, columns), lambda i, at: (0, 0)),
            scratch_shapes=scratch,
        ),
        compiler_params=pltpu.CompilerParams(vmem_limit_bytes=56 << 20),
        name="head_query",
    )(at, queries, x, gate, up, down, *first)


def swap(a, axis):
    return lax.ppermute(a, axis, [(0, 1), (1, 0)])


def ring(a, shift):
    return lax.ppermute(a, "z", [(i, (i + shift) % 4) for i in range(4)])


def plane_scatter(a):
    return jnp.sum(lax.all_to_all(a, PLANE, 0, 0, tiled=True), axis=0)


def plane_gather(a):
    same = jnp.broadcast_to(a[None], (SHARDS,) + a.shape)
    return lax.all_to_all(same, PLANE, 0, 0, tiled=True)


def project_scatter(rel, weight, cut):
    rows, depth = rel.shape[2:]
    left, right = weight[:, :cut], weight[:, cut:]
    part = lambda o, w: mm(o.reshape(-1, depth), w).reshape(o.shape[:-1] + (w.shape[1],))
    half = rows // 2

    b_far = part(rel[1], right)
    b_from_y = swap(b_far, "yl")
    a_two = part(rel[:, 2], left)
    a_up = ring(a_two[0], 1)
    a_down = ring(a_two[1], -1)
    a_one = part(rel[:, 1], left)
    a_three = part(rel[:, 3], left)
    b_near = part(rel[0], right)
    a_zero = part(rel[:, 0], left)

    a_one = jnp.stack([a_one[0] + a_up, a_one[1]])
    a_three = jnp.stack([a_three[0], a_three[1] + a_down])
    a_one = ring(a_one, 1)
    a_three = ring(a_three, -1)
    b = b_near + b_from_y
    b_up = ring(b[2, :half], 1)
    b_down = ring(b[2, half:], -1)
    a = a_zero + a_one + a_three
    a_from_y = swap(a[1], "yl")
    b_one = ring(jnp.concatenate([b[1, :half] + b_up, b[1, half:]]), 1)
    b_three = ring(jnp.concatenate([b[3, :half], b[3, half:] + b_down]), -1)
    return jnp.concatenate([a[0] + a_from_y, b[0] + b_one + b_three], axis=1)


def body(keys, queries, values, rates, gate, up, down, out_weight):
    core, yl, z = (lax.axis_index(name).astype(jnp.int32) for name in ("core", "yl", "z"))
    mine, other = jnp.stack([core, yl, z]), jnp.stack([1 - core, yl, z])
    weights = (gate, up, down)
    theirs = head_grads(other, keys, values, rates.T, *weights)
    received = swap(theirs, "core")
    ours = head_grads(mine, keys, values, rates.T, *weights)
    whole = plane_gather(plane_scatter(ours + received))
    x_mine = newton(whole)
    x_other = swap(x_mine, "core")
    o_mine = head_query(first_kernel, mine, queries, x_mine, *weights)
    joined = head_query(second_kernel, other, queries, x_other, *weights, o_mine)
    rel = joined.reshape(2, 4, -1, joined.shape[1])
    return project_scatter(rel, out_weight, 2816).astype(BF16)


def solution(mesh):
    fine = Mesh(mesh.devices.reshape(2, 4, 4, 2, 2), AXES)
    ctx, head = ("x", "yh", "core"), ("yl", "z")
    in_specs = (
        P(ctx, head),
        P(ctx, head),
        P(ctx, head),
        P(ctx, head),
        P(head, None, None),
        P(head, None, None),
        P(head, None, None),
        P(head, None),
    )
    out_specs = P(ctx + head, None)
    return jax.shard_map(body, mesh=fine, in_specs=in_specs, out_specs=out_specs, check_vma=False)
```

profile of v0, /device:TPU:0, one launch (start us, length us, event | category | flops | bytes accessed | tf_op | source)
XLA Modules:
  0.0 216.5 jit_solution(310553006163504888)
XLA Ops:
  0.6 7.2 %head_grads.3 = f32[8,3,40,640]{3,2,1,0:T(8,128)} custom-call(s32[3]{0:T(128)} %add_add_fusion.head_ref.at_ref, bf16[512,640]{1,0:T(8,128)(2,1)} %k_ref.3, bf16[512,640]{1,0:T(8,128)(2,1)} %v_ref.3, f32[2,512]{1,0:T(2,128)} %bitcast.78, f32[2,320,640]{2,1,0:T(8,128)} %g_ref.7, f32[2,320,640]{2,1,0:T(8,128)} %u_ref.7, f32[2,320,640]{2,1,0:T(8,128)} %d_ref.7), custom_call_target="tpu_custom_call" | custom-call | tf_op jit(solution)/shard_map/head_grads/pallas_call | solution.py:72
  7.7 0.7 add_add_fusion.1.head_ref.at_ref
  8.4 6.9 %head_grads.2 = f32[8,3,40,640]{3,2,1,0:T(8,128)} custom-call(s32[3]{0:T(128)} %add_add_fusion.1.head_ref.at_ref, bf16[512,640]{1,0:T(8,128)(2,1)} %k_ref.3, bf16[512,640]{1,0:T(8,128)(2,1)} %v_ref.3, f32[2,512]{1,0:T(2,128)} %bitcast.79, f32[2,320,640]{2,1,0:T(8,128)} %g_ref.7, f32[2,320,640]{2,1,0:T(8,128)} %u_ref.7, f32[2,320,640]{2,1,0:T(8,128)} %d_ref.7), custom_call_target="tpu_custom_call" | custom-call | tf_op jit(solution)/shard_map/head_grads/pallas_call | solution.py:72
  15.3 1.9 add.33
  17.3 39.9 %all_to_all.10 = f32[8,3,40,640]{3,2,1,0:T(8,128)S(1)} all-to-all(f32[8,3,40,640]{3,2,1,0:T(8,128)S(1)} %add.33), channel_id=1, replica_groups=mesh['yl'=2,'z'=4,'x'=4,'yh'=2,'core'=2] {'x','yh'}, dimensions={0} | all-to-all | bytes 4915200 | tf_op jit(solution)/shard_map/all_to_all | solution.py:223
  57.5 34.8 %all_to_all.11.g_ref = f32[8,3,40,640]{3,2,1,0:T(8,128)} all-to-all(f32[8,3,40,640]{3,2,1,0:T(8,128)S(1)} %broadcast_in_dim.2), channel_id=1, replica_groups=mesh['yl'=2,'z'=4,'x'=4,'yh'=2,'core'=2] {'x','yh'}, dimensions={0} | all-to-all | bytes 4915200 | tf_op jit(solution)/shard_map/all_to_all | solution.py:228
  92.3 21.8 %newton.1.x_ref = f32[3,320,640]{2,1,0:T(8,128)} custom-call(f32[8,3,40,640]{3,2,1,0:T(8,128)} %all_to_all.11.g_ref), custom_call_target="tpu_custom_call" | custom-call | tf_op jit(solution)/shard_map/newton/pallas_call | solution.py:140
  114.2 6.6 %head_query.2.p_ref = bf16[512,320]{1,0:T(8,128)(2,1)} custom-call(s32[3]{0:T(128)} %add_add_fusion.1.head_ref.at_ref, bf16[512,640]{1,0:T(8,128)(2,1)} %q_ref.3, f32[3,320,640]{2,1,0:T(8,128)} %newton.1.x_ref, f32[2,320,640]{2,1,0:T(8,128)} %g_ref.7, f32[2,320,640]{2,1,0:T(8,128)} %u_ref.7, f32[2,320,640]{2,1,0:T(8,128)} %d_ref.7), custom_call_target="tpu_custom_call" | custom-call | tf_op jit(solution)/shard_map/head_query/pallas_call | solution.py:199
  120.8 6.6 %head_query.3 = bf16[512,640]{1,0:T(8,128)(2,1)} custom-call(s32[3]{0:T(128)} %add_add_fusion.head_ref.at_ref, bf16[512,640]{1,0:T(8,128)(2,1)} %q_ref.3, f32[3,320,640]{2,1,0:T(8,128)} %collective-permute-done.1.x_ref, f32[2,320,640]{2,1,0:T(8,128)} %g_ref.7, f32[2,320,640]{2,1,0:T(8,128)} %u_ref.7, f32[2,320,640]{2,1,0:T(8,128)} %d_ref.7, ...), custom_call_target="tpu_custom_call" | custom-call | tf_op jit(solution)/shard_map/head_query/pallas_call | solution.py:199
  127.4 1.1 fusion.25
  128.5 1.1 fusion.24
  129.7 0.8 fusion.9
  130.6 2.0 collective-permute-start.2
  132.6 2.2 %collective-permute-start.4 = (f32[64,2816]{1,0:T(8,128)S(1)}, f32[64,2816]{1,0:T(8,128)S(1)}, u32[]{:S(2)}, u32[]{:S(2)}) collective-permute-start(f32[64,2816]{1,0:T(8,128)S(1)} %get-tuple-element.14), channel_id=1, source_target_pairs={{0,48},{16,0},{32,16},{48,32},{1,49},{17,1},{33,17},{49,33},{2,50}... | collective-permute-start | bytes 2162696 | tf_op jit(solution)/shard_map/ppermute | solution.py:219
  134.8 1.1 fusion.2
  135.9 0.8 collective-permute-start.7
  136.7 0.8 fusion.11
  137.4 0.8 fusion.7
  138.2 13.3 %collective-permute-done.2 = f32[64,2816]{1,0:T(8,128)S(1)} collective-permute-done((f32[64,2816]{1,0:T(8,128)S(1)}, f32[64,2816]{1,0:T(8,128)S(1)}, u32[]{:S(2)}, u32[]{:S(2)}) %collective-permute-start.2) | collective-permute-done | bytes 720928 | tf_op jit(solution)/shard_map/ppermute | solution.py:219
  152.1 3.3 %collective-permute-start.5 = (f32[2,64,2816]{2,1,0:T(8,128)S(1)}, f32[2,64,2816]{2,1,0:T(8,128)S(1)}, u32[]{:S(2)}, u32[]{:S(2)}) collective-permute-start(f32[2,64,2816]{2,1,0:T(8,128)S(1)} %pad_maximum_fusion.1), channel_id=1, source_target_pairs={{0,48},{16,0},{32,16},{48,32},{1,49},{17,1},{33,17},{49,33},{2,50}... | collective-permute-start | bytes 4325384 | tf_op jit(solution)/shard_map/ppermute | solution.py:219
  155.4 31.1 %collective-permute-done.3 = f32[2,64,2816]{2,1,0:T(8,128)S(1)} collective-permute-done((f32[2,64,2816]{2,1,0:T(8,128)S(1)}, f32[2,64,2816]{2,1,0:T(8,128)S(1)}, u32[]{:S(2)}, u32[]{:S(2)}) %collective-permute-start.3) | collective-permute-done | bytes 1441824 | tf_op jit(solution)/shard_map/ppermute | solution.py:219
  186.4 1.7 fusion
  188.2 1.2 collective-permute-done.7
  189.3 1.1 convolution_add_fusion
  190.6 2.2 %collective-permute-start.10 = (f32[32,2304]{1,0:T(8,128)S(1)}, f32[32,2304]{1,0:T(8,128)S(1)}, u32[]{:S(2)}, u32[]{:S(2)}) collective-permute-start(f32[32,2304]{1,0:T(8,128)S(1)} %get-tuple-element.8), channel_id=1, source_target_pairs={{0,48},{16,0},{32,16},{48,32},{1,49},{17,1},{33,17},{49,33},{2,50}... | collective-permute-start | bytes 884744 | tf_op jit(solution)/shard_map/ppermute | solution.py:219
  192.8 0.8 collective-permute-start.6
  193.6 5.4 %collective-permute-done.10 = f32[32,2304]{1,0:T(8,128)S(1)} collective-permute-done((f32[32,2304]{1,0:T(8,128)S(1)}, f32[32,2304]{1,0:T(8,128)S(1)}, u32[]{:S(2)}, u32[]{:S(2)}) %collective-permute-start.10) | collective-permute-done | bytes 294944 | tf_op jit(solution)/shard_map/ppermute | solution.py:219
  199.0 2.4 %collective-permute-done.8 = f32[32,2304]{1,0:T(8,128)S(1)} collective-permute-done((f32[32,2304]{1,0:T(8,128)S(1)}, f32[32,2304]{1,0:T(8,128)S(1)}, u32[]{:S(2)}, u32[]{:S(2)}) %collective-permute-start.8) | collective-permute-done | bytes 294944 | tf_op jit(solution)/shard_map/ppermute | solution.py:219
  201.6 3.3 %collective-permute-start.11 = (f32[64,2304]{1,0:T(8,128)S(1)}, f32[64,2304]{1,0:T(8,128)S(1)}, u32[]{:S(2)}, u32[]{:S(2)}) collective-permute-start(f32[64,2304]{1,0:T(8,128)S(1)} %pad_maximum_fusion.4), channel_id=1, source_target_pairs={{0,48},{16,0},{32,16},{48,32},{1,49},{17,1},{33,17},{49,33},{2,50}... | collective-permute-start | bytes 1769480 | tf_op jit(solution)/shard_map/ppermute | solution.py:219
  204.9 4.8 %collective-permute-done.6 = f32[64,2816]{1,0:T(8,128)S(1)} collective-permute-done((f32[64,2816]{1,0:T(8,128)S(1)}, f32[64,2816]{1,0:T(8,128)S(1)}, u32[]{:S(2)}, u32[]{:S(2)}) %collective-permute-start.6) | collective-permute-done | bytes 720928 | tf_op jit(solution)/shard_map/ppermute | solution.py:215
  209.8 5.8 %collective-permute-done.9 = f32[64,2304]{1,0:T(8,128)S(1)} collective-permute-done((f32[64,2304]{1,0:T(8,128)S(1)}, f32[64,2304]{1,0:T(8,128)S(1)}, u32[]{:S(2)}, u32[]{:S(2)}) %collective-permute-start.9) | collective-permute-done | bytes 589856 | tf_op jit(solution)/shard_map/ppermute | solution.py:219
  215.6 0.9 pad_maximum_fusion.2
  (30 shorter events, 2.1 us)
Async XLA Ops:
  7.7 7.6 %collective-permute-start = (f32[8,3,40,640]{3,2,1,0:T(8,128)}, f32[8,3,40,640]{3,2,1,0:T(8,128)S(1)}, u32[]{:S(2)}, u32[]{:S(2)}) collective-permute-start(f32[8,3,40,640]{3,2,1,0:T(8,128)} %head_grads.3), channel_id=1, source_target_pairs={{0,1},{1,0},{2,3},{3,2},{4,5},{5,4},{6,7},{7,6},{8,9},{9,8},{10,11... | collective-permute-start | bytes 7372808 | tf_op jit(solution)/shard_map/ppermute | solution.py:215
  114.2 6.6 %collective-permute-start.1 = (f32[3,320,640]{2,1,0:T(8,128)}, f32[3,320,640]{2,1,0:T(8,128)}, u32[]{:S(2)}, u32[]{:S(2)}) collective-permute-start(f32[3,320,640]{2,1,0:T(8,128)} %newton.1.x_ref), channel_id=1, source_target_pairs={{0,1},{1,0},{2,3},{3,2},{4,5},{5,4},{6,7},{7,6},{8,9},{9,8},{10,11... | collective-permute-start | bytes 7372808 | tf_op jit(solution)/shard_map/ppermute | solution.py:215
  114.2 15.5 %slice-start = ((s8[6553600]{0:T(1024)(128)(4,1)}), s8[4194304]{0:T(1024)(128)(4,1)S(1)}, s32[]{:S(2)}) async-start(s8[6553600]{0:T(1024)(128)(4,1)} %bitcast.69), calls=%async_computation.2 | async-start | bytes 8388608
  120.8 8.9 %slice-start.1 = ((s8[6553600]{0:T(1024)(128)(4,1)}), s8[2359296]{0:T(1024)(128)(4,1)S(1)}, s32[]{:S(2)}) async-start(s8[6553600]{0:T(1024)(128)(4,1)} %bitcast.69), calls=%async_computation.3 | async-start | bytes 4718592
  130.6 20.9 %collective-permute-start.2 = (f32[64,2816]{1,0:T(8,128)S(1)}, f32[64,2816]{1,0:T(8,128)S(1)}, u32[]{:S(2)}, u32[]{:S(2)}) collective-permute-start(f32[64,2816]{1,0:T(8,128)S(1)} %get-tuple-element.13), channel_id=1, source_target_pairs={{0,16},{16,32},{32,48},{48,0},{1,17},{17,33},{33,49},{49,1},{2,18}... | collective-permute-start | bytes 2162696 | tf_op jit(solution)/shard_map/ppermute | solution.py:219
  132.6 19.2 %collective-permute-start.4 = (f32[64,2816]{1,0:T(8,128)S(1)}, f32[64,2816]{1,0:T(8,128)S(1)}, u32[]{:S(2)}, u32[]{:S(2)}) collective-permute-start(f32[64,2816]{1,0:T(8,128)S(1)} %get-tuple-element.14), channel_id=1, source_target_pairs={{0,48},{16,0},{32,16},{48,32},{1,49},{17,1},{33,17},{49,33},{2,50}... | collective-permute-start | bytes 2162696 | tf_op jit(solution)/shard_map/ppermute | solution.py:219
  135.9 53.4 %collective-permute-start.7 = (f32[4,64,2304]{2,1,0:T(8,128)S(1)}, f32[4,64,2304]{2,1,0:T(8,128)S(1)}, u32[]{:S(2)}, u32[]{:S(2)}) collective-permute-start(f32[4,64,2304]{2,1,0:T(8,128)S(1)} %fusion.2), channel_id=1, source_target_pairs={{0,64},{64,0},{1,65},{65,1},{2,66},{66,2},{3,67},{67,3},{4,68},{68... | collective-permute-start | bytes 7077896 | tf_op jit(solution)/shard_map/ppermute | solution.py:215
  151.7 34.7 %collective-permute-start.3 = (f32[2,64,2816]{2,1,0:T(8,128)S(1)}, f32[2,64,2816]{2,1,0:T(8,128)S(1)}, u32[]{:S(2)}, u32[]{:S(2)}) collective-permute-start(f32[2,64,2816]{2,1,0:T(8,128)S(1)} %pad_maximum_fusion), channel_id=1, source_target_pairs={{0,16},{16,32},{32,48},{48,0},{1,17},{17,33},{33,49},{49,1},{2,18}... | collective-permute-start | bytes 4325384 | tf_op jit(solution)/shard_map/ppermute | solution.py:219
  152.1 34.3 %collective-permute-start.5 = (f32[2,64,2816]{2,1,0:T(8,128)S(1)}, f32[2,64,2816]{2,1,0:T(8,128)S(1)}, u32[]{:S(2)}, u32[]{:S(2)}) collective-permute-start(f32[2,64,2816]{2,1,0:T(8,128)S(1)} %pad_maximum_fusion.1), channel_id=1, source_target_pairs={{0,48},{16,0},{32,16},{48,32},{1,49},{17,1},{33,17},{49,33},{2,50}... | collective-permute-start | bytes 4325384 | tf_op jit(solution)/shard_map/ppermute | solution.py:219
  190.6 8.4 %collective-permute-start.10 = (f32[32,2304]{1,0:T(8,128)S(1)}, f32[32,2304]{1,0:T(8,128)S(1)}, u32[]{:S(2)}, u32[]{:S(2)}) collective-permute-start(f32[32,2304]{1,0:T(8,128)S(1)} %get-tuple-element.8), channel_id=1, source_target_pairs={{0,48},{16,0},{32,16},{48,32},{1,49},{17,1},{33,17},{49,33},{2,50}... | collective-permute-start | bytes 884744 | tf_op jit(solution)/shard_map/ppermute | solution.py:219
  192.8 8.6 %collective-permute-start.8 = (f32[32,2304]{1,0:T(8,128)S(1)}, f32[32,2304]{1,0:T(8,128)S(1)}, u32[]{:S(2)}, u32[]{:S(2)}) collective-permute-start(f32[32,2304]{1,0:T(8,128)S(1)} %get-tuple-element.7), channel_id=1, source_target_pairs={{0,16},{16,32},{32,48},{48,0},{1,17},{17,33},{33,49},{49,1},{2,18}... | collective-permute-start | bytes 884744 | tf_op jit(solution)/shard_map/ppermute | solution.py:219
  192.8 16.9 %collective-permute-start.6 = (f32[64,2816]{1,0:T(8,128)S(1)}, f32[64,2816]{1,0:T(8,128)S(1)}, u32[]{:S(2)}, u32[]{:S(2)}) collective-permute-start(f32[64,2816]{1,0:T(8,128)S(1)} %slice_bitcast_fusion), channel_id=1, source_target_pairs={{0,64},{64,0},{1,65},{65,1},{2,66},{66,2},{3,67},{67,3},{4,68},{68... | collective-permute-start | bytes 2162696 | tf_op jit(solution)/shard_map/ppermute | solution.py:215
  201.5 14.1 %collective-permute-start.9 = (f32[64,2304]{1,0:T(8,128)S(1)}, f32[64,2304]{1,0:T(8,128)S(1)}, u32[]{:S(2)}, u32[]{:S(2)}) collective-permute-start(f32[64,2304]{1,0:T(8,128)S(1)} %pad_maximum_fusion.3), channel_id=1, source_target_pairs={{0,16},{16,32},{32,48},{48,0},{1,17},{17,33},{33,49},{49,1},{2,18}... | collective-permute-start | bytes 1769480 | tf_op jit(solution)/shard_map/ppermute | solution.py:219
  201.6 13.9 %collective-permute-start.11 = (f32[64,2304]{1,0:T(8,128)S(1)}, f32[64,2304]{1,0:T(8,128)S(1)}, u32[]{:S(2)}, u32[]{:S(2)}) collective-permute-start(f32[64,2304]{1,0:T(8,128)S(1)} %pad_maximum_fusion.4), channel_id=1, source_target_pairs={{0,48},{16,0},{32,16},{48,32},{1,49},{17,1},{33,17},{49,33},{2,50}... | collective-permute-start | bytes 1769480 | tf_op jit(solution)/shard_map/ppermute | solution.py:219
where the time goes:
time: 217 us
  blocking collectives  74.8 us (34%)
  waiting for transfers between devices  63.8 us (29%)
  Pallas kernels  49.1 us (23%)
  starting transfers between devices  14.6 us (7%)
  matrix products  6.32 us (3%)
  other arithmetic  5.04 us (2%)
  local copies, waits for them, and re-layouts  2.64 us (1%)
    ppermute x8, waiting for transfers between devices, ring(): return lax.ppermute(a, 'z', [(i, (i + shift) % 4) for i in range(4)])  57.9 us
    all_to_all x1, blocking collectives, plane_scatter(): return jnp.sum(lax.all_to_all(a, PLANE, 0, 0, tiled=True), axis=0)  39.9 us
    all_to_all x1, blocking collectives, plane_gather(): return lax.all_to_all(same, PLANE, 0, 0, tiled=True)  34.8 us
    pallas_call x1, Pallas kernels, newton(): pl.pallas_call(newton_kernel, out_shape=jax.ShapeDtypeStruct(shape, F32),...  21.8 us
    pallas_call x2, Pallas kernels, head_grads(): pl.pallas_call(grads_kernel, out_shape=jax.ShapeDtypeStruct(shape, F32),...  14.1 us
    pallas_call x2, Pallas kernels, head_query(): pl.pallas_call(kernel, out_shape=jax.ShapeDtypeStruct((rows, columns), BF...  13.2 us
    ppermute x8, starting transfers between devices, ring(): return lax.ppermute(a, 'z', [(i, (i + shift) % 4) for i in range(4)])  13.1 us
    dot_general x6, matrix products, mm(): return jnp.dot(a, b, preferred_element_type=F32)  6.32 us
  transfers between devices with their start and end apart: 12, of which 7 were waited for; matrix products, arithmetic and copies ran while one was open for 3% of the time, Pallas kernels for 6%

commit v1 on v0

v1 whole, which is shorter than its diff:
```python
import jax
import jax.numpy as jnp
from jax import lax
from jax.experimental import pallas as pl
from jax.experimental.pallas import tpu as pltpu
from jax.sharding import Mesh, PartitionSpec as P

NS_STEPS = 5
ns_a = 3.4445
ns_b = -4.775
ns_c = 2.0315
eps_value = 1e-06

AXES = ("yl", "z", "x", "yh", "core")
PLANE = ("x", "yh")
SHARDS = 8
TILE = 256
VMEM_LIMIT = 24 << 20
SHARES = (14, 10, 9, 7)
F32 = jnp.float32
BF16 = jnp.bfloat16


def mm(a, b):
    return jnp.dot(a, b, preferred_element_type=F32)


def mm_nt(a, b):
    return lax.dot_general(a, b, (((1,), (1,)), ((), ())), preferred_element_type=F32)


def grads_kernel(head_ref, k_ref, v_ref, r_ref, g_ref, u_ref, d_ref, o_ref, k_s, v_s, hk_s, dg_s, du_s):
    head = head_ref[0]
    rows, width = k_s.shape
    for h in range(2):

        @pl.when(head == h)
        def _():
            k_s[...] = k_ref[:, h * width : (h + 1) * width]
            rate = r_ref[h : h + 1, :].T
            v = v_ref[:, h * width : (h + 1) * width].astype(F32)
            v_s[...] = (-rate * v).astype(BF16)

    wg = g_ref[head].astype(BF16)
    wu = u_ref[head].astype(BF16)
    wd = d_ref[head].astype(BF16)
    step = 256
    for t in range(0, rows, step):
        at = slice(t, t + step)
        k = k_s[at, :]
        gate = mm(k, wg)
        upper = mm(k, wu)
        dhid = mm(v_s[at, :], wd)
        sig = jax.nn.sigmoid(gate)
        act = gate * sig
        hk_s[at, :] = (act * upper).astype(BF16)
        dg_s[at, :] = (dhid * upper * sig * (1.0 + gate * (1.0 - sig))).astype(BF16)
        du_s[at, :] = (dhid * act).astype(BF16)
    kt = k_s[...].T
    vt = v_s[...].T
    part = width // SHARDS
    for m, (left, right) in enumerate(((kt, dg_s), (kt, du_s), (vt, hk_s))):
        grad = mm(left, right[...])
        for j in range(SHARDS):
            o_ref[j, m] = grad[j * part : (j + 1) * part, :]


def call(kernel, name, outs, scratch, scalars, *operands):
    specs = [pl.BlockSpec(memory_space=pltpu.SMEM)] + [pl.BlockSpec(memory_space=pltpu.VMEM)] * len(operands)
    return pl.pallas_call(
        kernel,
        out_shape=outs,
        in_specs=specs,
        out_specs=jax.tree.map(lambda _: pl.BlockSpec(memory_space=pltpu.VMEM), outs),
        scratch_shapes=scratch,
        compiler_params=pltpu.CompilerParams(vmem_limit_bytes=VMEM_LIMIT),
        name=name,
    )(scalars, *operands)


def head_grads(at, keys, values, rates, gate, up, down):
    rows = keys.shape[0]
    heads, width, hidden = gate.shape
    scratch = [pltpu.VMEM((rows, width), BF16)] * 2 + [pltpu.VMEM((rows, hidden), BF16)] * 3
    shape = jax.ShapeDtypeStruct((SHARDS, 3, width // SHARDS, hidden), F32)
    return call(grads_kernel, "head_grads", shape, scratch, at, keys, values, rates, gate, up, down)


def split(x):
    high = x.astype(BF16)
    return high, (x - high.astype(F32)).astype(BF16)


def packed(high, low):
    return jnp.concatenate([high, high, low], axis=1)


def mirrored(left, corner):
    at = left.shape[1]
    return jnp.concatenate([left, jnp.concatenate([left[at:].T, corner], axis=0)], axis=1)


def gram_of(xh, xl):
    a, b = packed(xh, xl), jnp.concatenate([xh, xl, xh], axis=1)
    return mirrored(mm_nt(a, b[:TILE]), mm_nt(a[TILE:], b[TILE:]))


def square_of(ah, al):
    a, b = packed(ah, al), jnp.concatenate([ah, al, ah], axis=0)
    return mirrored(mm(a, b[:, :TILE]), mm(a[TILE:], b[:, TILE:]))


def newton_kernel(g_ref, o_ref):
    matrices, width, hidden = o_ref.shape
    every = range(matrices)
    for m in every:
        grad = g_ref[:, m].reshape(width, hidden)
        total = jnp.sum(jnp.sum(grad * grad, axis=1, keepdims=True), axis=0, keepdims=True)
        o_ref[m] = grad * lax.rsqrt(total + eps_value)

    def sweep(_, carry):
        xs = [o_ref[m] for m in every]
        parts = [split(x) for x in xs]
        grams = [gram_of(*p) for p in parts]
        squares = [square_of(*split(g)) for g in grams]
        mixers = [split(ns_b * g + ns_c * q) for g, q in zip(grams, squares)]
        for m, x, (xh, xl), mixer in zip(every, xs, parts, mixers):
            o_ref[m] = ns_a * x + mm(packed(*mixer), jnp.concatenate([xh, xl, xh], axis=0))
        return carry

    lax.fori_loop(0, NS_STEPS, sweep, 0)


def newton(grads):
    shape = (grads.shape[1], grads.shape[0] * grads.shape[2], grads.shape[3])
    return pl.pallas_call(
        newton_kernel,
        out_shape=jax.ShapeDtypeStruct(shape, F32),
        compiler_params=pltpu.CompilerParams(vmem_limit_bytes=VMEM_LIMIT),
        name="newton",
    )(grads)


def query_rows(at_ref, q_ref, q_s):
    rows, width = q_s.shape
    block = rows // 8
    for h in range(2):

        @pl.when(at_ref[0] == h)
        def _():
            for r in range(8):
                row = ((at_ref[1] + r // 4) % 2) * 4 + (at_ref[2] + r % 4) % 4
                source = pl.ds(pl.multiple_of(row * block, block), block)
                q_s[r * block : (r + 1) * block, :] = q_ref[source, h * width : (h + 1) * width]


def query_chunks(at_ref, q_s, x_ref, g_ref, u_ref, d_ref):
    head = at_ref[0]
    vg = (g_ref[head] - x_ref[0]).astype(BF16)
    vu = (u_ref[head] - x_ref[1]).astype(BF16)
    vd = (d_ref[head] - x_ref[2]).astype(BF16)
    step = 256
    for t in range(0, q_s.shape[0], step):
        q = q_s[t : t + step, :]
        gate = mm(q, vg)
        hidden = (gate * jax.nn.sigmoid(gate) * mm(q, vu)).astype(BF16)
        yield slice(t, t + step), mm_nt(hidden, vd).astype(BF16)


def first_kernel(at_ref, q_ref, x_ref, g_ref, u_ref, d_ref, o_ref, q_s):
    query_rows(at_ref, q_ref, q_s)
    for rows, o in query_chunks(at_ref, q_s, x_ref, g_ref, u_ref, d_ref):
        o_ref[rows, :] = o


def second_kernel(at_ref, q_ref, x_ref, g_ref, u_ref, d_ref, p_ref, y_ref, z_ref, q_s, o_s):
    width = q_s.shape[1]
    query_rows(at_ref, q_ref, q_s)
    for rows, o in query_chunks(at_ref, q_s, x_ref, g_ref, u_ref, d_ref):
        o_s[rows, :] = o
    block = q_s.shape[0] // 8
    for h in range(2):

        @pl.when(at_ref[0] == h)
        def _():
            for dy in range(2):
                for dz in range(4):
                    rows = pl.ds((dy * 4 + dz) * block, block)
                    to_y, to_z = pl.ds(dz * block, block), pl.ds(dy * block, block)
                    for at, ref in ((h, o_s), (1 - h, p_ref)):
                        columns = pl.ds(at * width, width)
                        y_ref[dy, to_y, columns] = ref[rows, :]
                        z_ref[dz, to_z, columns] = ref[rows, :]


def first_query(at, queries, x, *weights):
    rows, width = queries.shape[0], x.shape[1]
    scratch = [pltpu.VMEM((rows, width), BF16)]
    shape = jax.ShapeDtypeStruct((rows, width), BF16)
    return call(first_kernel, "first_query", shape, scratch, at, queries, x, *weights)


def second_query(at, queries, x, gate, up, down, first):
    rows, width = first.shape
    scratch = [pltpu.VMEM((rows, width), BF16)] * 2
    shapes = [jax.ShapeDtypeStruct((n, rows // n, 2 * width), BF16) for n in (2, 4)]
    return call(second_kernel, "second_query", shapes, scratch, at, queries, x, gate, up, down, first)


def swap(a, axis):
    return lax.ppermute(a, axis, [(0, 1), (1, 0)])


def ring(a, shift):
    return lax.ppermute(a, "z", [(i, (i + shift) % 4) for i in range(4)])


def plane_scatter(a):
    return jnp.sum(lax.all_to_all(a, PLANE, 0, 0, tiled=True), axis=0)


def plane_gather(a):
    same = jnp.broadcast_to(a[None], (SHARDS,) + a.shape)
    return lax.all_to_all(same, PLANE, 0, 0, tiled=True)


def along_z(parts, split_parts):
    two_up, two_down, join = split_parts(parts[2])
    up, down = ring(two_up, 1), ring(two_down, -1)
    one_up, one_down, _ = split_parts(parts[1])
    three_up, three_down, _ = split_parts(parts[3])
    one = ring(join(one_up + up, one_down), 1)
    three = ring(join(three_up, three_down + down), -1)
    return parts[0] + one + three


def z_first(by_z, weight):
    parts = [mm(o, weight) for o in by_z]
    half = by_z.shape[1] // 2
    split_parts = lambda a: (a[:half], a[half:], lambda u, d: jnp.concatenate([u, d], axis=0))
    a = along_z(parts, split_parts)
    return a[:half] + swap(a[half:], "yl")


def y_first(by_y, weight):
    far = swap(mm(by_y[1], weight), "yl")
    b = mm(by_y[0], weight) + far
    b = b.reshape(4, -1, b.shape[1])
    half = b.shape[1] // 2
    split_parts = lambda a: (a[:half], a[half:], lambda u, d: jnp.concatenate([u, d], axis=0))
    return along_z([b[d] for d in range(4)], split_parts)


def project_scatter(by_y, by_z, weight):
    cuts = [0]
    for share in SHARES:
        cuts.append(cuts[-1] + share * weight.shape[1] // sum(SHARES))
    pieces = [weight[:, i:j] for i, j in zip(cuts, cuts[1:])]
    right = [y_first(by_y, w) for w in pieces[2:]]
    left = [z_first(by_z, w) for w in pieces[:2]]
    return jnp.concatenate(left + right, axis=1)


def body(keys, queries, values, rates, gate, up, down, out_weight):
    core, yl, z = (lax.axis_index(name).astype(jnp.int32) for name in ("core", "yl", "z"))
    mine, other = jnp.stack([core, yl, z]), jnp.stack([1 - core, yl, z])
    weights = (gate, up, down)
    theirs = head_grads(other, keys, values, rates.T, *weights)
    received = swap(theirs, "core")
    ours = head_grads(mine, keys, values, rates.T, *weights)
    whole = plane_gather(plane_scatter(ours + received))
    x_mine = newton(whole)
    x_other = swap(x_mine, "core")
    o_mine = first_query(mine, queries, x_mine, *weights)
    by_y, by_z = second_query(other, queries, x_other, *weights, o_mine)
    return project_scatter(by_y, by_z, out_weight).astype(BF16)


def solution(mesh):
    fine = Mesh(mesh.devices.reshape(2, 4, 4, 2, 2), AXES)
    ctx, head = ("x", "yh", "core"), ("yl", "z")
    in_specs = (
        P(ctx, head),
        P(ctx, head),
        P(ctx, head),
        P(ctx, head),
        P(head, None, None),
        P(head, None, None),
        P(head, None, None),
        P(head, None),
    )
    out_specs = P(ctx + head, None)
    return jax.shard_map(body, mesh=fine, in_specs=in_specs, out_specs=out_specs, check_vma=False)
```

time: 217 us -> 227 us (1.046)
  Pallas kernels: 49.1 us -> 29.8 us
  waiting for transfers between devices: 63.8 us -> 82 us
  starting transfers between devices: 14.6 us -> 23.5 us
  local copies, waits for them, and re-layouts: 2.64 us -> 7.53 us
    ppermute x4 -> x6, waiting for transfers between devices: 5.95 us -> 34.3 us  [swap(): return lax.ppermute(a, axis, [(0, 1), (1, 0)])]
    pallas_call x4, Pallas kernels: 27.3 us -> 11.2 us  [call(): pl.pallas_call(kernel, out_shape=outs, in_specs=specs, out_specs=jax.tree...]
    ppermute x8 -> x16, waiting for transfers between devices: 57.9 us -> 47.7 us  [ring(): return lax.ppermute(a, 'z', [(i, (i + shift) % 4) for i in range(4)])]
    ppermute x8 -> x16, starting transfers between devices: 13.1 us -> 20.5 us  [ring(): return lax.ppermute(a, 'z', [(i, (i + shift) % 4) for i in range(4)])]
    unnamed x4 -> x26, local copies, waits for them, and re-layouts: 0.01 us -> 7.19 us
    pallas_call x1, Pallas kernels: 21.8 us -> 18.6 us  [newton(): pl.pallas_call(newton_kernel, out_shape=jax.ShapeDtypeStruct(shape, F32),...]
    dot_general x6 -> x12, matrix products: 6.32 us -> 6.27 us  [mm(): return jnp.dot(a, b, preferred_element_type=F32)]
  transfers between devices with their start and end apart: 12 -> 22, of which waited for: 7 -> 11; matrix products, arithmetic and copies ran while one was open for 3% -> 2% of each run, Pallas kernels for 6% -> 2%
where the time goes in v1:
time: 227 us
  waiting for transfers between devices  82 us (36%)
  blocking collectives  73.4 us (32%)
  Pallas kernels  29.8 us (13%)
  starting transfers between devices  23.5 us (10%)
  local copies, waits for them, and re-layouts  7.53 us (3%)
  matrix products  6.27 us (3%)
  other arithmetic  4.01 us (2%)
    ppermute x16, waiting for transfers between devices, ring(): return lax.ppermute(a, 'z', [(i, (i + shift) % 4) for i in range(4)])  47.7 us
    all_to_all x1, blocking collectives, plane_scatter(): return jnp.sum(lax.all_to_all(a, PLANE, 0, 0, tiled=True), axis=0)  39.4 us
    ppermute x6, waiting for transfers between devices, swap(): return lax.ppermute(a, axis, [(0, 1), (1, 0)])  34.3 us
    all_to_all x1, blocking collectives, plane_gather(): return lax.all_to_all(same, PLANE, 0, 0, tiled=True)  34 us
    ppermute x16, starting transfers between devices, ring(): return lax.ppermute(a, 'z', [(i, (i + shift) % 4) for i in range(4)])  20.5 us
    pallas_call x1, Pallas kernels, newton(): pl.pallas_call(newton_kernel, out_shape=jax.ShapeDtypeStruct(shape, F32),...  18.6 us
    pallas_call x4, Pallas kernels, call(): pl.pallas_call(kernel, out_shape=outs, in_specs=specs, out_specs=jax.tree...  11.2 us
    unnamed x26, local copies, waits for them, and re-layouts  7.19 us
  transfers between devices with their start and end apart: 22, of which 11 were waited for; matrix products, arithmetic and copies ran while one was open for 2% of the time, Pallas kernels for 2%

profile of v1, /device:TPU:0, one launch (start us, length us, event | category | flops | bytes accessed | tf_op | source)
XLA Modules:
  0.0 227.0 jit_solution(12731487968622611821)
XLA Ops:
  0.1 1.4 copy-done
  1.5 1.4 copy-done.2
  2.9 1.4 copy-done.4
  5.5 1.1 copy-done.9
  7.2 3.4 %head_grads.3 = f32[8,3,40,640]{3,2,1,0:T(8,128)S(1)} custom-call(s32[3]{0:T(128)S(1)} %add_add_fusion.head_ref.at_ref, bf16[512,640]{1,0:T(8,128)(2,1)S(1)} %copy-done.7, bf16[512,640]{1,0:T(8,128)(2,1)S(1)} %copy-done.9, f32[2,512]{1,0:T(2,128)S(1)} %bitcast.35, f32[2,320,640]{2,1,0:T(8,128)S(1)} %copy-done, f32[2,320,640]{2,1,0:T(8,128)S(1)} %copy-done.2, ...), custom_call_target="tpu_custom_call" | custom-call | tf_op jit(solution)/shard_map/head_grads/pallas_call | solution.py:70
  10.8 3.1 %head_grads.2 = f32[8,3,40,640]{3,2,1,0:T(8,128)S(1)} custom-call(s32[3]{0:T(128)S(1)} %add_add_fusion.1.head_ref.at_ref, bf16[512,640]{1,0:T(8,128)(2,1)S(1)} %copy-done.8, bf16[512,640]{1,0:T(8,128)(2,1)S(1)} %copy-done.9, f32[2,512]{1,0:T(2,128)S(1)} %bitcast.36, f32[2,320,640]{2,1,0:T(8,128)S(1)} %copy-done.1, f32[2,320,640]{2,1,0:T(8,128)S(1)} %copy-done.2, ...), custom_call_target="tpu_custom_call" | custom-call | tf_op jit(solution)/shard_map/head_grads/pallas_call | solution.py:70
  13.9 1.4 collective-permute-done
  15.7 39.4 %all_to_all.10 = f32[8,3,40,640]{3,2,1,0:T(8,128)} all-to-all(f32[8,3,40,640]{3,2,1,0:T(8,128)S(1)} %add.63), channel_id=1, replica_groups=mesh['yl'=2,'z'=4,'x'=4,'yh'=2,'core'=2] {'x','yh'}, dimensions={0} | all-to-all | bytes 4915200 | tf_op jit(solution)/shard_map/all_to_all | solution.py:219
  55.1 1.9 reduce_sum.9
  57.1 34.0 %all_to_all.11.g_ref = f32[8,3,40,640]{3,2,1,0:T(8,128)S(1)} all-to-all(f32[8,3,40,640]{3,2,1,0:T(8,128)S(1)} %broadcast_in_dim.2), channel_id=1, replica_groups=mesh['yl'=2,'z'=4,'x'=4,'yh'=2,'core'=2] {'x','yh'}, dimensions={0} | all-to-all | bytes 4915200 | tf_op jit(solution)/shard_map/all_to_all | solution.py:224
  91.1 18.6 %newton.1.x_ref = f32[3,320,640]{2,1,0:T(8,128)S(1)} custom-call(f32[8,3,40,640]{3,2,1,0:T(8,128)S(1)} %all_to_all.11.g_ref), custom_call_target="tpu_custom_call" | custom-call | tf_op jit(solution)/shard_map/newton/pallas_call | solution.py:136
  109.9 2.2 first_query.1.p_ref
  112.1 2.4 %collective-permute-done.1.x_ref = f32[3,320,640]{2,1,0:T(8,128)S(1)} collective-permute-done((f32[3,320,640]{2,1,0:T(8,128)S(1)}, f32[3,320,640]{2,1,0:T(8,128)S(1)}, u32[]{:S(2)}, u32[]{:S(2)}) %collective-permute-start.1) | collective-permute-done | bytes 2457632 | tf_op jit(solution)/shard_map/ppermute | solution.py:211
  114.5 2.5 %second_query.1 = (bf16[2,256,640]{2,1,0:T(8,128)(2,1)S(1)}, bf16[4,128,640]{2,1,0:T(8,128)(2,1)S(1)}) custom-call(s32[3]{0:T(128)S(1)} %add_add_fusion.head_ref.at_ref, bf16[512,640]{1,0:T(8,128)(2,1)S(1)} %copy-done.6, f32[3,320,640]{2,1,0:T(8,128)S(1)} %collective-permute-done.1.x_ref, f32[2,320,640]{2,1,0:T(8,128)S(1)} %copy-done.1, ...), custom_call_target="tpu_custom_call" | custom-call | tf_op jit(solution)/shard_map/second_query/pallas_call | solution.py:70
  119.5 2.0 collective-permute-start.7
  122.7 2.0 collective-permute-start.2
  124.7 1.3 collective-permute-start.4
  128.2 3.9 %collective-permute-done.7 = f32[64,1280]{1,0:T(8,128)S(1)} collective-permute-done((f32[64,1280]{1,0:T(8,128)S(1)}, f32[64,1280]{1,0:T(8,128)S(1)}, u32[]{:S(2)}, u32[]{:S(2)}) %collective-permute-start.7) | collective-permute-done | bytes 327712 | tf_op jit(solution)/shard_map/ppermute | solution.py:215
  133.0 10.6 %collective-permute-done.9 = f32[64,1280]{1,0:T(8,128)S(1)} collective-permute-done((f32[64,1280]{1,0:T(8,128)S(1)}, f32[64,1280]{1,0:T(8,128)S(1)}, u32[]{:S(2)}, u32[]{:S(2)}) %collective-permute-start.9) | collective-permute-done | bytes 327712 | tf_op jit(solution)/shard_map/ppermute | solution.py:215
  143.6 1.6 collective-permute-start.8
  145.3 1.7 collective-permute-start.10
  147.8 25.9 %collective-permute-done.17 = f32[256,896]{1,0:T(8,128)S(1)} collective-permute-done((f32[256,896]{1,0:T(8,128)S(1)}, f32[256,896]{1,0:T(8,128)S(1)}, u32[]{:S(2)}, u32[]{:S(2)}) %collective-permute-start.17) | collective-permute-done | bytes 917536 | tf_op jit(solution)/shard_map/ppermute | solution.py:211
  173.7 1.7 collective-permute-start.5
  177.8 4.4 %collective-permute-done.18 = f32[32,896]{1,0:T(8,128)S(1)} collective-permute-done((f32[32,896]{1,0:T(8,128)S(1)}, f32[32,896]{1,0:T(8,128)S(1)}, u32[]{:S(2)}, u32[]{:S(2)}) %collective-permute-start.18) | collective-permute-done | bytes 114720 | tf_op jit(solution)/shard_map/ppermute | solution.py:215
  182.3 1.1 collective-permute-start.20
  183.4 13.2 %collective-permute-done.20 = f32[32,896]{1,0:T(8,128)S(1)} collective-permute-done((f32[32,896]{1,0:T(8,128)S(1)}, f32[32,896]{1,0:T(8,128)S(1)}, u32[]{:S(2)}, u32[]{:S(2)}) %collective-permute-start.20) | collective-permute-done | bytes 114720 | tf_op jit(solution)/shard_map/ppermute | solution.py:215
  197.1 2.8 %collective-permute-start.21 = (f32[64,896]{1,0:T(8,128)S(1)}, f32[64,896]{1,0:T(8,128)S(1)}, u32[]{:S(2)}, u32[]{:S(2)}) collective-permute-start(f32[64,896]{1,0:T(8,128)S(1)} %pad_maximum_fusion.8), channel_id=1, source_target_pairs={{0,48},{16,0},{32,16},{48,32},{1,49},{17,1},{33,17},{49,33},{2,50}... | collective-permute-start | bytes 688136 | tf_op jit(solution)/shard_map/ppermute | solution.py:215
  200.8 6.3 %collective-permute-done.13 = f32[32,1152]{1,0:T(8,128)S(1)} collective-permute-done((f32[32,1152]{1,0:T(8,128)S(1)}, f32[32,1152]{1,0:T(8,128)S(1)}, u32[]{:S(2)}, u32[]{:S(2)}) %collective-permute-start.13) | collective-permute-done | bytes 147488 | tf_op jit(solution)/shard_map/ppermute | solution.py:215
  207.4 6.1 %collective-permute-done.15 = f32[32,1152]{1,0:T(8,128)S(1)} collective-permute-done((f32[32,1152]{1,0:T(8,128)S(1)}, f32[32,1152]{1,0:T(8,128)S(1)}, u32[]{:S(2)}, u32[]{:S(2)}) %collective-permute-start.15) | collective-permute-done | bytes 147488 | tf_op jit(solution)/shard_map/ppermute | solution.py:215
  213.6 3.3 %collective-permute-start.16 = (f32[64,1152]{1,0:T(8,128)S(1)}, f32[64,1152]{1,0:T(8,128)S(1)}, u32[]{:S(2)}, u32[]{:S(2)}) collective-permute-start(f32[64,1152]{1,0:T(8,128)S(1)} %pad_maximum_fusion.6), channel_id=1, source_target_pairs={{0,48},{16,0},{32,16},{48,32},{1,49},{17,1},{33,17},{49,33},{2,50}... | collective-permute-start | bytes 884744 | tf_op jit(solution)/shard_map/ppermute | solution.py:215
  218.3 3.2 %collective-permute-done.14 = f32[64,1152]{1,0:T(8,128)S(1)} collective-permute-done((f32[64,1152]{1,0:T(8,128)S(1)}, f32[64,1152]{1,0:T(8,128)S(1)}, u32[]{:S(2)}, u32[]{:S(2)}) %collective-permute-start.14) | collective-permute-done | bytes 294944 | tf_op jit(solution)/shard_map/ppermute | solution.py:215
  221.5 4.5 %collective-permute-done.6 = f32[64,1792]{1,0:T(8,128)S(1)} collective-permute-done((f32[64,1792]{1,0:T(8,128)S(1)}, f32[64,1792]{1,0:T(8,128)S(1)}, u32[]{:S(2)}, u32[]{:S(2)}) %collective-permute-start.6) | collective-permute-done | bytes 458784 | tf_op jit(solution)/shard_map/ppermute | solution.py:211
  (90 shorter events, 16.6 us)
Async XLA Ops:
  0.1 1.4 copy-start
  1.5 1.4 copy-start.2
  2.9 1.4 copy-start.4
  7.2 3.6 %copy-start.1 = (f32[2,320,640]{2,1,0:T(8,128)S(1)}, f32[2,320,640]{2,1,0:T(8,128)}, u32[]{:S(2)}) copy-start(f32[2,320,640]{2,1,0:T(8,128)} %g_ref.7) | copy-start | bytes 4915204
  7.2 3.6 %copy-start.8 = (bf16[512,640]{1,0:T(8,128)(2,1)S(1)}, bf16[512,640]{1,0:T(8,128)(2,1)}, u32[]{:S(2)}) copy-start(bf16[512,640]{1,0:T(8,128)(2,1)} %k_ref.3) | copy-start | bytes 1966084
  10.6 4.8 %collective-permute-start = (f32[8,3,40,640]{3,2,1,0:T(8,128)S(1)}, f32[8,3,40,640]{3,2,1,0:T(8,128)S(1)}, u32[]{:S(2)}, u32[]{:S(2)}) collective-permute-start(f32[8,3,40,640]{3,2,1,0:T(8,128)S(1)} %head_grads.3), channel_id=1, source_target_pairs={{0,1},{1,0},{2,3},{3,2},{4,5},{5,4},{6,7},{7,6},{8,9},{9,8},{10,11... | collective-permute-start | bytes 7372808 | tf_op jit(solution)/shard_map/ppermute | solution.py:211
  91.1 18.8 %copy-start.3 = (f32[2,320,640]{2,1,0:T(8,128)S(1)}, f32[2,320,640]{2,1,0:T(8,128)}, u32[]{:S(2)}) copy-start(f32[2,320,640]{2,1,0:T(8,128)} %u_ref.7) | copy-start | bytes 4915204
  91.1 18.8 %copy-start.5 = (f32[2,320,640]{2,1,0:T(8,128)S(1)}, f32[2,320,640]{2,1,0:T(8,128)}, u32[]{:S(2)}) copy-start(f32[2,320,640]{2,1,0:T(8,128)} %d_ref.7) | copy-start | bytes 4915204
  91.1 18.8 %copy-start.6 = (bf16[512,640]{1,0:T(8,128)(2,1)S(1)}, bf16[512,640]{1,0:T(8,128)(2,1)}, u32[]{:S(2)}) copy-start(bf16[512,640]{1,0:T(8,128)(2,1)} %q_ref.3) | copy-start | bytes 1966084
  109.7 4.8 %collective-permute-start.1 = (f32[3,320,640]{2,1,0:T(8,128)S(1)}, f32[3,320,640]{2,1,0:T(8,128)S(1)}, u32[]{:S(2)}, u32[]{:S(2)}) collective-permute-start(f32[3,320,640]{2,1,0:T(8,128)S(1)} %newton.1.x_ref), channel_id=1, source_target_pairs={{0,1},{1,0},{2,3},{3,2},{4,5},{5,4},{6,7},{7,6},{8,9},{9,8},{10,11... | collective-permute-start | bytes 7372808 | tf_op jit(solution)/shard_map/ppermute | solution.py:211
  109.9 7.1 %slice-start = ((s8[6553600]{0:T(1024)(128)(4,1)}), s8[4194304]{0:T(1024)(128)(4,1)S(1)}, s32[]{:S(2)}) async-start(s8[6553600]{0:T(1024)(128)(4,1)} %bitcast.37), calls=%async_computation.2 | async-start | bytes 8388608
  112.1 5.0 %slice-start.1 = ((s8[6553600]{0:T(1024)(128)(4,1)}), s8[2359296]{0:T(1024)(128)(4,1)S(1)}, s32[]{:S(2)}) async-start(s8[6553600]{0:T(1024)(128)(4,1)} %bitcast.37), calls=%async_computation.3 | async-start | bytes 4718592
  119.5 12.6 %collective-permute-start.7 = (f32[64,1280]{1,0:T(8,128)S(1)}, f32[64,1280]{1,0:T(8,128)S(1)}, u32[]{:S(2)}, u32[]{:S(2)}) collective-permute-start(f32[64,1280]{1,0:T(8,128)S(1)} %get-tuple-element.25), channel_id=1, source_target_pairs={{0,16},{16,32},{32,48},{48,0},{1,17},{17,33},{33,49},{49,1},{2,18}... | collective-permute-start | bytes 983048 | tf_op jit(solution)/shard_map/ppermute | solution.py:215
  122.7 22.6 %collective-permute-start.2 = (f32[64,1792]{1,0:T(8,128)S(1)}, f32[64,1792]{1,0:T(8,128)S(1)}, u32[]{:S(2)}, u32[]{:S(2)}) collective-permute-start(f32[64,1792]{1,0:T(8,128)S(1)} %get-tuple-element.15), channel_id=1, source_target_pairs={{0,16},{16,32},{32,48},{48,0},{1,17},{17,33},{33,49},{49,1},{2,18}... | collective-permute-start | bytes 1376264 | tf_op jit(solution)/shard_map/ppermute | solution.py:215
  124.7 22.4 %collective-permute-start.4 = (f32[64,1792]{1,0:T(8,128)S(1)}, f32[64,1792]{1,0:T(8,128)S(1)}, u32[]{:S(2)}, u32[]{:S(2)}) collective-permute-start(f32[64,1792]{1,0:T(8,128)S(1)} %get-tuple-element.16), channel_id=1, source_target_pairs={{0,48},{16,0},{32,16},{48,32},{1,49},{17,1},{33,17},{49,33},{2,50}... | collective-permute-start | bytes 1376264 | tf_op jit(solution)/shard_map/ppermute | solution.py:215
  126.1 17.5 %collective-permute-start.9 = (f32[64,1280]{1,0:T(8,128)S(1)}, f32[64,1280]{1,0:T(8,128)S(1)}, u32[]{:S(2)}, u32[]{:S(2)}) collective-permute-start(f32[64,1280]{1,0:T(8,128)S(1)} %get-tuple-element.26), channel_id=1, source_target_pairs={{0,48},{16,0},{32,16},{48,32},{1,49},{17,1},{33,17},{49,33},{2,50}... | collective-permute-start | bytes 983048 | tf_op jit(solution)/shard_map/ppermute | solution.py:215
  127.0 70.1 %collective-permute-start.12 = (f32[256,1152]{1,0:T(8,128)S(1)}, f32[256,1152]{1,0:T(8,128)S(1)}, u32[]{:S(2)}, u32[]{:S(2)}) collective-permute-start(f32[256,1152]{1,0:T(8,128)S(1)} %fusion.9), channel_id=1, source_target_pairs={{0,64},{64,0},{1,65},{65,1},{2,66},{66,2},{3,67},{67,3},{4,68},{68... | collective-permute-start | bytes 3538952 | tf_op jit(solution)/shard_map/ppermute | solution.py:211
  132.2 41.5 %collective-permute-start.17 = (f32[256,896]{1,0:T(8,128)S(1)}, f32[256,896]{1,0:T(8,128)S(1)}, u32[]{:S(2)}, u32[]{:S(2)}) collective-permute-start(f32[256,896]{1,0:T(8,128)S(1)} %fusion.19), channel_id=1, source_target_pairs={{0,64},{64,0},{1,65},{65,1},{2,66},{66,2},{3,67},{67,3},{4,68},{68... | collective-permute-start | bytes 2752520 | tf_op jit(solution)/shard_map/ppermute | solution.py:211
  143.6 32.4 %collective-permute-start.8 = (f32[128,1280]{1,0:T(8,128)S(1)}, f32[128,1280]{1,0:T(8,128)S(1)}, u32[]{:S(2)}, u32[]{:S(2)}) collective-permute-start(f32[128,1280]{1,0:T(8,128)S(1)} %pad_maximum_fusion.2), channel_id=1, source_target_pairs={{0,16},{16,32},{32,48},{48,0},{1,17},{17,33},{33,49},{49,1},{2,18}... | collective-permute-start | bytes 1966088 | tf_op jit(solution)/shard_map/ppermute | solution.py:215
  145.3 31.3 %collective-permute-start.10 = (f32[128,1280]{1,0:T(8,128)S(1)}, f32[128,1280]{1,0:T(8,128)S(1)}, u32[]{:S(2)}, u32[]{:S(2)}) collective-permute-start(f32[128,1280]{1,0:T(8,128)S(1)} %pad_maximum_fusion.3), channel_id=1, source_target_pairs={{0,48},{16,0},{32,16},{48,32},{1,49},{17,1},{33,17},{49,33},{2,50}... | collective-permute-start | bytes 1966088 | tf_op jit(solution)/shard_map/ppermute | solution.py:215
  147.2 66.4 %collective-permute-start.3 = (f32[128,1792]{1,0:T(8,128)S(1)}, f32[128,1792]{1,0:T(8,128)S(1)}, u32[]{:S(2)}, u32[]{:S(2)}) collective-permute-start(f32[128,1792]{1,0:T(8,128)S(1)} %pad_maximum_fusion), channel_id=1, source_target_pairs={{0,16},{16,32},{32,48},{48,0},{1,17},{17,33},{33,49},{49,1},{2,18}... | collective-permute-start | bytes 2752520 | tf_op jit(solution)/shard_map/ppermute | solution.py:215
  173.7 43.2 %collective-permute-start.5 = (f32[128,1792]{1,0:T(8,128)S(1)}, f32[128,1792]{1,0:T(8,128)S(1)}, u32[]{:S(2)}, u32[]{:S(2)}) collective-permute-start(f32[128,1792]{1,0:T(8,128)S(1)} %pad_maximum_fusion.1), channel_id=1, source_target_pairs={{0,48},{16,0},{32,16},{48,32},{1,49},{17,1},{33,17},{49,33},{2,50}... | collective-permute-start | bytes 2752520 | tf_op jit(solution)/shard_map/ppermute | solution.py:215
  175.9 6.3 %collective-permute-start.18 = (f32[32,896]{1,0:T(8,128)S(1)}, f32[32,896]{1,0:T(8,128)S(1)}, u32[]{:S(2)}, u32[]{:S(2)}) collective-permute-start(f32[32,896]{1,0:T(8,128)S(1)} %slice.203), channel_id=1, source_target_pairs={{0,16},{16,32},{32,48},{48,0},{1,17},{17,33},{33,49},{49,1},{2,18}... | collective-permute-start | bytes 344072 | tf_op jit(solution)/shard_map/ppermute | solution.py:215
  177.1 23.5 %collective-permute-start.11 = (f32[64,1280]{1,0:T(8,128)S(1)}, f32[64,1280]{1,0:T(8,128)S(1)}, u32[]{:S(2)}, u32[]{:S(2)}) collective-permute-start(f32[64,1280]{1,0:T(8,128)S(1)} %slice.193), channel_id=1, source_target_pairs={{0,64},{64,0},{1,65},{65,1},{2,66},{66,2},{3,67},{67,3},{4,68},{68... | collective-permute-start | bytes 983048 | tf_op jit(solution)/shard_map/ppermute | solution.py:211
  182.3 14.3 %collective-permute-start.20 = (f32[32,896]{1,0:T(8,128)S(1)}, f32[32,896]{1,0:T(8,128)S(1)}, u32[]{:S(2)}, u32[]{:S(2)}) collective-permute-start(f32[32,896]{1,0:T(8,128)S(1)} %get-tuple-element.20), channel_id=1, source_target_pairs={{0,48},{16,0},{32,16},{48,32},{1,49},{17,1},{33,17},{49,33},{2,50}... | collective-permute-start | bytes 344072 | tf_op jit(solution)/shard_map/ppermute | solution.py:215
  196.6 21.6 %collective-permute-start.19 = (f32[64,896]{1,0:T(8,128)S(1)}, f32[64,896]{1,0:T(8,128)S(1)}, u32[]{:S(2)}, u32[]{:S(2)}) collective-permute-start(f32[64,896]{1,0:T(8,128)S(1)} %pad_maximum_fusion.7), channel_id=1, source_target_pairs={{0,16},{16,32},{32,48},{48,0},{1,17},{17,33},{33,49},{49,1},{2,18}... | collective-permute-start | bytes 688136 | tf_op jit(solution)/shard_map/ppermute | solution.py:215
  197.1 21.1 %collective-permute-start.21 = (f32[64,896]{1,0:T(8,128)S(1)}, f32[64,896]{1,0:T(8,128)S(1)}, u32[]{:S(2)}, u32[]{:S(2)}) collective-permute-start(f32[64,896]{1,0:T(8,128)S(1)} %pad_maximum_fusion.8), channel_id=1, source_target_pairs={{0,48},{16,0},{32,16},{48,32},{1,49},{17,1},{33,17},{49,33},{2,50}... | collective-permute-start | bytes 688136 | tf_op jit(solution)/shard_map/ppermute | solution.py:215
  200.6 6.4 %collective-permute-start.13 = (f32[32,1152]{1,0:T(8,128)S(1)}, f32[32,1152]{1,0:T(8,128)S(1)}, u32[]{:S(2)}, u32[]{:S(2)}) collective-permute-start(f32[32,1152]{1,0:T(8,128)S(1)} %slice.196), channel_id=1, source_target_pairs={{0,16},{16,32},{32,48},{48,0},{1,17},{17,33},{33,49},{49,1},{2,18}... | collective-permute-start | bytes 442376 | tf_op jit(solution)/shard_map/ppermute | solution.py:215
  207.1 6.4 %collective-permute-start.15 = (f32[32,1152]{1,0:T(8,128)S(1)}, f32[32,1152]{1,0:T(8,128)S(1)}, u32[]{:S(2)}, u32[]{:S(2)}) collective-permute-start(f32[32,1152]{1,0:T(8,128)S(1)} %get-tuple-element.10), channel_id=1, source_target_pairs={{0,48},{16,0},{32,16},{48,32},{1,49},{17,1},{33,17},{49,33},{2,50}... | collective-permute-start | bytes 442376 | tf_op jit(solution)/shard_map/ppermute | solution.py:215
  213.5 7.9 %collective-permute-start.14 = (f32[64,1152]{1,0:T(8,128)S(1)}, f32[64,1152]{1,0:T(8,128)S(1)}, u32[]{:S(2)}, u32[]{:S(2)}) collective-permute-start(f32[64,1152]{1,0:T(8,128)S(1)} %pad_maximum_fusion.5), channel_id=1, source_target_pairs={{0,16},{16,32},{32,48},{48,0},{1,17},{17,33},{33,49},{49,1},{2,18}... | collective-permute-start | bytes 884744 | tf_op jit(solution)/shard_map/ppermute | solution.py:215
  213.6 7.9 %collective-permute-start.16 = (f32[64,1152]{1,0:T(8,128)S(1)}, f32[64,1152]{1,0:T(8,128)S(1)}, u32[]{:S(2)}, u32[]{:S(2)}) collective-permute-start(f32[64,1152]{1,0:T(8,128)S(1)} %pad_maximum_fusion.6), channel_id=1, source_target_pairs={{0,48},{16,0},{32,16},{48,32},{1,49},{17,1},{33,17},{49,33},{2,50}... | collective-permute-start | bytes 884744 | tf_op jit(solution)/shard_map/ppermute | solution.py:215
  217.5 8.6 %collective-permute-start.6 = (f32[64,1792]{1,0:T(8,128)S(1)}, f32[64,1792]{1,0:T(8,128)S(1)}, u32[]{:S(2)}, u32[]{:S(2)}) collective-permute-start(f32[64,1792]{1,0:T(8,128)S(1)} %slice.185), channel_id=1, source_target_pairs={{0,64},{64,0},{1,65},{65,1},{2,66},{66,2},{3,67},{67,3},{4,68},{68... | collective-permute-start | bytes 1376264 | tf_op jit(solution)/shard_map/ppermute | solution.py:211
  (3 other events, 2.9 us)

commit v2 on v1

v2 whole, which is shorter than its diff:
```python
import jax
import jax.numpy as jnp
from jax import lax
from jax.experimental import pallas as pl
from jax.experimental.pallas import tpu as pltpu
from jax.sharding import Mesh, PartitionSpec as P

NS_STEPS = 5
ns_a = 3.4445
ns_b = -4.775
ns_c = 2.0315
eps_value = 1e-06

AXES = ("yl", "z", "x", "yh", "core")
PLANE = ("x", "yh")
SHARDS = 8
TILE = 256
VMEM_LIMIT = 24 << 20
CUT = 3072
F32 = jnp.float32
BF16 = jnp.bfloat16


def mm(a, b):
    return jnp.dot(a, b, preferred_element_type=F32)


def mm_nt(a, b):
    return lax.dot_general(a, b, (((1,), (1,)), ((), ())), preferred_element_type=F32)


def call(kernel, name, outs, scratch, *operands):
    specs = [pl.BlockSpec(memory_space=pltpu.SMEM if a.dtype == jnp.int32 else pltpu.VMEM) for a in operands]
    return pl.pallas_call(
        kernel,
        out_shape=outs,
        in_specs=specs,
        out_specs=jax.tree.map(lambda _: pl.BlockSpec(memory_space=pltpu.VMEM), outs),
        scratch_shapes=scratch,
        compiler_params=pltpu.CompilerParams(vmem_limit_bytes=VMEM_LIMIT),
        name=name,
    )(*operands)


def out(shape, dtype):
    return jax.ShapeDtypeStruct(shape, dtype)


def sort_tokens_kernel(at_ref, k_ref, v_ref, r_ref, k_o, d_o, sent):
    width = k_o.shape[1]
    for h in range(2):

        @pl.when(at_ref[0] == h)
        def _():
            near, far = slice(h * width, (h + 1) * width), slice((1 - h) * width, (2 - h) * width)
            k_o[...] = k_ref[:, near]
            sent[:, :width] = k_ref[:, far].astype(F32)
            for head, columns in ((h, near), (1 - h, far)):
                rate = r_ref[head : head + 1, :].T
                d = (-rate * v_ref[:, columns].astype(F32)).astype(BF16)
                if head == h:
                    d_o[...] = d
                else:
                    sent[:, width:] = d.astype(F32)


def sort_tokens(at, keys, values, rates):
    shape = (keys.shape[0], keys.shape[1] // 2)
    shapes = [out(shape, BF16), out(shape, BF16), out(keys.shape, F32)]
    return call(sort_tokens_kernel, "sort_tokens", shapes, [], at, keys, values, rates)


def side_by_side(rows, r, block, width):
    top = (r * block) % (rows // 2)
    left = width * ((r * block) // (rows // 2))
    return slice(top, top + block), slice(left, left + width)


def sort_queries_kernel(at_ref, q_ref, q_o, sent):
    rows, width = q_o.shape
    block = rows // 8
    for h in range(2):

        @pl.when(at_ref[0] == h)
        def _():
            near, far = slice(h * width, (h + 1) * width), slice((1 - h) * width, (2 - h) * width)
            for r in range(8):
                row = ((at_ref[1] + r // 4) % 2) * 4 + (at_ref[2] + r % 4) % 4
                source = pl.ds(pl.multiple_of(row * block, block), block)
                q_o[r * block : (r + 1) * block, :] = q_ref[source, near]
                to_rows, to_columns = side_by_side(rows, r, block, width)
                sent[to_rows, to_columns] = q_ref[source, far].astype(F32)


def sort_queries(at, queries):
    rows, columns = queries.shape
    shapes = [out((rows, columns // 2), BF16), out((rows // 2, columns), F32)]
    return call(sort_queries_kernel, "sort_queries", shapes, [], at, queries)


def grads_of(k_ref, d_ref, w_ref, hk_s, dg_s, du_s):
    rows = k_ref.shape[0]
    wg, wu, wd = w_ref[0], w_ref[1], w_ref[2]
    step = 256
    for t in range(0, rows, step):
        at = slice(t, t + step)
        k = k_ref[at, :]
        gate = mm(k, wg)
        upper = mm(k, wu)
        dhid = mm(d_ref[at, :], wd)
        sig = jax.nn.sigmoid(gate)
        act = gate * sig
        hk_s[at, :] = (act * upper).astype(BF16)
        dg_s[at, :] = (dhid * upper * sig * (1.0 + gate * (1.0 - sig))).astype(BF16)
        du_s[at, :] = (dhid * act).astype(BF16)
    kt = k_ref[...].T
    dt = d_ref[...].T
    for m, (left, right) in enumerate(((kt, dg_s), (kt, du_s), (dt, hk_s))):
        yield m, mm(left, right[...])


def near_grads_kernel(at_ref, k_ref, d_ref, g_ref, u_ref, w_ref, o_ref, b_ref, f_s, hk_s, dg_s, du_s, sems):
    copies = [
        pltpu.make_async_copy(ref.at[at_ref[0]], f_s.at[m], sems.at[m]) for m, ref in enumerate((g_ref, u_ref, w_ref))
    ]
    for copy in copies:
        copy.start()
    for m, copy in enumerate(copies):
        copy.wait()
        b_ref[m] = f_s[m].astype(BF16)
    for m, grad in grads_of(k_ref, d_ref, b_ref, hk_s, dg_s, du_s):
        o_ref[m] = grad


def far_grads_kernel(came, b_ref, p_ref, o_ref, k_s, d_s, hk_s, dg_s, du_s):
    part = o_ref.shape[2]
    width = k_s.shape[1]
    k_s[...] = came[:, :width].astype(BF16)
    d_s[...] = came[:, width:].astype(BF16)
    for m, grad in grads_of(k_s, d_s, b_ref, hk_s, dg_s, du_s):
        for j in range(SHARDS):
            rows = slice(j * part, (j + 1) * part)
            o_ref[j, m] = grad[rows, :] + p_ref[m, rows, :]


def near_grads(at, k, d, gate, up, down):
    heads, width, hidden = gate.shape
    vmem, hbm = pl.BlockSpec(memory_space=pltpu.VMEM), pl.BlockSpec(memory_space=pltpu.HBM)
    shape = (3, width, hidden)
    return pl.pallas_call(
        near_grads_kernel,
        out_shape=[out(shape, F32), out(shape, BF16)],
        in_specs=[pl.BlockSpec(memory_space=pltpu.SMEM), vmem, vmem, hbm, hbm, hbm],
        out_specs=[vmem, vmem],
        scratch_shapes=[pltpu.VMEM(shape, F32)]
        + [pltpu.VMEM((k.shape[0], hidden), BF16)] * 3
        + [pltpu.SemaphoreType.DMA((3,))],
        compiler_params=pltpu.CompilerParams(vmem_limit_bytes=VMEM_LIMIT),
        name="near_grads",
    )(at, k, d, gate, up, down)


def far_grads(came, w, partial):
    heads, width, hidden = partial.shape
    rows = came.shape[0]
    scratch = [pltpu.VMEM((rows, width), BF16)] * 2 + [pltpu.VMEM((rows, hidden), BF16)] * 3
    shape = out((SHARDS, 3, width // SHARDS, hidden), F32)
    return call(far_grads_kernel, "far_grads", shape, scratch, came, w, partial)


def split(x):
    high = x.astype(BF16)
    return high, (x - high.astype(F32)).astype(BF16)


def packed(high, low):
    return jnp.concatenate([high, high, low], axis=1)


def mirrored(left, corner):
    at = left.shape[1]
    return jnp.concatenate([left, jnp.concatenate([left[at:].T, corner], axis=0)], axis=1)


def gram_of(xh, xl):
    a, b = packed(xh, xl), jnp.concatenate([xh, xl, xh], axis=1)
    return mirrored(mm_nt(a, b[:TILE]), mm_nt(a[TILE:], b[TILE:]))


def square_of(ah, al):
    a, b = packed(ah, al), jnp.concatenate([ah, al, ah], axis=0)
    return mirrored(mm(a, b[:, :TILE]), mm(a[TILE:], b[:, TILE:]))


def newton_kernel(at_ref, g_ref, wg_ref, wu_ref, wd_ref, v_ref, x_s, f_s, sems):
    copies = [
        pltpu.make_async_copy(ref.at[at_ref[0]], f_s.at[m], sems.at[m])
        for m, ref in enumerate((wg_ref, wu_ref, wd_ref))
    ]
    for copy in copies:
        copy.start()
    matrices, width, hidden = x_s.shape
    every = range(matrices)
    for m in every:
        grad = g_ref[:, m].reshape(width, hidden)
        total = jnp.sum(jnp.sum(grad * grad, axis=1, keepdims=True), axis=0, keepdims=True)
        x_s[m] = grad * lax.rsqrt(total + eps_value)

    def sweep(_, carry):
        xs = [x_s[m] for m in every]
        parts = [split(x) for x in xs]
        grams = [gram_of(*p) for p in parts]
        squares = [square_of(*split(g)) for g in grams]
        mixers = [split(ns_b * g + ns_c * q) for g, q in zip(grams, squares)]
        for m, x, (xh, xl), mixer in zip(every, xs, parts, mixers):
            x_s[m] = ns_a * x + mm(packed(*mixer), jnp.concatenate([xh, xl, xh], axis=0))
        return carry

    lax.fori_loop(0, NS_STEPS, sweep, 0)
    for m, copy in enumerate(copies):
        copy.wait()
        v_ref[m] = (f_s[m] - x_s[m]).astype(BF16)


def newton(at, grads, gate, up, down):
    shape = (grads.shape[1], grads.shape[0] * grads.shape[2], grads.shape[3])
    vmem, hbm = pl.BlockSpec(memory_space=pltpu.VMEM), pl.BlockSpec(memory_space=pltpu.HBM)
    return pl.pallas_call(
        newton_kernel,
        out_shape=out(shape, BF16),
        in_specs=[pl.BlockSpec(memory_space=pltpu.SMEM), vmem, hbm, hbm, hbm],
        out_specs=vmem,
        scratch_shapes=[pltpu.VMEM(shape, F32)] * 2 + [pltpu.SemaphoreType.DMA((3,))],
        compiler_params=pltpu.CompilerParams(vmem_limit_bytes=VMEM_LIMIT),
        name="newton",
    )(at, grads, gate, up, down)


def query_rows(q, v_ref):
    gate = mm(q, v_ref[0])
    hidden = (gate * jax.nn.sigmoid(gate) * mm(q, v_ref[1])).astype(BF16)
    return mm_nt(hidden, v_ref[2]).astype(BF16)


def far_query_kernel(came, v_ref, o_ref):
    width = came.shape[1] // 2
    for left in (0, width):
        columns = slice(left, left + width)
        o_ref[:, columns] = query_rows(came[:, columns].astype(BF16), v_ref).astype(F32)


def near_query_kernel(q_ref, v_ref, o_ref):
    half = q_ref.shape[0] // 2
    for top in (0, half):
        rows = slice(top, top + half)
        o_ref[rows, :] = query_rows(q_ref[rows, :], v_ref)


def join_kernel(at_ref, o_ref, came, y_ref, z_ref):
    rows, width = o_ref.shape
    block = rows // 8
    for h in range(2):

        @pl.when(at_ref[0] == h)
        def _():
            near, far = slice(h * width, (h + 1) * width), slice((1 - h) * width, (2 - h) * width)
            for dy in range(2):
                for dz in range(4):
                    r = dy * 4 + dz
                    to_y, to_z = pl.ds(dz * block, block), pl.ds(dy * block, block)
                    mine = o_ref[r * block : (r + 1) * block, :]
                    other = came[side_by_side(rows, r, block, width)].astype(BF16)
                    for columns, piece in ((near, mine), (far, other)):
                        y_ref[dy, to_y, columns] = piece
                        z_ref[dz, to_z, columns] = piece


def join(at, mine, came):
    rows, width = mine.shape
    shapes = [out((n, rows // n, 2 * width), BF16) for n in (2, 4)]
    return call(join_kernel, "join", shapes, [], at, mine, came)


def swap(a, axis):
    return lax.ppermute(a, axis, [(0, 1), (1, 0)])


def ring(a, shift):
    return lax.ppermute(a, "z", [(i, (i + shift) % 4) for i in range(4)])


def plane_scatter(a):
    return jnp.sum(lax.all_to_all(a, PLANE, 0, 0, tiled=True), axis=0)


def plane_gather(a):
    same = jnp.broadcast_to(a[None], (SHARDS,) + a.shape)
    return lax.all_to_all(same, PLANE, 0, 0, tiled=True)


def after(a, *others):
    return lax.optimization_barrier((a, others))[0]


def halves(a):
    half = a.shape[0] // 2
    return a[:half], a[half:]


def pass_two(a):
    up, down = halves(a)
    return ring(up, 1), ring(down, -1)


def pass_one(one, three, came):
    up, down = came
    one = jnp.concatenate([one[: up.shape[0]] + up, one[up.shape[0] :]], axis=0)
    three = jnp.concatenate([three[: up.shape[0]], three[up.shape[0] :] + down], axis=0)
    return (ring(one, 1), ring(three, -1)), (one, three)


def project_scatter(by_y, by_z, weight):
    wa, wb = weight[:, :CUT], weight[:, CUT:]
    b_far = mm(by_y[1], wb)
    b_came = swap(b_far, "yl")
    by_z = after(by_z, b_far)
    up, down = halves(by_z[2])
    a_came = ring(mm(up, wa), 1), ring(mm(down, wa), -1)
    a_came, a_sent = pass_one(mm(by_z[1], wa), mm(by_z[3], wa), a_came)
    b = mm(by_y[0], wb) + after(b_came, a_sent)
    b = b.reshape(4, -1, b.shape[1])
    b_came = pass_two(b[2])
    a = mm(by_z[0], wa) + sum(a_came)
    a, a_far = halves(a)
    a_came = swap(a_far, "yl")
    b_came, _ = pass_one(b[1], b[3], b_came)
    return jnp.concatenate([a + a_came, b[0] + sum(b_came)], axis=1)


def body(keys, queries, values, rates, gate, up, down, out_weight):
    at = jnp.stack([lax.axis_index(name).astype(jnp.int32) for name in ("core", "yl", "z")])
    weights = tuple(pltpu.with_memory_space_constraint(w, pltpu.HBM) for w in (gate, up, down))
    k, d, sent = sort_tokens(at, keys, values, rates.T)
    came = swap(sent, "core")
    partial, rounded = near_grads(at, k, d, *weights)
    q, q_sent = sort_queries(at, after(queries, partial))
    whole = plane_gather(plane_scatter(far_grads(came, rounded, partial)))
    q_came = swap(q_sent, "core")
    v = newton(at, whole, *weights)
    o_came = swap(call(far_query_kernel, "far_query", out(q_sent.shape, F32), [], q_came, v), "core")
    o = call(near_query_kernel, "near_query", out(q.shape, BF16), [], q, v)
    by_y, by_z = join(at, o, o_came)
    return project_scatter(by_y, by_z, out_weight).astype(BF16)


def solution(mesh):
    fine = Mesh(mesh.devices.reshape(2, 4, 4, 2, 2), AXES)
    ctx, head = ("x", "yh", "core"), ("yl", "z")
    in_specs = (
        P(ctx, head),
        P(ctx, head),
        P(ctx, head),
        P(ctx, head),
        P(head, None, None),
        P(head, None, None),
        P(head, None, None),
        P(head, None),
    )
    out_specs = P(ctx + head, None)
    return jax.shard_map(body, mesh=fine, in_specs=in_specs, out_specs=out_specs, check_vma=False)
```

time: 227 us -> 207 us (0.912)
  blocking collectives: 73.4 us -> 39.7 us
  waiting for transfers between devices: 82 us -> 98.8 us
  local copies, waits for them, and re-layouts: 7.53 us -> 4.61 us
  Pallas kernels: 29.8 us -> 32.4 us
    all_to_all x1 -> x0, blocking collectives: 34 us -> none  [plane_gather(): return lax.all_to_all(same, PLANE, 0, 0, tiled=True)]
    all_to_all x0 -> x1, waiting for transfers between devices: none -> 33.9 us  [plane_gather(): return lax.all_to_all(same, PLANE, 0, 0, tiled=True)]
    ppermute x16 -> x8, waiting for transfers between devices: 47.7 us -> 36.4 us  [ring(): return lax.ppermute(a, 'z', [(i, (i + shift) % 4) for i in range(4)])]
    ppermute x6 -> x5, waiting for transfers between devices: 34.3 us -> 28.6 us  [swap(): return lax.ppermute(a, axis, [(0, 1), (1, 0)])]
    pallas_call x1 -> x2, Pallas kernels: 18.6 us -> 24 us  [the longest x1 19.5 us: newton(): pl.pallas_call(newton_kernel, out_shape=out(shape, BF16), in_specs=[pl.Bl...]
    ppermute x16 -> x8, starting transfers between devices: 20.5 us -> 15.3 us  [ring(): return lax.ppermute(a, 'z', [(i, (i + shift) % 4) for i in range(4)])]
    unnamed x26 -> x12, local copies, waits for them, and re-layouts: 7.19 us -> 2.88 us
    all_to_all x0 -> x1, starting transfers between devices: none -> 3.75 us  [plane_gather(): return lax.all_to_all(same, PLANE, 0, 0, tiled=True)]
  transfers between devices with their start and end apart: 22 -> 14, of which waited for: 11 -> 8; matrix products, arithmetic and copies ran while one was open for 2% -> 3% of each run, Pallas kernels for 2% -> 13%
where the time goes in v2:
time: 207 us
  waiting for transfers between devices  98.8 us (48%)
  blocking collectives  39.7 us (19%)
  Pallas kernels  32.4 us (16%)
  starting transfers between devices  21.5 us (10%)
  matrix products  7.65 us (4%)
  local copies, waits for them, and re-layouts  4.61 us (2%)
  other arithmetic  2.27 us (1%)
    all_to_all x1, blocking collectives, plane_scatter(): return jnp.sum(lax.all_to_all(a, PLANE, 0, 0, tiled=True), axis=0)  39.7 us
    ppermute x8, waiting for transfers between devices, ring(): return lax.ppermute(a, 'z', [(i, (i + shift) % 4) for i in range(4)])  36.4 us
    all_to_all x1, waiting for transfers between devices, plane_gather(): return lax.all_to_all(same, PLANE, 0, 0, tiled=True)  33.9 us
    ppermute x5, waiting for transfers between devices, swap(): return lax.ppermute(a, axis, [(0, 1), (1, 0)])  28.6 us
    pallas_call x1, Pallas kernels, newton(): pl.pallas_call(newton_kernel, out_shape=out(shape, BF16), in_specs=[pl.Bl...  19.5 us
    ppermute x8, starting transfers between devices, ring(): return lax.ppermute(a, 'z', [(i, (i + shift) % 4) for i in range(4)])  15.3 us
    pallas_call x6, Pallas kernels, call(): pl.pallas_call(kernel, out_shape=outs, in_specs=specs, out_specs=jax.tree...  8.36 us
    dot_general x7, matrix products, mm(): return jnp.dot(a, b, preferred_element_type=F32)  7.65 us
  transfers between devices with their start and end apart: 14, of which 8 were waited for; matrix products, arithmetic and copies ran while one was open for 3% of the time, Pallas kernels for 13%

profile of v2, /device:TPU:0, one launch (start us, length us, event | category | flops | bytes accessed | tf_op | source)
XLA Modules:
  0.0 207.0 jit_solution(10988148171209965828)
XLA Ops:
  0.1 1.1 copy-done
  1.2 1.1 copy-done.1
  2.9 1.1 sort_tokens.1
  4.1 4.5 %near_grads.1 = (f32[3,320,640]{2,1,0:T(8,128)S(1)}, bf16[3,320,640]{2,1,0:T(8,128)(2,1)S(1)}) custom-call(s32[3]{0:T(128)S(1)} %pad_add_fusion.at_ref, bf16[512,320]{1,0:T(8,128)(2,1)S(1)} %get-tuple-element.17.k_ref, bf16[512,320]{1,0:T(8,128)(2,1)S(1)} %get-tuple-element.18.d_ref, f32[2,320,640]{2,1,0:T(8,128)} %wg_ref.1, f32[2,320,640]{2,1,0:T(8,128)} %wu_ref.1, ...), custom_call_target="tpu_custom_call" | custom-call | tf_op jit(solution)/shard_map/near_grads/pallas_call | solution.py:150
  8.7 2.3 %far_grads.1 = f32[8,3,40,640]{3,2,1,0:T(8,128)S(1)} custom-call(f32[512,640]{1,0:T(8,128)S(1)} %collective-permute-done.came, bf16[3,320,640]{2,1,0:T(8,128)(2,1)S(1)} %get-tuple-element.23.b_ref, f32[3,320,640]{2,1,0:T(8,128)S(1)} %get-tuple-element.19.p_ref), custom_call_target="tpu_custom_call" | custom-call | tf_op jit(solution)/shard_map/far_grads/pallas_call | solution.py:34
  11.0 39.7 %all_to_all.10 = f32[8,3,40,640]{3,2,1,0:T(8,128)S(1)} all-to-all(f32[8,3,40,640]{3,2,1,0:T(8,128)S(1)} %far_grads.1), channel_id=1, replica_groups=mesh['yl'=2,'z'=4,'x'=4,'yh'=2,'core'=2] {'x','yh'}, dimensions={0} | all-to-all | bytes 4915200 | tf_op jit(solution)/shard_map/all_to_all | solution.py:293
  50.8 1.6 broadcast_in_dim.2
  52.4 3.8 %all-to-all-start.1 = ((f32[8,3,40,640]{3,2,1,0:T(8,128)}), f32[8,3,40,640]{3,2,1,0:T(8,128)S(1)}, u32[]{:S(2)}, u32[]{:S(2)}) async-start(f32[8,3,40,640]{3,2,1,0:T(8,128)} %broadcast_in_dim.2), calls=%async_computation.1 | async-start | bytes 4915200 | tf_op jit(solution)/shard_map/all_to_all | solution.py:298
  56.2 1.5 sort_queries.1
  57.7 33.9 %all-to-all-done.1.g_ref = f32[8,3,40,640]{3,2,1,0:T(8,128)S(1)} async-done(((f32[8,3,40,640]{3,2,1,0:T(8,128)}), f32[8,3,40,640]{3,2,1,0:T(8,128)S(1)}, u32[]{:S(2)}, u32[]{:S(2)}) %all-to-all-start.1) | async-done | bytes 2457632 | tf_op jit(solution)/shard_map/all_to_all | solution.py:298
  91.6 19.5 %newton.1.v_ref = bf16[3,320,640]{2,1,0:T(8,128)(2,1)S(1)} custom-call(s32[3]{0:T(128)S(1)} %pad_add_fusion.at_ref, f32[8,3,40,640]{3,2,1,0:T(8,128)S(1)} %all-to-all-done.1.g_ref, f32[2,320,640]{2,1,0:T(8,128)} %wg_ref.1, f32[2,320,640]{2,1,0:T(8,128)} %wu_ref.1, f32[2,320,640]{2,1,0:T(8,128)} %wd_ref.1), custom_call_target="tpu_custom_call" | custom-call | tf_op jit(solution)/shard_map/newton/pallas_call | solution.py:228
  111.1 1.4 far_query.1
  112.6 1.3 near_query.1.o_ref
  115.4 2.7 %fusion.1 = f32[256,2048]{1,0:T(8,128)S(1)} fusion(bf16[640,5120]{1,0:T(8,128)(2,1)} %param.15, bf16[2,256,640]{2,1,0:T(8,128)(2,1)S(1)} %get-tuple-element.26), kind=kOutput, calls=%fused_computation.2 | convolution fusion | flops 671088640 | bytes 5046272 | tf_op jit(solution)/shard_map/dot_general | solution.py:25
  118.9 0.8 fusion.7
  119.7 2.0 collective-permute-start.3
  121.7 0.8 fusion.3
  122.5 2.2 %collective-permute-start.5 = (f32[64,3072]{1,0:T(8,128)S(1)}, f32[64,3072]{1,0:T(8,128)S(1)}, u32[]{:S(2)}, u32[]{:S(2)}) collective-permute-start(f32[64,3072]{1,0:T(8,128)S(1)} %fusion.3), channel_id=1, source_target_pairs={{0,48},{16,0},{32,16},{48,32},{1,49},{17,1},{33,17},{49,33},{2,50}... | collective-permute-start | bytes 2359304 | tf_op jit(solution)/shard_map/ppermute | solution.py:289
  124.7 0.8 fusion.9
  125.5 0.8 fusion.5
  126.3 15.2 %collective-permute-done.3 = f32[64,3072]{1,0:T(8,128)S(1)} collective-permute-done((f32[64,3072]{1,0:T(8,128)S(1)}, f32[64,3072]{1,0:T(8,128)S(1)}, u32[]{:S(2)}, u32[]{:S(2)}) %collective-permute-start.3) | collective-permute-done | bytes 786464 | tf_op jit(solution)/shard_map/ppermute | solution.py:289
  142.4 3.3 %collective-permute-start.6 = (f32[128,3072]{1,0:T(8,128)S(1)}, f32[128,3072]{1,0:T(8,128)S(1)}, u32[]{:S(2)}, u32[]{:S(2)}) collective-permute-start(f32[128,3072]{1,0:T(8,128)S(1)} %pad_maximum_fusion.1), channel_id=1, source_target_pairs={{0,48},{16,0},{32,16},{48,32},{1,49},{17,1},{33,17},{49,33},{2,50}... | collective-permute-start | bytes 4718600 | tf_op jit(solution)/shard_map/ppermute | solution.py:289
  145.7 20.3 %collective-permute-done.8 = f32[256,2048]{1,0:T(8,128)S(1)} collective-permute-done((f32[256,2048]{1,0:T(8,128)S(1)}, f32[256,2048]{1,0:T(8,128)S(1)}, u32[]{:S(2)}, u32[]{:S(2)}) %collective-permute-start.8) | collective-permute-done | bytes 2097184 | tf_op jit(solution)/shard_map/ppermute | solution.py:285
  166.0 1.0 convolution_add_fusion
  167.1 4.1 %collective-permute-start.11 = (f32[32,2048]{1,0:T(8,128)S(1)}, f32[32,2048]{1,0:T(8,128)S(1)}, u32[]{:S(2)}, u32[]{:S(2)}) collective-permute-start(f32[32,2048]{1,0:T(8,128)S(1)} %get-tuple-element.30), channel_id=1, source_target_pairs={{0,48},{16,0},{32,16},{48,32},{1,49},{17,1},{33,17},{49,33},{2,50}... | collective-permute-start | bytes 786440 | tf_op jit(solution)/shard_map/ppermute | solution.py:289
  171.2 0.8 fusion.11
  171.9 12.3 %collective-permute-done.11 = f32[32,2048]{1,0:T(8,128)S(1)} collective-permute-done((f32[32,2048]{1,0:T(8,128)S(1)}, f32[32,2048]{1,0:T(8,128)S(1)}, u32[]{:S(2)}, u32[]{:S(2)}) %collective-permute-start.11) | collective-permute-done | bytes 262176 | tf_op jit(solution)/shard_map/ppermute | solution.py:289
  185.0 3.3 %collective-permute-start.12 = (f32[64,2048]{1,0:T(8,128)S(1)}, f32[64,2048]{1,0:T(8,128)S(1)}, u32[]{:S(2)}, u32[]{:S(2)}) collective-permute-start(f32[64,2048]{1,0:T(8,128)S(1)} %pad_maximum_fusion.4), channel_id=1, source_target_pairs={{0,48},{16,0},{32,16},{48,32},{1,49},{17,1},{33,17},{49,33},{2,50}... | collective-permute-start | bytes 1572872 | tf_op jit(solution)/shard_map/ppermute | solution.py:289
  188.6 1.4 collective-permute-start.7
  190.0 8.4 %collective-permute-done.10 = f32[64,2048]{1,0:T(8,128)S(1)} collective-permute-done((f32[64,2048]{1,0:T(8,128)S(1)}, f32[64,2048]{1,0:T(8,128)S(1)}, u32[]{:S(2)}, u32[]{:S(2)}) %collective-permute-start.10) | collective-permute-done | bytes 524320 | tf_op jit(solution)/shard_map/ppermute | solution.py:289
  198.6 7.5 %collective-permute-done.7 = f32[64,3072]{1,0:T(8,128)S(1)} collective-permute-done((f32[64,3072]{1,0:T(8,128)S(1)}, f32[64,3072]{1,0:T(8,128)S(1)}, u32[]{:S(2)}, u32[]{:S(2)}) %collective-permute-start.7) | collective-permute-done | bytes 786464 | tf_op jit(solution)/shard_map/ppermute | solution.py:285
  206.2 0.9 pad_maximum_fusion.2
  (41 shorter events, 5.5 us)
Async XLA Ops:
  0.1 1.1 copy-start
  1.2 1.1 copy-start.1
  2.3 0.7 copy-start.3
  4.0 4.6 %collective-permute-start = (f32[512,640]{1,0:T(8,128)S(1)}, f32[512,640]{1,0:T(8,128)S(1)}, u32[]{:S(2)}, u32[]{:S(2)}) collective-permute-start(f32[512,640]{1,0:T(8,128)S(1)} %get-tuple-element.22), channel_id=1, source_target_pairs={{0,1},{1,0},{2,3},{3,2},{4,5},{5,4},{6,7},{7,6},{8,9},{9,8},{10,11... | collective-permute-start | bytes 3932168 | tf_op jit(solution)/shard_map/ppermute | solution.py:285
  52.4 3.8 %copy-start.2 = (bf16[512,640]{1,0:T(8,128)(2,1)S(1)}, bf16[512,640]{1,0:T(8,128)(2,1)}, u32[]{:S(2)}) copy-start(bf16[512,640]{1,0:T(8,128)(2,1)} %q_ref) | copy-start | bytes 1966084
  52.4 39.2 %all-to-all-start.1 = ((f32[8,3,40,640]{3,2,1,0:T(8,128)}), f32[8,3,40,640]{3,2,1,0:T(8,128)S(1)}, u32[]{:S(2)}, u32[]{:S(2)}) async-start(f32[8,3,40,640]{3,2,1,0:T(8,128)} %broadcast_in_dim.2), calls=%async_computation.1 | async-start | bytes 4915200 | tf_op jit(solution)/shard_map/all_to_all | solution.py:298
  57.7 53.3 %collective-permute-start.1 = (f32[256,640]{1,0:T(8,128)}, f32[256,640]{1,0:T(8,128)S(1)}, u32[]{:S(2)}, u32[]{:S(2)}) collective-permute-start(f32[256,640]{1,0:T(8,128)} %get-tuple-element.24), channel_id=1, source_target_pairs={{0,1},{1,0},{2,3},{3,2},{4,5},{5,4},{6,7},{7,6},{8,9},{9,8},{10,11... | collective-permute-start | bytes 1966088 | tf_op jit(solution)/shard_map/ppermute | solution.py:285
  91.6 27.3 %slice-start = ((s8[6553600]{0:T(1024)(128)(4,1)}), s8[4194304]{0:T(1024)(128)(4,1)S(1)}, s32[]{:S(2)}) async-start(s8[6553600]{0:T(1024)(128)(4,1)} %bitcast.26), calls=%async_computation.2 | async-start | bytes 8388608
  111.1 7.8 %slice-start.1 = ((s8[6553600]{0:T(1024)(128)(4,1)}), s8[2359296]{0:T(1024)(128)(4,1)S(1)}, s32[]{:S(2)}) async-start(s8[6553600]{0:T(1024)(128)(4,1)} %bitcast.26), calls=%async_computation.3 | async-start | bytes 4718592
  112.5 2.2 %collective-permute-start.2 = (f32[256,640]{1,0:T(8,128)S(1)}, f32[256,640]{1,0:T(8,128)S(1)}, u32[]{:S(2)}, u32[]{:S(2)}) collective-permute-start(f32[256,640]{1,0:T(8,128)S(1)} %far_query.1), channel_id=1, source_target_pairs={{0,1},{1,0},{2,3},{3,2},{4,5},{5,4},{6,7},{7,6},{8,9},{9,8},{10,11... | collective-permute-start | bytes 1966088 | tf_op jit(solution)/shard_map/ppermute | solution.py:285
  118.1 47.9 %collective-permute-start.8 = (f32[256,2048]{1,0:T(8,128)S(1)}, f32[256,2048]{1,0:T(8,128)S(1)}, u32[]{:S(2)}, u32[]{:S(2)}) collective-permute-start(f32[256,2048]{1,0:T(8,128)S(1)} %fusion.1), channel_id=1, source_target_pairs={{0,64},{64,0},{1,65},{65,1},{2,66},{66,2},{3,67},{67,3},{4,68},{68... | collective-permute-start | bytes 6291464 | tf_op jit(solution)/shard_map/ppermute | solution.py:285
  119.7 21.8 %collective-permute-start.3 = (f32[64,3072]{1,0:T(8,128)S(1)}, f32[64,3072]{1,0:T(8,128)S(1)}, u32[]{:S(2)}, u32[]{:S(2)}) collective-permute-start(f32[64,3072]{1,0:T(8,128)S(1)} %fusion.7), channel_id=1, source_target_pairs={{0,16},{16,32},{32,48},{48,0},{1,17},{17,33},{33,49},{49,1},{2,18}... | collective-permute-start | bytes 2359304 | tf_op jit(solution)/shard_map/ppermute | solution.py:289
  122.5 19.6 %collective-permute-start.5 = (f32[64,3072]{1,0:T(8,128)S(1)}, f32[64,3072]{1,0:T(8,128)S(1)}, u32[]{:S(2)}, u32[]{:S(2)}) collective-permute-start(f32[64,3072]{1,0:T(8,128)S(1)} %fusion.3), channel_id=1, source_target_pairs={{0,48},{16,0},{32,16},{48,32},{1,49},{17,1},{33,17},{49,33},{2,50}... | collective-permute-start | bytes 2359304 | tf_op jit(solution)/shard_map/ppermute | solution.py:289
  141.8 46.5 %collective-permute-start.4 = (f32[128,3072]{1,0:T(8,128)S(1)}, f32[128,3072]{1,0:T(8,128)S(1)}, u32[]{:S(2)}, u32[]{:S(2)}) collective-permute-start(f32[128,3072]{1,0:T(8,128)S(1)} %pad_maximum_fusion), channel_id=1, source_target_pairs={{0,16},{16,32},{32,48},{48,0},{1,17},{17,33},{33,49},{49,1},{2,18}... | collective-permute-start | bytes 4718600 | tf_op jit(solution)/shard_map/ppermute | solution.py:289
  142.4 45.9 %collective-permute-start.6 = (f32[128,3072]{1,0:T(8,128)S(1)}, f32[128,3072]{1,0:T(8,128)S(1)}, u32[]{:S(2)}, u32[]{:S(2)}) collective-permute-start(f32[128,3072]{1,0:T(8,128)S(1)} %pad_maximum_fusion.1), channel_id=1, source_target_pairs={{0,48},{16,0},{32,16},{48,32},{1,49},{17,1},{33,17},{49,33},{2,50}... | collective-permute-start | bytes 4718600 | tf_op jit(solution)/shard_map/ppermute | solution.py:289
  167.1 17.2 %collective-permute-start.11 = (f32[32,2048]{1,0:T(8,128)S(1)}, f32[32,2048]{1,0:T(8,128)S(1)}, u32[]{:S(2)}, u32[]{:S(2)}) collective-permute-start(f32[32,2048]{1,0:T(8,128)S(1)} %get-tuple-element.30), channel_id=1, source_target_pairs={{0,48},{16,0},{32,16},{48,32},{1,49},{17,1},{33,17},{49,33},{2,50}... | collective-permute-start | bytes 786440 | tf_op jit(solution)/shard_map/ppermute | solution.py:289
  171.2 13.5 %collective-permute-start.9 = (f32[32,2048]{1,0:T(8,128)S(1)}, f32[32,2048]{1,0:T(8,128)S(1)}, u32[]{:S(2)}, u32[]{:S(2)}) collective-permute-start(f32[32,2048]{1,0:T(8,128)S(1)} %get-tuple-element.32), channel_id=1, source_target_pairs={{0,16},{16,32},{32,48},{48,0},{1,17},{17,33},{33,49},{49,1},{2,18}... | collective-permute-start | bytes 786440 | tf_op jit(solution)/shard_map/ppermute | solution.py:289
  184.7 13.7 %collective-permute-start.10 = (f32[64,2048]{1,0:T(8,128)S(1)}, f32[64,2048]{1,0:T(8,128)S(1)}, u32[]{:S(2)}, u32[]{:S(2)}) collective-permute-start(f32[64,2048]{1,0:T(8,128)S(1)} %pad_maximum_fusion.3), channel_id=1, source_target_pairs={{0,16},{16,32},{32,48},{48,0},{1,17},{17,33},{33,49},{49,1},{2,18}... | collective-permute-start | bytes 1572872 | tf_op jit(solution)/shard_map/ppermute | solution.py:289
  185.0 13.5 %collective-permute-start.12 = (f32[64,2048]{1,0:T(8,128)S(1)}, f32[64,2048]{1,0:T(8,128)S(1)}, u32[]{:S(2)}, u32[]{:S(2)}) collective-permute-start(f32[64,2048]{1,0:T(8,128)S(1)} %pad_maximum_fusion.4), channel_id=1, source_target_pairs={{0,48},{16,0},{32,16},{48,32},{1,49},{17,1},{33,17},{49,33},{2,50}... | collective-permute-start | bytes 1572872 | tf_op jit(solution)/shard_map/ppermute | solution.py:289
  188.6 17.5 %collective-permute-start.7 = (f32[64,3072]{1,0:T(8,128)S(1)}, f32[64,3072]{1,0:T(8,128)S(1)}, u32[]{:S(2)}, u32[]{:S(2)}) collective-permute-start(f32[64,3072]{1,0:T(8,128)S(1)} %slice.120), channel_id=1, source_target_pairs={{0,64},{64,0},{1,65},{65,1},{2,66},{66,2},{3,67},{67,3},{4,68},{68... | collective-permute-start | bytes 2359304 | tf_op jit(solution)/shard_map/ppermute | solution.py:285

commit v3 on v2

--- a/solution.py
+++ b/solution.py
@@ -1,3 +1,5 @@
+import functools
+
 import jax
 import jax.numpy as jnp
 from jax import lax
@@ -15,8 +17,8 @@
 PLANE = ("x", "yh")
 SHARDS = 8
 TILE = 256
-VMEM_LIMIT = 24 << 20
-CUT = 3072
+VMEM_LIMIT = 16 << 20
+CUTS = (2048, 3968)
 F32 = jnp.float32
 BF16 = jnp.bfloat16
 
@@ -256,29 +258,61 @@
         o_ref[rows, :] = query_rows(q_ref[rows, :], v_ref)
 
 
-def join_kernel(at_ref, o_ref, came, y_ref, z_ref):
+def join_kernel(at_ref, o_ref, came, y_ref, z_ref, *sent):
     rows, width = o_ref.shape
     block = rows // 8
-    for h in range(2):
-
-        @pl.when(at_ref[0] == h)
-        def _():
-            near, far = slice(h * width, (h + 1) * width), slice((1 - h) * width, (2 - h) * width)
-            for dy in range(2):
-                for dz in range(4):
-                    r = dy * 4 + dz
-                    to_y, to_z = pl.ds(dz * block, block), pl.ds(dy * block, block)
-                    mine = o_ref[r * block : (r + 1) * block, :]
-                    other = came[side_by_side(rows, r, block, width)].astype(BF16)
-                    for columns, piece in ((near, mine), (far, other)):
+    for dy in range(2):
+        for dz in range(4):
+            r = dy * 4 + dz
+            to_y, to_z = pl.ds(dz * block, block), pl.ds(dy * block, block)
+            mine = o_ref[r * block : (r + 1) * block, :]
+            other = came[side_by_side(rows, r, block, width)]
+            if dz > 0:
+                sent[dz - 1][to_z, :width] = mine.astype(F32)
+                sent[dz - 1][to_z, width:] = other
+            for h in range(2):
+
+                @pl.when(at_ref[0] == h)
+                def _():
+                    near, far = slice(h * width, (h + 1) * width), slice((1 - h) * width, (2 - h) * width)
+                    for columns, piece in ((near, mine), (far, other.astype(BF16))):
                         y_ref[dy, to_y, columns] = piece
                         z_ref[dz, to_z, columns] = piece
 
 
 def join(at, mine, came):
     rows, width = mine.shape
-    shapes = [out((n, rows // n, 2 * width), BF16) for n in (2, 4)]
+    shapes = [out((n, rows // n, 2 * width), BF16) for n in (2, 4)] + [out((rows // 4, 2 * width), F32)] * 3
     return call(join_kernel, "join", shapes, [], at, mine, came)
+
+
+def gathered_kernel(counts, o_ref, w_ref, *refs):
+    lefts, pieces, (near_ref, far_ref) = refs[:3], list(refs[3:-2]), refs[-2:]
+    total = mm(o_ref[0], w_ref[...])
+    for left, count in zip(lefts, counts):
+        right = jnp.concatenate([pieces.pop(0)[...].astype(BF16) for _ in range(count)], axis=0)
+        total = total + mm(left[...].astype(BF16), right)
+    half = near_ref.shape[0]
+    near_ref[...] = total[:half]
+    far_ref[...] = total[half:]
+
+
+def gathered_product(by_z, weight, lefts, sources):
+    rows, depth = by_z.shape[1:]
+    pieces = [piece for source in sources for piece in source]
+    columns, step = pieces[0].shape[1], 512
+    whole = pl.BlockSpec((rows, depth), lambda n: (0, 0))
+    specs = [pl.BlockSpec((1, rows, depth), lambda n: (0, 0, 0)), pl.BlockSpec((depth, step), lambda n: (0, n))]
+    specs += [whole] * len(lefts) + [pl.BlockSpec((a.shape[0], step), lambda n: (0, n)) for a in pieces]
+    return pl.pallas_call(
+        functools.partial(gathered_kernel, [len(source) for source in sources]),
+        out_shape=[out((rows // 2, columns), F32)] * 2,
+        grid=(columns // step,),
+        in_specs=specs,
+        out_specs=[pl.BlockSpec((rows // 2, step), lambda n: (0, n))] * 2,
+        compiler_params=pltpu.CompilerParams(vmem_limit_bytes=VMEM_LIMIT),
+        name="gathered_product",
+    )(by_z, weight, *lefts, *pieces)
 
 
 def swap(a, axis):
@@ -319,22 +353,35 @@
     return (ring(one, 1), ring(three, -1)), (one, three)
 
 
-def project_scatter(by_y, by_z, weight):
-    wa, wb = weight[:, :CUT], weight[:, CUT:]
+def own_part(weight):
+    depth = weight.shape[0]
+    half = lax.dynamic_slice_in_dim(weight[:, : CUTS[0]], lax.axis_index("core") * (depth // 2), depth // 2)
+    return half.astype(F32)
+
+
+def swapped(parts):
+    return [swap(part, "core") for part in parts]
+
+
+def project_scatter(by_y, by_z, sent, weight, sources):
+    wa, wb = weight[:, CUTS[0] : CUTS[1]], weight[:, CUTS[1] :]
     b_far = mm(by_y[1], wb)
     b_came = swap(b_far, "yl")
+    sent = after(sent, b_far)
+    lefts = [ring(o, d) for o, d in zip(sent, (1, 2, -1))]
     by_z = after(by_z, b_far)
-    up, down = halves(by_z[2])
-    a_came = ring(mm(up, wa), 1), ring(mm(down, wa), -1)
+    a_came = pass_two(mm(by_z[2], wa))
     a_came, a_sent = pass_one(mm(by_z[1], wa), mm(by_z[3], wa), a_came)
     b = mm(by_y[0], wb) + after(b_came, a_sent)
     b = b.reshape(4, -1, b.shape[1])
     b_came = pass_two(b[2])
-    a = mm(by_z[0], wa) + sum(a_came)
+    c, c_far = gathered_product(by_z, weight, after(lefts, b), sources)
+    c_came = swap(c_far, "yl")
+    b_came, b_sent = pass_one(b[1], b[3], after(b_came, c_far))
+    a = mm(by_z[0], wa) + sum(after(a_came, b_sent))
     a, a_far = halves(a)
     a_came = swap(a_far, "yl")
-    b_came, _ = pass_one(b[1], b[3], b_came)
-    return jnp.concatenate([a + a_came, b[0] + sum(b_came)], axis=1)
+    return jnp.concatenate([c + c_came, a + a_came, b[0] + sum(b_came)], axis=1)
 
 
 def body(keys, queries, values, rates, gate, up, down, out_weight):
@@ -342,15 +389,32 @@
     weights = tuple(pltpu.with_memory_space_constraint(w, pltpu.HBM) for w in (gate, up, down))
     k, d, sent = sort_tokens(at, keys, values, rates.T)
     came = swap(sent, "core")
+    part = own_part(after(out_weight, sent))
+    rows = part.shape[0] // 4
+    cut = lambda i, j: part[i * rows : j * rows]
+    first = [ring(cut(0, 2), 1), ring(cut(2, 4), -1), ring(cut(2, 3), 1), ring(cut(1, 2), -1)]
     partial, rounded = near_grads(at, k, d, *weights)
-    q, q_sent = sort_queries(at, after(queries, partial))
-    whole = plane_gather(plane_scatter(far_grads(came, rounded, partial)))
-    q_came = swap(q_sent, "core")
+    total = plane_scatter(far_grads(came, rounded, partial))
+    total, first = lax.optimization_barrier((total, first))
+    ends = after((cut(3, 4), cut(0, 1)), total)
+    second = [ring(first[0], 1), ring(first[1], -1), ring(ends[0], 1), ring(ends[1], -1)]
+    first_core = swapped(first)
+    q, q_sent = sort_queries(at, after(queries, total))
+    whole = plane_gather(total)
+    whole, second, first_core = lax.optimization_barrier((whole, second, first_core))
+    second_core = swapped(second)
+    pieces = []
+    for came_first, came_second in ((first, second), (first_core, second_core)):
+        below = [came_first[0], came_first[2], came_second[2]]
+        above = [came_second[3], came_first[3], came_first[1]]
+        pieces.append((below, came_second[:2], above))
+    sources = [mine + others for mine, others in zip(*pieces)]
+    q_came = swap(after(q_sent, whole), "core")
     v = newton(at, whole, *weights)
     o_came = swap(call(far_query_kernel, "far_query", out(q_sent.shape, F32), [], q_came, v), "core")
     o = call(near_query_kernel, "near_query", out(q.shape, BF16), [], q, v)
-    by_y, by_z = join(at, o, o_came)
-    return project_scatter(by_y, by_z, out_weight).astype(BF16)
+    by_y, by_z, *sent = join(at, o, o_came)
+    return project_scatter(by_y, by_z, sent, out_weight, sources).astype(BF16)
 
 
 def solution(mesh):

time: 207 us -> 232 us (1.12)
  blocking collectives: 39.7 us -> 0 us
  starting transfers between devices: 21.5 us -> 45.7 us
  waiting for transfers between devices: 98.8 us -> 121 us
  local copies, waits for them, and re-layouts: 4.61 us -> 15.7 us
  Pallas kernels: 32.4 us -> 40.2 us
  matrix products: 7.65 us -> 3.72 us
    all_to_all x1 -> x0, blocking collectives: 39.7 us -> none  [plane_scatter(): return jnp.sum(lax.all_to_all(a, PLANE, 0, 0, tiled=True), axis=0)]
    ppermute x8 -> x19, waiting for transfers between devices: 36.4 us -> 72.1 us  [ring(): return lax.ppermute(a, 'z', [(i, (i + shift) % 4) for i in range(4)])]
    all_to_all x1, waiting for transfers between devices: 33.9 us -> 0.01 us  [plane_gather(): return lax.all_to_all(same, PLANE, 0, 0, tiled=True)]
    all_to_all x0 -> x1, waiting for transfers between devices: none -> 25 us  [plane_scatter(): return jnp.sum(lax.all_to_all(a, PLANE, 0, 0, tiled=True), axis=0)]
    ppermute x8 -> x19, starting transfers between devices: 15.3 us -> 25.9 us  [ring(): return lax.ppermute(a, 'z', [(i, (i + shift) % 4) for i in range(4)])]
    all_to_all x0 -> x1, starting transfers between devices: none -> 7.08 us  [plane_scatter(): return jnp.sum(lax.all_to_all(a, PLANE, 0, 0, tiled=True), axis=0)]
    unnamed x12 -> x40, local copies, waits for them, and re-layouts: 2.88 us -> 9.57 us
    pallas_call x0 -> x1, Pallas kernels: none -> 5 us  [gathered_product(): pl.pallas_call(functools.partial(gathered_kernel, [len(source) for source...]
  transfers between devices with their start and end apart: 14 -> 35, of which waited for: 8 -> 14; matrix products, arithmetic and copies ran while one was open for 3% -> 4% of each run, Pallas kernels for 13% -> 15%
where the time goes in v3:
time: 232 us; the launch traced here: 231 us
  waiting for transfers between devices  121 us (52%)
  starting transfers between devices  45.7 us (20%)
  Pallas kernels  40.2 us (17%)
  local copies, waits for them, and re-layouts  15.7 us (7%)
  other arithmetic  3.92 us (2%)
  matrix products  3.72 us (2%)
    ppermute x19, waiting for transfers between devices, ring(): return lax.ppermute(a, 'z', [(i, (i + shift) % 4) for i in range(4)])  72.1 us
    ppermute x19, starting transfers between devices, ring(): return lax.ppermute(a, 'z', [(i, (i + shift) % 4) for i in range(4)])  25.9 us
    all_to_all x1, waiting for transfers between devices, plane_scatter(): return jnp.sum(lax.all_to_all(a, PLANE, 0, 0, tiled=True), axis=0)  25 us
    ppermute x14, waiting for transfers between devices, swap(): return lax.ppermute(a, axis, [(0, 1), (1, 0)])  24.4 us
    pallas_call x1, Pallas kernels, newton(): pl.pallas_call(newton_kernel, out_shape=out(shape, BF16), in_specs=[pl.Bl...  20.8 us
    pallas_call x6, Pallas kernels, call(): pl.pallas_call(kernel, out_shape=outs, in_specs=specs, out_specs=jax.tree...  9.81 us
    unnamed x40, local copies, waits for them, and re-layouts  9.57 us
    all_to_all x1, starting transfers between devices, plane_scatter(): return jnp.sum(lax.all_to_all(a, PLANE, 0, 0, tiled=True), axis=0)  7.08 us
  transfers between devices with their start and end apart: 35, of which 14 were waited for; matrix products, arithmetic and copies ran while one was open for 4% of the time, Pallas kernels for 15%

profile of v3, /device:TPU:0, one launch (start us, length us, event | category | flops | bytes accessed | tf_op | source)
XLA Modules:
  0.0 231.2 jit_solution(2063739495573760365)
XLA Ops:
  4.1 4.6 %near_grads.1 = (f32[3,320,640]{2,1,0:T(8,128)S(1)}, bf16[3,320,640]{2,1,0:T(8,128)(2,1)S(1)}) custom-call(s32[3]{0:T(128)S(1)} %pad_add_fusion.at_ref, bf16[512,320]{1,0:T(8,128)(2,1)S(1)} %get-tuple-element.51.k_ref, bf16[512,320]{1,0:T(8,128)(2,1)S(1)} %get-tuple-element.52.d_ref, f32[2,320,640]{2,1,0:T(8,128)} %wg_ref.1, f32[2,320,640]{2,1,0:T(8,128)} %wu_ref.1, ...), custom_call_target="tpu_custom_call" | custom-call | tf_op jit(solution)/shard_map/near_grads/pallas_call | solution.py:152
  8.8 3.9 %far_grads.1 = f32[8,3,40,640]{3,2,1,0:T(8,128)} custom-call(f32[512,640]{1,0:T(8,128)S(1)} %collective-permute-done.came, bf16[3,320,640]{2,1,0:T(8,128)(2,1)S(1)} %get-tuple-element.53.b_ref, f32[3,320,640]{2,1,0:T(8,128)S(1)} %get-tuple-element.54.p_ref), custom_call_target="tpu_custom_call" | custom-call | tf_op jit(solution)/shard_map/far_grads/pallas_call | solution.py:36
  12.6 7.1 %all-to-all-start = ((f32[8,3,40,640]{3,2,1,0:T(8,128)}), f32[8,3,40,640]{3,2,1,0:T(8,128)}, u32[]{:S(2)}, u32[]{:S(2)}) async-start(f32[8,3,40,640]{3,2,1,0:T(8,128)} %far_grads.1), calls=%async_computation | async-start | bytes 4915200 | tf_op jit(solution)/shard_map/all_to_all | solution.py:327
  19.7 1.7 slice-done.2
  23.1 1.9 collective-permute-start.1
  25.0 2.1 collective-permute-start.2
  28.5 3.2 %collective-permute-start.4 = (f32[80,2048]{1,0:T(8,128)}, f32[80,2048]{1,0:T(8,128)}, u32[]{:S(2)}, u32[]{:S(2)}) collective-permute-start(f32[80,2048]{1,0:T(8,128)} %get-tuple-element.97), channel_id=1, source_target_pairs={{0,48},{16,0},{32,16},{48,32},{1,49},{17,1},{33,17},{49,33},{2,50}... | collective-permute-start | bytes 1966088 | tf_op jit(solution)/shard_map/ppermute | solution.py:323
  31.7 25.0 %all-to-all-done = f32[8,3,40,640]{3,2,1,0:T(8,128)} async-done(((f32[8,3,40,640]{3,2,1,0:T(8,128)}), f32[8,3,40,640]{3,2,1,0:T(8,128)}, u32[]{:S(2)}, u32[]{:S(2)}) %all-to-all-start) | async-done | bytes 2457632 | tf_op jit(solution)/shard_map/all_to_all | solution.py:327
  56.7 1.8 reduce_sum.9
  58.5 12.0 %collective-permute-done.3.refs_4_ = f32[80,2048]{1,0:T(8,128)S(1)} collective-permute-done((f32[80,2048]{1,0:T(8,128)}, f32[80,2048]{1,0:T(8,128)S(1)}, u32[]{:S(2)}, u32[]{:S(2)}) %collective-permute-start.3) | collective-permute-done | bytes 655392 | tf_op jit(solution)/shard_map/ppermute | solution.py:323
  70.5 1.6 broadcast_in_dim.2
  72.1 7.1 %all-to-all-start.1 = ((f32[8,3,40,640]{3,2,1,0:T(8,128)}), f32[8,3,40,640]{3,2,1,0:T(8,128)}, u32[]{:S(2)}, u32[]{:S(2)}) async-start(f32[8,3,40,640]{3,2,1,0:T(8,128)} %broadcast_in_dim.2), calls=%async_computation.1 | async-start | bytes 4915200 | tf_op jit(solution)/shard_map/all_to_all | solution.py:332
  80.4 2.1 collective-permute-start.8
  83.0 1.6 collective-permute-start.6
  84.6 11.5 %collective-permute-done.7.refs_5_ = f32[80,2048]{1,0:T(8,128)S(1)} collective-permute-done((f32[80,2048]{1,0:T(8,128)S(1)}, f32[80,2048]{1,0:T(8,128)S(1)}, u32[]{:S(2)}, u32[]{:S(2)}) %collective-permute-start.7) | collective-permute-done | bytes 655392 | tf_op jit(solution)/shard_map/ppermute | solution.py:323
  96.2 1.9 collective-permute-done.8.refs_13_
  104.6 22.0 %collective-permute-done.5.refs_9_ = f32[160,2048]{1,0:T(8,128)} collective-permute-done((f32[160,2048]{1,0:T(8,128)}, f32[160,2048]{1,0:T(8,128)}, u32[]{:S(2)}, u32[]{:S(2)}) %collective-permute-start.5) | collective-permute-done | bytes 1310752 | tf_op jit(solution)/shard_map/ppermute | solution.py:323
  127.7 20.8 %newton.1.v_ref = bf16[3,320,640]{2,1,0:T(8,128)(2,1)S(1)} custom-call(s32[3]{0:T(128)S(1)} %pad_add_fusion.at_ref, f32[8,3,40,640]{3,2,1,0:T(8,128)} %all-to-all-done.1.g_ref, f32[2,320,640]{2,1,0:T(8,128)} %wg_ref.1, f32[2,320,640]{2,1,0:T(8,128)} %wu_ref.1, f32[2,320,640]{2,1,0:T(8,128)} %wd_ref.1), custom_call_target="tpu_custom_call" | custom-call | tf_op jit(solution)/shard_map/newton/pallas_call | solution.py:230
  154.3 2.1 collective-permute-start.16
  158.2 14.4 %collective-permute-done.15.refs_0_ = f32[128,640]{1,0:T(8,128)S(1)} collective-permute-done((f32[128,640]{1,0:T(8,128)S(1)}, f32[128,640]{1,0:T(8,128)S(1)}, u32[]{:S(2)}, u32[]{:S(2)}) %collective-permute-start.15) | collective-permute-done | bytes 327712 | tf_op jit(solution)/shard_map/ppermute | solution.py:323
  173.8 1.8 collective-permute-start.25
  178.1 5.0 %gathered_product.1 = (f32[64,2048]{1,0:T(8,128)S(1)}, f32[64,2048]{1,0:T(8,128)S(1)}) custom-call(bf16[4,128,640]{2,1,0:T(8,128)(2,1)S(1)} %get-tuple-element.70.o_ref, bf16[640,5120]{1,0:T(8,128)(2,1)S(1)} %bitcast.23, f32[128,640]{1,0:T(8,128)S(1)} %collective-permute-done.15.refs_0_, f32[128,640]{1,0:T(8,128)S(1)} %collective-permute-done.16.refs_1_, ...), custom_call_target="tpu_custom_call" | custom-call | tf_op jit(solution)/shard_map/gathered_product/pallas_call | solution.py:307
  183.1 1.4 collective-permute-start.22
  184.6 2.7 %collective-permute-done.25 = f32[64,1920]{1,0:T(8,128)S(1)} collective-permute-done((f32[64,1920]{1,0:T(8,128)S(1)}, f32[64,1920]{1,0:T(8,128)S(1)}, u32[]{:S(2)}, u32[]{:S(2)}) %collective-permute-start.25) | collective-permute-done | bytes 491552 | tf_op jit(solution)/shard_map/ppermute | solution.py:323
  187.4 2.5 %collective-permute-start.26 = (f32[128,1920]{1,0:T(8,128)S(1)}, f32[128,1920]{1,0:T(8,128)S(1)}, u32[]{:S(2)}, u32[]{:S(2)}) collective-permute-start(f32[128,1920]{1,0:T(8,128)S(1)} %pad_maximum_fusion.1), channel_id=1, source_target_pairs={{0,48},{16,0},{32,16},{48,32},{1,49},{17,1},{33,17},{49,33},{2,50}... | collective-permute-start | bytes 2949128 | tf_op jit(solution)/shard_map/ppermute | solution.py:323
  191.4 14.4 %collective-permute-done.27 = f32[256,1152]{1,0:T(8,128)S(1)} collective-permute-done((f32[256,1152]{1,0:T(8,128)S(1)}, f32[256,1152]{1,0:T(8,128)S(1)}, u32[]{:S(2)}, u32[]{:S(2)}) %collective-permute-start.27) | collective-permute-done | bytes 1179680 | tf_op jit(solution)/shard_map/ppermute | solution.py:319
  207.0 2.8 %collective-permute-start.29 = (f32[32,1152]{1,0:T(8,128)S(1)}, f32[32,1152]{1,0:T(8,128)S(1)}, u32[]{:S(2)}, u32[]{:S(2)}) collective-permute-start(f32[32,1152]{1,0:T(8,128)S(1)} %get-tuple-element.105), channel_id=1, source_target_pairs={{0,48},{16,0},{32,16},{48,32},{1,49},{17,1},{33,17},{49,33},{2,50}... | collective-permute-start | bytes 442376 | tf_op jit(solution)/shard_map/ppermute | solution.py:323
  209.8 5.7 %collective-permute-done.22 = f32[64,2048]{1,0:T(8,128)S(1)} collective-permute-done((f32[64,2048]{1,0:T(8,128)S(1)}, f32[64,2048]{1,0:T(8,128)S(1)}, u32[]{:S(2)}, u32[]{:S(2)}) %collective-permute-start.22) | collective-permute-done | bytes 524320 | tf_op jit(solution)/shard_map/ppermute | solution.py:319
  215.6 2.1 collective-permute-done.28
  217.9 2.1 collective-permute-start.31
  221.7 2.9 %collective-permute-done.32 = f32[64,1152]{1,0:T(8,128)S(1)} collective-permute-done((f32[64,1152]{1,0:T(8,128)S(1)}, f32[64,1152]{1,0:T(8,128)S(1)}, u32[]{:S(2)}, u32[]{:S(2)}) %collective-permute-start.32) | collective-permute-done | bytes 294944 | tf_op jit(solution)/shard_map/ppermute | solution.py:323
  225.9 4.3 %collective-permute-done.30 = f32[64,1920]{1,0:T(8,128)S(1)} collective-permute-done((f32[64,1920]{1,0:T(8,128)S(1)}, f32[64,1920]{1,0:T(8,128)S(1)}, u32[]{:S(2)}, u32[]{:S(2)}) %collective-permute-start.30) | collective-permute-done | bytes 491552 | tf_op jit(solution)/shard_map/ppermute | solution.py:319
  (117 shorter events, 34.5 us)
Async XLA Ops:
  4.0 4.7 %collective-permute-start = (f32[512,640]{1,0:T(8,128)S(1)}, f32[512,640]{1,0:T(8,128)S(1)}, u32[]{:S(2)}, u32[]{:S(2)}) collective-permute-start(f32[512,640]{1,0:T(8,128)S(1)} %get-tuple-element.50), channel_id=1, source_target_pairs={{0,1},{1,0},{2,3},{3,2},{4,5},{5,4},{6,7},{7,6},{8,9},{9,8},{10,11... | collective-permute-start | bytes 3932168 | tf_op jit(solution)/shard_map/ppermute | solution.py:319
  12.6 44.0 %all-to-all-start = ((f32[8,3,40,640]{3,2,1,0:T(8,128)}), f32[8,3,40,640]{3,2,1,0:T(8,128)}, u32[]{:S(2)}, u32[]{:S(2)}) async-start(f32[8,3,40,640]{3,2,1,0:T(8,128)} %far_grads.1), calls=%async_computation | async-start | bytes 4915200 | tf_op jit(solution)/shard_map/all_to_all | solution.py:327
  23.1 47.4 %collective-permute-start.1 = (f32[160,2048]{1,0:T(8,128)}, f32[160,2048]{1,0:T(8,128)}, u32[]{:S(2)}, u32[]{:S(2)}) collective-permute-start(f32[160,2048]{1,0:T(8,128)} %get-tuple-element.100), channel_id=1, source_target_pairs={{0,16},{16,32},{32,48},{48,0},{1,17},{17,33},{33,49},{49,1},{2,18}... | collective-permute-start | bytes 3932168 | tf_op jit(solution)/shard_map/ppermute | solution.py:323
  25.0 45.5 %collective-permute-start.2 = (f32[160,2048]{1,0:T(8,128)S(1)}, f32[160,2048]{1,0:T(8,128)}, u32[]{:S(2)}, u32[]{:S(2)}) collective-permute-start(f32[160,2048]{1,0:T(8,128)S(1)} %get-tuple-element.99), channel_id=1, source_target_pairs={{0,48},{16,0},{32,16},{48,32},{1,49},{17,1},{33,17},{49,33},{2,50}... | collective-permute-start | bytes 3932168 | tf_op jit(solution)/shard_map/ppermute | solution.py:323
  28.5 42.0 %collective-permute-start.3 = (f32[80,2048]{1,0:T(8,128)}, f32[80,2048]{1,0:T(8,128)S(1)}, u32[]{:S(2)}, u32[]{:S(2)}) collective-permute-start(f32[80,2048]{1,0:T(8,128)} %get-tuple-element.98), channel_id=1, source_target_pairs={{0,16},{16,32},{32,48},{48,0},{1,17},{17,33},{33,49},{49,1},{2,18}... | collective-permute-start | bytes 1966088 | tf_op jit(solution)/shard_map/ppermute | solution.py:323
  28.5 42.0 %collective-permute-start.4 = (f32[80,2048]{1,0:T(8,128)}, f32[80,2048]{1,0:T(8,128)}, u32[]{:S(2)}, u32[]{:S(2)}) collective-permute-start(f32[80,2048]{1,0:T(8,128)} %get-tuple-element.97), channel_id=1, source_target_pairs={{0,48},{16,0},{32,16},{48,32},{1,49},{17,1},{33,17},{49,33},{2,50}... | collective-permute-start | bytes 1966088 | tf_op jit(solution)/shard_map/ppermute | solution.py:323
  72.1 55.6 %all-to-all-start.1 = ((f32[8,3,40,640]{3,2,1,0:T(8,128)}), f32[8,3,40,640]{3,2,1,0:T(8,128)}, u32[]{:S(2)}, u32[]{:S(2)}) async-start(f32[8,3,40,640]{3,2,1,0:T(8,128)} %broadcast_in_dim.2), calls=%async_computation.1 | async-start | bytes 4915200 | tf_op jit(solution)/shard_map/all_to_all | solution.py:332
  79.2 17.0 %collective-permute-start.7 = (f32[80,2048]{1,0:T(8,128)S(1)}, f32[80,2048]{1,0:T(8,128)S(1)}, u32[]{:S(2)}, u32[]{:S(2)}) collective-permute-start(f32[80,2048]{1,0:T(8,128)S(1)} %copy-done.17), channel_id=1, source_target_pairs={{0,16},{16,32},{32,48},{48,0},{1,17},{17,33},{33,49},{49,1},{2,18}... | collective-permute-start | bytes 1966088 | tf_op jit(solution)/shard_map/ppermute | solution.py:323
  80.4 17.7 %collective-permute-start.8 = (f32[80,2048]{1,0:T(8,128)S(1)}, f32[80,2048]{1,0:T(8,128)S(1)}, u32[]{:S(2)}, u32[]{:S(2)}) collective-permute-start(f32[80,2048]{1,0:T(8,128)S(1)} %get-tuple-element.62), channel_id=1, source_target_pairs={{0,48},{16,0},{32,16},{48,32},{1,49},{17,1},{33,17},{49,33},{2,50}... | collective-permute-start | bytes 1966088 | tf_op jit(solution)/shard_map/ppermute | solution.py:323
  82.5 15.6 %collective-permute-start.11 = (f32[80,2048]{1,0:T(8,128)S(1)}, f32[80,2048]{1,0:T(8,128)S(1)}, u32[]{:S(2)}, u32[]{:S(2)}) collective-permute-start(f32[80,2048]{1,0:T(8,128)S(1)} %collective-permute-done.3.refs_4_), channel_id=1, source_target_pairs={{0,1},{1,0},{2,3},{3,2},{4,5},{5,4},{6,7},{7,6},{8,9},{9,8},{10,11... | collective-permute-start | bytes 1966088 | tf_op jit(solution)/shard_map/ppermute | solution.py:319
  82.5 21.0 %collective-permute-start.10 = (f32[160,2048]{1,0:T(8,128)}, f32[160,2048]{1,0:T(8,128)S(1)}, u32[]{:S(2)}, u32[]{:S(2)}) collective-permute-start(f32[160,2048]{1,0:T(8,128)} %collective-permute-done.2.refs_15_), channel_id=1, source_target_pairs={{0,1},{1,0},{2,3},{3,2},{4,5},{5,4},{6,7},{7,6},{8,9},{9,8},{10,11... | collective-permute-start | bytes 3932168 | tf_op jit(solution)/shard_map/ppermute | solution.py:319
  83.0 43.6 %collective-permute-start.6 = (f32[160,2048]{1,0:T(8,128)}, f32[160,2048]{1,0:T(8,128)}, u32[]{:S(2)}, u32[]{:S(2)}) collective-permute-start(f32[160,2048]{1,0:T(8,128)} %collective-permute-done.2.refs_15_), channel_id=1, source_target_pairs={{0,48},{16,0},{32,16},{48,32},{1,49},{17,1},{33,17},{49,33},{2,50}... | collective-permute-start | bytes 3932168 | tf_op jit(solution)/shard_map/ppermute | solution.py:323
  96.2 30.4 %collective-permute-start.5 = (f32[160,2048]{1,0:T(8,128)}, f32[160,2048]{1,0:T(8,128)}, u32[]{:S(2)}, u32[]{:S(2)}) collective-permute-start(f32[160,2048]{1,0:T(8,128)} %collective-permute-done.1.refs_3_), channel_id=1, source_target_pairs={{0,16},{16,32},{32,48},{48,0},{1,17},{17,33},{33,49},{49,1},{2,18}... | collective-permute-start | bytes 3932168 | tf_op jit(solution)/shard_map/ppermute | solution.py:323
  98.1 28.5 %collective-permute-start.9 = (f32[160,2048]{1,0:T(8,128)}, f32[160,2048]{1,0:T(8,128)S(1)}, u32[]{:S(2)}, u32[]{:S(2)}) collective-permute-start(f32[160,2048]{1,0:T(8,128)} %collective-permute-done.1.refs_3_), channel_id=1, source_target_pairs={{0,1},{1,0},{2,3},{3,2},{4,5},{5,4},{6,7},{7,6},{8,9},{9,8},{10,11... | collective-permute-start | bytes 3932168 | tf_op jit(solution)/shard_map/ppermute | solution.py:319
  127.7 20.8 %collective-permute-start.13 = (f32[256,640]{1,0:T(8,128)}, f32[256,640]{1,0:T(8,128)S(1)}, u32[]{:S(2)}, u32[]{:S(2)}) collective-permute-start(f32[256,640]{1,0:T(8,128)} %copy-done.16), channel_id=1, source_target_pairs={{0,1},{1,0},{2,3},{3,2},{4,5},{5,4},{6,7},{7,6},{8,9},{9,8},{10,11... | collective-permute-start | bytes 1966088 | tf_op jit(solution)/shard_map/ppermute | solution.py:319
  151.6 26.5 %collective-permute-start.19 = (f32[160,2048]{1,0:T(8,128)}, f32[160,2048]{1,0:T(8,128)S(1)}, u32[]{:S(2)}, u32[]{:S(2)}) collective-permute-start(f32[160,2048]{1,0:T(8,128)} %collective-permute-done.5.refs_9_), channel_id=1, source_target_pairs={{0,1},{1,0},{2,3},{3,2},{4,5},{5,4},{6,7},{7,6},{8,9},{9,8},{10,11... | collective-permute-start | bytes 3932168 | tf_op jit(solution)/shard_map/ppermute | solution.py:319
  151.9 26.2 %collective-permute-start.20 = (f32[160,2048]{1,0:T(8,128)}, f32[160,2048]{1,0:T(8,128)S(1)}, u32[]{:S(2)}, u32[]{:S(2)}) collective-permute-start(f32[160,2048]{1,0:T(8,128)} %collective-permute-done.6.refs_10_), channel_id=1, source_target_pairs={{0,1},{1,0},{2,3},{3,2},{4,5},{5,4},{6,7},{7,6},{8,9},{9,8},{10,11... | collective-permute-start | bytes 3932168 | tf_op jit(solution)/shard_map/ppermute | solution.py:319
  154.2 18.4 %collective-permute-start.15 = (f32[128,640]{1,0:T(8,128)S(1)}, f32[128,640]{1,0:T(8,128)S(1)}, u32[]{:S(2)}, u32[]{:S(2)}) collective-permute-start(f32[128,640]{1,0:T(8,128)S(1)} %get-tuple-element.74), channel_id=1, source_target_pairs={{0,16},{16,32},{32,48},{48,0},{1,17},{17,33},{33,49},{49,1},{2,18}... | collective-permute-start | bytes 983048 | tf_op jit(solution)/shard_map/ppermute | solution.py:323
  154.3 18.4 %collective-permute-start.16 = (f32[128,640]{1,0:T(8,128)S(1)}, f32[128,640]{1,0:T(8,128)S(1)}, u32[]{:S(2)}, u32[]{:S(2)}) collective-permute-start(f32[128,640]{1,0:T(8,128)S(1)} %get-tuple-element.75), channel_id=1, source_target_pairs={{0,32},{16,48},{32,0},{48,16},{1,33},{17,49},{33,1},{49,17},{2,34}... | collective-permute-start | bytes 983048 | tf_op jit(solution)/shard_map/ppermute | solution.py:323
  156.4 17.3 %collective-permute-start.17 = (f32[128,640]{1,0:T(8,128)S(1)}, f32[128,640]{1,0:T(8,128)S(1)}, u32[]{:S(2)}, u32[]{:S(2)}) collective-permute-start(f32[128,640]{1,0:T(8,128)S(1)} %get-tuple-element.76), channel_id=1, source_target_pairs={{0,48},{16,0},{32,16},{48,32},{1,49},{17,1},{33,17},{49,33},{2,50}... | collective-permute-start | bytes 983048 | tf_op jit(solution)/shard_map/ppermute | solution.py:323
  172.7 4.9 %collective-permute-start.21 = (f32[80,2048]{1,0:T(8,128)S(1)}, f32[80,2048]{1,0:T(8,128)S(1)}, u32[]{:S(2)}, u32[]{:S(2)}) collective-permute-start(f32[80,2048]{1,0:T(8,128)S(1)} %copy-done.7), channel_id=1, source_target_pairs={{0,1},{1,0},{2,3},{3,2},{4,5},{5,4},{6,7},{7,6},{8,9},{9,8},{10,11... | collective-permute-start | bytes 1966088 | tf_op jit(solution)/shard_map/ppermute | solution.py:319
  173.8 13.5 %collective-permute-start.25 = (f32[64,1920]{1,0:T(8,128)S(1)}, f32[64,1920]{1,0:T(8,128)S(1)}, u32[]{:S(2)}, u32[]{:S(2)}) collective-permute-start(f32[64,1920]{1,0:T(8,128)S(1)} %get-tuple-element.109), channel_id=1, source_target_pairs={{0,48},{16,0},{32,16},{48,32},{1,49},{17,1},{33,17},{49,33},{2,50}... | collective-permute-start | bytes 1474568 | tf_op jit(solution)/shard_map/ppermute | solution.py:323
  176.8 29.0 %collective-permute-start.27 = (f32[256,1152]{1,0:T(8,128)S(1)}, f32[256,1152]{1,0:T(8,128)S(1)}, u32[]{:S(2)}, u32[]{:S(2)}) collective-permute-start(f32[256,1152]{1,0:T(8,128)S(1)} %fusion.9), channel_id=1, source_target_pairs={{0,64},{64,0},{1,65},{65,1},{2,66},{66,2},{3,67},{67,3},{4,68},{68... | collective-permute-start | bytes 3538952 | tf_op jit(solution)/shard_map/ppermute | solution.py:319
  177.6 13.5 %collective-permute-start.23 = (f32[64,1920]{1,0:T(8,128)S(1)}, f32[64,1920]{1,0:T(8,128)S(1)}, u32[]{:S(2)}, u32[]{:S(2)}) collective-permute-start(f32[64,1920]{1,0:T(8,128)S(1)} %get-tuple-element.110), channel_id=1, source_target_pairs={{0,16},{16,32},{32,48},{48,0},{1,17},{17,33},{33,49},{49,1},{2,18}... | collective-permute-start | bytes 1474568 | tf_op jit(solution)/shard_map/ppermute | solution.py:323
  183.1 32.4 %collective-permute-start.22 = (f32[64,2048]{1,0:T(8,128)S(1)}, f32[64,2048]{1,0:T(8,128)S(1)}, u32[]{:S(2)}, u32[]{:S(2)}) collective-permute-start(f32[64,2048]{1,0:T(8,128)S(1)} %get-tuple-element.89), channel_id=1, source_target_pairs={{0,64},{64,0},{1,65},{65,1},{2,66},{66,2},{3,67},{67,3},{4,68},{68... | collective-permute-start | bytes 1572872 | tf_op jit(solution)/shard_map/ppermute | solution.py:319
  187.4 32.5 %collective-permute-start.26 = (f32[128,1920]{1,0:T(8,128)S(1)}, f32[128,1920]{1,0:T(8,128)S(1)}, u32[]{:S(2)}, u32[]{:S(2)}) collective-permute-start(f32[128,1920]{1,0:T(8,128)S(1)} %pad_maximum_fusion.1), channel_id=1, source_target_pairs={{0,48},{16,0},{32,16},{48,32},{1,49},{17,1},{33,17},{49,33},{2,50}... | collective-permute-start | bytes 2949128 | tf_op jit(solution)/shard_map/ppermute | solution.py:323
  191.3 28.7 %collective-permute-start.24 = (f32[128,1920]{1,0:T(8,128)S(1)}, f32[128,1920]{1,0:T(8,128)S(1)}, u32[]{:S(2)}, u32[]{:S(2)}) collective-permute-start(f32[128,1920]{1,0:T(8,128)S(1)} %pad_maximum_fusion), channel_id=1, source_target_pairs={{0,16},{16,32},{32,48},{48,0},{1,17},{17,33},{33,49},{49,1},{2,18}... | collective-permute-start | bytes 2949128 | tf_op jit(solution)/shard_map/ppermute | solution.py:323
  206.5 11.2 %collective-permute-start.28 = (f32[32,1152]{1,0:T(8,128)S(1)}, f32[32,1152]{1,0:T(8,128)S(1)}, u32[]{:S(2)}, u32[]{:S(2)}) collective-permute-start(f32[32,1152]{1,0:T(8,128)S(1)} %get-tuple-element.106), channel_id=1, source_target_pairs={{0,16},{16,32},{32,48},{48,0},{1,17},{17,33},{33,49},{49,1},{2,18}... | collective-permute-start | bytes 442376 | tf_op jit(solution)/shard_map/ppermute | solution.py:323
  207.0 10.7 %collective-permute-start.29 = (f32[32,1152]{1,0:T(8,128)S(1)}, f32[32,1152]{1,0:T(8,128)S(1)}, u32[]{:S(2)}, u32[]{:S(2)}) collective-permute-start(f32[32,1152]{1,0:T(8,128)S(1)} %get-tuple-element.105), channel_id=1, source_target_pairs={{0,48},{16,0},{32,16},{48,32},{1,49},{17,1},{33,17},{49,33},{2,50}... | collective-permute-start | bytes 442376 | tf_op jit(solution)/shard_map/ppermute | solution.py:323
  217.8 6.8 %collective-permute-start.32 = (f32[64,1152]{1,0:T(8,128)S(1)}, f32[64,1152]{1,0:T(8,128)S(1)}, u32[]{:S(2)}, u32[]{:S(2)}) collective-permute-start(f32[64,1152]{1,0:T(8,128)S(1)} %pad_maximum_fusion.4), channel_id=1, source_target_pairs={{0,48},{16,0},{32,16},{48,32},{1,49},{17,1},{33,17},{49,33},{2,50}... | collective-permute-start | bytes 884744 | tf_op jit(solution)/shard_map/ppermute | solution.py:323
  217.9 8.0 %collective-permute-start.31 = (f32[64,1152]{1,0:T(8,128)S(1)}, f32[64,1152]{1,0:T(8,128)S(1)}, u32[]{:S(2)}, u32[]{:S(2)}) collective-permute-start(f32[64,1152]{1,0:T(8,128)S(1)} %pad_maximum_fusion.3), channel_id=1, source_target_pairs={{0,16},{16,32},{32,48},{48,0},{1,17},{17,33},{33,49},{49,1},{2,18}... | collective-permute-start | bytes 884744 | tf_op jit(solution)/shard_map/ppermute | solution.py:323
  220.3 10.0 %collective-permute-start.30 = (f32[64,1920]{1,0:T(8,128)S(1)}, f32[64,1920]{1,0:T(8,128)S(1)}, u32[]{:S(2)}, u32[]{:S(2)}) collective-permute-start(f32[64,1920]{1,0:T(8,128)S(1)} %slice.155), channel_id=1, source_target_pairs={{0,64},{64,0},{1,65},{65,1},{2,66},{66,2},{3,67},{67,3},{4,68},{68... | collective-permute-start | bytes 1474568 | tf_op jit(solution)/shard_map/ppermute | solution.py:319
  (24 other events, 145.4 us)

commit v4 on v2

--- a/solution.py
+++ b/solution.py
@@ -16,7 +16,7 @@
 SHARDS = 8
 TILE = 256
 VMEM_LIMIT = 24 << 20
-CUT = 3072
+CUT = 2816
 F32 = jnp.float32
 BF16 = jnp.bfloat16
 
@@ -298,8 +298,8 @@
     return lax.all_to_all(same, PLANE, 0, 0, tiled=True)
 
 
-def after(a, *others):
-    return lax.optimization_barrier((a, others))[0]
+def together(*arrays):
+    return lax.optimization_barrier(arrays)
 
 
 def halves(a):
@@ -321,13 +321,11 @@
 
 def project_scatter(by_y, by_z, weight):
     wa, wb = weight[:, :CUT], weight[:, CUT:]
-    b_far = mm(by_y[1], wb)
+    b_far, by_z = together(mm(by_y[1], wb), by_z)
     b_came = swap(b_far, "yl")
-    by_z = after(by_z, b_far)
-    up, down = halves(by_z[2])
-    a_came = ring(mm(up, wa), 1), ring(mm(down, wa), -1)
+    a_came = pass_two(mm(by_z[2], wa))
     a_came, a_sent = pass_one(mm(by_z[1], wa), mm(by_z[3], wa), a_came)
-    b = mm(by_y[0], wb) + after(b_came, a_sent)
+    b = mm(by_y[0], wb) + b_came
     b = b.reshape(4, -1, b.shape[1])
     b_came = pass_two(b[2])
     a = mm(by_z[0], wa) + sum(a_came)
@@ -343,8 +341,10 @@
     k, d, sent = sort_tokens(at, keys, values, rates.T)
     came = swap(sent, "core")
     partial, rounded = near_grads(at, k, d, *weights)
-    q, q_sent = sort_queries(at, after(queries, partial))
-    whole = plane_gather(plane_scatter(far_grads(came, rounded, partial)))
+    total = plane_scatter(far_grads(came, rounded, partial))
+    total, queries = together(total, queries)
+    q, q_sent = sort_queries(at, queries)
+    whole, q_sent = together(plane_gather(total), q_sent)
     q_came = swap(q_sent, "core")
     v = newton(at, whole, *weights)
     o_came = swap(call(far_query_kernel, "far_query", out(q_sent.shape, F32), [], q_came, v), "core")

time: 207 us -> 203 us (0.981)
  matrix products: 7.65 us -> 5.12 us
    ppermute x8, waiting for transfers between devices: 36.4 us -> 29.8 us  [ring(): return lax.ppermute(a, 'z', [(i, (i + shift) % 4) for i in range(4)])]
    ppermute x5, waiting for transfers between devices: 28.6 us -> 34.7 us  [swap(): return lax.ppermute(a, axis, [(0, 1), (1, 0)])]
    dot_general x7 -> x6, matrix products: 7.65 us -> 5.12 us  [mm(): return jnp.dot(a, b, preferred_element_type=F32)]
  transfers between devices with their start and end apart: 14 -> 14, of which waited for: 8 -> 8; matrix products, arithmetic and copies ran while one was open for 3% -> 2% of each run, Pallas kernels for 13% -> 13%
where the time goes in v4:
time: 203 us; the launch traced here: 202 us
  waiting for transfers between devices  98.4 us (48%)
  blocking collectives  39.7 us (20%)
  Pallas kernels  31.5 us (16%)
  starting transfers between devices  19.6 us (10%)
  local copies, waits for them, and re-layouts  5.53 us (3%)
  matrix products  5.12 us (3%)
  other arithmetic  2.13 us (1%)
    all_to_all x1, blocking collectives, plane_scatter(): return jnp.sum(lax.all_to_all(a, PLANE, 0, 0, tiled=True), axis=0)  39.7 us
    ppermute x5, waiting for transfers between devices, swap(): return lax.ppermute(a, axis, [(0, 1), (1, 0)])  34.7 us
    all_to_all x1, waiting for transfers between devices, plane_gather(): return lax.all_to_all(same, PLANE, 0, 0, tiled=True)  33.9 us
    ppermute x8, waiting for transfers between devices, ring(): return lax.ppermute(a, 'z', [(i, (i + shift) % 4) for i in range(4)])  29.8 us
    pallas_call x1, Pallas kernels, newton(): pl.pallas_call(newton_kernel, out_shape=out(shape, BF16), in_specs=[pl.Bl...  19.5 us
    ppermute x8, starting transfers between devices, ring(): return lax.ppermute(a, 'z', [(i, (i + shift) % 4) for i in range(4)])  13.7 us
    pallas_call x6, Pallas kernels, call(): pl.pallas_call(kernel, out_shape=outs, in_specs=specs, out_specs=jax.tree...  7.51 us
    dot_general x6, matrix products, mm(): return jnp.dot(a, b, preferred_element_type=F32)  5.12 us
  transfers between devices with their start and end apart: 14, of which 8 were waited for; matrix products, arithmetic and copies ran while one was open for 2% of the time, Pallas kernels for 13%

profile of v4, /device:TPU:0, one launch (start us, length us, event | category | flops | bytes accessed | tf_op | source)
XLA Modules:
  0.0 202.2 jit_solution(14701606165742908638)
XLA Ops:
  0.1 1.1 copy-done
  1.2 1.1 copy-done.1
  2.9 1.1 sort_tokens.1
  4.1 4.5 %near_grads.1 = (f32[3,320,640]{2,1,0:T(8,128)S(1)}, bf16[3,320,640]{2,1,0:T(8,128)(2,1)S(1)}) custom-call(s32[3]{0:T(128)S(1)} %pad_add_fusion.at_ref, bf16[512,320]{1,0:T(8,128)(2,1)S(1)} %get-tuple-element.21.k_ref, bf16[512,320]{1,0:T(8,128)(2,1)S(1)} %get-tuple-element.22.d_ref, f32[2,320,640]{2,1,0:T(8,128)} %wg_ref.1, f32[2,320,640]{2,1,0:T(8,128)} %wu_ref.1, ...), custom_call_target="tpu_custom_call" | custom-call | tf_op jit(solution)/shard_map/near_grads/pallas_call | solution.py:150
  8.7 2.3 %far_grads.1 = f32[8,3,40,640]{3,2,1,0:T(8,128)S(1)} custom-call(f32[512,640]{1,0:T(8,128)S(1)} %collective-permute-done.came, bf16[3,320,640]{2,1,0:T(8,128)(2,1)S(1)} %get-tuple-element.23.b_ref, f32[3,320,640]{2,1,0:T(8,128)S(1)} %get-tuple-element.24.p_ref), custom_call_target="tpu_custom_call" | custom-call | tf_op jit(solution)/shard_map/far_grads/pallas_call | solution.py:34
  11.0 39.7 %all_to_all.10 = f32[8,3,40,640]{3,2,1,0:T(8,128)S(1)} all-to-all(f32[8,3,40,640]{3,2,1,0:T(8,128)S(1)} %far_grads.1), channel_id=1, replica_groups=mesh['yl'=2,'z'=4,'x'=4,'yh'=2,'core'=2] {'x','yh'}, dimensions={0} | all-to-all | bytes 4915200 | tf_op jit(solution)/shard_map/all_to_all | solution.py:293
  50.8 1.6 broadcast_in_dim.2
  52.4 3.8 %all-to-all-start.1 = ((f32[8,3,40,640]{3,2,1,0:T(8,128)}), f32[8,3,40,640]{3,2,1,0:T(8,128)S(1)}, u32[]{:S(2)}, u32[]{:S(2)}) async-start(f32[8,3,40,640]{3,2,1,0:T(8,128)} %broadcast_in_dim.2), calls=%async_computation.1 | async-start | bytes 4915200 | tf_op jit(solution)/shard_map/all_to_all | solution.py:298
  56.9 0.8 copy-done.4
  57.7 33.9 %all-to-all-done.1.g_ref = f32[8,3,40,640]{3,2,1,0:T(8,128)S(1)} async-done(((f32[8,3,40,640]{3,2,1,0:T(8,128)}), f32[8,3,40,640]{3,2,1,0:T(8,128)S(1)}, u32[]{:S(2)}, u32[]{:S(2)}) %all-to-all-start.1) | async-done | bytes 2457632 | tf_op jit(solution)/shard_map/all_to_all | solution.py:298
  91.6 19.5 %newton.1.v_ref = bf16[3,320,640]{2,1,0:T(8,128)(2,1)S(1)} custom-call(s32[3]{0:T(128)S(1)} %pad_add_fusion.at_ref, f32[8,3,40,640]{3,2,1,0:T(8,128)S(1)} %all-to-all-done.1.g_ref, f32[2,320,640]{2,1,0:T(8,128)} %wg_ref.1, f32[2,320,640]{2,1,0:T(8,128)} %wu_ref.1, f32[2,320,640]{2,1,0:T(8,128)} %wd_ref.1), custom_call_target="tpu_custom_call" | custom-call | tf_op jit(solution)/shard_map/newton/pallas_call | solution.py:228
  111.1 1.4 far_query.1
  113.1 1.3 near_query.1.o_ref
  115.5 1.1 fusion.1
  116.6 0.7 fusion.5
  117.5 2.0 collective-permute-start.3
  120.1 2.2 %collective-permute-start.5 = (f32[64,2816]{1,0:T(8,128)S(1)}, f32[64,2816]{1,0:T(8,128)S(1)}, u32[]{:S(2)}, u32[]{:S(2)}) collective-permute-start(f32[64,2816]{1,0:T(8,128)S(1)} %get-tuple-element.43), channel_id=1, source_target_pairs={{0,48},{16,0},{32,16},{48,32},{1,49},{17,1},{33,17},{49,33},{2,50}... | collective-permute-start | bytes 2162696 | tf_op jit(solution)/shard_map/ppermute | solution.py:289
  122.3 0.7 fusion.7
  123.1 0.7 fusion.3
  123.8 14.5 %collective-permute-done.3 = f32[64,2816]{1,0:T(8,128)S(1)} collective-permute-done((f32[64,2816]{1,0:T(8,128)S(1)}, f32[64,2816]{1,0:T(8,128)S(1)}, u32[]{:S(2)}, u32[]{:S(2)}) %collective-permute-start.3) | collective-permute-done | bytes 720928 | tf_op jit(solution)/shard_map/ppermute | solution.py:289
  138.9 3.5 %collective-permute-start.6 = (f32[128,2816]{1,0:T(8,128)S(1)}, f32[128,2816]{1,0:T(8,128)S(1)}, u32[]{:S(2)}, u32[]{:S(2)}) collective-permute-start(f32[128,2816]{1,0:T(8,128)S(1)} %pad_maximum_fusion.1), channel_id=1, source_target_pairs={{0,48},{16,0},{32,16},{48,32},{1,49},{17,1},{33,17},{49,33},{2,50}... | collective-permute-start | bytes 4325384 | tf_op jit(solution)/shard_map/ppermute | solution.py:289
  142.4 0.7 fusion.9
  143.2 29.6 %collective-permute-done.8 = f32[256,2304]{1,0:T(8,128)S(1)} collective-permute-done((f32[256,2304]{1,0:T(8,128)S(1)}, f32[256,2304]{1,0:T(8,128)S(1)}, u32[]{:S(2)}, u32[]{:S(2)}) %collective-permute-start.8) | collective-permute-done | bytes 2359328 | tf_op jit(solution)/shard_map/ppermute | solution.py:285
  172.8 1.1 convolution_add_fusion
  174.0 2.6 %collective-permute-start.11 = (f32[32,2304]{1,0:T(8,128)S(1)}, f32[32,2304]{1,0:T(8,128)S(1)}, u32[]{:S(2)}, u32[]{:S(2)}) collective-permute-start(f32[32,2304]{1,0:T(8,128)S(1)} %get-tuple-element.36), channel_id=1, source_target_pairs={{0,48},{16,0},{32,16},{48,32},{1,49},{17,1},{33,17},{49,33},{2,50}... | collective-permute-start | bytes 884744 | tf_op jit(solution)/shard_map/ppermute | solution.py:289
  176.8 0.8 collective-permute-start.7
  177.6 5.1 %collective-permute-done.11 = f32[32,2304]{1,0:T(8,128)S(1)} collective-permute-done((f32[32,2304]{1,0:T(8,128)S(1)}, f32[32,2304]{1,0:T(8,128)S(1)}, u32[]{:S(2)}, u32[]{:S(2)}) %collective-permute-start.11) | collective-permute-done | bytes 294944 | tf_op jit(solution)/shard_map/ppermute | solution.py:289
  182.7 3.4 %collective-permute-done.9 = f32[32,2304]{1,0:T(8,128)S(1)} collective-permute-done((f32[32,2304]{1,0:T(8,128)S(1)}, f32[32,2304]{1,0:T(8,128)S(1)}, u32[]{:S(2)}, u32[]{:S(2)}) %collective-permute-start.9) | collective-permute-done | bytes 294944 | tf_op jit(solution)/shard_map/ppermute | solution.py:289
  186.4 3.3 %collective-permute-start.12 = (f32[64,2304]{1,0:T(8,128)S(1)}, f32[64,2304]{1,0:T(8,128)S(1)}, u32[]{:S(2)}, u32[]{:S(2)}) collective-permute-start(f32[64,2304]{1,0:T(8,128)S(1)} %pad_maximum_fusion.4), channel_id=1, source_target_pairs={{0,48},{16,0},{32,16},{48,32},{1,49},{17,1},{33,17},{49,33},{2,50}... | collective-permute-start | bytes 1769480 | tf_op jit(solution)/shard_map/ppermute | solution.py:289
  189.6 4.7 %collective-permute-done.7 = f32[64,2816]{1,0:T(8,128)S(1)} collective-permute-done((f32[64,2816]{1,0:T(8,128)S(1)}, f32[64,2816]{1,0:T(8,128)S(1)}, u32[]{:S(2)}, u32[]{:S(2)}) %collective-permute-start.7) | collective-permute-done | bytes 720928 | tf_op jit(solution)/shard_map/ppermute | solution.py:285
  194.5 6.8 %collective-permute-done.10 = f32[64,2304]{1,0:T(8,128)S(1)} collective-permute-done((f32[64,2304]{1,0:T(8,128)S(1)}, f32[64,2304]{1,0:T(8,128)S(1)}, u32[]{:S(2)}, u32[]{:S(2)}) %collective-permute-start.10) | collective-permute-done | bytes 589856 | tf_op jit(solution)/shard_map/ppermute | solution.py:289
  201.4 0.9 pad_maximum_fusion.2
  (43 shorter events, 5.5 us)
Async XLA Ops:
  0.1 1.1 copy-start
  1.2 1.1 copy-start.1
  2.3 0.7 copy-start.3
  4.0 4.6 %collective-permute-start = (f32[512,640]{1,0:T(8,128)S(1)}, f32[512,640]{1,0:T(8,128)S(1)}, u32[]{:S(2)}, u32[]{:S(2)}) collective-permute-start(f32[512,640]{1,0:T(8,128)S(1)} %get-tuple-element.20), channel_id=1, source_target_pairs={{0,1},{1,0},{2,3},{3,2},{4,5},{5,4},{6,7},{7,6},{8,9},{9,8},{10,11... | collective-permute-start | bytes 3932168 | tf_op jit(solution)/shard_map/ppermute | solution.py:285
  52.4 3.8 %copy-start.2 = (bf16[512,640]{1,0:T(8,128)(2,1)S(1)}, bf16[512,640]{1,0:T(8,128)(2,1)}, u32[]{:S(2)}) copy-start(bf16[512,640]{1,0:T(8,128)(2,1)} %q_ref) | copy-start | bytes 1966084
  52.4 39.2 %all-to-all-start.1 = ((f32[8,3,40,640]{3,2,1,0:T(8,128)}), f32[8,3,40,640]{3,2,1,0:T(8,128)S(1)}, u32[]{:S(2)}, u32[]{:S(2)}) async-start(f32[8,3,40,640]{3,2,1,0:T(8,128)} %broadcast_in_dim.2), calls=%async_computation.1 | async-start | bytes 4915200 | tf_op jit(solution)/shard_map/all_to_all | solution.py:298
  56.9 0.8 copy-start.4
  91.6 23.9 %slice-start = ((s8[6553600]{0:T(1024)(128)(4,1)}), s8[4194304]{0:T(1024)(128)(4,1)S(1)}, s32[]{:S(2)}) async-start(s8[6553600]{0:T(1024)(128)(4,1)} %bitcast.23), calls=%async_computation.2 | async-start | bytes 8388608
  91.6 23.9 %slice-start.1 = ((s8[6553600]{0:T(1024)(128)(4,1)}), s8[2359296]{0:T(1024)(128)(4,1)S(1)}, s32[]{:S(2)}) async-start(s8[6553600]{0:T(1024)(128)(4,1)} %bitcast.23), calls=%async_computation.3 | async-start | bytes 4718592
  91.6 19.5 %collective-permute-start.1 = (f32[256,640]{1,0:T(8,128)}, f32[256,640]{1,0:T(8,128)S(1)}, u32[]{:S(2)}, u32[]{:S(2)}) collective-permute-start(f32[256,640]{1,0:T(8,128)} %copy-done.4), channel_id=1, source_target_pairs={{0,1},{1,0},{2,3},{3,2},{4,5},{5,4},{6,7},{7,6},{8,9},{9,8},{10,11... | collective-permute-start | bytes 1966088 | tf_op jit(solution)/shard_map/ppermute | solution.py:285
  112.5 2.3 %collective-permute-start.2 = (f32[256,640]{1,0:T(8,128)S(1)}, f32[256,640]{1,0:T(8,128)S(1)}, u32[]{:S(2)}, u32[]{:S(2)}) collective-permute-start(f32[256,640]{1,0:T(8,128)S(1)} %far_query.1), channel_id=1, source_target_pairs={{0,1},{1,0},{2,3},{3,2},{4,5},{5,4},{6,7},{7,6},{8,9},{9,8},{10,11... | collective-permute-start | bytes 1966088 | tf_op jit(solution)/shard_map/ppermute | solution.py:285
  117.5 20.9 %collective-permute-start.3 = (f32[64,2816]{1,0:T(8,128)S(1)}, f32[64,2816]{1,0:T(8,128)S(1)}, u32[]{:S(2)}, u32[]{:S(2)}) collective-permute-start(f32[64,2816]{1,0:T(8,128)S(1)} %get-tuple-element.44), channel_id=1, source_target_pairs={{0,16},{16,32},{32,48},{48,0},{1,17},{17,33},{33,49},{49,1},{2,18}... | collective-permute-start | bytes 2162696 | tf_op jit(solution)/shard_map/ppermute | solution.py:289
  119.4 53.4 %collective-permute-start.8 = (f32[256,2304]{1,0:T(8,128)S(1)}, f32[256,2304]{1,0:T(8,128)S(1)}, u32[]{:S(2)}, u32[]{:S(2)}) collective-permute-start(f32[256,2304]{1,0:T(8,128)S(1)} %fusion.1), channel_id=1, source_target_pairs={{0,64},{64,0},{1,65},{65,1},{2,66},{66,2},{3,67},{67,3},{4,68},{68... | collective-permute-start | bytes 7077896 | tf_op jit(solution)/shard_map/ppermute | solution.py:285
  120.1 18.6 %collective-permute-start.5 = (f32[64,2816]{1,0:T(8,128)S(1)}, f32[64,2816]{1,0:T(8,128)S(1)}, u32[]{:S(2)}, u32[]{:S(2)}) collective-permute-start(f32[64,2816]{1,0:T(8,128)S(1)} %get-tuple-element.43), channel_id=1, source_target_pairs={{0,48},{16,0},{32,16},{48,32},{1,49},{17,1},{33,17},{49,33},{2,50}... | collective-permute-start | bytes 2162696 | tf_op jit(solution)/shard_map/ppermute | solution.py:289
  138.6 37.9 %collective-permute-start.4 = (f32[128,2816]{1,0:T(8,128)S(1)}, f32[128,2816]{1,0:T(8,128)S(1)}, u32[]{:S(2)}, u32[]{:S(2)}) collective-permute-start(f32[128,2816]{1,0:T(8,128)S(1)} %pad_maximum_fusion), channel_id=1, source_target_pairs={{0,16},{16,32},{32,48},{48,0},{1,17},{17,33},{33,49},{49,1},{2,18}... | collective-permute-start | bytes 4325384 | tf_op jit(solution)/shard_map/ppermute | solution.py:289
  138.9 37.6 %collective-permute-start.6 = (f32[128,2816]{1,0:T(8,128)S(1)}, f32[128,2816]{1,0:T(8,128)S(1)}, u32[]{:S(2)}, u32[]{:S(2)}) collective-permute-start(f32[128,2816]{1,0:T(8,128)S(1)} %pad_maximum_fusion.1), channel_id=1, source_target_pairs={{0,48},{16,0},{32,16},{48,32},{1,49},{17,1},{33,17},{49,33},{2,50}... | collective-permute-start | bytes 4325384 | tf_op jit(solution)/shard_map/ppermute | solution.py:289
  174.0 8.7 %collective-permute-start.11 = (f32[32,2304]{1,0:T(8,128)S(1)}, f32[32,2304]{1,0:T(8,128)S(1)}, u32[]{:S(2)}, u32[]{:S(2)}) collective-permute-start(f32[32,2304]{1,0:T(8,128)S(1)} %get-tuple-element.36), channel_id=1, source_target_pairs={{0,48},{16,0},{32,16},{48,32},{1,49},{17,1},{33,17},{49,33},{2,50}... | collective-permute-start | bytes 884744 | tf_op jit(solution)/shard_map/ppermute | solution.py:289
  176.5 9.6 %collective-permute-start.9 = (f32[32,2304]{1,0:T(8,128)S(1)}, f32[32,2304]{1,0:T(8,128)S(1)}, u32[]{:S(2)}, u32[]{:S(2)}) collective-permute-start(f32[32,2304]{1,0:T(8,128)S(1)} %get-tuple-element.38), channel_id=1, source_target_pairs={{0,16},{16,32},{32,48},{48,0},{1,17},{17,33},{33,49},{49,1},{2,18}... | collective-permute-start | bytes 884744 | tf_op jit(solution)/shard_map/ppermute | solution.py:289
  176.8 17.6 %collective-permute-start.7 = (f32[64,2816]{1,0:T(8,128)S(1)}, f32[64,2816]{1,0:T(8,128)S(1)}, u32[]{:S(2)}, u32[]{:S(2)}) collective-permute-start(f32[64,2816]{1,0:T(8,128)S(1)} %slice.115), channel_id=1, source_target_pairs={{0,64},{64,0},{1,65},{65,1},{2,66},{66,2},{3,67},{67,3},{4,68},{68... | collective-permute-start | bytes 2162696 | tf_op jit(solution)/shard_map/ppermute | solution.py:285
  186.2 15.0 %collective-permute-start.10 = (f32[64,2304]{1,0:T(8,128)S(1)}, f32[64,2304]{1,0:T(8,128)S(1)}, u32[]{:S(2)}, u32[]{:S(2)}) collective-permute-start(f32[64,2304]{1,0:T(8,128)S(1)} %pad_maximum_fusion.3), channel_id=1, source_target_pairs={{0,16},{16,32},{32,48},{48,0},{1,17},{17,33},{33,49},{49,1},{2,18}... | collective-permute-start | bytes 1769480 | tf_op jit(solution)/shard_map/ppermute | solution.py:289
  186.4 14.9 %collective-permute-start.12 = (f32[64,2304]{1,0:T(8,128)S(1)}, f32[64,2304]{1,0:T(8,128)S(1)}, u32[]{:S(2)}, u32[]{:S(2)}) collective-permute-start(f32[64,2304]{1,0:T(8,128)S(1)} %pad_maximum_fusion.4), channel_id=1, source_target_pairs={{0,48},{16,0},{32,16},{48,32},{1,49},{17,1},{33,17},{49,33},{2,50}... | collective-permute-start | bytes 1769480 | tf_op jit(solution)/shard_map/ppermute | solution.py:289

commit v5 on v4

--- a/solution.py
+++ b/solution.py
@@ -17,6 +17,7 @@
 TILE = 256
 VMEM_LIMIT = 24 << 20
 CUT = 2816
+Y_ORDER = (2, 0, 1, 3)
 F32 = jnp.float32
 BF16 = jnp.bfloat16
 
@@ -267,7 +268,7 @@
             for dy in range(2):
                 for dz in range(4):
                     r = dy * 4 + dz
-                    to_y, to_z = pl.ds(dz * block, block), pl.ds(dy * block, block)
+                    to_y, to_z = pl.ds(Y_ORDER.index(dz) * block, block), pl.ds(dy * block, block)
                     mine = o_ref[r * block : (r + 1) * block, :]
                     other = came[side_by_side(rows, r, block, width)].astype(BF16)
                     for columns, piece in ((near, mine), (far, other)):
@@ -307,32 +308,34 @@
     return a[:half], a[half:]
 
 
-def pass_two(a):
-    up, down = halves(a)
+def both_ways(up, down):
     return ring(up, 1), ring(down, -1)
-
-
-def pass_one(one, three, came):
-    up, down = came
-    one = jnp.concatenate([one[: up.shape[0]] + up, one[up.shape[0] :]], axis=0)
-    three = jnp.concatenate([three[: up.shape[0]], three[up.shape[0] :] + down], axis=0)
-    return (ring(one, 1), ring(three, -1)), (one, three)
 
 
 def project_scatter(by_y, by_z, weight):
     wa, wb = weight[:, :CUT], weight[:, CUT:]
-    b_far, by_z = together(mm(by_y[1], wb), by_z)
-    b_came = swap(b_far, "yl")
-    a_came = pass_two(mm(by_z[2], wa))
-    a_came, a_sent = pass_one(mm(by_z[1], wa), mm(by_z[3], wa), a_came)
-    b = mm(by_y[0], wb) + b_came
-    b = b.reshape(4, -1, b.shape[1])
-    b_came = pass_two(b[2])
+    block = by_z.shape[1] // 2
+    far_two, far_rest = mm(by_y[1, :block], wb), mm(by_y[1, block:], wb)
+    far_two, far_rest, by_z = together(far_two, far_rest, by_z)
+    b_two, b_rest = swap(far_two, "yl"), swap(far_rest, "yl")
+    up, down = both_ways(*halves(mm(by_z[2], wa)))
+    one, three = mm(by_z[1], wa), mm(by_z[3], wa)
+    one = jnp.concatenate([one[:block] + up, one[block:]], axis=0)
+    three = jnp.concatenate([three[:block], three[block:] + down], axis=0)
+    one, three, b_two = together(one, three, b_two)
+    a_came = both_ways(one, three)
+    b_two = b_two + mm(by_y[0, :block], wb)
+    b_up, b_down = both_ways(*halves(b_two))
+    b_rest = b_rest + mm(by_y[0, block:], wb)
+    half = block // 2
+    b_one, b_three = b_rest[block : 2 * block], b_rest[2 * block :]
+    b_one = jnp.concatenate([b_one[:half] + b_up, b_one[half:]], axis=0)
+    b_three = jnp.concatenate([b_three[:half], b_three[half:] + b_down], axis=0)
     a = mm(by_z[0], wa) + sum(a_came)
-    a, a_far = halves(a)
-    a_came = swap(a_far, "yl")
-    b_came, _ = pass_one(b[1], b[3], b_came)
-    return jnp.concatenate([a + a_came, b[0] + sum(b_came)], axis=1)
+    a, b_one, b_three = together(a, b_one, b_three)
+    b_came = both_ways(b_one, b_three)
+    a_came = swap(a[block:], "yl")
+    return jnp.concatenate([a[:block] + a_came, b_rest[:block] + sum(b_came)], axis=1)
 
 
 def body(keys, queries, values, rates, gate, up, down, out_weight):
@@ -341,9 +344,11 @@
     k, d, sent = sort_tokens(at, keys, values, rates.T)
     came = swap(sent, "core")
     partial, rounded = near_grads(at, k, d, *weights)
-    total = plane_scatter(far_grads(came, rounded, partial))
-    total, queries = together(total, queries)
+    queries, partial = together(queries, partial)
     q, q_sent = sort_queries(at, queries)
+    summed = far_grads(came, rounded, partial)
+    q_sent, summed = together(q_sent, summed)
+    total = plane_scatter(summed)
     whole, q_sent = together(plane_gather(total), q_sent)
     q_came = swap(q_sent, "core")
     v = newton(at, whole, *weights)

time: 203 us -> 201 us (level)
  blocking collectives: 39.7 us -> 74.5 us
  waiting for transfers between devices: 98.4 us -> 65.3 us
  starting transfers between devices: 19.6 us -> 16.3 us
    all_to_all x0 -> x1, blocking collectives: none -> 34.7 us  [plane_gather(): return lax.all_to_all(same, PLANE, 0, 0, tiled=True)]
    all_to_all x1 -> x0, waiting for transfers between devices: 33.9 us -> none  [plane_gather(): return lax.all_to_all(same, PLANE, 0, 0, tiled=True)]
    all_to_all x1 -> x0, starting transfers between devices: 3.75 us -> none  [plane_gather(): return lax.all_to_all(same, PLANE, 0, 0, tiled=True)]
    ppermute x8, waiting for transfers between devices: 29.8 us -> 32.5 us  [ring(): return lax.ppermute(a, 'z', [(i, (i + shift) % 4) for i in range(4)])]
    ppermute x5 -> x6, waiting for transfers between devices: 34.7 us -> 32.9 us  [swap(): return lax.ppermute(a, axis, [(0, 1), (1, 0)])]
    dot_general x6 -> x8, matrix products: 5.12 us -> 5.73 us  [mm(): return jnp.dot(a, b, preferred_element_type=F32)]
  transfers between devices with their start and end apart: 14 -> 14, of which waited for: 8 -> 7; matrix products, arithmetic and copies ran while one was open for 2% -> 2% of each run, Pallas kernels for 13% -> 13%
where the time goes in v5:
time: 201 us
  blocking collectives  74.5 us (37%)
  waiting for transfers between devices  65.3 us (32%)
  Pallas kernels  31.6 us (16%)
  starting transfers between devices  16.3 us (8%)
  matrix products  5.73 us (3%)
  local copies, waits for them, and re-layouts  4.19 us (2%)
  other arithmetic  3.07 us (2%)
    all_to_all x1, blocking collectives, plane_scatter(): return jnp.sum(lax.all_to_all(a, PLANE, 0, 0, tiled=True), axis=0)  39.8 us
    all_to_all x1, blocking collectives, plane_gather(): return lax.all_to_all(same, PLANE, 0, 0, tiled=True)  34.7 us
    ppermute x6, waiting for transfers between devices, swap(): return lax.ppermute(a, axis, [(0, 1), (1, 0)])  32.9 us
    ppermute x8, waiting for transfers between devices, ring(): return lax.ppermute(a, 'z', [(i, (i + shift) % 4) for i in range(4)])  32.5 us
    pallas_call x1, Pallas kernels, newton(): pl.pallas_call(newton_kernel, out_shape=out(shape, BF16), in_specs=[pl.Bl...  19.5 us
    ppermute x8, starting transfers between devices, ring(): return lax.ppermute(a, 'z', [(i, (i + shift) % 4) for i in range(4)])  12.8 us
    pallas_call x6, Pallas kernels, call(): pl.pallas_call(kernel, out_shape=outs, in_specs=specs, out_specs=jax.tree...  7.56 us
    dot_general x8, matrix products, mm(): return jnp.dot(a, b, preferred_element_type=F32)  5.73 us
  transfers between devices with their start and end apart: 14, of which 7 were waited for; matrix products, arithmetic and copies ran while one was open for 2% of the time, Pallas kernels for 13%

profile of v5, /device:TPU:0, one launch (start us, length us, event | category | flops | bytes accessed | tf_op | source)
XLA Modules:
  0.0 201.0 jit_solution(6037162414233029244)
XLA Ops:
  0.1 1.1 copy-done
  1.2 1.1 copy-done.1
  2.9 1.1 sort_tokens.1
  4.1 4.5 %near_grads.1 = (f32[3,320,640]{2,1,0:T(8,128)S(1)}, bf16[3,320,640]{2,1,0:T(8,128)(2,1)S(1)}) custom-call(s32[3]{0:T(128)S(1)} %pad_add_fusion.at_ref, bf16[512,320]{1,0:T(8,128)(2,1)S(1)} %get-tuple-element.29.k_ref, bf16[512,320]{1,0:T(8,128)(2,1)S(1)} %get-tuple-element.30.d_ref, f32[2,320,640]{2,1,0:T(8,128)} %wg_ref.1, f32[2,320,640]{2,1,0:T(8,128)} %wu_ref.1, ...), custom_call_target="tpu_custom_call" | custom-call | tf_op jit(solution)/shard_map/near_grads/pallas_call | solution.py:151
  9.4 2.3 %far_grads.1 = f32[8,3,40,640]{3,2,1,0:T(8,128)S(1)} custom-call(f32[512,640]{1,0:T(8,128)S(1)} %collective-permute-done.came, bf16[3,320,640]{2,1,0:T(8,128)(2,1)S(1)} %get-tuple-element.36.b_ref, f32[3,320,640]{2,1,0:T(8,128)S(1)} %get-tuple-element.37.p_ref), custom_call_target="tpu_custom_call" | custom-call | tf_op jit(solution)/shard_map/far_grads/pallas_call | solution.py:35
  11.7 39.8 %all_to_all.10 = f32[8,3,40,640]{3,2,1,0:T(8,128)S(1)} all-to-all(f32[8,3,40,640]{3,2,1,0:T(8,128)S(1)} %far_grads.1), channel_id=1, replica_groups=mesh['yl'=2,'z'=4,'x'=4,'yh'=2,'core'=2] {'x','yh'}, dimensions={0} | all-to-all | bytes 4915200 | tf_op jit(solution)/shard_map/all_to_all | solution.py:294
  51.5 0.9 reduce_sum.9
  52.4 1.1 broadcast_in_dim.2
  53.5 34.7 %all_to_all.11.g_ref = f32[8,3,40,640]{3,2,1,0:T(8,128)S(1)} all-to-all(f32[8,3,40,640]{3,2,1,0:T(8,128)S(1)} %broadcast_in_dim.2), channel_id=1, replica_groups=mesh['yl'=2,'z'=4,'x'=4,'yh'=2,'core'=2] {'x','yh'}, dimensions={0} | all-to-all | bytes 4915200 | tf_op jit(solution)/shard_map/all_to_all | solution.py:299
  88.2 19.5 %newton.1.v_ref = bf16[3,320,640]{2,1,0:T(8,128)(2,1)S(1)} custom-call(s32[3]{0:T(128)S(1)} %pad_add_fusion.at_ref, f32[8,3,40,640]{3,2,1,0:T(8,128)S(1)} %all_to_all.11.g_ref, f32[2,320,640]{2,1,0:T(8,128)} %wg_ref.1, f32[2,320,640]{2,1,0:T(8,128)} %wu_ref.1, f32[2,320,640]{2,1,0:T(8,128)} %wd_ref.1), custom_call_target="tpu_custom_call" | custom-call | tf_op jit(solution)/shard_map/newton/pallas_call | solution.py:229
  107.7 1.4 far_query.1
  109.7 1.3 near_query.1.o_ref
  112.2 0.9 fusion.11
  113.6 0.7 fusion.2
  114.3 0.7 fusion
  115.2 4.1 %collective-permute-start.4 = (f32[64,2816]{1,0:T(8,128)S(1)}, f32[64,2816]{1,0:T(8,128)S(1)}, u32[]{:S(2)}, u32[]{:S(2)}) collective-permute-start(f32[64,2816]{1,0:T(8,128)S(1)} %get-tuple-element.59), channel_id=1, source_target_pairs={{0,48},{16,0},{32,16},{48,32},{1,49},{17,1},{33,17},{49,33},{2,50}... | collective-permute-start | bytes 2162696 | tf_op jit(solution)/shard_map/ppermute | solution.py:290
  119.9 0.8 collective-permute-start.5
  120.6 1.4 collective-permute-start.8
  122.0 0.7 fusion.4
  122.7 0.7 fusion.6
  123.5 11.8 %collective-permute-done.4 = f32[64,2816]{1,0:T(8,128)S(1)} collective-permute-done((f32[64,2816]{1,0:T(8,128)S(1)}, f32[64,2816]{1,0:T(8,128)S(1)}, u32[]{:S(2)}, u32[]{:S(2)}) %collective-permute-start.4) | collective-permute-done | bytes 720928 | tf_op jit(solution)/shard_map/ppermute | solution.py:290
  135.5 3.8 %collective-permute-done.3 = f32[64,2816]{1,0:T(8,128)S(1)} collective-permute-done((f32[64,2816]{1,0:T(8,128)S(1)}, f32[64,2816]{1,0:T(8,128)S(1)}, u32[]{:S(2)}, u32[]{:S(2)}) %collective-permute-start.3) | collective-permute-done | bytes 720928 | tf_op jit(solution)/shard_map/ppermute | solution.py:290
  139.9 2.0 %collective-permute-start.9 = (f32[32,2304]{1,0:T(8,128)S(1)}, f32[32,2304]{1,0:T(8,128)S(1)}, u32[]{:S(2)}, u32[]{:S(2)}) collective-permute-start(f32[32,2304]{1,0:T(8,128)S(1)} %get-tuple-element.64), channel_id=1, source_target_pairs={{0,16},{16,32},{32,48},{48,0},{1,17},{17,33},{33,49},{49,1},{2,18}... | collective-permute-start | bytes 884744 | tf_op jit(solution)/shard_map/ppermute | solution.py:290
  142.0 3.2 %collective-permute-start.7 = (f32[128,2816]{1,0:T(8,128)S(1)}, f32[128,2816]{1,0:T(8,128)S(1)}, u32[]{:S(2)}, u32[]{:S(2)}) collective-permute-start(f32[128,2816]{1,0:T(8,128)S(1)} %get-tuple-element.47), channel_id=1, source_target_pairs={{0,48},{16,0},{32,16},{48,32},{1,49},{17,1},{33,17},{49,33},{2,50}... | collective-permute-start | bytes 4325384 | tf_op jit(solution)/shard_map/ppermute | solution.py:290
  145.2 28.2 %collective-permute-done.8 = f32[192,2304]{1,0:T(8,128)S(1)} collective-permute-done((f32[192,2304]{1,0:T(8,128)S(1)}, f32[192,2304]{1,0:T(8,128)S(1)}, u32[]{:S(2)}, u32[]{:S(2)}) %collective-permute-start.8) | collective-permute-done | bytes 1769504 | tf_op jit(solution)/shard_map/ppermute | solution.py:286
  173.3 0.9 convolution_add_fusion
  174.4 6.0 %collective-permute-done.6 = f32[128,2816]{1,0:T(8,128)S(1)} collective-permute-done((f32[128,2816]{1,0:T(8,128)S(1)}, f32[128,2816]{1,0:T(8,128)S(1)}, u32[]{:S(2)}, u32[]{:S(2)}) %collective-permute-start.6) | collective-permute-done | bytes 1441824 | tf_op jit(solution)/shard_map/ppermute | solution.py:290
  181.2 2.8 %collective-permute-start.13 = (f32[64,2304]{1,0:T(8,128)S(1)}, f32[64,2304]{1,0:T(8,128)S(1)}, u32[]{:S(2)}, u32[]{:S(2)}) collective-permute-start(f32[64,2304]{1,0:T(8,128)S(1)} %pad_maximum_fusion.4), channel_id=1, source_target_pairs={{0,48},{16,0},{32,16},{48,32},{1,49},{17,1},{33,17},{49,33},{2,50}... | collective-permute-start | bytes 1769480 | tf_op jit(solution)/shard_map/ppermute | solution.py:290
  184.0 0.8 collective-permute-start.11
  184.8 10.9 %collective-permute-done.12 = f32[64,2304]{1,0:T(8,128)S(1)} collective-permute-done((f32[64,2304]{1,0:T(8,128)S(1)}, f32[64,2304]{1,0:T(8,128)S(1)}, u32[]{:S(2)}, u32[]{:S(2)}) %collective-permute-start.12) | collective-permute-done | bytes 589856 | tf_op jit(solution)/shard_map/ppermute | solution.py:290
  195.7 4.3 %collective-permute-done.11 = f32[64,2816]{1,0:T(8,128)S(1)} collective-permute-done((f32[64,2816]{1,0:T(8,128)S(1)}, f32[64,2816]{1,0:T(8,128)S(1)}, u32[]{:S(2)}, u32[]{:S(2)}) %collective-permute-start.11) | collective-permute-done | bytes 720928 | tf_op jit(solution)/shard_map/ppermute | solution.py:286
  200.1 0.9 pad_maximum_fusion.2
  (44 shorter events, 6.4 us)
Async XLA Ops:
  0.1 1.1 copy-start
  1.2 1.1 copy-start.1
  2.3 0.7 copy-start.3
  4.0 5.4 %collective-permute-start = (f32[512,640]{1,0:T(8,128)S(1)}, f32[512,640]{1,0:T(8,128)S(1)}, u32[]{:S(2)}, u32[]{:S(2)}) collective-permute-start(f32[512,640]{1,0:T(8,128)S(1)} %get-tuple-element.35), channel_id=1, source_target_pairs={{0,1},{1,0},{2,3},{3,2},{4,5},{5,4},{6,7},{7,6},{8,9},{9,8},{10,11... | collective-permute-start | bytes 3932168 | tf_op jit(solution)/shard_map/ppermute | solution.py:286
  4.1 4.6 %copy-start.2 = (bf16[512,640]{1,0:T(8,128)(2,1)S(1)}, bf16[512,640]{1,0:T(8,128)(2,1)}, u32[]{:S(2)}) copy-start(bf16[512,640]{1,0:T(8,128)(2,1)} %q_ref) | copy-start | bytes 1966084
  53.5 58.7 %slice-start = ((s8[6553600]{0:T(1024)(128)(4,1)}), s8[4194304]{0:T(1024)(128)(4,1)S(1)}, s32[]{:S(2)}) async-start(s8[6553600]{0:T(1024)(128)(4,1)} %bitcast.29), calls=%async_computation.2 | async-start | bytes 8388608
  88.2 23.9 %slice-start.1 = ((s8[6553600]{0:T(1024)(128)(4,1)}), s8[2359296]{0:T(1024)(128)(4,1)S(1)}, s32[]{:S(2)}) async-start(s8[6553600]{0:T(1024)(128)(4,1)} %bitcast.29), calls=%async_computation.3 | async-start | bytes 4718592
  88.2 19.5 %collective-permute-start.1 = (f32[256,640]{1,0:T(8,128)S(1)}, f32[256,640]{1,0:T(8,128)S(1)}, u32[]{:S(2)}, u32[]{:S(2)}) collective-permute-start(f32[256,640]{1,0:T(8,128)S(1)} %get-tuple-element.41), channel_id=1, source_target_pairs={{0,1},{1,0},{2,3},{3,2},{4,5},{5,4},{6,7},{7,6},{8,9},{9,8},{10,11... | collective-permute-start | bytes 1966088 | tf_op jit(solution)/shard_map/ppermute | solution.py:286
  109.1 2.3 %collective-permute-start.2 = (f32[256,640]{1,0:T(8,128)S(1)}, f32[256,640]{1,0:T(8,128)S(1)}, u32[]{:S(2)}, u32[]{:S(2)}) collective-permute-start(f32[256,640]{1,0:T(8,128)S(1)} %far_query.1), channel_id=1, source_target_pairs={{0,1},{1,0},{2,3},{3,2},{4,5},{5,4},{6,7},{7,6},{8,9},{9,8},{10,11... | collective-permute-start | bytes 1966088 | tf_op jit(solution)/shard_map/ppermute | solution.py:286
  115.2 20.1 %collective-permute-start.4 = (f32[64,2816]{1,0:T(8,128)S(1)}, f32[64,2816]{1,0:T(8,128)S(1)}, u32[]{:S(2)}, u32[]{:S(2)}) collective-permute-start(f32[64,2816]{1,0:T(8,128)S(1)} %get-tuple-element.59), channel_id=1, source_target_pairs={{0,48},{16,0},{32,16},{48,32},{1,49},{17,1},{33,17},{49,33},{2,50}... | collective-permute-start | bytes 2162696 | tf_op jit(solution)/shard_map/ppermute | solution.py:290
  119.8 19.5 %collective-permute-start.3 = (f32[64,2816]{1,0:T(8,128)S(1)}, f32[64,2816]{1,0:T(8,128)S(1)}, u32[]{:S(2)}, u32[]{:S(2)}) collective-permute-start(f32[64,2816]{1,0:T(8,128)S(1)} %get-tuple-element.60), channel_id=1, source_target_pairs={{0,16},{16,32},{32,48},{48,0},{1,17},{17,33},{33,49},{49,1},{2,18}... | collective-permute-start | bytes 2162696 | tf_op jit(solution)/shard_map/ppermute | solution.py:290
  119.9 19.8 %collective-permute-start.5 = (f32[64,2304]{1,0:T(8,128)S(1)}, f32[64,2304]{1,0:T(8,128)S(1)}, u32[]{:S(2)}, u32[]{:S(2)}) collective-permute-start(f32[64,2304]{1,0:T(8,128)S(1)} %fusion.13), channel_id=1, source_target_pairs={{0,64},{64,0},{1,65},{65,1},{2,66},{66,2},{3,67},{67,3},{4,68},{68... | collective-permute-start | bytes 1769480 | tf_op jit(solution)/shard_map/ppermute | solution.py:286
  120.6 52.7 %collective-permute-start.8 = (f32[192,2304]{1,0:T(8,128)S(1)}, f32[192,2304]{1,0:T(8,128)S(1)}, u32[]{:S(2)}, u32[]{:S(2)}) collective-permute-start(f32[192,2304]{1,0:T(8,128)S(1)} %fusion.11), channel_id=1, source_target_pairs={{0,64},{64,0},{1,65},{65,1},{2,66},{66,2},{3,67},{67,3},{4,68},{68... | collective-permute-start | bytes 5308424 | tf_op jit(solution)/shard_map/ppermute | solution.py:286
  139.8 34.4 %collective-permute-start.10 = (f32[32,2304]{1,0:T(8,128)S(1)}, f32[32,2304]{1,0:T(8,128)S(1)}, u32[]{:S(2)}, u32[]{:S(2)}) collective-permute-start(f32[32,2304]{1,0:T(8,128)S(1)} %get-tuple-element.63), channel_id=1, source_target_pairs={{0,48},{16,0},{32,16},{48,32},{1,49},{17,1},{33,17},{49,33},{2,50}... | collective-permute-start | bytes 884744 | tf_op jit(solution)/shard_map/ppermute | solution.py:290
  139.9 34.3 %collective-permute-start.9 = (f32[32,2304]{1,0:T(8,128)S(1)}, f32[32,2304]{1,0:T(8,128)S(1)}, u32[]{:S(2)}, u32[]{:S(2)}) collective-permute-start(f32[32,2304]{1,0:T(8,128)S(1)} %get-tuple-element.64), channel_id=1, source_target_pairs={{0,16},{16,32},{32,48},{48,0},{1,17},{17,33},{33,49},{49,1},{2,18}... | collective-permute-start | bytes 884744 | tf_op jit(solution)/shard_map/ppermute | solution.py:290
  141.9 38.5 %collective-permute-start.6 = (f32[128,2816]{1,0:T(8,128)S(1)}, f32[128,2816]{1,0:T(8,128)S(1)}, u32[]{:S(2)}, u32[]{:S(2)}) collective-permute-start(f32[128,2816]{1,0:T(8,128)S(1)} %get-tuple-element.46), channel_id=1, source_target_pairs={{0,16},{16,32},{32,48},{48,0},{1,17},{17,33},{33,49},{49,1},{2,18}... | collective-permute-start | bytes 4325384 | tf_op jit(solution)/shard_map/ppermute | solution.py:290
  142.0 38.4 %collective-permute-start.7 = (f32[128,2816]{1,0:T(8,128)S(1)}, f32[128,2816]{1,0:T(8,128)S(1)}, u32[]{:S(2)}, u32[]{:S(2)}) collective-permute-start(f32[128,2816]{1,0:T(8,128)S(1)} %get-tuple-element.47), channel_id=1, source_target_pairs={{0,48},{16,0},{32,16},{48,32},{1,49},{17,1},{33,17},{49,33},{2,50}... | collective-permute-start | bytes 4325384 | tf_op jit(solution)/shard_map/ppermute | solution.py:290
  180.7 15.0 %collective-permute-start.12 = (f32[64,2304]{1,0:T(8,128)S(1)}, f32[64,2304]{1,0:T(8,128)S(1)}, u32[]{:S(2)}, u32[]{:S(2)}) collective-permute-start(f32[64,2304]{1,0:T(8,128)S(1)} %pad_maximum_fusion.3), channel_id=1, source_target_pairs={{0,16},{16,32},{32,48},{48,0},{1,17},{17,33},{33,49},{49,1},{2,18}... | collective-permute-start | bytes 1769480 | tf_op jit(solution)/shard_map/ppermute | solution.py:290
  181.2 14.5 %collective-permute-start.13 = (f32[64,2304]{1,0:T(8,128)S(1)}, f32[64,2304]{1,0:T(8,128)S(1)}, u32[]{:S(2)}, u32[]{:S(2)}) collective-permute-start(f32[64,2304]{1,0:T(8,128)S(1)} %pad_maximum_fusion.4), channel_id=1, source_target_pairs={{0,48},{16,0},{32,16},{48,32},{1,49},{17,1},{33,17},{49,33},{2,50}... | collective-permute-start | bytes 1769480 | tf_op jit(solution)/shard_map/ppermute | solution.py:290
  184.0 16.0 %collective-permute-start.11 = (f32[64,2816]{1,0:T(8,128)S(1)}, f32[64,2816]{1,0:T(8,128)S(1)}, u32[]{:S(2)}, u32[]{:S(2)}) collective-permute-start(f32[64,2816]{1,0:T(8,128)S(1)} %slice.104), channel_id=1, source_target_pairs={{0,64},{64,0},{1,65},{65,1},{2,66},{66,2},{3,67},{67,3},{4,68},{68... | collective-permute-start | bytes 2162696 | tf_op jit(solution)/shard_map/ppermute | solution.py:286

commit v6 on v5

--- a/solution.py
+++ b/solution.py
@@ -16,7 +16,7 @@
 SHARDS = 8
 TILE = 256
 VMEM_LIMIT = 24 << 20
-CUT = 2816
+CUT = 2944
 Y_ORDER = (2, 0, 1, 3)
 F32 = jnp.float32
 BF16 = jnp.bfloat16
@@ -315,24 +315,23 @@
 def project_scatter(by_y, by_z, weight):
     wa, wb = weight[:, :CUT], weight[:, CUT:]
     block = by_z.shape[1] // 2
-    far_two, far_rest = mm(by_y[1, :block], wb), mm(by_y[1, block:], wb)
-    far_two, far_rest, by_z = together(far_two, far_rest, by_z)
-    b_two, b_rest = swap(far_two, "yl"), swap(far_rest, "yl")
+    far_two, by_y, by_z = together(mm(by_y[1, :block], wb), by_y, by_z)
+    b_two = swap(far_two, "yl")
     up, down = both_ways(*halves(mm(by_z[2], wa)))
+    far_rest, b_two, by_y, by_z = together(mm(by_y[1, block:], wb), b_two, by_y, by_z)
+    b_rest = swap(far_rest, "yl")
+    b_two = b_two + mm(by_y[0, :block], wb)
+    b_up, b_down = both_ways(*halves(b_two))
     one, three = mm(by_z[1], wa), mm(by_z[3], wa)
     one = jnp.concatenate([one[:block] + up, one[block:]], axis=0)
     three = jnp.concatenate([three[:block], three[block:] + down], axis=0)
-    one, three, b_two = together(one, three, b_two)
     a_came = both_ways(one, three)
-    b_two = b_two + mm(by_y[0, :block], wb)
-    b_up, b_down = both_ways(*halves(b_two))
     b_rest = b_rest + mm(by_y[0, block:], wb)
     half = block // 2
     b_one, b_three = b_rest[block : 2 * block], b_rest[2 * block :]
     b_one = jnp.concatenate([b_one[:half] + b_up, b_one[half:]], axis=0)
     b_three = jnp.concatenate([b_three[:half], b_three[half:] + b_down], axis=0)
     a = mm(by_z[0], wa) + sum(a_came)
-    a, b_one, b_three = together(a, b_one, b_three)
     b_came = both_ways(b_one, b_three)
     a_came = swap(a[block:], "yl")
     return jnp.concatenate([a[:block] + a_came, b_rest[:block] + sum(b_came)], axis=1)

time: 201 us -> 195 us (0.970)
  waiting for transfers between devices: 65.3 us -> 55.3 us
  starting transfers between devices: 16.3 us -> 19.5 us
    ppermute x8, waiting for transfers between devices: 32.5 us -> 12.9 us  [ring(): return lax.ppermute(a, 'z', [(i, (i + shift) % 4) for i in range(4)])]
    ppermute x6, waiting for transfers between devices: 32.9 us -> 42.3 us  [swap(): return lax.ppermute(a, axis, [(0, 1), (1, 0)])]
    ppermute x8, starting transfers between devices: 12.8 us -> 15.9 us  [ring(): return lax.ppermute(a, 'z', [(i, (i + shift) % 4) for i in range(4)])]
  transfers between devices with their start and end apart: 14 -> 14, of which waited for: 7 -> 6; matrix products, arithmetic and copies ran while one was open for 2% -> 4% of each run, Pallas kernels for 13% -> 13%
where the time goes in v6:
time: 195 us
  blocking collectives  74.5 us (38%)
  waiting for transfers between devices  55.3 us (28%)
  Pallas kernels  31.7 us (16%)
  starting transfers between devices  19.5 us (10%)
  matrix products  6.32 us (3%)
  local copies, waits for them, and re-layouts  4.19 us (2%)
  other arithmetic  2.97 us (2%)
    ppermute x6, waiting for transfers between devices, swap(): return lax.ppermute(a, axis, [(0, 1), (1, 0)])  42.3 us
    all_to_all x1, blocking collectives, plane_scatter(): return jnp.sum(lax.all_to_all(a, PLANE, 0, 0, tiled=True), axis=0)  39.8 us
    all_to_all x1, blocking collectives, plane_gather(): return lax.all_to_all(same, PLANE, 0, 0, tiled=True)  34.7 us
    pallas_call x1, Pallas kernels, newton(): pl.pallas_call(newton_kernel, out_shape=out(shape, BF16), in_specs=[pl.Bl...  19.5 us
    ppermute x8, starting transfers between devices, ring(): return lax.ppermute(a, 'z', [(i, (i + shift) % 4) for i in range(4)])  15.9 us
    ppermute x8, waiting for transfers between devices, ring(): return lax.ppermute(a, 'z', [(i, (i + shift) % 4) for i in range(4)])  12.9 us
    pallas_call x6, Pallas kernels, call(): pl.pallas_call(kernel, out_shape=outs, in_specs=specs, out_specs=jax.tree...  7.6 us
    dot_general x8, matrix products, mm(): return jnp.dot(a, b, preferred_element_type=F32)  6.32 us
  transfers between devices with their start and end apart: 14, of which 6 were waited for; matrix products, arithmetic and copies ran while one was open for 4% of the time, Pallas kernels for 13%

profile of v6, /device:TPU:0, one launch (start us, length us, event | category | flops | bytes accessed | tf_op | source)
XLA Modules:
  0.0 194.8 jit_solution(14363753637676859156)
XLA Ops:
  0.1 1.1 copy-done
  1.2 1.1 copy-done.1
  2.9 1.1 sort_tokens.1
  4.1 4.6 %near_grads.1 = (f32[3,320,640]{2,1,0:T(8,128)S(1)}, bf16[3,320,640]{2,1,0:T(8,128)(2,1)S(1)}) custom-call(s32[3]{0:T(128)S(1)} %pad_add_fusion.at_ref, bf16[512,320]{1,0:T(8,128)(2,1)S(1)} %get-tuple-element.27.k_ref, bf16[512,320]{1,0:T(8,128)(2,1)S(1)} %get-tuple-element.28.d_ref, f32[2,320,640]{2,1,0:T(8,128)} %wg_ref.1, f32[2,320,640]{2,1,0:T(8,128)} %wu_ref.1, ...), custom_call_target="tpu_custom_call" | custom-call | tf_op jit(solution)/shard_map/near_grads/pallas_call | solution.py:151
  9.5 2.4 %far_grads.1 = f32[8,3,40,640]{3,2,1,0:T(8,128)S(1)} custom-call(f32[512,640]{1,0:T(8,128)S(1)} %collective-permute-done.came, bf16[3,320,640]{2,1,0:T(8,128)(2,1)S(1)} %get-tuple-element.34.b_ref, f32[3,320,640]{2,1,0:T(8,128)S(1)} %get-tuple-element.35.p_ref), custom_call_target="tpu_custom_call" | custom-call | tf_op jit(solution)/shard_map/far_grads/pallas_call | solution.py:35
  11.9 39.8 %all_to_all.10 = f32[8,3,40,640]{3,2,1,0:T(8,128)S(1)} all-to-all(f32[8,3,40,640]{3,2,1,0:T(8,128)S(1)} %far_grads.1), channel_id=1, replica_groups=mesh['yl'=2,'z'=4,'x'=4,'yh'=2,'core'=2] {'x','yh'}, dimensions={0} | all-to-all | bytes 4915200 | tf_op jit(solution)/shard_map/all_to_all | solution.py:294
  51.7 0.9 reduce_sum.9
  52.6 1.1 broadcast_in_dim.2
  53.7 34.7 %all_to_all.11.g_ref = f32[8,3,40,640]{3,2,1,0:T(8,128)S(1)} all-to-all(f32[8,3,40,640]{3,2,1,0:T(8,128)S(1)} %broadcast_in_dim.2), channel_id=1, replica_groups=mesh['yl'=2,'z'=4,'x'=4,'yh'=2,'core'=2] {'x','yh'}, dimensions={0} | all-to-all | bytes 4915200 | tf_op jit(solution)/shard_map/all_to_all | solution.py:299
  88.4 19.5 %newton.1.v_ref = bf16[3,320,640]{2,1,0:T(8,128)(2,1)S(1)} custom-call(s32[3]{0:T(128)S(1)} %pad_add_fusion.at_ref, f32[8,3,40,640]{3,2,1,0:T(8,128)S(1)} %all_to_all.11.g_ref, f32[2,320,640]{2,1,0:T(8,128)} %wg_ref.1, f32[2,320,640]{2,1,0:T(8,128)} %wu_ref.1, f32[2,320,640]{2,1,0:T(8,128)} %wd_ref.1), custom_call_target="tpu_custom_call" | custom-call | tf_op jit(solution)/shard_map/newton/pallas_call | solution.py:229
  107.9 1.4 far_query.1
  109.9 1.3 near_query.1.o_ref
  113.0 0.8 collective-permute-start.3
  113.7 0.8 fusion.2
  114.7 2.0 %collective-permute-start.4 = (f32[64,2944]{1,0:T(8,128)S(1)}, f32[64,2944]{1,0:T(8,128)S(1)}, u32[]{:S(2)}, u32[]{:S(2)}) collective-permute-start(f32[64,2944]{1,0:T(8,128)S(1)} %get-tuple-element.56), channel_id=1, source_target_pairs={{0,16},{16,32},{32,48},{48,0},{1,17},{17,33},{33,49},{49,1},{2,18}... | collective-permute-start | bytes 2261000 | tf_op jit(solution)/shard_map/ppermute | solution.py:290
  116.7 2.2 %collective-permute-start.6 = (f32[64,2944]{1,0:T(8,128)S(1)}, f32[64,2944]{1,0:T(8,128)S(1)}, u32[]{:S(2)}, u32[]{:S(2)}) collective-permute-start(f32[64,2944]{1,0:T(8,128)S(1)} %get-tuple-element.55), channel_id=1, source_target_pairs={{0,48},{16,0},{32,16},{48,32},{1,49},{17,1},{33,17},{49,33},{2,50}... | collective-permute-start | bytes 2261000 | tf_op jit(solution)/shard_map/ppermute | solution.py:290
  118.9 0.9 fusion.12
  119.8 8.3 %collective-permute-done.3 = f32[64,2176]{1,0:T(8,128)S(1)} collective-permute-done((f32[64,2176]{1,0:T(8,128)S(1)}, f32[64,2176]{1,0:T(8,128)S(1)}, u32[]{:S(2)}, u32[]{:S(2)}) %collective-permute-start.3) | collective-permute-done | bytes 557088 | tf_op jit(solution)/shard_map/ppermute | solution.py:286
  128.1 0.9 fusion.10
  130.5 4.1 %collective-permute-start.12 = (f32[32,2176]{1,0:T(8,128)S(1)}, f32[32,2176]{1,0:T(8,128)S(1)}, u32[]{:S(2)}, u32[]{:S(2)}) collective-permute-start(f32[32,2176]{1,0:T(8,128)S(1)} %get-tuple-element.59), channel_id=1, source_target_pairs={{0,48},{16,0},{32,16},{48,32},{1,49},{17,1},{33,17},{49,33},{2,50}... | collective-permute-start | bytes 835592 | tf_op jit(solution)/shard_map/ppermute | solution.py:290
  134.6 0.8 fusion.4
  135.4 0.8 fusion
  136.9 3.2 %collective-permute-start.7 = (f32[128,2944]{1,0:T(8,128)S(1)}, f32[128,2944]{1,0:T(8,128)S(1)}, u32[]{:S(2)}, u32[]{:S(2)}) collective-permute-start(f32[128,2944]{1,0:T(8,128)S(1)} %pad_maximum_fusion.1), channel_id=1, source_target_pairs={{0,48},{16,0},{32,16},{48,32},{1,49},{17,1},{33,17},{49,33},{2,50}... | collective-permute-start | bytes 4521992 | tf_op jit(solution)/shard_map/ppermute | solution.py:290
  140.1 27.6 %collective-permute-done.9 = f32[192,2176]{1,0:T(8,128)S(1)} collective-permute-done((f32[192,2176]{1,0:T(8,128)S(1)}, f32[192,2176]{1,0:T(8,128)S(1)}, u32[]{:S(2)}, u32[]{:S(2)}) %collective-permute-start.9) | collective-permute-done | bytes 1671200 | tf_op jit(solution)/shard_map/ppermute | solution.py:286
  168.2 2.0 %collective-permute-start.11 = (f32[64,2176]{1,0:T(8,128)S(1)}, f32[64,2176]{1,0:T(8,128)S(1)}, u32[]{:S(2)}, u32[]{:S(2)}) collective-permute-start(f32[64,2176]{1,0:T(8,128)S(1)} %pad_maximum_fusion.3), channel_id=1, source_target_pairs={{0,16},{16,32},{32,48},{48,0},{1,17},{17,33},{33,49},{49,1},{2,18}... | collective-permute-start | bytes 1671176 | tf_op jit(solution)/shard_map/ppermute | solution.py:290
  170.2 2.2 %collective-permute-start.13 = (f32[64,2176]{1,0:T(8,128)S(1)}, f32[64,2176]{1,0:T(8,128)S(1)}, u32[]{:S(2)}, u32[]{:S(2)}) collective-permute-start(f32[64,2176]{1,0:T(8,128)S(1)} %pad_maximum_fusion.4), channel_id=1, source_target_pairs={{0,48},{16,0},{32,16},{48,32},{1,49},{17,1},{33,17},{49,33},{2,50}... | collective-permute-start | bytes 1671176 | tf_op jit(solution)/shard_map/ppermute | solution.py:290
  172.4 5.2 %collective-permute-done.5 = f32[128,2944]{1,0:T(8,128)S(1)} collective-permute-done((f32[128,2944]{1,0:T(8,128)S(1)}, f32[128,2944]{1,0:T(8,128)S(1)}, u32[]{:S(2)}, u32[]{:S(2)}) %collective-permute-start.5) | collective-permute-done | bytes 1507360 | tf_op jit(solution)/shard_map/ppermute | solution.py:290
  177.7 0.9 add_add_fusion
  178.6 1.4 collective-permute-start.8
  180.1 7.7 %collective-permute-done.11 = f32[64,2176]{1,0:T(8,128)S(1)} collective-permute-done((f32[64,2176]{1,0:T(8,128)S(1)}, f32[64,2176]{1,0:T(8,128)S(1)}, u32[]{:S(2)}, u32[]{:S(2)}) %collective-permute-start.11) | collective-permute-done | bytes 557088 | tf_op jit(solution)/shard_map/ppermute | solution.py:290
  187.9 5.9 %collective-permute-done.8 = f32[64,2944]{1,0:T(8,128)S(1)} collective-permute-done((f32[64,2944]{1,0:T(8,128)S(1)}, f32[64,2944]{1,0:T(8,128)S(1)}, u32[]{:S(2)}, u32[]{:S(2)}) %collective-permute-start.8) | collective-permute-done | bytes 753696 | tf_op jit(solution)/shard_map/ppermute | solution.py:286
  193.9 0.9 pad_maximum_fusion.2
  (45 shorter events, 6.8 us)
Async XLA Ops:
  0.1 1.1 copy-start
  1.2 1.1 copy-start.1
  2.3 0.7 copy-start.3
  4.0 5.5 %collective-permute-start = (f32[512,640]{1,0:T(8,128)S(1)}, f32[512,640]{1,0:T(8,128)S(1)}, u32[]{:S(2)}, u32[]{:S(2)}) collective-permute-start(f32[512,640]{1,0:T(8,128)S(1)} %get-tuple-element.33), channel_id=1, source_target_pairs={{0,1},{1,0},{2,3},{3,2},{4,5},{5,4},{6,7},{7,6},{8,9},{9,8},{10,11... | collective-permute-start | bytes 3932168 | tf_op jit(solution)/shard_map/ppermute | solution.py:286
  4.1 4.7 %copy-start.2 = (bf16[512,640]{1,0:T(8,128)(2,1)S(1)}, bf16[512,640]{1,0:T(8,128)(2,1)}, u32[]{:S(2)}) copy-start(bf16[512,640]{1,0:T(8,128)(2,1)} %q_ref) | copy-start | bytes 1966084
  53.7 58.6 %slice-start = ((s8[6553600]{0:T(1024)(128)(4,1)}), s8[4194304]{0:T(1024)(128)(4,1)S(1)}, s32[]{:S(2)}) async-start(s8[6553600]{0:T(1024)(128)(4,1)} %bitcast.31), calls=%async_computation.2 | async-start | bytes 8388608
  88.4 23.9 %slice-start.1 = ((s8[6553600]{0:T(1024)(128)(4,1)}), s8[2359296]{0:T(1024)(128)(4,1)S(1)}, s32[]{:S(2)}) async-start(s8[6553600]{0:T(1024)(128)(4,1)} %bitcast.31), calls=%async_computation.3 | async-start | bytes 4718592
  88.4 19.5 %collective-permute-start.1 = (f32[256,640]{1,0:T(8,128)S(1)}, f32[256,640]{1,0:T(8,128)S(1)}, u32[]{:S(2)}, u32[]{:S(2)}) collective-permute-start(f32[256,640]{1,0:T(8,128)S(1)} %get-tuple-element.39), channel_id=1, source_target_pairs={{0,1},{1,0},{2,3},{3,2},{4,5},{5,4},{6,7},{7,6},{8,9},{9,8},{10,11... | collective-permute-start | bytes 1966088 | tf_op jit(solution)/shard_map/ppermute | solution.py:286
  109.3 2.3 %collective-permute-start.2 = (f32[256,640]{1,0:T(8,128)S(1)}, f32[256,640]{1,0:T(8,128)S(1)}, u32[]{:S(2)}, u32[]{:S(2)}) collective-permute-start(f32[256,640]{1,0:T(8,128)S(1)} %far_query.1), channel_id=1, source_target_pairs={{0,1},{1,0},{2,3},{3,2},{4,5},{5,4},{6,7},{7,6},{8,9},{9,8},{10,11... | collective-permute-start | bytes 1966088 | tf_op jit(solution)/shard_map/ppermute | solution.py:286
  113.0 15.1 %collective-permute-start.3 = (f32[64,2176]{1,0:T(8,128)S(1)}, f32[64,2176]{1,0:T(8,128)S(1)}, u32[]{:S(2)}, u32[]{:S(2)}) collective-permute-start(f32[64,2176]{1,0:T(8,128)S(1)} %fusion.14), channel_id=1, source_target_pairs={{0,64},{64,0},{1,65},{65,1},{2,66},{66,2},{3,67},{67,3},{4,68},{68... | collective-permute-start | bytes 1671176 | tf_op jit(solution)/shard_map/ppermute | solution.py:286
  114.7 21.6 %collective-permute-start.4 = (f32[64,2944]{1,0:T(8,128)S(1)}, f32[64,2944]{1,0:T(8,128)S(1)}, u32[]{:S(2)}, u32[]{:S(2)}) collective-permute-start(f32[64,2944]{1,0:T(8,128)S(1)} %get-tuple-element.56), channel_id=1, source_target_pairs={{0,16},{16,32},{32,48},{48,0},{1,17},{17,33},{33,49},{49,1},{2,18}... | collective-permute-start | bytes 2261000 | tf_op jit(solution)/shard_map/ppermute | solution.py:290
  116.7 20.0 %collective-permute-start.6 = (f32[64,2944]{1,0:T(8,128)S(1)}, f32[64,2944]{1,0:T(8,128)S(1)}, u32[]{:S(2)}, u32[]{:S(2)}) collective-permute-start(f32[64,2944]{1,0:T(8,128)S(1)} %get-tuple-element.55), channel_id=1, source_target_pairs={{0,48},{16,0},{32,16},{48,32},{1,49},{17,1},{33,17},{49,33},{2,50}... | collective-permute-start | bytes 2261000 | tf_op jit(solution)/shard_map/ppermute | solution.py:290
  129.6 38.2 %collective-permute-start.9 = (f32[192,2176]{1,0:T(8,128)S(1)}, f32[192,2176]{1,0:T(8,128)S(1)}, u32[]{:S(2)}, u32[]{:S(2)}) collective-permute-start(f32[192,2176]{1,0:T(8,128)S(1)} %fusion.12), channel_id=1, source_target_pairs={{0,64},{64,0},{1,65},{65,1},{2,66},{66,2},{3,67},{67,3},{4,68},{68... | collective-permute-start | bytes 5013512 | tf_op jit(solution)/shard_map/ppermute | solution.py:286
  130.5 37.6 %collective-permute-start.12 = (f32[32,2176]{1,0:T(8,128)S(1)}, f32[32,2176]{1,0:T(8,128)S(1)}, u32[]{:S(2)}, u32[]{:S(2)}) collective-permute-start(f32[32,2176]{1,0:T(8,128)S(1)} %get-tuple-element.59), channel_id=1, source_target_pairs={{0,48},{16,0},{32,16},{48,32},{1,49},{17,1},{33,17},{49,33},{2,50}... | collective-permute-start | bytes 835592 | tf_op jit(solution)/shard_map/ppermute | solution.py:290
  134.6 33.5 %collective-permute-start.10 = (f32[32,2176]{1,0:T(8,128)S(1)}, f32[32,2176]{1,0:T(8,128)S(1)}, u32[]{:S(2)}, u32[]{:S(2)}) collective-permute-start(f32[32,2176]{1,0:T(8,128)S(1)} %get-tuple-element.60), channel_id=1, source_target_pairs={{0,16},{16,32},{32,48},{48,0},{1,17},{17,33},{33,49},{49,1},{2,18}... | collective-permute-start | bytes 835592 | tf_op jit(solution)/shard_map/ppermute | solution.py:290
  136.5 41.2 %collective-permute-start.5 = (f32[128,2944]{1,0:T(8,128)S(1)}, f32[128,2944]{1,0:T(8,128)S(1)}, u32[]{:S(2)}, u32[]{:S(2)}) collective-permute-start(f32[128,2944]{1,0:T(8,128)S(1)} %pad_maximum_fusion), channel_id=1, source_target_pairs={{0,16},{16,32},{32,48},{48,0},{1,17},{17,33},{33,49},{49,1},{2,18}... | collective-permute-start | bytes 4521992 | tf_op jit(solution)/shard_map/ppermute | solution.py:290
  136.9 40.8 %collective-permute-start.7 = (f32[128,2944]{1,0:T(8,128)S(1)}, f32[128,2944]{1,0:T(8,128)S(1)}, u32[]{:S(2)}, u32[]{:S(2)}) collective-permute-start(f32[128,2944]{1,0:T(8,128)S(1)} %pad_maximum_fusion.1), channel_id=1, source_target_pairs={{0,48},{16,0},{32,16},{48,32},{1,49},{17,1},{33,17},{49,33},{2,50}... | collective-permute-start | bytes 4521992 | tf_op jit(solution)/shard_map/ppermute | solution.py:290
  168.2 19.6 %collective-permute-start.11 = (f32[64,2176]{1,0:T(8,128)S(1)}, f32[64,2176]{1,0:T(8,128)S(1)}, u32[]{:S(2)}, u32[]{:S(2)}) collective-permute-start(f32[64,2176]{1,0:T(8,128)S(1)} %pad_maximum_fusion.3), channel_id=1, source_target_pairs={{0,16},{16,32},{32,48},{48,0},{1,17},{17,33},{33,49},{49,1},{2,18}... | collective-permute-start | bytes 1671176 | tf_op jit(solution)/shard_map/ppermute | solution.py:290
  170.2 17.5 %collective-permute-start.13 = (f32[64,2176]{1,0:T(8,128)S(1)}, f32[64,2176]{1,0:T(8,128)S(1)}, u32[]{:S(2)}, u32[]{:S(2)}) collective-permute-start(f32[64,2176]{1,0:T(8,128)S(1)} %pad_maximum_fusion.4), channel_id=1, source_target_pairs={{0,48},{16,0},{32,16},{48,32},{1,49},{17,1},{33,17},{49,33},{2,50}... | collective-permute-start | bytes 1671176 | tf_op jit(solution)/shard_map/ppermute | solution.py:290
  178.6 15.2 %collective-permute-start.8 = (f32[64,2944]{1,0:T(8,128)S(1)}, f32[64,2944]{1,0:T(8,128)S(1)}, u32[]{:S(2)}, u32[]{:S(2)}) collective-permute-start(f32[64,2944]{1,0:T(8,128)S(1)} %slice.113), channel_id=1, source_target_pairs={{0,64},{64,0},{1,65},{65,1},{2,66},{66,2},{3,67},{67,3},{4,68},{68... | collective-permute-start | bytes 2261000 | tf_op jit(solution)/shard_map/ppermute | solution.py:286

commit v7 on v6

--- a/solution.py
+++ b/solution.py
@@ -16,7 +16,8 @@
 SHARDS = 8
 TILE = 256
 VMEM_LIMIT = 24 << 20
-CUT = 2944
+CUT = 2304
+MIDDLE = 1408
 Y_ORDER = (2, 0, 1, 3)
 F32 = jnp.float32
 BF16 = jnp.bfloat16
@@ -313,7 +314,7 @@
 
 
 def project_scatter(by_y, by_z, weight):
-    wa, wb = weight[:, :CUT], weight[:, CUT:]
+    wb, wa = weight[:, :CUT], weight[:, CUT:]
     block = by_z.shape[1] // 2
     far_two, by_y, by_z = together(mm(by_y[1, :block], wb), by_y, by_z)
     b_two = swap(far_two, "yl")
@@ -325,16 +326,23 @@
     one, three = mm(by_z[1], wa), mm(by_z[3], wa)
     one = jnp.concatenate([one[:block] + up, one[block:]], axis=0)
     three = jnp.concatenate([three[:block], three[block:] + down], axis=0)
-    a_came = both_ways(one, three)
+    a_came = both_ways(one[:, :MIDDLE], three[:, :MIDDLE])
+    later, b_up, b_down = together((one[:, MIDDLE:], three[:, MIDDLE:]), b_up, b_down)
+    a_more = both_ways(*later)
+    a = mm(by_z[0], wa[:, :MIDDLE]) + sum(a_came)
     b_rest = b_rest + mm(by_y[0, block:], wb)
     half = block // 2
     b_one, b_three = b_rest[block : 2 * block], b_rest[2 * block :]
     b_one = jnp.concatenate([b_one[:half] + b_up, b_one[half:]], axis=0)
     b_three = jnp.concatenate([b_three[:half], b_three[half:] + b_down], axis=0)
-    a = mm(by_z[0], wa) + sum(a_came)
+    a, b_one, b_three, by_z = together(a, b_one, b_three, by_z)
+    a_came = swap(a[block:], "yl")
     b_came = both_ways(b_one, b_three)
-    a_came = swap(a[block:], "yl")
-    return jnp.concatenate([a[:block] + a_came, b_rest[:block] + sum(b_came)], axis=1)
+    more = mm(by_z[0], wa[:, MIDDLE:]) + sum(a_more)
+    more_came = swap(more[block:], "yl")
+    return jnp.concatenate(
+        [b_rest[:block] + sum(b_came), a[:block] + a_came, more[:block] + more_came], axis=1
+    )
 
 
 def body(keys, queries, values, rates, gate, up, down, out_weight):

time: 195 us -> 193 us (0.990)
  waiting for transfers between devices: 55.3 us -> 51.1 us
  starting transfers between devices: 19.5 us -> 21.6 us
    ppermute x6 -> x7, waiting for transfers between devices: 42.3 us -> 22.2 us  [swap(): return lax.ppermute(a, axis, [(0, 1), (1, 0)])]
    ppermute x8 -> x10, waiting for transfers between devices: 12.9 us -> 28.8 us  [ring(): return lax.ppermute(a, 'z', [(i, (i + shift) % 4) for i in range(4)])]
    ppermute x8 -> x10, starting transfers between devices: 15.9 us -> 17 us  [ring(): return lax.ppermute(a, 'z', [(i, (i + shift) % 4) for i in range(4)])]
    ppermute x6 -> x7, starting transfers between devices: 3.61 us -> 4.59 us  [swap(): return lax.ppermute(a, axis, [(0, 1), (1, 0)])]
    dot_general x8 -> x9, matrix products: 6.32 us -> 6.22 us  [mm(): return jnp.dot(a, b, preferred_element_type=F32)]
  transfers between devices with their start and end apart: 14 -> 17, of which waited for: 6 -> 10; matrix products, arithmetic and copies ran while one was open for 4% -> 4% of each run, Pallas kernels for 13% -> 14%
where the time goes in v7:
time: 193 us
  blocking collectives  74.5 us (39%)
  waiting for transfers between devices  51.1 us (26%)
  Pallas kernels  31.7 us (16%)
  starting transfers between devices  21.6 us (11%)
  matrix products  6.22 us (3%)
  local copies, waits for them, and re-layouts  4.19 us (2%)
  other arithmetic  3.36 us (2%)
    all_to_all x1, blocking collectives, plane_scatter(): return jnp.sum(lax.all_to_all(a, PLANE, 0, 0, tiled=True), axis=0)  39.8 us
    all_to_all x1, blocking collectives, plane_gather(): return lax.all_to_all(same, PLANE, 0, 0, tiled=True)  34.7 us
    ppermute x10, waiting for transfers between devices, ring(): return lax.ppermute(a, 'z', [(i, (i + shift) % 4) for i in range(4)])  28.8 us
    ppermute x7, waiting for transfers between devices, swap(): return lax.ppermute(a, axis, [(0, 1), (1, 0)])  22.2 us
    pallas_call x1, Pallas kernels, newton(): pl.pallas_call(newton_kernel, out_shape=out(shape, BF16), in_specs=[pl.Bl...  19.5 us
    ppermute x10, starting transfers between devices, ring(): return lax.ppermute(a, 'z', [(i, (i + shift) % 4) for i in range(4)])  17 us
    pallas_call x6, Pallas kernels, call(): pl.pallas_call(kernel, out_shape=outs, in_specs=specs, out_specs=jax.tree...  7.6 us
    dot_general x9, matrix products, mm(): return jnp.dot(a, b, preferred_element_type=F32)  6.22 us
  transfers between devices with their start and end apart: 17, of which 10 were waited for; matrix products, arithmetic and copies ran while one was open for 4% of the time, Pallas kernels for 14%

profile of v7, /device:TPU:0, one launch (start us, length us, event | category | flops | bytes accessed | tf_op | source)
XLA Modules:
  0.0 192.9 jit_solution(17949527372594575504)
XLA Ops:
  0.1 1.1 copy-done
  1.2 1.1 copy-done.1
  2.9 1.1 sort_tokens.1
  4.1 4.6 %near_grads.1 = (f32[3,320,640]{2,1,0:T(8,128)S(1)}, bf16[3,320,640]{2,1,0:T(8,128)(2,1)S(1)}) custom-call(s32[3]{0:T(128)S(1)} %pad_add_fusion.at_ref, bf16[512,320]{1,0:T(8,128)(2,1)S(1)} %get-tuple-element.35.k_ref, bf16[512,320]{1,0:T(8,128)(2,1)S(1)} %get-tuple-element.36.d_ref, f32[2,320,640]{2,1,0:T(8,128)} %wg_ref.1, f32[2,320,640]{2,1,0:T(8,128)} %wu_ref.1, ...), custom_call_target="tpu_custom_call" | custom-call | tf_op jit(solution)/shard_map/near_grads/pallas_call | solution.py:152
  9.5 2.4 %far_grads.1 = f32[8,3,40,640]{3,2,1,0:T(8,128)S(1)} custom-call(f32[512,640]{1,0:T(8,128)S(1)} %collective-permute-done.came, bf16[3,320,640]{2,1,0:T(8,128)(2,1)S(1)} %get-tuple-element.42.b_ref, f32[3,320,640]{2,1,0:T(8,128)S(1)} %get-tuple-element.43.p_ref), custom_call_target="tpu_custom_call" | custom-call | tf_op jit(solution)/shard_map/far_grads/pallas_call | solution.py:36
  11.9 39.8 %all_to_all.10 = f32[8,3,40,640]{3,2,1,0:T(8,128)S(1)} all-to-all(f32[8,3,40,640]{3,2,1,0:T(8,128)S(1)} %far_grads.1), channel_id=1, replica_groups=mesh['yl'=2,'z'=4,'x'=4,'yh'=2,'core'=2] {'x','yh'}, dimensions={0} | all-to-all | bytes 4915200 | tf_op jit(solution)/shard_map/all_to_all | solution.py:295
  51.7 0.9 reduce_sum.9
  52.6 1.1 broadcast_in_dim.2
  53.7 34.7 %all_to_all.11.g_ref = f32[8,3,40,640]{3,2,1,0:T(8,128)S(1)} all-to-all(f32[8,3,40,640]{3,2,1,0:T(8,128)S(1)} %broadcast_in_dim.2), channel_id=1, replica_groups=mesh['yl'=2,'z'=4,'x'=4,'yh'=2,'core'=2] {'x','yh'}, dimensions={0} | all-to-all | bytes 4915200 | tf_op jit(solution)/shard_map/all_to_all | solution.py:300
  88.4 19.5 %newton.1.v_ref = bf16[3,320,640]{2,1,0:T(8,128)(2,1)S(1)} custom-call(s32[3]{0:T(128)S(1)} %pad_add_fusion.at_ref, f32[8,3,40,640]{3,2,1,0:T(8,128)S(1)} %all_to_all.11.g_ref, f32[2,320,640]{2,1,0:T(8,128)} %wg_ref.1, f32[2,320,640]{2,1,0:T(8,128)} %wu_ref.1, f32[2,320,640]{2,1,0:T(8,128)} %wd_ref.1), custom_call_target="tpu_custom_call" | custom-call | tf_op jit(solution)/shard_map/newton/pallas_call | solution.py:230
  107.9 1.4 far_query.1
  109.9 1.3 near_query.1.o_ref
  114.5 2.0 %collective-permute-start.5 = (f32[64,2816]{1,0:T(8,128)S(1)}, f32[64,2816]{1,0:T(8,128)S(1)}, u32[]{:S(2)}, u32[]{:S(2)}) collective-permute-start(f32[64,2816]{1,0:T(8,128)S(1)} %get-tuple-element.76), channel_id=1, source_target_pairs={{0,16},{16,32},{32,48},{48,0},{1,17},{17,33},{33,49},{49,1},{2,18}... | collective-permute-start | bytes 2162696 | tf_op jit(solution)/shard_map/ppermute | solution.py:291
  116.6 2.2 %collective-permute-start.7 = (f32[64,2816]{1,0:T(8,128)S(1)}, f32[64,2816]{1,0:T(8,128)S(1)}, u32[]{:S(2)}, u32[]{:S(2)}) collective-permute-start(f32[64,2816]{1,0:T(8,128)S(1)} %get-tuple-element.75), channel_id=1, source_target_pairs={{0,48},{16,0},{32,16},{48,32},{1,49},{17,1},{33,17},{49,33},{2,50}... | collective-permute-start | bytes 2162696 | tf_op jit(solution)/shard_map/ppermute | solution.py:291
  118.8 0.9 fusion.10
  119.7 9.0 %collective-permute-done.3 = f32[64,2304]{1,0:T(8,128)S(1)} collective-permute-done((f32[64,2304]{1,0:T(8,128)S(1)}, f32[64,2304]{1,0:T(8,128)S(1)}, u32[]{:S(2)}, u32[]{:S(2)}) %collective-permute-start.3) | collective-permute-done | bytes 589856 | tf_op jit(solution)/shard_map/ppermute | solution.py:287
  129.3 1.0 collective-permute-start.4
  131.9 3.3 %collective-permute-done.5 = f32[64,2816]{1,0:T(8,128)S(1)} collective-permute-done((f32[64,2816]{1,0:T(8,128)S(1)}, f32[64,2816]{1,0:T(8,128)S(1)}, u32[]{:S(2)}, u32[]{:S(2)}) %collective-permute-start.5) | collective-permute-done | bytes 720928 | tf_op jit(solution)/shard_map/ppermute | solution.py:291
  135.9 1.1 collective-permute-start.6
  137.0 2.2 %collective-permute-start.8 = (f32[128,1408]{1,0:T(8,128)S(1)}, f32[128,1408]{1,0:T(8,128)S(1)}, u32[]{:S(2)}, u32[]{:S(2)}) collective-permute-start(f32[128,1408]{1,0:T(8,128)S(1)} %get-tuple-element.70), channel_id=1, source_target_pairs={{0,48},{16,0},{32,16},{48,32},{1,49},{17,1},{33,17},{49,33},{2,50}... | collective-permute-start | bytes 2162696 | tf_op jit(solution)/shard_map/ppermute | solution.py:291
  139.2 1.7 collective-permute-start.10
  141.3 0.9 fusion.8
  142.2 18.3 %collective-permute-done.10 = f32[32,2304]{1,0:T(8,128)S(1)} collective-permute-done((f32[32,2304]{1,0:T(8,128)S(1)}, f32[32,2304]{1,0:T(8,128)S(1)}, u32[]{:S(2)}, u32[]{:S(2)}) %collective-permute-start.10) | collective-permute-done | bytes 294944 | tf_op jit(solution)/shard_map/ppermute | solution.py:291
  162.0 2.5 %collective-permute-start.15 = (f32[128,1408]{1,0:T(8,128)S(1)}, f32[128,1408]{1,0:T(8,128)S(1)}, u32[]{:S(2)}, u32[]{:S(2)}) collective-permute-start(f32[128,1408]{1,0:T(8,128)S(1)} %get-tuple-element.64), channel_id=1, source_target_pairs={{0,48},{16,0},{32,16},{48,32},{1,49},{17,1},{33,17},{49,33},{2,50}... | collective-permute-start | bytes 2162696 | tf_op jit(solution)/shard_map/ppermute | solution.py:291
  165.0 4.8 %collective-permute-done.4 = f32[192,2304]{1,0:T(8,128)S(1)} collective-permute-done((f32[192,2304]{1,0:T(8,128)S(1)}, f32[192,2304]{1,0:T(8,128)S(1)}, u32[]{:S(2)}, u32[]{:S(2)}) %collective-permute-start.4) | collective-permute-done | bytes 1769504 | tf_op jit(solution)/shard_map/ppermute | solution.py:287
  170.2 2.0 %collective-permute-start.11 = (f32[64,2304]{1,0:T(8,128)S(1)}, f32[64,2304]{1,0:T(8,128)S(1)}, u32[]{:S(2)}, u32[]{:S(2)}) collective-permute-start(f32[64,2304]{1,0:T(8,128)S(1)} %pad_maximum_fusion.3), channel_id=1, source_target_pairs={{0,16},{16,32},{32,48},{48,0},{1,17},{17,33},{33,49},{49,1},{2,18}... | collective-permute-start | bytes 1769480 | tf_op jit(solution)/shard_map/ppermute | solution.py:291
  172.2 2.2 %collective-permute-start.12 = (f32[64,2304]{1,0:T(8,128)S(1)}, f32[64,2304]{1,0:T(8,128)S(1)}, u32[]{:S(2)}, u32[]{:S(2)}) collective-permute-start(f32[64,2304]{1,0:T(8,128)S(1)} %pad_maximum_fusion.4), channel_id=1, source_target_pairs={{0,48},{16,0},{32,16},{48,32},{1,49},{17,1},{33,17},{49,33},{2,50}... | collective-permute-start | bytes 1769480 | tf_op jit(solution)/shard_map/ppermute | solution.py:291
  175.7 5.8 %collective-permute-done.14 = f32[128,1408]{1,0:T(8,128)S(1)} collective-permute-done((f32[128,1408]{1,0:T(8,128)S(1)}, f32[128,1408]{1,0:T(8,128)S(1)}, u32[]{:S(2)}, u32[]{:S(2)}) %collective-permute-start.14) | collective-permute-done | bytes 720928 | tf_op jit(solution)/shard_map/ppermute | solution.py:291
  181.7 1.4 collective-permute-start.16
  183.1 2.8 %collective-permute-done.13 = f32[64,1408]{1,0:T(8,128)S(1)} collective-permute-done((f32[64,1408]{1,0:T(8,128)S(1)}, f32[64,1408]{1,0:T(8,128)S(1)}, u32[]{:S(2)}, u32[]{:S(2)}) %collective-permute-start.13) | collective-permute-done | bytes 360480 | tf_op jit(solution)/shard_map/ppermute | solution.py:287
  185.9 5.2 %collective-permute-done.16 = f32[64,1408]{1,0:T(8,128)S(1)} collective-permute-done((f32[64,1408]{1,0:T(8,128)S(1)}, f32[64,1408]{1,0:T(8,128)S(1)}, u32[]{:S(2)}, u32[]{:S(2)}) %collective-permute-start.16) | collective-permute-done | bytes 360480 | tf_op jit(solution)/shard_map/ppermute | solution.py:287
  192.1 0.9 pad_maximum_fusion.2
  (54 shorter events, 13.6 us)
Async XLA Ops:
  0.1 1.1 copy-start
  1.2 1.1 copy-start.1
  2.3 0.7 copy-start.3
  4.0 5.5 %collective-permute-start = (f32[512,640]{1,0:T(8,128)S(1)}, f32[512,640]{1,0:T(8,128)S(1)}, u32[]{:S(2)}, u32[]{:S(2)}) collective-permute-start(f32[512,640]{1,0:T(8,128)S(1)} %get-tuple-element.41), channel_id=1, source_target_pairs={{0,1},{1,0},{2,3},{3,2},{4,5},{5,4},{6,7},{7,6},{8,9},{9,8},{10,11... | collective-permute-start | bytes 3932168 | tf_op jit(solution)/shard_map/ppermute | solution.py:287
  4.1 4.7 %copy-start.2 = (bf16[512,640]{1,0:T(8,128)(2,1)S(1)}, bf16[512,640]{1,0:T(8,128)(2,1)}, u32[]{:S(2)}) copy-start(bf16[512,640]{1,0:T(8,128)(2,1)} %q_ref) | copy-start | bytes 1966084
  53.7 58.6 %slice-start = ((s8[6553600]{0:T(1024)(128)(4,1)}), s8[4194304]{0:T(1024)(128)(4,1)S(1)}, s32[]{:S(2)}) async-start(s8[6553600]{0:T(1024)(128)(4,1)} %bitcast.34), calls=%async_computation.2 | async-start | bytes 8388608
  88.4 23.9 %slice-start.1 = ((s8[6553600]{0:T(1024)(128)(4,1)}), s8[2359296]{0:T(1024)(128)(4,1)S(1)}, s32[]{:S(2)}) async-start(s8[6553600]{0:T(1024)(128)(4,1)} %bitcast.34), calls=%async_computation.3 | async-start | bytes 4718592
  88.4 19.5 %collective-permute-start.1 = (f32[256,640]{1,0:T(8,128)S(1)}, f32[256,640]{1,0:T(8,128)S(1)}, u32[]{:S(2)}, u32[]{:S(2)}) collective-permute-start(f32[256,640]{1,0:T(8,128)S(1)} %get-tuple-element.47), channel_id=1, source_target_pairs={{0,1},{1,0},{2,3},{3,2},{4,5},{5,4},{6,7},{7,6},{8,9},{9,8},{10,11... | collective-permute-start | bytes 1966088 | tf_op jit(solution)/shard_map/ppermute | solution.py:287
  109.3 2.3 %collective-permute-start.2 = (f32[256,640]{1,0:T(8,128)S(1)}, f32[256,640]{1,0:T(8,128)S(1)}, u32[]{:S(2)}, u32[]{:S(2)}) collective-permute-start(f32[256,640]{1,0:T(8,128)S(1)} %far_query.1), channel_id=1, source_target_pairs={{0,1},{1,0},{2,3},{3,2},{4,5},{5,4},{6,7},{7,6},{8,9},{9,8},{10,11... | collective-permute-start | bytes 1966088 | tf_op jit(solution)/shard_map/ppermute | solution.py:287
  112.9 15.8 %collective-permute-start.3 = (f32[64,2304]{1,0:T(8,128)S(1)}, f32[64,2304]{1,0:T(8,128)S(1)}, u32[]{:S(2)}, u32[]{:S(2)}) collective-permute-start(f32[64,2304]{1,0:T(8,128)S(1)} %fusion.12), channel_id=1, source_target_pairs={{0,64},{64,0},{1,65},{65,1},{2,66},{66,2},{3,67},{67,3},{4,68},{68... | collective-permute-start | bytes 1769480 | tf_op jit(solution)/shard_map/ppermute | solution.py:287
  114.5 20.6 %collective-permute-start.5 = (f32[64,2816]{1,0:T(8,128)S(1)}, f32[64,2816]{1,0:T(8,128)S(1)}, u32[]{:S(2)}, u32[]{:S(2)}) collective-permute-start(f32[64,2816]{1,0:T(8,128)S(1)} %get-tuple-element.76), channel_id=1, source_target_pairs={{0,16},{16,32},{32,48},{48,0},{1,17},{17,33},{33,49},{49,1},{2,18}... | collective-permute-start | bytes 2162696 | tf_op jit(solution)/shard_map/ppermute | solution.py:291
  116.6 18.8 %collective-permute-start.7 = (f32[64,2816]{1,0:T(8,128)S(1)}, f32[64,2816]{1,0:T(8,128)S(1)}, u32[]{:S(2)}, u32[]{:S(2)}) collective-permute-start(f32[64,2816]{1,0:T(8,128)S(1)} %get-tuple-element.75), channel_id=1, source_target_pairs={{0,48},{16,0},{32,16},{48,32},{1,49},{17,1},{33,17},{49,33},{2,50}... | collective-permute-start | bytes 2162696 | tf_op jit(solution)/shard_map/ppermute | solution.py:291
  129.3 40.5 %collective-permute-start.4 = (f32[192,2304]{1,0:T(8,128)S(1)}, f32[192,2304]{1,0:T(8,128)S(1)}, u32[]{:S(2)}, u32[]{:S(2)}) collective-permute-start(f32[192,2304]{1,0:T(8,128)S(1)} %fusion.10), channel_id=1, source_target_pairs={{0,64},{64,0},{1,65},{65,1},{2,66},{66,2},{3,67},{67,3},{4,68},{68... | collective-permute-start | bytes 5308424 | tf_op jit(solution)/shard_map/ppermute | solution.py:287
  135.9 28.6 %collective-permute-start.6 = (f32[128,1408]{1,0:T(8,128)S(1)}, f32[128,1408]{1,0:T(8,128)S(1)}, u32[]{:S(2)}, u32[]{:S(2)}) collective-permute-start(f32[128,1408]{1,0:T(8,128)S(1)} %get-tuple-element.81), channel_id=1, source_target_pairs={{0,16},{16,32},{32,48},{48,0},{1,17},{17,33},{33,49},{49,1},{2,18}... | collective-permute-start | bytes 2162696 | tf_op jit(solution)/shard_map/ppermute | solution.py:291
  137.0 27.4 %collective-permute-start.8 = (f32[128,1408]{1,0:T(8,128)S(1)}, f32[128,1408]{1,0:T(8,128)S(1)}, u32[]{:S(2)}, u32[]{:S(2)}) collective-permute-start(f32[128,1408]{1,0:T(8,128)S(1)} %get-tuple-element.70), channel_id=1, source_target_pairs={{0,48},{16,0},{32,16},{48,32},{1,49},{17,1},{33,17},{49,33},{2,50}... | collective-permute-start | bytes 2162696 | tf_op jit(solution)/shard_map/ppermute | solution.py:291
  139.2 21.3 %collective-permute-start.10 = (f32[32,2304]{1,0:T(8,128)S(1)}, f32[32,2304]{1,0:T(8,128)S(1)}, u32[]{:S(2)}, u32[]{:S(2)}) collective-permute-start(f32[32,2304]{1,0:T(8,128)S(1)} %get-tuple-element.79), channel_id=1, source_target_pairs={{0,48},{16,0},{32,16},{48,32},{1,49},{17,1},{33,17},{49,33},{2,50}... | collective-permute-start | bytes 884744 | tf_op jit(solution)/shard_map/ppermute | solution.py:291
  141.0 20.3 %collective-permute-start.9 = (f32[32,2304]{1,0:T(8,128)S(1)}, f32[32,2304]{1,0:T(8,128)S(1)}, u32[]{:S(2)}, u32[]{:S(2)}) collective-permute-start(f32[32,2304]{1,0:T(8,128)S(1)} %get-tuple-element.80), channel_id=1, source_target_pairs={{0,16},{16,32},{32,48},{48,0},{1,17},{17,33},{33,49},{49,1},{2,18}... | collective-permute-start | bytes 884744 | tf_op jit(solution)/shard_map/ppermute | solution.py:291
  161.2 20.3 %collective-permute-start.14 = (f32[128,1408]{1,0:T(8,128)S(1)}, f32[128,1408]{1,0:T(8,128)S(1)}, u32[]{:S(2)}, u32[]{:S(2)}) collective-permute-start(f32[128,1408]{1,0:T(8,128)S(1)} %get-tuple-element.63), channel_id=1, source_target_pairs={{0,16},{16,32},{32,48},{48,0},{1,17},{17,33},{33,49},{49,1},{2,18}... | collective-permute-start | bytes 2162696 | tf_op jit(solution)/shard_map/ppermute | solution.py:291
  162.0 19.5 %collective-permute-start.15 = (f32[128,1408]{1,0:T(8,128)S(1)}, f32[128,1408]{1,0:T(8,128)S(1)}, u32[]{:S(2)}, u32[]{:S(2)}) collective-permute-start(f32[128,1408]{1,0:T(8,128)S(1)} %get-tuple-element.64), channel_id=1, source_target_pairs={{0,48},{16,0},{32,16},{48,32},{1,49},{17,1},{33,17},{49,33},{2,50}... | collective-permute-start | bytes 2162696 | tf_op jit(solution)/shard_map/ppermute | solution.py:291
  170.2 21.7 %collective-permute-start.11 = (f32[64,2304]{1,0:T(8,128)S(1)}, f32[64,2304]{1,0:T(8,128)S(1)}, u32[]{:S(2)}, u32[]{:S(2)}) collective-permute-start(f32[64,2304]{1,0:T(8,128)S(1)} %pad_maximum_fusion.3), channel_id=1, source_target_pairs={{0,16},{16,32},{32,48},{48,0},{1,17},{17,33},{33,49},{49,1},{2,18}... | collective-permute-start | bytes 1769480 | tf_op jit(solution)/shard_map/ppermute | solution.py:291
  172.2 19.7 %collective-permute-start.12 = (f32[64,2304]{1,0:T(8,128)S(1)}, f32[64,2304]{1,0:T(8,128)S(1)}, u32[]{:S(2)}, u32[]{:S(2)}) collective-permute-start(f32[64,2304]{1,0:T(8,128)S(1)} %pad_maximum_fusion.4), channel_id=1, source_target_pairs={{0,48},{16,0},{32,16},{48,32},{1,49},{17,1},{33,17},{49,33},{2,50}... | collective-permute-start | bytes 1769480 | tf_op jit(solution)/shard_map/ppermute | solution.py:291
  174.5 11.4 %collective-permute-start.13 = (f32[64,1408]{1,0:T(8,128)S(1)}, f32[64,1408]{1,0:T(8,128)S(1)}, u32[]{:S(2)}, u32[]{:S(2)}) collective-permute-start(f32[64,1408]{1,0:T(8,128)S(1)} %slice.139), channel_id=1, source_target_pairs={{0,64},{64,0},{1,65},{65,1},{2,66},{66,2},{3,67},{67,3},{4,68},{68... | collective-permute-start | bytes 1081352 | tf_op jit(solution)/shard_map/ppermute | solution.py:287
  181.7 9.5 %collective-permute-start.16 = (f32[64,1408]{1,0:T(8,128)S(1)}, f32[64,1408]{1,0:T(8,128)S(1)}, u32[]{:S(2)}, u32[]{:S(2)}) collective-permute-start(f32[64,1408]{1,0:T(8,128)S(1)} %slice.162), channel_id=1, source_target_pairs={{0,64},{64,0},{1,65},{65,1},{2,66},{66,2},{3,67},{67,3},{4,68},{68... | collective-permute-start | bytes 1081352 | tf_op jit(solution)/shard_map/ppermute | solution.py:287

commit v8 on v7

--- a/solution.py
+++ b/solution.py
@@ -17,7 +17,7 @@
 TILE = 256
 VMEM_LIMIT = 24 << 20
 CUT = 2304
-MIDDLE = 1408
+MIDDLE = 1920
 Y_ORDER = (2, 0, 1, 3)
 F32 = jnp.float32
 BF16 = jnp.bfloat16
@@ -44,22 +44,36 @@
     )(*operands)
 
 
+def in_hbm(a):
+    return pltpu.with_memory_space_constraint(a, pltpu.HBM)
+
+
 def out(shape, dtype):
     return jax.ShapeDtypeStruct(shape, dtype)
 
 
-def sort_tokens_kernel(at_ref, k_ref, v_ref, r_ref, k_o, d_o, sent):
-    width = k_o.shape[1]
+def sort_tokens_kernel(at_ref, r_ref, k_ref, v_ref, k_o, d_o, sent, k_s, v_s, sems):
+    rows, width = k_o.shape
+    half = rows // 2
+    copies = [
+        pltpu.make_async_copy(ref.at[pl.ds(i * half, half)], to.at[pl.ds(i * half, half)], sems.at[2 * n + i])
+        for n, (ref, to) in enumerate(((k_ref, k_s), (v_ref, v_s)))
+        for i in range(2)
+    ]
+    for copy in copies:
+        copy.start()
+    for copy in copies:
+        copy.wait()
     for h in range(2):
 
         @pl.when(at_ref[0] == h)
         def _():
             near, far = slice(h * width, (h + 1) * width), slice((1 - h) * width, (2 - h) * width)
-            k_o[...] = k_ref[:, near]
-            sent[:, :width] = k_ref[:, far].astype(F32)
+            k_o[...] = k_s[:, near]
+            sent[:, :width] = k_s[:, far].astype(F32)
             for head, columns in ((h, near), (1 - h, far)):
                 rate = r_ref[head : head + 1, :].T
-                d = (-rate * v_ref[:, columns].astype(F32)).astype(BF16)
+                d = (-rate * v_s[:, columns].astype(F32)).astype(BF16)
                 if head == h:
                     d_o[...] = d
                 else:
@@ -68,8 +82,16 @@
 
 def sort_tokens(at, keys, values, rates):
     shape = (keys.shape[0], keys.shape[1] // 2)
-    shapes = [out(shape, BF16), out(shape, BF16), out(keys.shape, F32)]
-    return call(sort_tokens_kernel, "sort_tokens", shapes, [], at, keys, values, rates)
+    vmem, hbm = pl.BlockSpec(memory_space=pltpu.VMEM), pl.BlockSpec(memory_space=pltpu.HBM)
+    return pl.pallas_call(
+        sort_tokens_kernel,
+        out_shape=[out(shape, BF16), out(shape, BF16), out(keys.shape, F32)],
+        in_specs=[pl.BlockSpec(memory_space=pltpu.SMEM), vmem, hbm, hbm],
+        out_specs=[vmem] * 3,
+        scratch_shapes=[pltpu.VMEM(keys.shape, BF16)] * 2 + [pltpu.SemaphoreType.DMA((4,))],
+        compiler_params=pltpu.CompilerParams(vmem_limit_bytes=VMEM_LIMIT),
+        name="sort_tokens",
+    )(at, rates, in_hbm(keys), in_hbm(values))
 
 
 def side_by_side(rows, r, block, width):
@@ -347,7 +369,7 @@
 
 def body(keys, queries, values, rates, gate, up, down, out_weight):
     at = jnp.stack([lax.axis_index(name).astype(jnp.int32) for name in ("core", "yl", "z")])
-    weights = tuple(pltpu.with_memory_space_constraint(w, pltpu.HBM) for w in (gate, up, down))
+    weights = tuple(in_hbm(w) for w in (gate, up, down))
     k, d, sent = sort_tokens(at, keys, values, rates.T)
     came = swap(sent, "core")
     partial, rounded = near_grads(at, k, d, *weights)

time: 193 us -> 196 us (1.016)
  waiting for transfers between devices: 51.1 us -> 53.7 us
  local copies, waits for them, and re-layouts: 4.19 us -> 2.02 us
    ppermute x10, waiting for transfers between devices: 28.8 us -> 40.7 us  [ring(): return lax.ppermute(a, 'z', [(i, (i + shift) % 4) for i in range(4)])]
    ppermute x7, waiting for transfers between devices: 22.2 us -> 13.1 us  [swap(): return lax.ppermute(a, axis, [(0, 1), (1, 0)])]
    pallas_call x0 -> x1, Pallas kernels: none -> 2.37 us  [sort_tokens(): pl.pallas_call(sort_tokens_kernel, out_shape=[out(shape, BF16), out(shape...]
    unnamed x12 -> x8, local copies, waits for them, and re-layouts: 2.88 us -> 0.71 us
    pallas_call x6 -> x5, Pallas kernels: 7.6 us -> 6.52 us  [call(): pl.pallas_call(kernel, out_shape=outs, in_specs=specs, out_specs=jax.tree...]
  transfers between devices with their start and end apart: 17 -> 17, of which waited for: 10 -> 8; matrix products, arithmetic and copies ran while one was open for 4% -> 4% of each run, Pallas kernels for 14% -> 13%
where the time goes in v8:
time: 196 us
  blocking collectives  74.5 us (38%)
  waiting for transfers between devices  53.7 us (27%)
  Pallas kernels  33 us (17%)
  starting transfers between devices  23 us (12%)
  matrix products  6.23 us (3%)
  other arithmetic  3.1 us (2%)
  local copies, waits for them, and re-layouts  2.02 us (1%)
    ppermute x10, waiting for transfers between devices, ring(): return lax.ppermute(a, 'z', [(i, (i + shift) % 4) for i in range(4)])  40.7 us
    all_to_all x1, blocking collectives, plane_scatter(): return jnp.sum(lax.all_to_all(a, PLANE, 0, 0, tiled=True), axis=0)  39.8 us
    all_to_all x1, blocking collectives, plane_gather(): return lax.all_to_all(same, PLANE, 0, 0, tiled=True)  34.7 us
    pallas_call x1, Pallas kernels, newton(): pl.pallas_call(newton_kernel, out_shape=out(shape, BF16), in_specs=[pl.Bl...  19.5 us
    ppermute x10, starting transfers between devices, ring(): return lax.ppermute(a, 'z', [(i, (i + shift) % 4) for i in range(4)])  17.7 us
    ppermute x7, waiting for transfers between devices, swap(): return lax.ppermute(a, axis, [(0, 1), (1, 0)])  13.1 us
    pallas_call x5, Pallas kernels, call(): pl.pallas_call(kernel, out_shape=outs, in_specs=specs, out_specs=jax.tree...  6.52 us
    dot_general x9, matrix products, mm(): return jnp.dot(a, b, preferred_element_type=F32)  6.23 us
  transfers between devices with their start and end apart: 17, of which 8 were waited for; matrix products, arithmetic and copies ran while one was open for 4% of the time, Pallas kernels for 13%

profile of v8, /device:TPU:0, one launch (start us, length us, event | category | flops | bytes accessed | tf_op | source)
XLA Modules:
  0.0 195.9 jit_solution(13141717512304280211)
XLA Ops:
  0.8 2.4 %sort_tokens.1 = (bf16[512,320]{1,0:T(8,128)(2,1)S(1)}, bf16[512,320]{1,0:T(8,128)(2,1)S(1)}, f32[512,640]{1,0:T(8,128)S(1)}) custom-call(s32[3]{0:T(128)S(1)} %pad_add_fusion.at_ref, f32[2,512]{1,0:T(2,128)S(1)} %bitcast.33, bf16[512,640]{1,0:T(8,128)(2,1)} %k_ref.1, bf16[512,640]{1,0:T(8,128)(2,1)} %v_ref.1), custom_call_target="tpu_custom_call" | custom-call | tf_op jit(solution)/shard_map/sort_tokens/pallas_call | solution.py:86
  3.3 4.6 %near_grads.1 = (f32[3,320,640]{2,1,0:T(8,128)S(1)}, bf16[3,320,640]{2,1,0:T(8,128)(2,1)S(1)}) custom-call(s32[3]{0:T(128)S(1)} %pad_add_fusion.at_ref, bf16[512,320]{1,0:T(8,128)(2,1)S(1)} %get-tuple-element.35.k_ref, bf16[512,320]{1,0:T(8,128)(2,1)S(1)} %get-tuple-element.36.d_ref, f32[2,320,640]{2,1,0:T(8,128)} %wg_ref.1, f32[2,320,640]{2,1,0:T(8,128)} %wu_ref.1, ...), custom_call_target="tpu_custom_call" | custom-call | tf_op jit(solution)/shard_map/near_grads/pallas_call | solution.py:174
  8.6 2.4 %far_grads.1 = f32[8,3,40,640]{3,2,1,0:T(8,128)S(1)} custom-call(f32[512,640]{1,0:T(8,128)S(1)} %collective-permute-done.came, bf16[3,320,640]{2,1,0:T(8,128)(2,1)S(1)} %get-tuple-element.42.b_ref, f32[3,320,640]{2,1,0:T(8,128)S(1)} %get-tuple-element.43.p_ref), custom_call_target="tpu_custom_call" | custom-call | tf_op jit(solution)/shard_map/far_grads/pallas_call | solution.py:36
  11.0 39.8 %all_to_all.10 = f32[8,3,40,640]{3,2,1,0:T(8,128)S(1)} all-to-all(f32[8,3,40,640]{3,2,1,0:T(8,128)S(1)} %far_grads.1), channel_id=1, replica_groups=mesh['yl'=2,'z'=4,'x'=4,'yh'=2,'core'=2] {'x','yh'}, dimensions={0} | all-to-all | bytes 4915200 | tf_op jit(solution)/shard_map/all_to_all | solution.py:317
  50.8 0.9 reduce_sum.9
  51.7 1.1 broadcast_in_dim.2
  52.8 34.7 %all_to_all.11.g_ref = f32[8,3,40,640]{3,2,1,0:T(8,128)S(1)} all-to-all(f32[8,3,40,640]{3,2,1,0:T(8,128)S(1)} %broadcast_in_dim.2), channel_id=1, replica_groups=mesh['yl'=2,'z'=4,'x'=4,'yh'=2,'core'=2] {'x','yh'}, dimensions={0} | all-to-all | bytes 4915200 | tf_op jit(solution)/shard_map/all_to_all | solution.py:322
  87.5 19.5 %newton.1.v_ref = bf16[3,320,640]{2,1,0:T(8,128)(2,1)S(1)} custom-call(s32[3]{0:T(128)S(1)} %pad_add_fusion.at_ref, f32[8,3,40,640]{3,2,1,0:T(8,128)S(1)} %all_to_all.11.g_ref, f32[2,320,640]{2,1,0:T(8,128)} %wg_ref.1, f32[2,320,640]{2,1,0:T(8,128)} %wu_ref.1, f32[2,320,640]{2,1,0:T(8,128)} %wd_ref.1), custom_call_target="tpu_custom_call" | custom-call | tf_op jit(solution)/shard_map/newton/pallas_call | solution.py:252
  107.0 1.4 far_query.1
  109.0 1.3 near_query.1.o_ref
  112.0 0.8 collective-permute-start.3
  112.8 0.8 fusion.2
  113.7 4.1 %collective-permute-start.7 = (f32[64,2816]{1,0:T(8,128)S(1)}, f32[64,2816]{1,0:T(8,128)S(1)}, u32[]{:S(2)}, u32[]{:S(2)}) collective-permute-start(f32[64,2816]{1,0:T(8,128)S(1)} %get-tuple-element.71), channel_id=1, source_target_pairs={{0,48},{16,0},{32,16},{48,32},{1,49},{17,1},{33,17},{49,33},{2,50}... | collective-permute-start | bytes 2162696 | tf_op jit(solution)/shard_map/ppermute | solution.py:313
  117.8 0.9 fusion.12
  118.7 9.1 %collective-permute-done.3 = f32[64,2304]{1,0:T(8,128)S(1)} collective-permute-done((f32[64,2304]{1,0:T(8,128)S(1)}, f32[64,2304]{1,0:T(8,128)S(1)}, u32[]{:S(2)}, u32[]{:S(2)}) %collective-permute-start.3) | collective-permute-done | bytes 589856 | tf_op jit(solution)/shard_map/ppermute | solution.py:309
  128.4 1.0 collective-permute-start.4
  129.5 0.8 fusion
  130.2 0.8 fusion.4
  131.0 2.5 %collective-permute-done.7 = f32[64,2816]{1,0:T(8,128)S(1)} collective-permute-done((f32[64,2816]{1,0:T(8,128)S(1)}, f32[64,2816]{1,0:T(8,128)S(1)}, u32[]{:S(2)}, u32[]{:S(2)}) %collective-permute-start.7) | collective-permute-done | bytes 720928 | tf_op jit(solution)/shard_map/ppermute | solution.py:313
  133.7 3.8 %collective-permute-start.8 = (f32[128,1920]{1,0:T(8,128)S(1)}, f32[128,1920]{1,0:T(8,128)S(1)}, u32[]{:S(2)}, u32[]{:S(2)}) collective-permute-start(f32[128,1920]{1,0:T(8,128)S(1)} %fusion.18), channel_id=1, source_target_pairs={{0,48},{16,0},{32,16},{48,32},{1,49},{17,1},{33,17},{49,33},{2,50}... | collective-permute-start | bytes 2949128 | tf_op jit(solution)/shard_map/ppermute | solution.py:313
  137.8 3.3 %collective-permute-start.10 = (f32[32,2304]{1,0:T(8,128)S(1)}, f32[32,2304]{1,0:T(8,128)S(1)}, u32[]{:S(2)}, u32[]{:S(2)}) collective-permute-start(f32[32,2304]{1,0:T(8,128)S(1)} %get-tuple-element.75), channel_id=1, source_target_pairs={{0,48},{16,0},{32,16},{48,32},{1,49},{17,1},{33,17},{49,33},{2,50}... | collective-permute-start | bytes 884744 | tf_op jit(solution)/shard_map/ppermute | solution.py:313
  141.1 0.9 fusion.10
  142.1 22.3 %collective-permute-done.10 = f32[32,2304]{1,0:T(8,128)S(1)} collective-permute-done((f32[32,2304]{1,0:T(8,128)S(1)}, f32[32,2304]{1,0:T(8,128)S(1)}, u32[]{:S(2)}, u32[]{:S(2)}) %collective-permute-start.10) | collective-permute-done | bytes 294944 | tf_op jit(solution)/shard_map/ppermute | solution.py:313
  164.4 3.7 %collective-permute-done.9 = f32[32,2304]{1,0:T(8,128)S(1)} collective-permute-done((f32[32,2304]{1,0:T(8,128)S(1)}, f32[32,2304]{1,0:T(8,128)S(1)}, u32[]{:S(2)}, u32[]{:S(2)}) %collective-permute-start.9) | collective-permute-done | bytes 294944 | tf_op jit(solution)/shard_map/ppermute | solution.py:313
  168.1 3.2 %collective-permute-start.15 = (f32[128,896]{1,0:T(8,128)S(1)}, f32[128,896]{1,0:T(8,128)S(1)}, u32[]{:S(2)}, u32[]{:S(2)}) collective-permute-start(f32[128,896]{1,0:T(8,128)S(1)} %pad_maximum_fusion.3), channel_id=1, source_target_pairs={{0,48},{16,0},{32,16},{48,32},{1,49},{17,1},{33,17},{49,33},{2,50}... | collective-permute-start | bytes 1376264 | tf_op jit(solution)/shard_map/ppermute | solution.py:313
  172.5 1.4 collective-permute-start.13
  174.3 5.6 %collective-permute-done.14 = f32[128,896]{1,0:T(8,128)S(1)} collective-permute-done((f32[128,896]{1,0:T(8,128)S(1)}, f32[128,896]{1,0:T(8,128)S(1)}, u32[]{:S(2)}, u32[]{:S(2)}) %collective-permute-start.14) | collective-permute-done | bytes 458784 | tf_op jit(solution)/shard_map/ppermute | solution.py:313
  180.0 1.4 collective-permute-start.16
  181.4 3.2 %collective-permute-start.12 = (f32[64,2304]{1,0:T(8,128)S(1)}, f32[64,2304]{1,0:T(8,128)S(1)}, u32[]{:S(2)}, u32[]{:S(2)}) collective-permute-start(f32[64,2304]{1,0:T(8,128)S(1)} %get-tuple-element.60), channel_id=1, source_target_pairs={{0,48},{16,0},{32,16},{48,32},{1,49},{17,1},{33,17},{49,33},{2,50}... | collective-permute-start | bytes 1769480 | tf_op jit(solution)/shard_map/ppermute | solution.py:313
  184.7 3.5 %collective-permute-done.16 = f32[64,896]{1,0:T(8,128)S(1)} collective-permute-done((f32[64,896]{1,0:T(8,128)S(1)}, f32[64,896]{1,0:T(8,128)S(1)}, u32[]{:S(2)}, u32[]{:S(2)}) %collective-permute-start.16) | collective-permute-done | bytes 229408 | tf_op jit(solution)/shard_map/ppermute | solution.py:309
  188.3 6.6 %collective-permute-done.11 = f32[64,2304]{1,0:T(8,128)S(1)} collective-permute-done((f32[64,2304]{1,0:T(8,128)S(1)}, f32[64,2304]{1,0:T(8,128)S(1)}, u32[]{:S(2)}, u32[]{:S(2)}) %collective-permute-start.11) | collective-permute-done | bytes 589856 | tf_op jit(solution)/shard_map/ppermute | solution.py:313
  195.0 0.9 pad_maximum_fusion
  (52 shorter events, 6.9 us)
Async XLA Ops:
  0.1 0.7 copy-start.1
  3.1 5.5 %collective-permute-start = (f32[512,640]{1,0:T(8,128)S(1)}, f32[512,640]{1,0:T(8,128)S(1)}, u32[]{:S(2)}, u32[]{:S(2)}) collective-permute-start(f32[512,640]{1,0:T(8,128)S(1)} %get-tuple-element.41), channel_id=1, source_target_pairs={{0,1},{1,0},{2,3},{3,2},{4,5},{5,4},{6,7},{7,6},{8,9},{9,8},{10,11... | collective-permute-start | bytes 3932168 | tf_op jit(solution)/shard_map/ppermute | solution.py:309
  3.2 4.7 %copy-start = (bf16[512,640]{1,0:T(8,128)(2,1)S(1)}, bf16[512,640]{1,0:T(8,128)(2,1)}, u32[]{:S(2)}) copy-start(bf16[512,640]{1,0:T(8,128)(2,1)} %q_ref) | copy-start | bytes 1966084
  52.8 58.6 %slice-start = ((s8[6553600]{0:T(1024)(128)(4,1)}), s8[4194304]{0:T(1024)(128)(4,1)S(1)}, s32[]{:S(2)}) async-start(s8[6553600]{0:T(1024)(128)(4,1)} %bitcast.34), calls=%async_computation.2 | async-start | bytes 8388608
  87.5 23.9 %slice-start.1 = ((s8[6553600]{0:T(1024)(128)(4,1)}), s8[2359296]{0:T(1024)(128)(4,1)S(1)}, s32[]{:S(2)}) async-start(s8[6553600]{0:T(1024)(128)(4,1)} %bitcast.34), calls=%async_computation.3 | async-start | bytes 4718592
  87.5 19.5 %collective-permute-start.1 = (f32[256,640]{1,0:T(8,128)S(1)}, f32[256,640]{1,0:T(8,128)S(1)}, u32[]{:S(2)}, u32[]{:S(2)}) collective-permute-start(f32[256,640]{1,0:T(8,128)S(1)} %get-tuple-element.47), channel_id=1, source_target_pairs={{0,1},{1,0},{2,3},{3,2},{4,5},{5,4},{6,7},{7,6},{8,9},{9,8},{10,11... | collective-permute-start | bytes 1966088 | tf_op jit(solution)/shard_map/ppermute | solution.py:309
  108.4 2.3 %collective-permute-start.2 = (f32[256,640]{1,0:T(8,128)S(1)}, f32[256,640]{1,0:T(8,128)S(1)}, u32[]{:S(2)}, u32[]{:S(2)}) collective-permute-start(f32[256,640]{1,0:T(8,128)S(1)} %far_query.1), channel_id=1, source_target_pairs={{0,1},{1,0},{2,3},{3,2},{4,5},{5,4},{6,7},{7,6},{8,9},{9,8},{10,11... | collective-permute-start | bytes 1966088 | tf_op jit(solution)/shard_map/ppermute | solution.py:309
  112.0 15.8 %collective-permute-start.3 = (f32[64,2304]{1,0:T(8,128)S(1)}, f32[64,2304]{1,0:T(8,128)S(1)}, u32[]{:S(2)}, u32[]{:S(2)}) collective-permute-start(f32[64,2304]{1,0:T(8,128)S(1)} %fusion.14), channel_id=1, source_target_pairs={{0,64},{64,0},{1,65},{65,1},{2,66},{66,2},{3,67},{67,3},{4,68},{68... | collective-permute-start | bytes 1769480 | tf_op jit(solution)/shard_map/ppermute | solution.py:309
  113.7 19.9 %collective-permute-start.7 = (f32[64,2816]{1,0:T(8,128)S(1)}, f32[64,2816]{1,0:T(8,128)S(1)}, u32[]{:S(2)}, u32[]{:S(2)}) collective-permute-start(f32[64,2816]{1,0:T(8,128)S(1)} %get-tuple-element.71), channel_id=1, source_target_pairs={{0,48},{16,0},{32,16},{48,32},{1,49},{17,1},{33,17},{49,33},{2,50}... | collective-permute-start | bytes 2162696 | tf_op jit(solution)/shard_map/ppermute | solution.py:313
  117.8 19.7 %collective-permute-start.5 = (f32[64,2816]{1,0:T(8,128)S(1)}, f32[64,2816]{1,0:T(8,128)S(1)}, u32[]{:S(2)}, u32[]{:S(2)}) collective-permute-start(f32[64,2816]{1,0:T(8,128)S(1)} %get-tuple-element.72), channel_id=1, source_target_pairs={{0,16},{16,32},{32,48},{48,0},{1,17},{17,33},{33,49},{49,1},{2,18}... | collective-permute-start | bytes 2162696 | tf_op jit(solution)/shard_map/ppermute | solution.py:313
  128.4 43.6 %collective-permute-start.4 = (f32[192,2304]{1,0:T(8,128)S(1)}, f32[192,2304]{1,0:T(8,128)S(1)}, u32[]{:S(2)}, u32[]{:S(2)}) collective-permute-start(f32[192,2304]{1,0:T(8,128)S(1)} %fusion.12), channel_id=1, source_target_pairs={{0,64},{64,0},{1,65},{65,1},{2,66},{66,2},{3,67},{67,3},{4,68},{68... | collective-permute-start | bytes 5308424 | tf_op jit(solution)/shard_map/ppermute | solution.py:309
  133.7 37.6 %collective-permute-start.8 = (f32[128,1920]{1,0:T(8,128)S(1)}, f32[128,1920]{1,0:T(8,128)S(1)}, u32[]{:S(2)}, u32[]{:S(2)}) collective-permute-start(f32[128,1920]{1,0:T(8,128)S(1)} %fusion.18), channel_id=1, source_target_pairs={{0,48},{16,0},{32,16},{48,32},{1,49},{17,1},{33,17},{49,33},{2,50}... | collective-permute-start | bytes 2949128 | tf_op jit(solution)/shard_map/ppermute | solution.py:313
  137.7 33.6 %collective-permute-start.6 = (f32[128,1920]{1,0:T(8,128)S(1)}, f32[128,1920]{1,0:T(8,128)S(1)}, u32[]{:S(2)}, u32[]{:S(2)}) collective-permute-start(f32[128,1920]{1,0:T(8,128)S(1)} %fusion.19), channel_id=1, source_target_pairs={{0,16},{16,32},{32,48},{48,0},{1,17},{17,33},{33,49},{49,1},{2,18}... | collective-permute-start | bytes 2949128 | tf_op jit(solution)/shard_map/ppermute | solution.py:313
  137.8 26.5 %collective-permute-start.10 = (f32[32,2304]{1,0:T(8,128)S(1)}, f32[32,2304]{1,0:T(8,128)S(1)}, u32[]{:S(2)}, u32[]{:S(2)}) collective-permute-start(f32[32,2304]{1,0:T(8,128)S(1)} %get-tuple-element.75), channel_id=1, source_target_pairs={{0,48},{16,0},{32,16},{48,32},{1,49},{17,1},{33,17},{49,33},{2,50}... | collective-permute-start | bytes 884744 | tf_op jit(solution)/shard_map/ppermute | solution.py:313
  141.1 26.9 %collective-permute-start.9 = (f32[32,2304]{1,0:T(8,128)S(1)}, f32[32,2304]{1,0:T(8,128)S(1)}, u32[]{:S(2)}, u32[]{:S(2)}) collective-permute-start(f32[32,2304]{1,0:T(8,128)S(1)} %get-tuple-element.76), channel_id=1, source_target_pairs={{0,16},{16,32},{32,48},{48,0},{1,17},{17,33},{33,49},{49,1},{2,18}... | collective-permute-start | bytes 884744 | tf_op jit(solution)/shard_map/ppermute | solution.py:313
  168.1 11.8 %collective-permute-start.14 = (f32[128,896]{1,0:T(8,128)S(1)}, f32[128,896]{1,0:T(8,128)S(1)}, u32[]{:S(2)}, u32[]{:S(2)}) collective-permute-start(f32[128,896]{1,0:T(8,128)S(1)} %pad_maximum_fusion.4), channel_id=1, source_target_pairs={{0,16},{16,32},{32,48},{48,0},{1,17},{17,33},{33,49},{49,1},{2,18}... | collective-permute-start | bytes 1376264 | tf_op jit(solution)/shard_map/ppermute | solution.py:313
  168.1 11.8 %collective-permute-start.15 = (f32[128,896]{1,0:T(8,128)S(1)}, f32[128,896]{1,0:T(8,128)S(1)}, u32[]{:S(2)}, u32[]{:S(2)}) collective-permute-start(f32[128,896]{1,0:T(8,128)S(1)} %pad_maximum_fusion.3), channel_id=1, source_target_pairs={{0,48},{16,0},{32,16},{48,32},{1,49},{17,1},{33,17},{49,33},{2,50}... | collective-permute-start | bytes 1376264 | tf_op jit(solution)/shard_map/ppermute | solution.py:313
  172.5 15.8 %collective-permute-start.13 = (f32[64,1920]{1,0:T(8,128)S(1)}, f32[64,1920]{1,0:T(8,128)S(1)}, u32[]{:S(2)}, u32[]{:S(2)}) collective-permute-start(f32[64,1920]{1,0:T(8,128)S(1)} %slice.139), channel_id=1, source_target_pairs={{0,64},{64,0},{1,65},{65,1},{2,66},{66,2},{3,67},{67,3},{4,68},{68... | collective-permute-start | bytes 1474568 | tf_op jit(solution)/shard_map/ppermute | solution.py:309
  180.0 8.2 %collective-permute-start.16 = (f32[64,896]{1,0:T(8,128)S(1)}, f32[64,896]{1,0:T(8,128)S(1)}, u32[]{:S(2)}, u32[]{:S(2)}) collective-permute-start(f32[64,896]{1,0:T(8,128)S(1)} %slice.162), channel_id=1, source_target_pairs={{0,64},{64,0},{1,65},{65,1},{2,66},{66,2},{3,67},{67,3},{4,68},{68... | collective-permute-start | bytes 688136 | tf_op jit(solution)/shard_map/ppermute | solution.py:309
  181.4 13.4 %collective-permute-start.11 = (f32[64,2304]{1,0:T(8,128)S(1)}, f32[64,2304]{1,0:T(8,128)S(1)}, u32[]{:S(2)}, u32[]{:S(2)}) collective-permute-start(f32[64,2304]{1,0:T(8,128)S(1)} %get-tuple-element.59), channel_id=1, source_target_pairs={{0,16},{16,32},{32,48},{48,0},{1,17},{17,33},{33,49},{49,1},{2,18}... | collective-permute-start | bytes 1769480 | tf_op jit(solution)/shard_map/ppermute | solution.py:313
  181.4 13.4 %collective-permute-start.12 = (f32[64,2304]{1,0:T(8,128)S(1)}, f32[64,2304]{1,0:T(8,128)S(1)}, u32[]{:S(2)}, u32[]{:S(2)}) collective-permute-start(f32[64,2304]{1,0:T(8,128)S(1)} %get-tuple-element.60), channel_id=1, source_target_pairs={{0,48},{16,0},{32,16},{48,32},{1,49},{17,1},{33,17},{49,33},{2,50}... | collective-permute-start | bytes 1769480 | tf_op jit(solution)/shard_map/ppermute | solution.py:313

commit v9 on v8

--- a/solution.py
+++ b/solution.py
@@ -17,7 +17,7 @@
 TILE = 256
 VMEM_LIMIT = 24 << 20
 CUT = 2304
-MIDDLE = 1920
+MIDDLE = 1408
 Y_ORDER = (2, 0, 1, 3)
 F32 = jnp.float32
 BF16 = jnp.bfloat16
@@ -313,12 +313,17 @@
     return lax.ppermute(a, "z", [(i, (i + shift) % 4) for i in range(4)])
 
 
-def plane_scatter(a):
-    return jnp.sum(lax.all_to_all(a, PLANE, 0, 0, tiled=True), axis=0)
-
-
-def plane_gather(a):
-    same = jnp.broadcast_to(a[None], (SHARDS,) + a.shape)
+def sum_kernel(a_ref, o_ref):
+    total = a_ref[0]
+    for j in range(1, SHARDS):
+        total = total + a_ref[j]
+    for j in range(SHARDS):
+        o_ref[j] = total
+
+
+def plane_sum(a):
+    came = lax.all_to_all(a, PLANE, 0, 0, tiled=True)
+    same = call(sum_kernel, "sum_parts", out(a.shape, a.dtype), [], came)
     return lax.all_to_all(same, PLANE, 0, 0, tiled=True)
 
 
@@ -377,8 +382,7 @@
     q, q_sent = sort_queries(at, queries)
     summed = far_grads(came, rounded, partial)
     q_sent, summed = together(q_sent, summed)
-    total = plane_scatter(summed)
-    whole, q_sent = together(plane_gather(total), q_sent)
+    whole, q_sent = together(plane_sum(summed), q_sent)
     q_came = swap(q_sent, "core")
     v = newton(at, whole, *weights)
     o_came = swap(call(far_query_kernel, "far_query", out(q_sent.shape, F32), [], q_came, v), "core")

time: 196 us -> 190 us (0.969)
  waiting for transfers between devices: 53.7 us -> 51 us
    ppermute x10, waiting for transfers between devices: 40.7 us -> 28.5 us  [ring(): return lax.ppermute(a, 'z', [(i, (i + shift) % 4) for i in range(4)])]
    ppermute x7, waiting for transfers between devices: 13.1 us -> 22.5 us  [swap(): return lax.ppermute(a, axis, [(0, 1), (1, 0)])]
    pallas_call x5 -> x6, Pallas kernels: 6.52 us -> 6.68 us  [call(): pl.pallas_call(kernel, out_shape=outs, in_specs=specs, out_specs=jax.tree...]
  transfers between devices with their start and end apart: 17 -> 17, of which waited for: 8 -> 10; matrix products, arithmetic and copies ran while one was open for 4% -> 4% of each run, Pallas kernels for 13% -> 14%
where the time goes in v9:
time: 190 us
  blocking collectives  74.5 us (39%)
  waiting for transfers between devices  51 us (27%)
  Pallas kernels  33.2 us (17%)
  starting transfers between devices  21.6 us (11%)
  matrix products  6.23 us (3%)
  other arithmetic  2.36 us (1%)
    all_to_all x1, blocking collectives, plane_sum(): came = lax.all_to_all(a, PLANE, 0, 0, tiled=True)  39.8 us
    all_to_all x1, blocking collectives, plane_sum(): return lax.all_to_all(same, PLANE, 0, 0, tiled=True)  34.7 us
    ppermute x10, waiting for transfers between devices, ring(): return lax.ppermute(a, 'z', [(i, (i + shift) % 4) for i in range(4)])  28.5 us
    ppermute x7, waiting for transfers between devices, swap(): return lax.ppermute(a, axis, [(0, 1), (1, 0)])  22.5 us
    pallas_call x1, Pallas kernels, newton(): pl.pallas_call(newton_kernel, out_shape=out(shape, BF16), in_specs=[pl.Bl...  19.5 us
    ppermute x10, starting transfers between devices, ring(): return lax.ppermute(a, 'z', [(i, (i + shift) % 4) for i in range(4)])  17 us
    pallas_call x6, Pallas kernels, call(): pl.pallas_call(kernel, out_shape=outs, in_specs=specs, out_specs=jax.tree...  6.68 us
    dot_general x9, matrix products, mm(): return jnp.dot(a, b, preferred_element_type=F32)  6.23 us
  transfers between devices with their start and end apart: 17, of which 10 were waited for; matrix products, arithmetic and copies ran while one was open for 4% of the time, Pallas kernels for 14%

profile of v9, /device:TPU:0, one launch (start us, length us, event | category | flops | bytes accessed | tf_op | source)
XLA Modules:
  0.0 190.0 jit_solution(9571248771165839636)
XLA Ops:
  0.8 2.4 %sort_tokens.1 = (bf16[512,320]{1,0:T(8,128)(2,1)S(1)}, bf16[512,320]{1,0:T(8,128)(2,1)S(1)}, f32[512,640]{1,0:T(8,128)S(1)}) custom-call(s32[3]{0:T(128)S(1)} %pad_add_fusion.at_ref, f32[2,512]{1,0:T(2,128)S(1)} %bitcast.33, bf16[512,640]{1,0:T(8,128)(2,1)} %k_ref.1, bf16[512,640]{1,0:T(8,128)(2,1)} %v_ref.1), custom_call_target="tpu_custom_call" | custom-call | tf_op jit(solution)/shard_map/sort_tokens/pallas_call | solution.py:86
  3.3 4.6 %near_grads.1 = (f32[3,320,640]{2,1,0:T(8,128)S(1)}, bf16[3,320,640]{2,1,0:T(8,128)(2,1)S(1)}) custom-call(s32[3]{0:T(128)S(1)} %pad_add_fusion.at_ref, bf16[512,320]{1,0:T(8,128)(2,1)S(1)} %get-tuple-element.35.k_ref, bf16[512,320]{1,0:T(8,128)(2,1)S(1)} %get-tuple-element.36.d_ref, f32[2,320,640]{2,1,0:T(8,128)} %wg_ref.1, f32[2,320,640]{2,1,0:T(8,128)} %wu_ref.1, ...), custom_call_target="tpu_custom_call" | custom-call | tf_op jit(solution)/shard_map/near_grads/pallas_call | solution.py:174
  8.6 2.4 %far_grads.1 = f32[8,3,40,640]{3,2,1,0:T(8,128)S(1)} custom-call(f32[512,640]{1,0:T(8,128)S(1)} %collective-permute-done.came, bf16[3,320,640]{2,1,0:T(8,128)(2,1)S(1)} %get-tuple-element.42.b_ref, f32[3,320,640]{2,1,0:T(8,128)S(1)} %get-tuple-element.43.p_ref), custom_call_target="tpu_custom_call" | custom-call | tf_op jit(solution)/shard_map/far_grads/pallas_call | solution.py:36
  11.0 39.8 %all_to_all.10.a_ref = f32[8,3,40,640]{3,2,1,0:T(8,128)S(1)} all-to-all(f32[8,3,40,640]{3,2,1,0:T(8,128)S(1)} %far_grads.1), channel_id=1, replica_groups=mesh['yl'=2,'z'=4,'x'=4,'yh'=2,'core'=2] {'x','yh'}, dimensions={0} | all-to-all | bytes 4915200 | tf_op jit(solution)/shard_map/all_to_all | solution.py:325
  51.0 34.7 %all_to_all.11.g_ref = f32[8,3,40,640]{3,2,1,0:T(8,128)S(1)} all-to-all(f32[8,3,40,640]{3,2,1,0:T(8,128)S(1)} %sum_parts.1), channel_id=1, replica_groups=mesh['yl'=2,'z'=4,'x'=4,'yh'=2,'core'=2] {'x','yh'}, dimensions={0} | all-to-all | bytes 4915200 | tf_op jit(solution)/shard_map/all_to_all | solution.py:327
  85.7 19.5 %newton.1.v_ref = bf16[3,320,640]{2,1,0:T(8,128)(2,1)S(1)} custom-call(s32[3]{0:T(128)S(1)} %pad_add_fusion.at_ref, f32[8,3,40,640]{3,2,1,0:T(8,128)S(1)} %all_to_all.11.g_ref, f32[2,320,640]{2,1,0:T(8,128)} %wg_ref.1, f32[2,320,640]{2,1,0:T(8,128)} %wu_ref.1, f32[2,320,640]{2,1,0:T(8,128)} %wd_ref.1), custom_call_target="tpu_custom_call" | custom-call | tf_op jit(solution)/shard_map/newton/pallas_call | solution.py:252
  105.2 1.4 far_query.1
  107.2 1.3 near_query.1.o_ref
  110.2 0.8 collective-permute-start.3
  111.0 0.8 fusion.2
  111.8 2.0 %collective-permute-start.5 = (f32[64,2816]{1,0:T(8,128)S(1)}, f32[64,2816]{1,0:T(8,128)S(1)}, u32[]{:S(2)}, u32[]{:S(2)}) collective-permute-start(f32[64,2816]{1,0:T(8,128)S(1)} %get-tuple-element.76), channel_id=1, source_target_pairs={{0,16},{16,32},{32,48},{48,0},{1,17},{17,33},{33,49},{49,1},{2,18}... | collective-permute-start | bytes 2162696 | tf_op jit(solution)/shard_map/ppermute | solution.py:313
  113.9 2.2 %collective-permute-start.7 = (f32[64,2816]{1,0:T(8,128)S(1)}, f32[64,2816]{1,0:T(8,128)S(1)}, u32[]{:S(2)}, u32[]{:S(2)}) collective-permute-start(f32[64,2816]{1,0:T(8,128)S(1)} %get-tuple-element.75), channel_id=1, source_target_pairs={{0,48},{16,0},{32,16},{48,32},{1,49},{17,1},{33,17},{49,33},{2,50}... | collective-permute-start | bytes 2162696 | tf_op jit(solution)/shard_map/ppermute | solution.py:313
  116.0 0.9 fusion.10
  116.9 9.1 %collective-permute-done.3 = f32[64,2304]{1,0:T(8,128)S(1)} collective-permute-done((f32[64,2304]{1,0:T(8,128)S(1)}, f32[64,2304]{1,0:T(8,128)S(1)}, u32[]{:S(2)}, u32[]{:S(2)}) %collective-permute-start.3) | collective-permute-done | bytes 589856 | tf_op jit(solution)/shard_map/ppermute | solution.py:309
  126.6 1.0 collective-permute-start.4
  127.6 0.8 fusion.4
  128.4 0.8 fusion
  129.2 3.2 %collective-permute-done.5 = f32[64,2816]{1,0:T(8,128)S(1)} collective-permute-done((f32[64,2816]{1,0:T(8,128)S(1)}, f32[64,2816]{1,0:T(8,128)S(1)}, u32[]{:S(2)}, u32[]{:S(2)}) %collective-permute-start.5) | collective-permute-done | bytes 720928 | tf_op jit(solution)/shard_map/ppermute | solution.py:313
  133.0 1.1 collective-permute-start.6
  134.1 2.2 %collective-permute-start.8 = (f32[128,1408]{1,0:T(8,128)S(1)}, f32[128,1408]{1,0:T(8,128)S(1)}, u32[]{:S(2)}, u32[]{:S(2)}) collective-permute-start(f32[128,1408]{1,0:T(8,128)S(1)} %get-tuple-element.70), channel_id=1, source_target_pairs={{0,48},{16,0},{32,16},{48,32},{1,49},{17,1},{33,17},{49,33},{2,50}... | collective-permute-start | bytes 2162696 | tf_op jit(solution)/shard_map/ppermute | solution.py:313
  136.3 1.7 collective-permute-start.10
  138.4 0.9 fusion.8
  139.3 18.3 %collective-permute-done.10 = f32[32,2304]{1,0:T(8,128)S(1)} collective-permute-done((f32[32,2304]{1,0:T(8,128)S(1)}, f32[32,2304]{1,0:T(8,128)S(1)}, u32[]{:S(2)}, u32[]{:S(2)}) %collective-permute-start.10) | collective-permute-done | bytes 294944 | tf_op jit(solution)/shard_map/ppermute | solution.py:313
  159.0 2.5 %collective-permute-start.15 = (f32[128,1408]{1,0:T(8,128)S(1)}, f32[128,1408]{1,0:T(8,128)S(1)}, u32[]{:S(2)}, u32[]{:S(2)}) collective-permute-start(f32[128,1408]{1,0:T(8,128)S(1)} %get-tuple-element.64), channel_id=1, source_target_pairs={{0,48},{16,0},{32,16},{48,32},{1,49},{17,1},{33,17},{49,33},{2,50}... | collective-permute-start | bytes 2162696 | tf_op jit(solution)/shard_map/ppermute | solution.py:313
  162.1 5.0 %collective-permute-done.4 = f32[192,2304]{1,0:T(8,128)S(1)} collective-permute-done((f32[192,2304]{1,0:T(8,128)S(1)}, f32[192,2304]{1,0:T(8,128)S(1)}, u32[]{:S(2)}, u32[]{:S(2)}) %collective-permute-start.4) | collective-permute-done | bytes 1769504 | tf_op jit(solution)/shard_map/ppermute | solution.py:309
  167.5 2.0 %collective-permute-start.11 = (f32[64,2304]{1,0:T(8,128)S(1)}, f32[64,2304]{1,0:T(8,128)S(1)}, u32[]{:S(2)}, u32[]{:S(2)}) collective-permute-start(f32[64,2304]{1,0:T(8,128)S(1)} %pad_maximum_fusion.3), channel_id=1, source_target_pairs={{0,16},{16,32},{32,48},{48,0},{1,17},{17,33},{33,49},{49,1},{2,18}... | collective-permute-start | bytes 1769480 | tf_op jit(solution)/shard_map/ppermute | solution.py:313
  169.5 2.2 %collective-permute-start.12 = (f32[64,2304]{1,0:T(8,128)S(1)}, f32[64,2304]{1,0:T(8,128)S(1)}, u32[]{:S(2)}, u32[]{:S(2)}) collective-permute-start(f32[64,2304]{1,0:T(8,128)S(1)} %pad_maximum_fusion.4), channel_id=1, source_target_pairs={{0,48},{16,0},{32,16},{48,32},{1,49},{17,1},{33,17},{49,33},{2,50}... | collective-permute-start | bytes 1769480 | tf_op jit(solution)/shard_map/ppermute | solution.py:313
  173.0 5.6 %collective-permute-done.14 = f32[128,1408]{1,0:T(8,128)S(1)} collective-permute-done((f32[128,1408]{1,0:T(8,128)S(1)}, f32[128,1408]{1,0:T(8,128)S(1)}, u32[]{:S(2)}, u32[]{:S(2)}) %collective-permute-start.14) | collective-permute-done | bytes 720928 | tf_op jit(solution)/shard_map/ppermute | solution.py:313
  178.8 1.4 collective-permute-start.16
  180.2 2.9 %collective-permute-done.13 = f32[64,1408]{1,0:T(8,128)S(1)} collective-permute-done((f32[64,1408]{1,0:T(8,128)S(1)}, f32[64,1408]{1,0:T(8,128)S(1)}, u32[]{:S(2)}, u32[]{:S(2)}) %collective-permute-start.13) | collective-permute-done | bytes 360480 | tf_op jit(solution)/shard_map/ppermute | solution.py:309
  183.2 5.2 %collective-permute-done.16 = f32[64,1408]{1,0:T(8,128)S(1)} collective-permute-done((f32[64,1408]{1,0:T(8,128)S(1)}, f32[64,1408]{1,0:T(8,128)S(1)}, u32[]{:S(2)}, u32[]{:S(2)}) %collective-permute-start.16) | collective-permute-done | bytes 360480 | tf_op jit(solution)/shard_map/ppermute | solution.py:309
  189.2 0.9 pad_maximum_fusion.2
  (49 shorter events, 10.3 us)
Async XLA Ops:
  0.1 0.7 copy-start.1
  3.1 5.5 %collective-permute-start = (f32[512,640]{1,0:T(8,128)S(1)}, f32[512,640]{1,0:T(8,128)S(1)}, u32[]{:S(2)}, u32[]{:S(2)}) collective-permute-start(f32[512,640]{1,0:T(8,128)S(1)} %get-tuple-element.41), channel_id=1, source_target_pairs={{0,1},{1,0},{2,3},{3,2},{4,5},{5,4},{6,7},{7,6},{8,9},{9,8},{10,11... | collective-permute-start | bytes 3932168 | tf_op jit(solution)/shard_map/ppermute | solution.py:309
  3.2 4.7 %copy-start = (bf16[512,640]{1,0:T(8,128)(2,1)S(1)}, bf16[512,640]{1,0:T(8,128)(2,1)}, u32[]{:S(2)}) copy-start(bf16[512,640]{1,0:T(8,128)(2,1)} %q_ref) | copy-start | bytes 1966084
  51.0 58.6 %slice-start = ((s8[6553600]{0:T(1024)(128)(4,1)}), s8[4194304]{0:T(1024)(128)(4,1)S(1)}, s32[]{:S(2)}) async-start(s8[6553600]{0:T(1024)(128)(4,1)} %bitcast.34), calls=%async_computation.2 | async-start | bytes 8388608
  85.7 23.9 %slice-start.1 = ((s8[6553600]{0:T(1024)(128)(4,1)}), s8[2359296]{0:T(1024)(128)(4,1)S(1)}, s32[]{:S(2)}) async-start(s8[6553600]{0:T(1024)(128)(4,1)} %bitcast.34), calls=%async_computation.3 | async-start | bytes 4718592
  85.7 19.5 %collective-permute-start.1 = (f32[256,640]{1,0:T(8,128)S(1)}, f32[256,640]{1,0:T(8,128)S(1)}, u32[]{:S(2)}, u32[]{:S(2)}) collective-permute-start(f32[256,640]{1,0:T(8,128)S(1)} %get-tuple-element.47), channel_id=1, source_target_pairs={{0,1},{1,0},{2,3},{3,2},{4,5},{5,4},{6,7},{7,6},{8,9},{9,8},{10,11... | collective-permute-start | bytes 1966088 | tf_op jit(solution)/shard_map/ppermute | solution.py:309
  106.6 2.3 %collective-permute-start.2 = (f32[256,640]{1,0:T(8,128)S(1)}, f32[256,640]{1,0:T(8,128)S(1)}, u32[]{:S(2)}, u32[]{:S(2)}) collective-permute-start(f32[256,640]{1,0:T(8,128)S(1)} %far_query.1), channel_id=1, source_target_pairs={{0,1},{1,0},{2,3},{3,2},{4,5},{5,4},{6,7},{7,6},{8,9},{9,8},{10,11... | collective-permute-start | bytes 1966088 | tf_op jit(solution)/shard_map/ppermute | solution.py:309
  110.2 15.8 %collective-permute-start.3 = (f32[64,2304]{1,0:T(8,128)S(1)}, f32[64,2304]{1,0:T(8,128)S(1)}, u32[]{:S(2)}, u32[]{:S(2)}) collective-permute-start(f32[64,2304]{1,0:T(8,128)S(1)} %fusion.12), channel_id=1, source_target_pairs={{0,64},{64,0},{1,65},{65,1},{2,66},{66,2},{3,67},{67,3},{4,68},{68... | collective-permute-start | bytes 1769480 | tf_op jit(solution)/shard_map/ppermute | solution.py:309
  111.8 20.6 %collective-permute-start.5 = (f32[64,2816]{1,0:T(8,128)S(1)}, f32[64,2816]{1,0:T(8,128)S(1)}, u32[]{:S(2)}, u32[]{:S(2)}) collective-permute-start(f32[64,2816]{1,0:T(8,128)S(1)} %get-tuple-element.76), channel_id=1, source_target_pairs={{0,16},{16,32},{32,48},{48,0},{1,17},{17,33},{33,49},{49,1},{2,18}... | collective-permute-start | bytes 2162696 | tf_op jit(solution)/shard_map/ppermute | solution.py:313
  113.9 18.8 %collective-permute-start.7 = (f32[64,2816]{1,0:T(8,128)S(1)}, f32[64,2816]{1,0:T(8,128)S(1)}, u32[]{:S(2)}, u32[]{:S(2)}) collective-permute-start(f32[64,2816]{1,0:T(8,128)S(1)} %get-tuple-element.75), channel_id=1, source_target_pairs={{0,48},{16,0},{32,16},{48,32},{1,49},{17,1},{33,17},{49,33},{2,50}... | collective-permute-start | bytes 2162696 | tf_op jit(solution)/shard_map/ppermute | solution.py:313
  126.6 40.5 %collective-permute-start.4 = (f32[192,2304]{1,0:T(8,128)S(1)}, f32[192,2304]{1,0:T(8,128)S(1)}, u32[]{:S(2)}, u32[]{:S(2)}) collective-permute-start(f32[192,2304]{1,0:T(8,128)S(1)} %fusion.10), channel_id=1, source_target_pairs={{0,64},{64,0},{1,65},{65,1},{2,66},{66,2},{3,67},{67,3},{4,68},{68... | collective-permute-start | bytes 5308424 | tf_op jit(solution)/shard_map/ppermute | solution.py:309
  133.0 28.6 %collective-permute-start.6 = (f32[128,1408]{1,0:T(8,128)S(1)}, f32[128,1408]{1,0:T(8,128)S(1)}, u32[]{:S(2)}, u32[]{:S(2)}) collective-permute-start(f32[128,1408]{1,0:T(8,128)S(1)} %get-tuple-element.81), channel_id=1, source_target_pairs={{0,16},{16,32},{32,48},{48,0},{1,17},{17,33},{33,49},{49,1},{2,18}... | collective-permute-start | bytes 2162696 | tf_op jit(solution)/shard_map/ppermute | solution.py:313
  134.1 27.5 %collective-permute-start.8 = (f32[128,1408]{1,0:T(8,128)S(1)}, f32[128,1408]{1,0:T(8,128)S(1)}, u32[]{:S(2)}, u32[]{:S(2)}) collective-permute-start(f32[128,1408]{1,0:T(8,128)S(1)} %get-tuple-element.70), channel_id=1, source_target_pairs={{0,48},{16,0},{32,16},{48,32},{1,49},{17,1},{33,17},{49,33},{2,50}... | collective-permute-start | bytes 2162696 | tf_op jit(solution)/shard_map/ppermute | solution.py:313
  136.3 21.3 %collective-permute-start.10 = (f32[32,2304]{1,0:T(8,128)S(1)}, f32[32,2304]{1,0:T(8,128)S(1)}, u32[]{:S(2)}, u32[]{:S(2)}) collective-permute-start(f32[32,2304]{1,0:T(8,128)S(1)} %get-tuple-element.79), channel_id=1, source_target_pairs={{0,48},{16,0},{32,16},{48,32},{1,49},{17,1},{33,17},{49,33},{2,50}... | collective-permute-start | bytes 884744 | tf_op jit(solution)/shard_map/ppermute | solution.py:313
  138.0 20.3 %collective-permute-start.9 = (f32[32,2304]{1,0:T(8,128)S(1)}, f32[32,2304]{1,0:T(8,128)S(1)}, u32[]{:S(2)}, u32[]{:S(2)}) collective-permute-start(f32[32,2304]{1,0:T(8,128)S(1)} %get-tuple-element.80), channel_id=1, source_target_pairs={{0,16},{16,32},{32,48},{48,0},{1,17},{17,33},{33,49},{49,1},{2,18}... | collective-permute-start | bytes 884744 | tf_op jit(solution)/shard_map/ppermute | solution.py:313
  158.3 20.3 %collective-permute-start.14 = (f32[128,1408]{1,0:T(8,128)S(1)}, f32[128,1408]{1,0:T(8,128)S(1)}, u32[]{:S(2)}, u32[]{:S(2)}) collective-permute-start(f32[128,1408]{1,0:T(8,128)S(1)} %get-tuple-element.63), channel_id=1, source_target_pairs={{0,16},{16,32},{32,48},{48,0},{1,17},{17,33},{33,49},{49,1},{2,18}... | collective-permute-start | bytes 2162696 | tf_op jit(solution)/shard_map/ppermute | solution.py:313
  159.0 19.6 %collective-permute-start.15 = (f32[128,1408]{1,0:T(8,128)S(1)}, f32[128,1408]{1,0:T(8,128)S(1)}, u32[]{:S(2)}, u32[]{:S(2)}) collective-permute-start(f32[128,1408]{1,0:T(8,128)S(1)} %get-tuple-element.64), channel_id=1, source_target_pairs={{0,48},{16,0},{32,16},{48,32},{1,49},{17,1},{33,17},{49,33},{2,50}... | collective-permute-start | bytes 2162696 | tf_op jit(solution)/shard_map/ppermute | solution.py:313
  167.5 21.5 %collective-permute-start.11 = (f32[64,2304]{1,0:T(8,128)S(1)}, f32[64,2304]{1,0:T(8,128)S(1)}, u32[]{:S(2)}, u32[]{:S(2)}) collective-permute-start(f32[64,2304]{1,0:T(8,128)S(1)} %pad_maximum_fusion.3), channel_id=1, source_target_pairs={{0,16},{16,32},{32,48},{48,0},{1,17},{17,33},{33,49},{49,1},{2,18}... | collective-permute-start | bytes 1769480 | tf_op jit(solution)/shard_map/ppermute | solution.py:313
  169.5 19.5 %collective-permute-start.12 = (f32[64,2304]{1,0:T(8,128)S(1)}, f32[64,2304]{1,0:T(8,128)S(1)}, u32[]{:S(2)}, u32[]{:S(2)}) collective-permute-start(f32[64,2304]{1,0:T(8,128)S(1)} %pad_maximum_fusion.4), channel_id=1, source_target_pairs={{0,48},{16,0},{32,16},{48,32},{1,49},{17,1},{33,17},{49,33},{2,50}... | collective-permute-start | bytes 1769480 | tf_op jit(solution)/shard_map/ppermute | solution.py:313
  171.7 11.4 %collective-permute-start.13 = (f32[64,1408]{1,0:T(8,128)S(1)}, f32[64,1408]{1,0:T(8,128)S(1)}, u32[]{:S(2)}, u32[]{:S(2)}) collective-permute-start(f32[64,1408]{1,0:T(8,128)S(1)} %slice.139), channel_id=1, source_target_pairs={{0,64},{64,0},{1,65},{65,1},{2,66},{66,2},{3,67},{67,3},{4,68},{68... | collective-permute-start | bytes 1081352 | tf_op jit(solution)/shard_map/ppermute | solution.py:309
  178.8 9.6 %collective-permute-start.16 = (f32[64,1408]{1,0:T(8,128)S(1)}, f32[64,1408]{1,0:T(8,128)S(1)}, u32[]{:S(2)}, u32[]{:S(2)}) collective-permute-start(f32[64,1408]{1,0:T(8,128)S(1)} %slice.162), channel_id=1, source_target_pairs={{0,64},{64,0},{1,65},{65,1},{2,66},{66,2},{3,67},{67,3},{4,68},{68... | collective-permute-start | bytes 1081352 | tf_op jit(solution)/shard_map/ppermute | solution.py:309

commit v10 on v9

--- a/solution.py
+++ b/solution.py
@@ -230,7 +230,7 @@
         total = jnp.sum(jnp.sum(grad * grad, axis=1, keepdims=True), axis=0, keepdims=True)
         x_s[m] = grad * lax.rsqrt(total + eps_value)
 
-    def sweep(_, carry):
+    def sweep():
         xs = [x_s[m] for m in every]
         parts = [split(x) for x in xs]
         grams = [gram_of(*p) for p in parts]
@@ -238,9 +238,15 @@
         mixers = [split(ns_b * g + ns_c * q) for g, q in zip(grams, squares)]
         for m, x, (xh, xl), mixer in zip(every, xs, parts, mixers):
             x_s[m] = ns_a * x + mm(packed(*mixer), jnp.concatenate([xh, xl, xh], axis=0))
+
+    def sweeps(_, carry):
+        sweep()
+        sweep()
         return carry
 
-    lax.fori_loop(0, NS_STEPS, sweep, 0)
+    lax.fori_loop(0, NS_STEPS // 2, sweeps, 0)
+    for _ in range(NS_STEPS % 2):
+        sweep()
     for m, copy in enumerate(copies):
         copy.wait()
         v_ref[m] = (f_s[m] - x_s[m]).astype(BF16)

time: 190 us -> 190 us (level)
  no operation moved by 1% of the time
where the time goes in v10:
time: 190 us
  blocking collectives  74.5 us (39%)
  waiting for transfers between devices  51.2 us (27%)
  Pallas kernels  32.8 us (17%)
  starting transfers between devices  21.6 us (11%)
  matrix products  6.24 us (3%)
  other arithmetic  2.36 us (1%)
    all_to_all x1, blocking collectives, plane_sum(): came = lax.all_to_all(a, PLANE, 0, 0, tiled=True)  39.8 us
    all_to_all x1, blocking collectives, plane_sum(): return lax.all_to_all(same, PLANE, 0, 0, tiled=True)  34.7 us
    ppermute x10, waiting for transfers between devices, ring(): return lax.ppermute(a, 'z', [(i, (i + shift) % 4) for i in range(4)])  29.1 us
    ppermute x7, waiting for transfers between devices, swap(): return lax.ppermute(a, axis, [(0, 1), (1, 0)])  22.1 us
    pallas_call x1, Pallas kernels, newton(): pl.pallas_call(newton_kernel, out_shape=out(shape, BF16), in_specs=[pl.Bl...  19.1 us
    ppermute x10, starting transfers between devices, ring(): return lax.ppermute(a, 'z', [(i, (i + shift) % 4) for i in range(4)])  17 us
    pallas_call x6, Pallas kernels, call(): pl.pallas_call(kernel, out_shape=outs, in_specs=specs, out_specs=jax.tree...  6.68 us
    dot_general x9, matrix products, mm(): return jnp.dot(a, b, preferred_element_type=F32)  6.24 us
  transfers between devices with their start and end apart: 17, of which 10 were waited for; matrix products, arithmetic and copies ran while one was open for 4% of the time, Pallas kernels for 14%

profile of v10, /device:TPU:0, one launch (start us, length us, event | category | flops | bytes accessed | tf_op | source)
XLA Modules:
  0.0 190.0 jit_solution(13706918653709662458)
XLA Ops:
  0.8 2.4 %sort_tokens.1 = (bf16[512,320]{1,0:T(8,128)(2,1)S(1)}, bf16[512,320]{1,0:T(8,128)(2,1)S(1)}, f32[512,640]{1,0:T(8,128)S(1)}) custom-call(s32[3]{0:T(128)S(1)} %pad_add_fusion.at_ref, f32[2,512]{1,0:T(2,128)S(1)} %bitcast.33, bf16[512,640]{1,0:T(8,128)(2,1)} %k_ref.1, bf16[512,640]{1,0:T(8,128)(2,1)} %v_ref.1), custom_call_target="tpu_custom_call" | custom-call | tf_op jit(solution)/shard_map/sort_tokens/pallas_call | solution.py:86
  3.3 4.6 %near_grads.1 = (f32[3,320,640]{2,1,0:T(8,128)S(1)}, bf16[3,320,640]{2,1,0:T(8,128)(2,1)S(1)}) custom-call(s32[3]{0:T(128)S(1)} %pad_add_fusion.at_ref, bf16[512,320]{1,0:T(8,128)(2,1)S(1)} %get-tuple-element.35.k_ref, bf16[512,320]{1,0:T(8,128)(2,1)S(1)} %get-tuple-element.36.d_ref, f32[2,320,640]{2,1,0:T(8,128)} %wg_ref.1, f32[2,320,640]{2,1,0:T(8,128)} %wu_ref.1, ...), custom_call_target="tpu_custom_call" | custom-call | tf_op jit(solution)/shard_map/near_grads/pallas_call | solution.py:174
  8.6 2.4 %far_grads.1 = f32[8,3,40,640]{3,2,1,0:T(8,128)S(1)} custom-call(f32[512,640]{1,0:T(8,128)S(1)} %collective-permute-done.came, bf16[3,320,640]{2,1,0:T(8,128)(2,1)S(1)} %get-tuple-element.42.b_ref, f32[3,320,640]{2,1,0:T(8,128)S(1)} %get-tuple-element.43.p_ref), custom_call_target="tpu_custom_call" | custom-call | tf_op jit(solution)/shard_map/far_grads/pallas_call | solution.py:36
  11.0 39.8 %all_to_all.10.a_ref = f32[8,3,40,640]{3,2,1,0:T(8,128)S(1)} all-to-all(f32[8,3,40,640]{3,2,1,0:T(8,128)S(1)} %far_grads.1), channel_id=1, replica_groups=mesh['yl'=2,'z'=4,'x'=4,'yh'=2,'core'=2] {'x','yh'}, dimensions={0} | all-to-all | bytes 4915200 | tf_op jit(solution)/shard_map/all_to_all | solution.py:331
  51.0 34.7 %all_to_all.11.g_ref = f32[8,3,40,640]{3,2,1,0:T(8,128)S(1)} all-to-all(f32[8,3,40,640]{3,2,1,0:T(8,128)S(1)} %sum_parts.1), channel_id=1, replica_groups=mesh['yl'=2,'z'=4,'x'=4,'yh'=2,'core'=2] {'x','yh'}, dimensions={0} | all-to-all | bytes 4915200 | tf_op jit(solution)/shard_map/all_to_all | solution.py:333
  85.7 19.1 %newton.1.v_ref = bf16[3,320,640]{2,1,0:T(8,128)(2,1)S(1)} custom-call(s32[3]{0:T(128)S(1)} %pad_add_fusion.at_ref, f32[8,3,40,640]{3,2,1,0:T(8,128)S(1)} %all_to_all.11.g_ref, f32[2,320,640]{2,1,0:T(8,128)} %wg_ref.1, f32[2,320,640]{2,1,0:T(8,128)} %wu_ref.1, f32[2,320,640]{2,1,0:T(8,128)} %wd_ref.1), custom_call_target="tpu_custom_call" | custom-call | tf_op jit(solution)/shard_map/newton/pallas_call | solution.py:258
  104.9 1.4 far_query.1
  106.3 0.8 collective-permute-start.2
  107.1 1.3 near_query.1.o_ref
  110.9 0.8 fusion.2
  111.8 2.0 %collective-permute-start.5 = (f32[64,2816]{1,0:T(8,128)S(1)}, f32[64,2816]{1,0:T(8,128)S(1)}, u32[]{:S(2)}, u32[]{:S(2)}) collective-permute-start(f32[64,2816]{1,0:T(8,128)S(1)} %get-tuple-element.76), channel_id=1, source_target_pairs={{0,16},{16,32},{32,48},{48,0},{1,17},{17,33},{33,49},{49,1},{2,18}... | collective-permute-start | bytes 2162696 | tf_op jit(solution)/shard_map/ppermute | solution.py:319
  113.8 2.2 %collective-permute-start.7 = (f32[64,2816]{1,0:T(8,128)S(1)}, f32[64,2816]{1,0:T(8,128)S(1)}, u32[]{:S(2)}, u32[]{:S(2)}) collective-permute-start(f32[64,2816]{1,0:T(8,128)S(1)} %get-tuple-element.75), channel_id=1, source_target_pairs={{0,48},{16,0},{32,16},{48,32},{1,49},{17,1},{33,17},{49,33},{2,50}... | collective-permute-start | bytes 2162696 | tf_op jit(solution)/shard_map/ppermute | solution.py:319
  115.9 0.9 fusion.10
  116.8 9.1 %collective-permute-done.3 = f32[64,2304]{1,0:T(8,128)S(1)} collective-permute-done((f32[64,2304]{1,0:T(8,128)S(1)}, f32[64,2304]{1,0:T(8,128)S(1)}, u32[]{:S(2)}, u32[]{:S(2)}) %collective-permute-start.3) | collective-permute-done | bytes 589856 | tf_op jit(solution)/shard_map/ppermute | solution.py:315
  127.3 0.8 fusion.4
  128.1 0.8 fusion
  128.9 3.5 %collective-permute-done.5 = f32[64,2816]{1,0:T(8,128)S(1)} collective-permute-done((f32[64,2816]{1,0:T(8,128)S(1)}, f32[64,2816]{1,0:T(8,128)S(1)}, u32[]{:S(2)}, u32[]{:S(2)}) %collective-permute-start.5) | collective-permute-done | bytes 720928 | tf_op jit(solution)/shard_map/ppermute | solution.py:319
  132.9 1.1 collective-permute-start.6
  134.0 2.2 %collective-permute-start.8 = (f32[128,1408]{1,0:T(8,128)S(1)}, f32[128,1408]{1,0:T(8,128)S(1)}, u32[]{:S(2)}, u32[]{:S(2)}) collective-permute-start(f32[128,1408]{1,0:T(8,128)S(1)} %get-tuple-element.70), channel_id=1, source_target_pairs={{0,48},{16,0},{32,16},{48,32},{1,49},{17,1},{33,17},{49,33},{2,50}... | collective-permute-start | bytes 2162696 | tf_op jit(solution)/shard_map/ppermute | solution.py:319
  136.2 1.7 collective-permute-start.10
  138.3 0.9 fusion.8
  139.2 18.3 %collective-permute-done.10 = f32[32,2304]{1,0:T(8,128)S(1)} collective-permute-done((f32[32,2304]{1,0:T(8,128)S(1)}, f32[32,2304]{1,0:T(8,128)S(1)}, u32[]{:S(2)}, u32[]{:S(2)}) %collective-permute-start.10) | collective-permute-done | bytes 294944 | tf_op jit(solution)/shard_map/ppermute | solution.py:319
  158.9 2.5 %collective-permute-start.15 = (f32[128,1408]{1,0:T(8,128)S(1)}, f32[128,1408]{1,0:T(8,128)S(1)}, u32[]{:S(2)}, u32[]{:S(2)}) collective-permute-start(f32[128,1408]{1,0:T(8,128)S(1)} %get-tuple-element.64), channel_id=1, source_target_pairs={{0,48},{16,0},{32,16},{48,32},{1,49},{17,1},{33,17},{49,33},{2,50}... | collective-permute-start | bytes 2162696 | tf_op jit(solution)/shard_map/ppermute | solution.py:319
  162.0 4.7 %collective-permute-done.4 = f32[192,2304]{1,0:T(8,128)S(1)} collective-permute-done((f32[192,2304]{1,0:T(8,128)S(1)}, f32[192,2304]{1,0:T(8,128)S(1)}, u32[]{:S(2)}, u32[]{:S(2)}) %collective-permute-start.4) | collective-permute-done | bytes 1769504 | tf_op jit(solution)/shard_map/ppermute | solution.py:315
  167.2 2.0 %collective-permute-start.11 = (f32[64,2304]{1,0:T(8,128)S(1)}, f32[64,2304]{1,0:T(8,128)S(1)}, u32[]{:S(2)}, u32[]{:S(2)}) collective-permute-start(f32[64,2304]{1,0:T(8,128)S(1)} %pad_maximum_fusion.3), channel_id=1, source_target_pairs={{0,16},{16,32},{32,48},{48,0},{1,17},{17,33},{33,49},{49,1},{2,18}... | collective-permute-start | bytes 1769480 | tf_op jit(solution)/shard_map/ppermute | solution.py:319
  169.2 2.2 %collective-permute-start.12 = (f32[64,2304]{1,0:T(8,128)S(1)}, f32[64,2304]{1,0:T(8,128)S(1)}, u32[]{:S(2)}, u32[]{:S(2)}) collective-permute-start(f32[64,2304]{1,0:T(8,128)S(1)} %pad_maximum_fusion.4), channel_id=1, source_target_pairs={{0,48},{16,0},{32,16},{48,32},{1,49},{17,1},{33,17},{49,33},{2,50}... | collective-permute-start | bytes 1769480 | tf_op jit(solution)/shard_map/ppermute | solution.py:319
  172.7 5.8 %collective-permute-done.14 = f32[128,1408]{1,0:T(8,128)S(1)} collective-permute-done((f32[128,1408]{1,0:T(8,128)S(1)}, f32[128,1408]{1,0:T(8,128)S(1)}, u32[]{:S(2)}, u32[]{:S(2)}) %collective-permute-start.14) | collective-permute-done | bytes 720928 | tf_op jit(solution)/shard_map/ppermute | solution.py:319
  178.7 1.4 collective-permute-start.16
  180.2 2.7 %collective-permute-done.13 = f32[64,1408]{1,0:T(8,128)S(1)} collective-permute-done((f32[64,1408]{1,0:T(8,128)S(1)}, f32[64,1408]{1,0:T(8,128)S(1)}, u32[]{:S(2)}, u32[]{:S(2)}) %collective-permute-start.13) | collective-permute-done | bytes 360480 | tf_op jit(solution)/shard_map/ppermute | solution.py:315
  182.9 5.2 %collective-permute-done.16 = f32[64,1408]{1,0:T(8,128)S(1)} collective-permute-done((f32[64,1408]{1,0:T(8,128)S(1)}, f32[64,1408]{1,0:T(8,128)S(1)}, u32[]{:S(2)}, u32[]{:S(2)}) %collective-permute-start.16) | collective-permute-done | bytes 360480 | tf_op jit(solution)/shard_map/ppermute | solution.py:315
  188.1 0.8 collective-permute-done.11
  189.1 0.9 pad_maximum_fusion.2
  (49 shorter events, 10.7 us)
Async XLA Ops:
  0.1 0.7 copy-start.1
  3.1 5.5 %collective-permute-start = (f32[512,640]{1,0:T(8,128)S(1)}, f32[512,640]{1,0:T(8,128)S(1)}, u32[]{:S(2)}, u32[]{:S(2)}) collective-permute-start(f32[512,640]{1,0:T(8,128)S(1)} %get-tuple-element.41), channel_id=1, source_target_pairs={{0,1},{1,0},{2,3},{3,2},{4,5},{5,4},{6,7},{7,6},{8,9},{9,8},{10,11... | collective-permute-start | bytes 3932168 | tf_op jit(solution)/shard_map/ppermute | solution.py:315
  3.2 4.7 %copy-start = (bf16[512,640]{1,0:T(8,128)(2,1)S(1)}, bf16[512,640]{1,0:T(8,128)(2,1)}, u32[]{:S(2)}) copy-start(bf16[512,640]{1,0:T(8,128)(2,1)} %q_ref) | copy-start | bytes 1966084
  51.0 58.5 %slice-start = ((s8[6553600]{0:T(1024)(128)(4,1)}), s8[4194304]{0:T(1024)(128)(4,1)S(1)}, s32[]{:S(2)}) async-start(s8[6553600]{0:T(1024)(128)(4,1)} %bitcast.34), calls=%async_computation.2 | async-start | bytes 8388608
  85.7 23.8 %slice-start.1 = ((s8[6553600]{0:T(1024)(128)(4,1)}), s8[2359296]{0:T(1024)(128)(4,1)S(1)}, s32[]{:S(2)}) async-start(s8[6553600]{0:T(1024)(128)(4,1)} %bitcast.34), calls=%async_computation.3 | async-start | bytes 4718592
  85.7 19.2 %collective-permute-start.1 = (f32[256,640]{1,0:T(8,128)S(1)}, f32[256,640]{1,0:T(8,128)S(1)}, u32[]{:S(2)}, u32[]{:S(2)}) collective-permute-start(f32[256,640]{1,0:T(8,128)S(1)} %get-tuple-element.47), channel_id=1, source_target_pairs={{0,1},{1,0},{2,3},{3,2},{4,5},{5,4},{6,7},{7,6},{8,9},{9,8},{10,11... | collective-permute-start | bytes 1966088 | tf_op jit(solution)/shard_map/ppermute | solution.py:315
  106.3 2.5 %collective-permute-start.2 = (f32[256,640]{1,0:T(8,128)S(1)}, f32[256,640]{1,0:T(8,128)S(1)}, u32[]{:S(2)}, u32[]{:S(2)}) collective-permute-start(f32[256,640]{1,0:T(8,128)S(1)} %far_query.1), channel_id=1, source_target_pairs={{0,1},{1,0},{2,3},{3,2},{4,5},{5,4},{6,7},{7,6},{8,9},{9,8},{10,11... | collective-permute-start | bytes 1966088 | tf_op jit(solution)/shard_map/ppermute | solution.py:315
  110.1 15.8 %collective-permute-start.3 = (f32[64,2304]{1,0:T(8,128)S(1)}, f32[64,2304]{1,0:T(8,128)S(1)}, u32[]{:S(2)}, u32[]{:S(2)}) collective-permute-start(f32[64,2304]{1,0:T(8,128)S(1)} %fusion.12), channel_id=1, source_target_pairs={{0,64},{64,0},{1,65},{65,1},{2,66},{66,2},{3,67},{67,3},{4,68},{68... | collective-permute-start | bytes 1769480 | tf_op jit(solution)/shard_map/ppermute | solution.py:315
  111.8 20.6 %collective-permute-start.5 = (f32[64,2816]{1,0:T(8,128)S(1)}, f32[64,2816]{1,0:T(8,128)S(1)}, u32[]{:S(2)}, u32[]{:S(2)}) collective-permute-start(f32[64,2816]{1,0:T(8,128)S(1)} %get-tuple-element.76), channel_id=1, source_target_pairs={{0,16},{16,32},{32,48},{48,0},{1,17},{17,33},{33,49},{49,1},{2,18}... | collective-permute-start | bytes 2162696 | tf_op jit(solution)/shard_map/ppermute | solution.py:319
  113.8 18.8 %collective-permute-start.7 = (f32[64,2816]{1,0:T(8,128)S(1)}, f32[64,2816]{1,0:T(8,128)S(1)}, u32[]{:S(2)}, u32[]{:S(2)}) collective-permute-start(f32[64,2816]{1,0:T(8,128)S(1)} %get-tuple-element.75), channel_id=1, source_target_pairs={{0,48},{16,0},{32,16},{48,32},{1,49},{17,1},{33,17},{49,33},{2,50}... | collective-permute-start | bytes 2162696 | tf_op jit(solution)/shard_map/ppermute | solution.py:319
  126.5 40.3 %collective-permute-start.4 = (f32[192,2304]{1,0:T(8,128)S(1)}, f32[192,2304]{1,0:T(8,128)S(1)}, u32[]{:S(2)}, u32[]{:S(2)}) collective-permute-start(f32[192,2304]{1,0:T(8,128)S(1)} %fusion.10), channel_id=1, source_target_pairs={{0,64},{64,0},{1,65},{65,1},{2,66},{66,2},{3,67},{67,3},{4,68},{68... | collective-permute-start | bytes 5308424 | tf_op jit(solution)/shard_map/ppermute | solution.py:315
  132.9 28.6 %collective-permute-start.6 = (f32[128,1408]{1,0:T(8,128)S(1)}, f32[128,1408]{1,0:T(8,128)S(1)}, u32[]{:S(2)}, u32[]{:S(2)}) collective-permute-start(f32[128,1408]{1,0:T(8,128)S(1)} %get-tuple-element.81), channel_id=1, source_target_pairs={{0,16},{16,32},{32,48},{48,0},{1,17},{17,33},{33,49},{49,1},{2,18}... | collective-permute-start | bytes 2162696 | tf_op jit(solution)/shard_map/ppermute | solution.py:319
  134.0 27.5 %collective-permute-start.8 = (f32[128,1408]{1,0:T(8,128)S(1)}, f32[128,1408]{1,0:T(8,128)S(1)}, u32[]{:S(2)}, u32[]{:S(2)}) collective-permute-start(f32[128,1408]{1,0:T(8,128)S(1)} %get-tuple-element.70), channel_id=1, source_target_pairs={{0,48},{16,0},{32,16},{48,32},{1,49},{17,1},{33,17},{49,33},{2,50}... | collective-permute-start | bytes 2162696 | tf_op jit(solution)/shard_map/ppermute | solution.py:319
  136.2 21.3 %collective-permute-start.10 = (f32[32,2304]{1,0:T(8,128)S(1)}, f32[32,2304]{1,0:T(8,128)S(1)}, u32[]{:S(2)}, u32[]{:S(2)}) collective-permute-start(f32[32,2304]{1,0:T(8,128)S(1)} %get-tuple-element.79), channel_id=1, source_target_pairs={{0,48},{16,0},{32,16},{48,32},{1,49},{17,1},{33,17},{49,33},{2,50}... | collective-permute-start | bytes 884744 | tf_op jit(solution)/shard_map/ppermute | solution.py:319
  137.9 20.3 %collective-permute-start.9 = (f32[32,2304]{1,0:T(8,128)S(1)}, f32[32,2304]{1,0:T(8,128)S(1)}, u32[]{:S(2)}, u32[]{:S(2)}) collective-permute-start(f32[32,2304]{1,0:T(8,128)S(1)} %get-tuple-element.80), channel_id=1, source_target_pairs={{0,16},{16,32},{32,48},{48,0},{1,17},{17,33},{33,49},{49,1},{2,18}... | collective-permute-start | bytes 884744 | tf_op jit(solution)/shard_map/ppermute | solution.py:319
  158.2 20.3 %collective-permute-start.14 = (f32[128,1408]{1,0:T(8,128)S(1)}, f32[128,1408]{1,0:T(8,128)S(1)}, u32[]{:S(2)}, u32[]{:S(2)}) collective-permute-start(f32[128,1408]{1,0:T(8,128)S(1)} %get-tuple-element.63), channel_id=1, source_target_pairs={{0,16},{16,32},{32,48},{48,0},{1,17},{17,33},{33,49},{49,1},{2,18}... | collective-permute-start | bytes 2162696 | tf_op jit(solution)/shard_map/ppermute | solution.py:319
  158.9 19.6 %collective-permute-start.15 = (f32[128,1408]{1,0:T(8,128)S(1)}, f32[128,1408]{1,0:T(8,128)S(1)}, u32[]{:S(2)}, u32[]{:S(2)}) collective-permute-start(f32[128,1408]{1,0:T(8,128)S(1)} %get-tuple-element.64), channel_id=1, source_target_pairs={{0,48},{16,0},{32,16},{48,32},{1,49},{17,1},{33,17},{49,33},{2,50}... | collective-permute-start | bytes 2162696 | tf_op jit(solution)/shard_map/ppermute | solution.py:319
  167.2 21.7 %collective-permute-start.11 = (f32[64,2304]{1,0:T(8,128)S(1)}, f32[64,2304]{1,0:T(8,128)S(1)}, u32[]{:S(2)}, u32[]{:S(2)}) collective-permute-start(f32[64,2304]{1,0:T(8,128)S(1)} %pad_maximum_fusion.3), channel_id=1, source_target_pairs={{0,16},{16,32},{32,48},{48,0},{1,17},{17,33},{33,49},{49,1},{2,18}... | collective-permute-start | bytes 1769480 | tf_op jit(solution)/shard_map/ppermute | solution.py:319
  169.2 19.7 %collective-permute-start.12 = (f32[64,2304]{1,0:T(8,128)S(1)}, f32[64,2304]{1,0:T(8,128)S(1)}, u32[]{:S(2)}, u32[]{:S(2)}) collective-permute-start(f32[64,2304]{1,0:T(8,128)S(1)} %pad_maximum_fusion.4), channel_id=1, source_target_pairs={{0,48},{16,0},{32,16},{48,32},{1,49},{17,1},{33,17},{49,33},{2,50}... | collective-permute-start | bytes 1769480 | tf_op jit(solution)/shard_map/ppermute | solution.py:319
  171.4 11.4 %collective-permute-start.13 = (f32[64,1408]{1,0:T(8,128)S(1)}, f32[64,1408]{1,0:T(8,128)S(1)}, u32[]{:S(2)}, u32[]{:S(2)}) collective-permute-start(f32[64,1408]{1,0:T(8,128)S(1)} %slice.139), channel_id=1, source_target_pairs={{0,64},{64,0},{1,65},{65,1},{2,66},{66,2},{3,67},{67,3},{4,68},{68... | collective-permute-start | bytes 1081352 | tf_op jit(solution)/shard_map/ppermute | solution.py:315
  178.7 9.4 %collective-permute-start.16 = (f32[64,1408]{1,0:T(8,128)S(1)}, f32[64,1408]{1,0:T(8,128)S(1)}, u32[]{:S(2)}, u32[]{:S(2)}) collective-permute-start(f32[64,1408]{1,0:T(8,128)S(1)} %slice.162), channel_id=1, source_target_pairs={{0,64},{64,0},{1,65},{65,1},{2,66},{66,2},{3,67},{67,3},{4,68},{68... | collective-permute-start | bytes 1081352 | tf_op jit(solution)/shard_map/ppermute | solution.py:315

commit v11 on v9

--- a/solution.py
+++ b/solution.py
@@ -354,7 +354,7 @@
     one = jnp.concatenate([one[:block] + up, one[block:]], axis=0)
     three = jnp.concatenate([three[:block], three[block:] + down], axis=0)
     a_came = both_ways(one[:, :MIDDLE], three[:, :MIDDLE])
-    later, b_up, b_down = together((one[:, MIDDLE:], three[:, MIDDLE:]), b_up, b_down)
+    later, a_came = together((one[:, MIDDLE:], three[:, MIDDLE:]), a_came)
     a_more = both_ways(*later)
     a = mm(by_z[0], wa[:, :MIDDLE]) + sum(a_came)
     b_rest = b_rest + mm(by_y[0, block:], wb)

time: 190 us -> 190 us (level)
    ppermute x10, waiting for transfers between devices: 28.5 us -> 23.9 us  [ring(): return lax.ppermute(a, 'z', [(i, (i + shift) % 4) for i in range(4)])]
    ppermute x7, waiting for transfers between devices: 22.5 us -> 25.3 us  [swap(): return lax.ppermute(a, axis, [(0, 1), (1, 0)])]
where the time goes in v11:
time: 190 us
  blocking collectives  74.5 us (39%)
  waiting for transfers between devices  49.2 us (26%)
  Pallas kernels  33.2 us (17%)
  starting transfers between devices  23.3 us (12%)
  matrix products  6.22 us (3%)
  other arithmetic  2.24 us (1%)
    all_to_all x1, blocking collectives, plane_sum(): came = lax.all_to_all(a, PLANE, 0, 0, tiled=True)  39.8 us
    all_to_all x1, blocking collectives, plane_sum(): return lax.all_to_all(same, PLANE, 0, 0, tiled=True)  34.7 us
    ppermute x7, waiting for transfers between devices, swap(): return lax.ppermute(a, axis, [(0, 1), (1, 0)])  25.3 us
    ppermute x10, waiting for transfers between devices, ring(): return lax.ppermute(a, 'z', [(i, (i + shift) % 4) for i in range(4)])  23.9 us
    pallas_call x1, Pallas kernels, newton(): pl.pallas_call(newton_kernel, out_shape=out(shape, BF16), in_specs=[pl.Bl...  19.5 us
    ppermute x10, starting transfers between devices, ring(): return lax.ppermute(a, 'z', [(i, (i + shift) % 4) for i in range(4)])  18.7 us
    pallas_call x6, Pallas kernels, call(): pl.pallas_call(kernel, out_shape=outs, in_specs=specs, out_specs=jax.tree...  6.68 us
    dot_general x9, matrix products, mm(): return jnp.dot(a, b, preferred_element_type=F32)  6.22 us
  transfers between devices with their start and end apart: 17, of which 10 were waited for; matrix products, arithmetic and copies ran while one was open for 4% of the time, Pallas kernels for 14%

profile of v11, /device:TPU:0, one launch (start us, length us, event | category | flops | bytes accessed | tf_op | source)
XLA Modules:
  0.0 189.8 jit_solution(15802577953772262368)
XLA Ops:
  0.8 2.4 %sort_tokens.1 = (bf16[512,320]{1,0:T(8,128)(2,1)S(1)}, bf16[512,320]{1,0:T(8,128)(2,1)S(1)}, f32[512,640]{1,0:T(8,128)S(1)}) custom-call(s32[3]{0:T(128)S(1)} %pad_add_fusion.at_ref, f32[2,512]{1,0:T(2,128)S(1)} %bitcast.33, bf16[512,640]{1,0:T(8,128)(2,1)} %k_ref.1, bf16[512,640]{1,0:T(8,128)(2,1)} %v_ref.1), custom_call_target="tpu_custom_call" | custom-call | tf_op jit(solution)/shard_map/sort_tokens/pallas_call | solution.py:86
  3.3 4.6 %near_grads.1 = (f32[3,320,640]{2,1,0:T(8,128)S(1)}, bf16[3,320,640]{2,1,0:T(8,128)(2,1)S(1)}) custom-call(s32[3]{0:T(128)S(1)} %pad_add_fusion.at_ref, bf16[512,320]{1,0:T(8,128)(2,1)S(1)} %get-tuple-element.35.k_ref, bf16[512,320]{1,0:T(8,128)(2,1)S(1)} %get-tuple-element.36.d_ref, f32[2,320,640]{2,1,0:T(8,128)} %wg_ref.1, f32[2,320,640]{2,1,0:T(8,128)} %wu_ref.1, ...), custom_call_target="tpu_custom_call" | custom-call | tf_op jit(solution)/shard_map/near_grads/pallas_call | solution.py:174
  8.6 2.4 %far_grads.1 = f32[8,3,40,640]{3,2,1,0:T(8,128)S(1)} custom-call(f32[512,640]{1,0:T(8,128)S(1)} %collective-permute-done.came, bf16[3,320,640]{2,1,0:T(8,128)(2,1)S(1)} %get-tuple-element.42.b_ref, f32[3,320,640]{2,1,0:T(8,128)S(1)} %get-tuple-element.43.p_ref), custom_call_target="tpu_custom_call" | custom-call | tf_op jit(solution)/shard_map/far_grads/pallas_call | solution.py:36
  11.0 39.8 %all_to_all.10.a_ref = f32[8,3,40,640]{3,2,1,0:T(8,128)S(1)} all-to-all(f32[8,3,40,640]{3,2,1,0:T(8,128)S(1)} %far_grads.1), channel_id=1, replica_groups=mesh['yl'=2,'z'=4,'x'=4,'yh'=2,'core'=2] {'x','yh'}, dimensions={0} | all-to-all | bytes 4915200 | tf_op jit(solution)/shard_map/all_to_all | solution.py:325
  51.0 34.7 %all_to_all.11.g_ref = f32[8,3,40,640]{3,2,1,0:T(8,128)S(1)} all-to-all(f32[8,3,40,640]{3,2,1,0:T(8,128)S(1)} %sum_parts.1), channel_id=1, replica_groups=mesh['yl'=2,'z'=4,'x'=4,'yh'=2,'core'=2] {'x','yh'}, dimensions={0} | all-to-all | bytes 4915200 | tf_op jit(solution)/shard_map/all_to_all | solution.py:327
  85.7 19.5 %newton.1.v_ref = bf16[3,320,640]{2,1,0:T(8,128)(2,1)S(1)} custom-call(s32[3]{0:T(128)S(1)} %pad_add_fusion.at_ref, f32[8,3,40,640]{3,2,1,0:T(8,128)S(1)} %all_to_all.11.g_ref, f32[2,320,640]{2,1,0:T(8,128)} %wg_ref.1, f32[2,320,640]{2,1,0:T(8,128)} %wu_ref.1, f32[2,320,640]{2,1,0:T(8,128)} %wd_ref.1), custom_call_target="tpu_custom_call" | custom-call | tf_op jit(solution)/shard_map/newton/pallas_call | solution.py:252
  105.2 1.4 far_query.1
  107.2 1.3 near_query.1.o_ref
  110.2 0.8 collective-permute-start.3
  111.0 0.8 fusion.2
  111.8 4.1 %collective-permute-start.6 = (f32[64,2816]{1,0:T(8,128)S(1)}, f32[64,2816]{1,0:T(8,128)S(1)}, u32[]{:S(2)}, u32[]{:S(2)}) collective-permute-start(f32[64,2816]{1,0:T(8,128)S(1)} %get-tuple-element.75), channel_id=1, source_target_pairs={{0,48},{16,0},{32,16},{48,32},{1,49},{17,1},{33,17},{49,33},{2,50}... | collective-permute-start | bytes 2162696 | tf_op jit(solution)/shard_map/ppermute | solution.py:313
  116.0 0.9 fusion.10
  116.9 9.1 %collective-permute-done.3 = f32[64,2304]{1,0:T(8,128)S(1)} collective-permute-done((f32[64,2304]{1,0:T(8,128)S(1)}, f32[64,2304]{1,0:T(8,128)S(1)}, u32[]{:S(2)}, u32[]{:S(2)}) %collective-permute-start.3) | collective-permute-done | bytes 589856 | tf_op jit(solution)/shard_map/ppermute | solution.py:309
  126.6 1.0 collective-permute-start.4
  127.6 0.8 fusion
  128.4 0.8 fusion.4
  129.2 2.5 %collective-permute-done.6 = f32[64,2816]{1,0:T(8,128)S(1)} collective-permute-done((f32[64,2816]{1,0:T(8,128)S(1)}, f32[64,2816]{1,0:T(8,128)S(1)}, u32[]{:S(2)}, u32[]{:S(2)}) %collective-permute-start.6) | collective-permute-done | bytes 720928 | tf_op jit(solution)/shard_map/ppermute | solution.py:313
  131.9 3.8 %collective-permute-start.8 = (f32[128,1408]{1,0:T(8,128)S(1)}, f32[128,1408]{1,0:T(8,128)S(1)}, u32[]{:S(2)}, u32[]{:S(2)}) collective-permute-start(f32[128,1408]{1,0:T(8,128)S(1)} %get-tuple-element.69), channel_id=1, source_target_pairs={{0,48},{16,0},{32,16},{48,32},{1,49},{17,1},{33,17},{49,33},{2,50}... | collective-permute-start | bytes 2162696 | tf_op jit(solution)/shard_map/ppermute | solution.py:313
  136.1 3.3 %collective-permute-start.10 = (f32[32,2304]{1,0:T(8,128)S(1)}, f32[32,2304]{1,0:T(8,128)S(1)}, u32[]{:S(2)}, u32[]{:S(2)}) collective-permute-start(f32[32,2304]{1,0:T(8,128)S(1)} %get-tuple-element.79), channel_id=1, source_target_pairs={{0,48},{16,0},{32,16},{48,32},{1,49},{17,1},{33,17},{49,33},{2,50}... | collective-permute-start | bytes 884744 | tf_op jit(solution)/shard_map/ppermute | solution.py:313
  139.4 0.9 fusion.8
  140.3 12.0 %collective-permute-done.8 = f32[128,1408]{1,0:T(8,128)S(1)} collective-permute-done((f32[128,1408]{1,0:T(8,128)S(1)}, f32[128,1408]{1,0:T(8,128)S(1)}, u32[]{:S(2)}, u32[]{:S(2)}) %collective-permute-start.8) | collective-permute-done | bytes 720928 | tf_op jit(solution)/shard_map/ppermute | solution.py:313
  152.3 4.0 %collective-permute-done.7 = f32[128,1408]{1,0:T(8,128)S(1)} collective-permute-done((f32[128,1408]{1,0:T(8,128)S(1)}, f32[128,1408]{1,0:T(8,128)S(1)}, u32[]{:S(2)}, u32[]{:S(2)}) %collective-permute-start.7) | collective-permute-done | bytes 720928 | tf_op jit(solution)/shard_map/ppermute | solution.py:313
  156.3 3.2 %collective-permute-start.15 = (f32[128,1408]{1,0:T(8,128)S(1)}, f32[128,1408]{1,0:T(8,128)S(1)}, u32[]{:S(2)}, u32[]{:S(2)}) collective-permute-start(f32[128,1408]{1,0:T(8,128)S(1)} %get-tuple-element.64), channel_id=1, source_target_pairs={{0,48},{16,0},{32,16},{48,32},{1,49},{17,1},{33,17},{49,33},{2,50}... | collective-permute-start | bytes 2162696 | tf_op jit(solution)/shard_map/ppermute | solution.py:313
  160.0 7.0 %collective-permute-done.4 = f32[192,2304]{1,0:T(8,128)S(1)} collective-permute-done((f32[192,2304]{1,0:T(8,128)S(1)}, f32[192,2304]{1,0:T(8,128)S(1)}, u32[]{:S(2)}, u32[]{:S(2)}) %collective-permute-start.4) | collective-permute-done | bytes 1769504 | tf_op jit(solution)/shard_map/ppermute | solution.py:309
  167.5 2.0 %collective-permute-start.11 = (f32[64,2304]{1,0:T(8,128)S(1)}, f32[64,2304]{1,0:T(8,128)S(1)}, u32[]{:S(2)}, u32[]{:S(2)}) collective-permute-start(f32[64,2304]{1,0:T(8,128)S(1)} %get-tuple-element.59), channel_id=1, source_target_pairs={{0,16},{16,32},{32,48},{48,0},{1,17},{17,33},{33,49},{49,1},{2,18}... | collective-permute-start | bytes 1769480 | tf_op jit(solution)/shard_map/ppermute | solution.py:313
  169.5 2.2 %collective-permute-start.12 = (f32[64,2304]{1,0:T(8,128)S(1)}, f32[64,2304]{1,0:T(8,128)S(1)}, u32[]{:S(2)}, u32[]{:S(2)}) collective-permute-start(f32[64,2304]{1,0:T(8,128)S(1)} %get-tuple-element.60), channel_id=1, source_target_pairs={{0,48},{16,0},{32,16},{48,32},{1,49},{17,1},{33,17},{49,33},{2,50}... | collective-permute-start | bytes 1769480 | tf_op jit(solution)/shard_map/ppermute | solution.py:313
  171.8 0.8 collective-permute-start.13
  173.0 5.1 %collective-permute-done.14 = f32[128,1408]{1,0:T(8,128)S(1)} collective-permute-done((f32[128,1408]{1,0:T(8,128)S(1)}, f32[128,1408]{1,0:T(8,128)S(1)}, u32[]{:S(2)}, u32[]{:S(2)}) %collective-permute-start.14) | collective-permute-done | bytes 720928 | tf_op jit(solution)/shard_map/ppermute | solution.py:313
  178.2 1.4 collective-permute-start.16
  179.6 3.5 %collective-permute-done.13 = f32[64,1408]{1,0:T(8,128)S(1)} collective-permute-done((f32[64,1408]{1,0:T(8,128)S(1)}, f32[64,1408]{1,0:T(8,128)S(1)}, u32[]{:S(2)}, u32[]{:S(2)}) %collective-permute-start.13) | collective-permute-done | bytes 360480 | tf_op jit(solution)/shard_map/ppermute | solution.py:309
  183.2 5.2 %collective-permute-done.16 = f32[64,1408]{1,0:T(8,128)S(1)} collective-permute-done((f32[64,1408]{1,0:T(8,128)S(1)}, f32[64,1408]{1,0:T(8,128)S(1)}, u32[]{:S(2)}, u32[]{:S(2)}) %collective-permute-start.16) | collective-permute-done | bytes 360480 | tf_op jit(solution)/shard_map/ppermute | solution.py:309
  188.9 0.9 pad_maximum_fusion.2
  (49 shorter events, 7.4 us)
Async XLA Ops:
  0.1 0.7 copy-start.1
  3.1 5.5 %collective-permute-start = (f32[512,640]{1,0:T(8,128)S(1)}, f32[512,640]{1,0:T(8,128)S(1)}, u32[]{:S(2)}, u32[]{:S(2)}) collective-permute-start(f32[512,640]{1,0:T(8,128)S(1)} %get-tuple-element.41), channel_id=1, source_target_pairs={{0,1},{1,0},{2,3},{3,2},{4,5},{5,4},{6,7},{7,6},{8,9},{9,8},{10,11... | collective-permute-start | bytes 3932168 | tf_op jit(solution)/shard_map/ppermute | solution.py:309
  3.2 4.7 %copy-start = (bf16[512,640]{1,0:T(8,128)(2,1)S(1)}, bf16[512,640]{1,0:T(8,128)(2,1)}, u32[]{:S(2)}) copy-start(bf16[512,640]{1,0:T(8,128)(2,1)} %q_ref) | copy-start | bytes 1966084
  51.0 58.6 %slice-start = ((s8[6553600]{0:T(1024)(128)(4,1)}), s8[4194304]{0:T(1024)(128)(4,1)S(1)}, s32[]{:S(2)}) async-start(s8[6553600]{0:T(1024)(128)(4,1)} %bitcast.34), calls=%async_computation.2 | async-start | bytes 8388608
  85.7 23.9 %slice-start.1 = ((s8[6553600]{0:T(1024)(128)(4,1)}), s8[2359296]{0:T(1024)(128)(4,1)S(1)}, s32[]{:S(2)}) async-start(s8[6553600]{0:T(1024)(128)(4,1)} %bitcast.34), calls=%async_computation.3 | async-start | bytes 4718592
  85.7 19.5 %collective-permute-start.1 = (f32[256,640]{1,0:T(8,128)S(1)}, f32[256,640]{1,0:T(8,128)S(1)}, u32[]{:S(2)}, u32[]{:S(2)}) collective-permute-start(f32[256,640]{1,0:T(8,128)S(1)} %get-tuple-element.47), channel_id=1, source_target_pairs={{0,1},{1,0},{2,3},{3,2},{4,5},{5,4},{6,7},{7,6},{8,9},{9,8},{10,11... | collective-permute-start | bytes 1966088 | tf_op jit(solution)/shard_map/ppermute | solution.py:309
  106.6 2.3 %collective-permute-start.2 = (f32[256,640]{1,0:T(8,128)S(1)}, f32[256,640]{1,0:T(8,128)S(1)}, u32[]{:S(2)}, u32[]{:S(2)}) collective-permute-start(f32[256,640]{1,0:T(8,128)S(1)} %far_query.1), channel_id=1, source_target_pairs={{0,1},{1,0},{2,3},{3,2},{4,5},{5,4},{6,7},{7,6},{8,9},{9,8},{10,11... | collective-permute-start | bytes 1966088 | tf_op jit(solution)/shard_map/ppermute | solution.py:309
  110.2 15.8 %collective-permute-start.3 = (f32[64,2304]{1,0:T(8,128)S(1)}, f32[64,2304]{1,0:T(8,128)S(1)}, u32[]{:S(2)}, u32[]{:S(2)}) collective-permute-start(f32[64,2304]{1,0:T(8,128)S(1)} %fusion.12), channel_id=1, source_target_pairs={{0,64},{64,0},{1,65},{65,1},{2,66},{66,2},{3,67},{67,3},{4,68},{68... | collective-permute-start | bytes 1769480 | tf_op jit(solution)/shard_map/ppermute | solution.py:309
  111.8 19.9 %collective-permute-start.6 = (f32[64,2816]{1,0:T(8,128)S(1)}, f32[64,2816]{1,0:T(8,128)S(1)}, u32[]{:S(2)}, u32[]{:S(2)}) collective-permute-start(f32[64,2816]{1,0:T(8,128)S(1)} %get-tuple-element.75), channel_id=1, source_target_pairs={{0,48},{16,0},{32,16},{48,32},{1,49},{17,1},{33,17},{49,33},{2,50}... | collective-permute-start | bytes 2162696 | tf_op jit(solution)/shard_map/ppermute | solution.py:313
  116.0 19.8 %collective-permute-start.5 = (f32[64,2816]{1,0:T(8,128)S(1)}, f32[64,2816]{1,0:T(8,128)S(1)}, u32[]{:S(2)}, u32[]{:S(2)}) collective-permute-start(f32[64,2816]{1,0:T(8,128)S(1)} %get-tuple-element.76), channel_id=1, source_target_pairs={{0,16},{16,32},{32,48},{48,0},{1,17},{17,33},{33,49},{49,1},{2,18}... | collective-permute-start | bytes 2162696 | tf_op jit(solution)/shard_map/ppermute | solution.py:313
  126.6 40.5 %collective-permute-start.4 = (f32[192,2304]{1,0:T(8,128)S(1)}, f32[192,2304]{1,0:T(8,128)S(1)}, u32[]{:S(2)}, u32[]{:S(2)}) collective-permute-start(f32[192,2304]{1,0:T(8,128)S(1)} %fusion.10), channel_id=1, source_target_pairs={{0,64},{64,0},{1,65},{65,1},{2,66},{66,2},{3,67},{67,3},{4,68},{68... | collective-permute-start | bytes 5308424 | tf_op jit(solution)/shard_map/ppermute | solution.py:309
  131.9 20.4 %collective-permute-start.8 = (f32[128,1408]{1,0:T(8,128)S(1)}, f32[128,1408]{1,0:T(8,128)S(1)}, u32[]{:S(2)}, u32[]{:S(2)}) collective-permute-start(f32[128,1408]{1,0:T(8,128)S(1)} %get-tuple-element.69), channel_id=1, source_target_pairs={{0,48},{16,0},{32,16},{48,32},{1,49},{17,1},{33,17},{49,33},{2,50}... | collective-permute-start | bytes 2162696 | tf_op jit(solution)/shard_map/ppermute | solution.py:313
  135.9 20.4 %collective-permute-start.7 = (f32[128,1408]{1,0:T(8,128)S(1)}, f32[128,1408]{1,0:T(8,128)S(1)}, u32[]{:S(2)}, u32[]{:S(2)}) collective-permute-start(f32[128,1408]{1,0:T(8,128)S(1)} %get-tuple-element.71), channel_id=1, source_target_pairs={{0,16},{16,32},{32,48},{48,0},{1,17},{17,33},{33,49},{49,1},{2,18}... | collective-permute-start | bytes 2162696 | tf_op jit(solution)/shard_map/ppermute | solution.py:313
  136.1 31.2 %collective-permute-start.10 = (f32[32,2304]{1,0:T(8,128)S(1)}, f32[32,2304]{1,0:T(8,128)S(1)}, u32[]{:S(2)}, u32[]{:S(2)}) collective-permute-start(f32[32,2304]{1,0:T(8,128)S(1)} %get-tuple-element.79), channel_id=1, source_target_pairs={{0,48},{16,0},{32,16},{48,32},{1,49},{17,1},{33,17},{49,33},{2,50}... | collective-permute-start | bytes 884744 | tf_op jit(solution)/shard_map/ppermute | solution.py:313
  139.4 28.0 %collective-permute-start.9 = (f32[32,2304]{1,0:T(8,128)S(1)}, f32[32,2304]{1,0:T(8,128)S(1)}, u32[]{:S(2)}, u32[]{:S(2)}) collective-permute-start(f32[32,2304]{1,0:T(8,128)S(1)} %get-tuple-element.80), channel_id=1, source_target_pairs={{0,16},{16,32},{32,48},{48,0},{1,17},{17,33},{33,49},{49,1},{2,18}... | collective-permute-start | bytes 884744 | tf_op jit(solution)/shard_map/ppermute | solution.py:313
  156.3 21.8 %collective-permute-start.14 = (f32[128,1408]{1,0:T(8,128)S(1)}, f32[128,1408]{1,0:T(8,128)S(1)}, u32[]{:S(2)}, u32[]{:S(2)}) collective-permute-start(f32[128,1408]{1,0:T(8,128)S(1)} %get-tuple-element.63), channel_id=1, source_target_pairs={{0,16},{16,32},{32,48},{48,0},{1,17},{17,33},{33,49},{49,1},{2,18}... | collective-permute-start | bytes 2162696 | tf_op jit(solution)/shard_map/ppermute | solution.py:313
  156.3 21.8 %collective-permute-start.15 = (f32[128,1408]{1,0:T(8,128)S(1)}, f32[128,1408]{1,0:T(8,128)S(1)}, u32[]{:S(2)}, u32[]{:S(2)}) collective-permute-start(f32[128,1408]{1,0:T(8,128)S(1)} %get-tuple-element.64), channel_id=1, source_target_pairs={{0,48},{16,0},{32,16},{48,32},{1,49},{17,1},{33,17},{49,33},{2,50}... | collective-permute-start | bytes 2162696 | tf_op jit(solution)/shard_map/ppermute | solution.py:313
  167.5 21.2 %collective-permute-start.11 = (f32[64,2304]{1,0:T(8,128)S(1)}, f32[64,2304]{1,0:T(8,128)S(1)}, u32[]{:S(2)}, u32[]{:S(2)}) collective-permute-start(f32[64,2304]{1,0:T(8,128)S(1)} %get-tuple-element.59), channel_id=1, source_target_pairs={{0,16},{16,32},{32,48},{48,0},{1,17},{17,33},{33,49},{49,1},{2,18}... | collective-permute-start | bytes 1769480 | tf_op jit(solution)/shard_map/ppermute | solution.py:313
  169.5 19.2 %collective-permute-start.12 = (f32[64,2304]{1,0:T(8,128)S(1)}, f32[64,2304]{1,0:T(8,128)S(1)}, u32[]{:S(2)}, u32[]{:S(2)}) collective-permute-start(f32[64,2304]{1,0:T(8,128)S(1)} %get-tuple-element.60), channel_id=1, source_target_pairs={{0,48},{16,0},{32,16},{48,32},{1,49},{17,1},{33,17},{49,33},{2,50}... | collective-permute-start | bytes 1769480 | tf_op jit(solution)/shard_map/ppermute | solution.py:313
  171.8 11.4 %collective-permute-start.13 = (f32[64,1408]{1,0:T(8,128)S(1)}, f32[64,1408]{1,0:T(8,128)S(1)}, u32[]{:S(2)}, u32[]{:S(2)}) collective-permute-start(f32[64,1408]{1,0:T(8,128)S(1)} %slice.139), channel_id=1, source_target_pairs={{0,64},{64,0},{1,65},{65,1},{2,66},{66,2},{3,67},{67,3},{4,68},{68... | collective-permute-start | bytes 1081352 | tf_op jit(solution)/shard_map/ppermute | solution.py:309
  178.2 10.2 %collective-permute-start.16 = (f32[64,1408]{1,0:T(8,128)S(1)}, f32[64,1408]{1,0:T(8,128)S(1)}, u32[]{:S(2)}, u32[]{:S(2)}) collective-permute-start(f32[64,1408]{1,0:T(8,128)S(1)} %slice.162), channel_id=1, source_target_pairs={{0,64},{64,0},{1,65},{65,1},{2,66},{66,2},{3,67},{67,3},{4,68},{68... | collective-permute-start | bytes 1081352 | tf_op jit(solution)/shard_map/ppermute | solution.py:309

commit v12 on v9

--- a/solution.py
+++ b/solution.py
@@ -14,6 +14,7 @@
 AXES = ("yl", "z", "x", "yh", "core")
 PLANE = ("x", "yh")
 SHARDS = 8
+PARTS = 4
 TILE = 256
 VMEM_LIMIT = 24 << 20
 CUT = 2304
@@ -144,14 +145,20 @@
 
 
 def near_grads_kernel(at_ref, k_ref, d_ref, g_ref, u_ref, w_ref, o_ref, b_ref, f_s, hk_s, dg_s, du_s, sems):
+    step = f_s.shape[1] // PARTS
     copies = [
-        pltpu.make_async_copy(ref.at[at_ref[0]], f_s.at[m], sems.at[m]) for m, ref in enumerate((g_ref, u_ref, w_ref))
+        pltpu.make_async_copy(
+            ref.at[at_ref[0], pl.ds(i * step, step)], f_s.at[m, pl.ds(i * step, step)], sems.at[PARTS * m + i]
+        )
+        for m, ref in enumerate((g_ref, u_ref, w_ref))
+        for i in range(PARTS)
     ]
     for copy in copies:
         copy.start()
-    for m, copy in enumerate(copies):
+    for n, copy in enumerate(copies):
         copy.wait()
-        b_ref[m] = f_s[m].astype(BF16)
+        rows = slice(n % PARTS * step, n % PARTS * step + step)
+        b_ref[n // PARTS, rows] = f_s[n // PARTS, rows].astype(BF16)
     for m, grad in grads_of(k_ref, d_ref, b_ref, hk_s, dg_s, du_s):
         o_ref[m] = grad
 
@@ -178,7 +185,7 @@
         out_specs=[vmem, vmem],
         scratch_shapes=[pltpu.VMEM(shape, F32)]
         + [pltpu.VMEM((k.shape[0], hidden), BF16)] * 3
-        + [pltpu.SemaphoreType.DMA((3,))],
+        + [pltpu.SemaphoreType.DMA((3 * PARTS,))],
         compiler_params=pltpu.CompilerParams(vmem_limit_bytes=VMEM_LIMIT),
         name="near_grads",
     )(at, k, d, gate, up, down)

time: 190 us -> 190 us (level)
  no operation moved by 1% of the time
where the time goes in v12:
time: 190 us
  blocking collectives  74.5 us (39%)
  waiting for transfers between devices  51 us (27%)
  Pallas kernels  33.3 us (18%)
  starting transfers between devices  21.6 us (11%)
  matrix products  6.24 us (3%)
  other arithmetic  2.36 us (1%)
    all_to_all x1, blocking collectives, plane_sum(): came = lax.all_to_all(a, PLANE, 0, 0, tiled=True)  39.8 us
    all_to_all x1, blocking collectives, plane_sum(): return lax.all_to_all(same, PLANE, 0, 0, tiled=True)  34.7 us
    ppermute x10, waiting for transfers between devices, ring(): return lax.ppermute(a, 'z', [(i, (i + shift) % 4) for i in range(4)])  28.5 us
    ppermute x7, waiting for transfers between devices, swap(): return lax.ppermute(a, axis, [(0, 1), (1, 0)])  22.6 us
    pallas_call x1, Pallas kernels, newton(): pl.pallas_call(newton_kernel, out_shape=out(shape, BF16), in_specs=[pl.Bl...  19.5 us
    ppermute x10, starting transfers between devices, ring(): return lax.ppermute(a, 'z', [(i, (i + shift) % 4) for i in range(4)])  17 us
    pallas_call x6, Pallas kernels, call(): pl.pallas_call(kernel, out_shape=outs, in_specs=specs, out_specs=jax.tree...  6.68 us
    dot_general x9, matrix products, mm(): return jnp.dot(a, b, preferred_element_type=F32)  6.24 us
  transfers between devices with their start and end apart: 17, of which 10 were waited for; matrix products, arithmetic and copies ran while one was open for 4% of the time, Pallas kernels for 14%

profile of v12, /device:TPU:0, one launch (start us, length us, event | category | flops | bytes accessed | tf_op | source)
XLA Modules:
  0.0 190.2 jit_solution(17074601968375637258)
XLA Ops:
  0.8 2.4 %sort_tokens.1 = (bf16[512,320]{1,0:T(8,128)(2,1)S(1)}, bf16[512,320]{1,0:T(8,128)(2,1)S(1)}, f32[512,640]{1,0:T(8,128)S(1)}) custom-call(s32[3]{0:T(128)S(1)} %pad_add_fusion.at_ref, f32[2,512]{1,0:T(2,128)S(1)} %bitcast.33, bf16[512,640]{1,0:T(8,128)(2,1)} %k_ref.1, bf16[512,640]{1,0:T(8,128)(2,1)} %v_ref.1), custom_call_target="tpu_custom_call" | custom-call | tf_op jit(solution)/shard_map/sort_tokens/pallas_call | solution.py:87
  3.3 4.8 %near_grads.1 = (f32[3,320,640]{2,1,0:T(8,128)S(1)}, bf16[3,320,640]{2,1,0:T(8,128)(2,1)S(1)}) custom-call(s32[3]{0:T(128)S(1)} %pad_add_fusion.at_ref, bf16[512,320]{1,0:T(8,128)(2,1)S(1)} %get-tuple-element.35.k_ref, bf16[512,320]{1,0:T(8,128)(2,1)S(1)} %get-tuple-element.36.d_ref, f32[2,320,640]{2,1,0:T(8,128)} %wg_ref.1, f32[2,320,640]{2,1,0:T(8,128)} %wu_ref.1, ...), custom_call_target="tpu_custom_call" | custom-call | tf_op jit(solution)/shard_map/near_grads/pallas_call | solution.py:181
  8.8 2.4 %far_grads.1 = f32[8,3,40,640]{3,2,1,0:T(8,128)S(1)} custom-call(f32[512,640]{1,0:T(8,128)S(1)} %collective-permute-done.came, bf16[3,320,640]{2,1,0:T(8,128)(2,1)S(1)} %get-tuple-element.42.b_ref, f32[3,320,640]{2,1,0:T(8,128)S(1)} %get-tuple-element.43.p_ref), custom_call_target="tpu_custom_call" | custom-call | tf_op jit(solution)/shard_map/far_grads/pallas_call | solution.py:37
  11.2 39.8 %all_to_all.10.a_ref = f32[8,3,40,640]{3,2,1,0:T(8,128)S(1)} all-to-all(f32[8,3,40,640]{3,2,1,0:T(8,128)S(1)} %far_grads.1), channel_id=1, replica_groups=mesh['yl'=2,'z'=4,'x'=4,'yh'=2,'core'=2] {'x','yh'}, dimensions={0} | all-to-all | bytes 4915200 | tf_op jit(solution)/shard_map/all_to_all | solution.py:332
  51.1 34.7 %all_to_all.11.g_ref = f32[8,3,40,640]{3,2,1,0:T(8,128)S(1)} all-to-all(f32[8,3,40,640]{3,2,1,0:T(8,128)S(1)} %sum_parts.1), channel_id=1, replica_groups=mesh['yl'=2,'z'=4,'x'=4,'yh'=2,'core'=2] {'x','yh'}, dimensions={0} | all-to-all | bytes 4915200 | tf_op jit(solution)/shard_map/all_to_all | solution.py:334
  85.9 19.5 %newton.1.v_ref = bf16[3,320,640]{2,1,0:T(8,128)(2,1)S(1)} custom-call(s32[3]{0:T(128)S(1)} %pad_add_fusion.at_ref, f32[8,3,40,640]{3,2,1,0:T(8,128)S(1)} %all_to_all.11.g_ref, f32[2,320,640]{2,1,0:T(8,128)} %wg_ref.1, f32[2,320,640]{2,1,0:T(8,128)} %wu_ref.1, f32[2,320,640]{2,1,0:T(8,128)} %wd_ref.1), custom_call_target="tpu_custom_call" | custom-call | tf_op jit(solution)/shard_map/newton/pallas_call | solution.py:259
  105.3 1.4 far_query.1
  107.3 1.3 near_query.1.o_ref
  110.3 0.8 collective-permute-start.3
  111.1 0.8 fusion.2
  112.0 2.0 %collective-permute-start.5 = (f32[64,2816]{1,0:T(8,128)S(1)}, f32[64,2816]{1,0:T(8,128)S(1)}, u32[]{:S(2)}, u32[]{:S(2)}) collective-permute-start(f32[64,2816]{1,0:T(8,128)S(1)} %get-tuple-element.76), channel_id=1, source_target_pairs={{0,16},{16,32},{32,48},{48,0},{1,17},{17,33},{33,49},{49,1},{2,18}... | collective-permute-start | bytes 2162696 | tf_op jit(solution)/shard_map/ppermute | solution.py:320
  114.0 2.2 %collective-permute-start.7 = (f32[64,2816]{1,0:T(8,128)S(1)}, f32[64,2816]{1,0:T(8,128)S(1)}, u32[]{:S(2)}, u32[]{:S(2)}) collective-permute-start(f32[64,2816]{1,0:T(8,128)S(1)} %get-tuple-element.75), channel_id=1, source_target_pairs={{0,48},{16,0},{32,16},{48,32},{1,49},{17,1},{33,17},{49,33},{2,50}... | collective-permute-start | bytes 2162696 | tf_op jit(solution)/shard_map/ppermute | solution.py:320
  116.2 0.9 fusion.10
  117.1 9.1 %collective-permute-done.3 = f32[64,2304]{1,0:T(8,128)S(1)} collective-permute-done((f32[64,2304]{1,0:T(8,128)S(1)}, f32[64,2304]{1,0:T(8,128)S(1)}, u32[]{:S(2)}, u32[]{:S(2)}) %collective-permute-start.3) | collective-permute-done | bytes 589856 | tf_op jit(solution)/shard_map/ppermute | solution.py:316
  126.7 1.0 collective-permute-start.4
  127.8 0.8 fusion.4
  128.6 0.8 fusion
  129.4 3.2 %collective-permute-done.5 = f32[64,2816]{1,0:T(8,128)S(1)} collective-permute-done((f32[64,2816]{1,0:T(8,128)S(1)}, f32[64,2816]{1,0:T(8,128)S(1)}, u32[]{:S(2)}, u32[]{:S(2)}) %collective-permute-start.5) | collective-permute-done | bytes 720928 | tf_op jit(solution)/shard_map/ppermute | solution.py:320
  133.1 1.1 collective-permute-start.6
  134.3 2.2 %collective-permute-start.8 = (f32[128,1408]{1,0:T(8,128)S(1)}, f32[128,1408]{1,0:T(8,128)S(1)}, u32[]{:S(2)}, u32[]{:S(2)}) collective-permute-start(f32[128,1408]{1,0:T(8,128)S(1)} %get-tuple-element.70), channel_id=1, source_target_pairs={{0,48},{16,0},{32,16},{48,32},{1,49},{17,1},{33,17},{49,33},{2,50}... | collective-permute-start | bytes 2162696 | tf_op jit(solution)/shard_map/ppermute | solution.py:320
  136.5 1.7 collective-permute-start.10
  138.6 0.9 fusion.8
  139.5 18.3 %collective-permute-done.10 = f32[32,2304]{1,0:T(8,128)S(1)} collective-permute-done((f32[32,2304]{1,0:T(8,128)S(1)}, f32[32,2304]{1,0:T(8,128)S(1)}, u32[]{:S(2)}, u32[]{:S(2)}) %collective-permute-start.10) | collective-permute-done | bytes 294944 | tf_op jit(solution)/shard_map/ppermute | solution.py:320
  159.2 2.5 %collective-permute-start.15 = (f32[128,1408]{1,0:T(8,128)S(1)}, f32[128,1408]{1,0:T(8,128)S(1)}, u32[]{:S(2)}, u32[]{:S(2)}) collective-permute-start(f32[128,1408]{1,0:T(8,128)S(1)} %get-tuple-element.64), channel_id=1, source_target_pairs={{0,48},{16,0},{32,16},{48,32},{1,49},{17,1},{33,17},{49,33},{2,50}... | collective-permute-start | bytes 2162696 | tf_op jit(solution)/shard_map/ppermute | solution.py:320
  162.2 5.0 %collective-permute-done.4 = f32[192,2304]{1,0:T(8,128)S(1)} collective-permute-done((f32[192,2304]{1,0:T(8,128)S(1)}, f32[192,2304]{1,0:T(8,128)S(1)}, u32[]{:S(2)}, u32[]{:S(2)}) %collective-permute-start.4) | collective-permute-done | bytes 1769504 | tf_op jit(solution)/shard_map/ppermute | solution.py:316
  167.7 2.0 %collective-permute-start.11 = (f32[64,2304]{1,0:T(8,128)S(1)}, f32[64,2304]{1,0:T(8,128)S(1)}, u32[]{:S(2)}, u32[]{:S(2)}) collective-permute-start(f32[64,2304]{1,0:T(8,128)S(1)} %pad_maximum_fusion.3), channel_id=1, source_target_pairs={{0,16},{16,32},{32,48},{48,0},{1,17},{17,33},{33,49},{49,1},{2,18}... | collective-permute-start | bytes 1769480 | tf_op jit(solution)/shard_map/ppermute | solution.py:320
  169.7 2.2 %collective-permute-start.12 = (f32[64,2304]{1,0:T(8,128)S(1)}, f32[64,2304]{1,0:T(8,128)S(1)}, u32[]{:S(2)}, u32[]{:S(2)}) collective-permute-start(f32[64,2304]{1,0:T(8,128)S(1)} %pad_maximum_fusion.4), channel_id=1, source_target_pairs={{0,48},{16,0},{32,16},{48,32},{1,49},{17,1},{33,17},{49,33},{2,50}... | collective-permute-start | bytes 1769480 | tf_op jit(solution)/shard_map/ppermute | solution.py:320
  173.1 5.6 %collective-permute-done.14 = f32[128,1408]{1,0:T(8,128)S(1)} collective-permute-done((f32[128,1408]{1,0:T(8,128)S(1)}, f32[128,1408]{1,0:T(8,128)S(1)}, u32[]{:S(2)}, u32[]{:S(2)}) %collective-permute-start.14) | collective-permute-done | bytes 720928 | tf_op jit(solution)/shard_map/ppermute | solution.py:320
  179.0 1.4 collective-permute-start.16
  180.4 2.9 %collective-permute-done.13 = f32[64,1408]{1,0:T(8,128)S(1)} collective-permute-done((f32[64,1408]{1,0:T(8,128)S(1)}, f32[64,1408]{1,0:T(8,128)S(1)}, u32[]{:S(2)}, u32[]{:S(2)}) %collective-permute-start.13) | collective-permute-done | bytes 360480 | tf_op jit(solution)/shard_map/ppermute | solution.py:316
  183.3 5.2 %collective-permute-done.16 = f32[64,1408]{1,0:T(8,128)S(1)} collective-permute-done((f32[64,1408]{1,0:T(8,128)S(1)}, f32[64,1408]{1,0:T(8,128)S(1)}, u32[]{:S(2)}, u32[]{:S(2)}) %collective-permute-start.16) | collective-permute-done | bytes 360480 | tf_op jit(solution)/shard_map/ppermute | solution.py:316
  189.3 0.9 pad_maximum_fusion.2
  (49 shorter events, 10.3 us)
Async XLA Ops:
  0.1 0.7 copy-start.1
  3.1 5.6 %collective-permute-start = (f32[512,640]{1,0:T(8,128)S(1)}, f32[512,640]{1,0:T(8,128)S(1)}, u32[]{:S(2)}, u32[]{:S(2)}) collective-permute-start(f32[512,640]{1,0:T(8,128)S(1)} %get-tuple-element.41), channel_id=1, source_target_pairs={{0,1},{1,0},{2,3},{3,2},{4,5},{5,4},{6,7},{7,6},{8,9},{9,8},{10,11... | collective-permute-start | bytes 3932168 | tf_op jit(solution)/shard_map/ppermute | solution.py:316
  3.2 4.8 %copy-start = (bf16[512,640]{1,0:T(8,128)(2,1)S(1)}, bf16[512,640]{1,0:T(8,128)(2,1)}, u32[]{:S(2)}) copy-start(bf16[512,640]{1,0:T(8,128)(2,1)} %q_ref) | copy-start | bytes 1966084
  51.1 58.6 %slice-start = ((s8[6553600]{0:T(1024)(128)(4,1)}), s8[4194304]{0:T(1024)(128)(4,1)S(1)}, s32[]{:S(2)}) async-start(s8[6553600]{0:T(1024)(128)(4,1)} %bitcast.34), calls=%async_computation.2 | async-start | bytes 8388608
  85.9 23.9 %slice-start.1 = ((s8[6553600]{0:T(1024)(128)(4,1)}), s8[2359296]{0:T(1024)(128)(4,1)S(1)}, s32[]{:S(2)}) async-start(s8[6553600]{0:T(1024)(128)(4,1)} %bitcast.34), calls=%async_computation.3 | async-start | bytes 4718592
  85.9 19.5 %collective-permute-start.1 = (f32[256,640]{1,0:T(8,128)S(1)}, f32[256,640]{1,0:T(8,128)S(1)}, u32[]{:S(2)}, u32[]{:S(2)}) collective-permute-start(f32[256,640]{1,0:T(8,128)S(1)} %get-tuple-element.47), channel_id=1, source_target_pairs={{0,1},{1,0},{2,3},{3,2},{4,5},{5,4},{6,7},{7,6},{8,9},{9,8},{10,11... | collective-permute-start | bytes 1966088 | tf_op jit(solution)/shard_map/ppermute | solution.py:316
  106.7 2.3 %collective-permute-start.2 = (f32[256,640]{1,0:T(8,128)S(1)}, f32[256,640]{1,0:T(8,128)S(1)}, u32[]{:S(2)}, u32[]{:S(2)}) collective-permute-start(f32[256,640]{1,0:T(8,128)S(1)} %far_query.1), channel_id=1, source_target_pairs={{0,1},{1,0},{2,3},{3,2},{4,5},{5,4},{6,7},{7,6},{8,9},{9,8},{10,11... | collective-permute-start | bytes 1966088 | tf_op jit(solution)/shard_map/ppermute | solution.py:316
  110.3 15.8 %collective-permute-start.3 = (f32[64,2304]{1,0:T(8,128)S(1)}, f32[64,2304]{1,0:T(8,128)S(1)}, u32[]{:S(2)}, u32[]{:S(2)}) collective-permute-start(f32[64,2304]{1,0:T(8,128)S(1)} %fusion.12), channel_id=1, source_target_pairs={{0,64},{64,0},{1,65},{65,1},{2,66},{66,2},{3,67},{67,3},{4,68},{68... | collective-permute-start | bytes 1769480 | tf_op jit(solution)/shard_map/ppermute | solution.py:316
  112.0 20.6 %collective-permute-start.5 = (f32[64,2816]{1,0:T(8,128)S(1)}, f32[64,2816]{1,0:T(8,128)S(1)}, u32[]{:S(2)}, u32[]{:S(2)}) collective-permute-start(f32[64,2816]{1,0:T(8,128)S(1)} %get-tuple-element.76), channel_id=1, source_target_pairs={{0,16},{16,32},{32,48},{48,0},{1,17},{17,33},{33,49},{49,1},{2,18}... | collective-permute-start | bytes 2162696 | tf_op jit(solution)/shard_map/ppermute | solution.py:320
  114.0 18.8 %collective-permute-start.7 = (f32[64,2816]{1,0:T(8,128)S(1)}, f32[64,2816]{1,0:T(8,128)S(1)}, u32[]{:S(2)}, u32[]{:S(2)}) collective-permute-start(f32[64,2816]{1,0:T(8,128)S(1)} %get-tuple-element.75), channel_id=1, source_target_pairs={{0,48},{16,0},{32,16},{48,32},{1,49},{17,1},{33,17},{49,33},{2,50}... | collective-permute-start | bytes 2162696 | tf_op jit(solution)/shard_map/ppermute | solution.py:320
  126.7 40.5 %collective-permute-start.4 = (f32[192,2304]{1,0:T(8,128)S(1)}, f32[192,2304]{1,0:T(8,128)S(1)}, u32[]{:S(2)}, u32[]{:S(2)}) collective-permute-start(f32[192,2304]{1,0:T(8,128)S(1)} %fusion.10), channel_id=1, source_target_pairs={{0,64},{64,0},{1,65},{65,1},{2,66},{66,2},{3,67},{67,3},{4,68},{68... | collective-permute-start | bytes 5308424 | tf_op jit(solution)/shard_map/ppermute | solution.py:316
  133.1 28.6 %collective-permute-start.6 = (f32[128,1408]{1,0:T(8,128)S(1)}, f32[128,1408]{1,0:T(8,128)S(1)}, u32[]{:S(2)}, u32[]{:S(2)}) collective-permute-start(f32[128,1408]{1,0:T(8,128)S(1)} %get-tuple-element.81), channel_id=1, source_target_pairs={{0,16},{16,32},{32,48},{48,0},{1,17},{17,33},{33,49},{49,1},{2,18}... | collective-permute-start | bytes 2162696 | tf_op jit(solution)/shard_map/ppermute | solution.py:320
  134.3 27.5 %collective-permute-start.8 = (f32[128,1408]{1,0:T(8,128)S(1)}, f32[128,1408]{1,0:T(8,128)S(1)}, u32[]{:S(2)}, u32[]{:S(2)}) collective-permute-start(f32[128,1408]{1,0:T(8,128)S(1)} %get-tuple-element.70), channel_id=1, source_target_pairs={{0,48},{16,0},{32,16},{48,32},{1,49},{17,1},{33,17},{49,33},{2,50}... | collective-permute-start | bytes 2162696 | tf_op jit(solution)/shard_map/ppermute | solution.py:320
  136.5 21.3 %collective-permute-start.10 = (f32[32,2304]{1,0:T(8,128)S(1)}, f32[32,2304]{1,0:T(8,128)S(1)}, u32[]{:S(2)}, u32[]{:S(2)}) collective-permute-start(f32[32,2304]{1,0:T(8,128)S(1)} %get-tuple-element.79), channel_id=1, source_target_pairs={{0,48},{16,0},{32,16},{48,32},{1,49},{17,1},{33,17},{49,33},{2,50}... | collective-permute-start | bytes 884744 | tf_op jit(solution)/shard_map/ppermute | solution.py:320
  138.2 20.3 %collective-permute-start.9 = (f32[32,2304]{1,0:T(8,128)S(1)}, f32[32,2304]{1,0:T(8,128)S(1)}, u32[]{:S(2)}, u32[]{:S(2)}) collective-permute-start(f32[32,2304]{1,0:T(8,128)S(1)} %get-tuple-element.80), channel_id=1, source_target_pairs={{0,16},{16,32},{32,48},{48,0},{1,17},{17,33},{33,49},{49,1},{2,18}... | collective-permute-start | bytes 884744 | tf_op jit(solution)/shard_map/ppermute | solution.py:320
  158.5 20.3 %collective-permute-start.14 = (f32[128,1408]{1,0:T(8,128)S(1)}, f32[128,1408]{1,0:T(8,128)S(1)}, u32[]{:S(2)}, u32[]{:S(2)}) collective-permute-start(f32[128,1408]{1,0:T(8,128)S(1)} %get-tuple-element.63), channel_id=1, source_target_pairs={{0,16},{16,32},{32,48},{48,0},{1,17},{17,33},{33,49},{49,1},{2,18}... | collective-permute-start | bytes 2162696 | tf_op jit(solution)/shard_map/ppermute | solution.py:320
  159.2 19.6 %collective-permute-start.15 = (f32[128,1408]{1,0:T(8,128)S(1)}, f32[128,1408]{1,0:T(8,128)S(1)}, u32[]{:S(2)}, u32[]{:S(2)}) collective-permute-start(f32[128,1408]{1,0:T(8,128)S(1)} %get-tuple-element.64), channel_id=1, source_target_pairs={{0,48},{16,0},{32,16},{48,32},{1,49},{17,1},{33,17},{49,33},{2,50}... | collective-permute-start | bytes 2162696 | tf_op jit(solution)/shard_map/ppermute | solution.py:320
  167.7 21.5 %collective-permute-start.11 = (f32[64,2304]{1,0:T(8,128)S(1)}, f32[64,2304]{1,0:T(8,128)S(1)}, u32[]{:S(2)}, u32[]{:S(2)}) collective-permute-start(f32[64,2304]{1,0:T(8,128)S(1)} %pad_maximum_fusion.3), channel_id=1, source_target_pairs={{0,16},{16,32},{32,48},{48,0},{1,17},{17,33},{33,49},{49,1},{2,18}... | collective-permute-start | bytes 1769480 | tf_op jit(solution)/shard_map/ppermute | solution.py:320
  169.7 19.5 %collective-permute-start.12 = (f32[64,2304]{1,0:T(8,128)S(1)}, f32[64,2304]{1,0:T(8,128)S(1)}, u32[]{:S(2)}, u32[]{:S(2)}) collective-permute-start(f32[64,2304]{1,0:T(8,128)S(1)} %pad_maximum_fusion.4), channel_id=1, source_target_pairs={{0,48},{16,0},{32,16},{48,32},{1,49},{17,1},{33,17},{49,33},{2,50}... | collective-permute-start | bytes 1769480 | tf_op jit(solution)/shard_map/ppermute | solution.py:320
  171.9 11.4 %collective-permute-start.13 = (f32[64,1408]{1,0:T(8,128)S(1)}, f32[64,1408]{1,0:T(8,128)S(1)}, u32[]{:S(2)}, u32[]{:S(2)}) collective-permute-start(f32[64,1408]{1,0:T(8,128)S(1)} %slice.139), channel_id=1, source_target_pairs={{0,64},{64,0},{1,65},{65,1},{2,66},{66,2},{3,67},{67,3},{4,68},{68... | collective-permute-start | bytes 1081352 | tf_op jit(solution)/shard_map/ppermute | solution.py:316
  179.0 9.6 %collective-permute-start.16 = (f32[64,1408]{1,0:T(8,128)S(1)}, f32[64,1408]{1,0:T(8,128)S(1)}, u32[]{:S(2)}, u32[]{:S(2)}) collective-permute-start(f32[64,1408]{1,0:T(8,128)S(1)} %slice.162), channel_id=1, source_target_pairs={{0,64},{64,0},{1,65},{65,1},{2,66},{66,2},{3,67},{67,3},{4,68},{68... | collective-permute-start | bytes 1081352 | tf_op jit(solution)/shard_map/ppermute | solution.py:316

commit v13 on v9

--- a/solution.py
+++ b/solution.py
@@ -122,16 +122,16 @@
     return call(sort_queries_kernel, "sort_queries", shapes, [], at, queries)
 
 
-def grads_of(k_ref, d_ref, w_ref, hk_s, dg_s, du_s):
-    rows = k_ref.shape[0]
-    wg, wu, wd = w_ref[0], w_ref[1], w_ref[2]
-    step = 256
-    for t in range(0, rows, step):
-        at = slice(t, t + step)
-        k = k_ref[at, :]
-        gate = mm(k, wg)
-        upper = mm(k, wu)
-        dhid = mm(d_ref[at, :], wd)
+def grads_of(k_ref, d_ref, w_ref, hk_s, dg_s, du_s, ready=lambda m: None):
+    rows, step = k_ref.shape[0], 256
+    chunks = [slice(t, t + step) for t in range(0, rows, step)]
+    ready(0)
+    gates = [mm(k_ref[at, :], w_ref[0]) for at in chunks]
+    ready(1)
+    uppers = [mm(k_ref[at, :], w_ref[1]) for at in chunks]
+    ready(2)
+    for at, gate, upper in zip(chunks, gates, uppers):
+        dhid = mm(d_ref[at, :], w_ref[2])
         sig = jax.nn.sigmoid(gate)
         act = gate * sig
         hk_s[at, :] = (act * upper).astype(BF16)
@@ -149,10 +149,12 @@
     ]
     for copy in copies:
         copy.start()
-    for m, copy in enumerate(copies):
-        copy.wait()
+
+    def ready(m):
+        copies[m].wait()
         b_ref[m] = f_s[m].astype(BF16)
-    for m, grad in grads_of(k_ref, d_ref, b_ref, hk_s, dg_s, du_s):
+
+    for m, grad in grads_of(k_ref, d_ref, b_ref, hk_s, dg_s, du_s, ready):
         o_ref[m] = grad
 
 

time: 190 us -> 190 us (level)
  no operation moved by 1% of the time
where the time goes in v13:
time: 190 us
  blocking collectives  74.5 us (39%)
  waiting for transfers between devices  51 us (27%)
  Pallas kernels  33.1 us (17%)
  starting transfers between devices  21.6 us (11%)
  matrix products  6.23 us (3%)
  other arithmetic  2.36 us (1%)
    all_to_all x1, blocking collectives, plane_sum(): came = lax.all_to_all(a, PLANE, 0, 0, tiled=True)  39.8 us
    all_to_all x1, blocking collectives, plane_sum(): return lax.all_to_all(same, PLANE, 0, 0, tiled=True)  34.7 us
    ppermute x10, waiting for transfers between devices, ring(): return lax.ppermute(a, 'z', [(i, (i + shift) % 4) for i in range(4)])  28.5 us
    ppermute x7, waiting for transfers between devices, swap(): return lax.ppermute(a, axis, [(0, 1), (1, 0)])  22.6 us
    pallas_call x1, Pallas kernels, newton(): pl.pallas_call(newton_kernel, out_shape=out(shape, BF16), in_specs=[pl.Bl...  19.5 us
    ppermute x10, starting transfers between devices, ring(): return lax.ppermute(a, 'z', [(i, (i + shift) % 4) for i in range(4)])  17 us
    pallas_call x6, Pallas kernels, call(): pl.pallas_call(kernel, out_shape=outs, in_specs=specs, out_specs=jax.tree...  6.7 us
    dot_general x9, matrix products, mm(): return jnp.dot(a, b, preferred_element_type=F32)  6.23 us
  transfers between devices with their start and end apart: 17, of which 10 were waited for; matrix products, arithmetic and copies ran while one was open for 4% of the time, Pallas kernels for 14%

profile of v13, /device:TPU:0, one launch (start us, length us, event | category | flops | bytes accessed | tf_op | source)
XLA Modules:
  0.0 190.0 jit_solution(16277558560467976665)
XLA Ops:
  0.8 2.4 %sort_tokens.1 = (bf16[512,320]{1,0:T(8,128)(2,1)S(1)}, bf16[512,320]{1,0:T(8,128)(2,1)S(1)}, f32[512,640]{1,0:T(8,128)S(1)}) custom-call(s32[3]{0:T(128)S(1)} %pad_add_fusion.at_ref, f32[2,512]{1,0:T(2,128)S(1)} %bitcast.33, bf16[512,640]{1,0:T(8,128)(2,1)} %k_ref.1, bf16[512,640]{1,0:T(8,128)(2,1)} %v_ref.1), custom_call_target="tpu_custom_call" | custom-call | tf_op jit(solution)/shard_map/sort_tokens/pallas_call | solution.py:86
  3.3 4.6 %near_grads.1 = (f32[3,320,640]{2,1,0:T(8,128)S(1)}, bf16[3,320,640]{2,1,0:T(8,128)(2,1)S(1)}) custom-call(s32[3]{0:T(128)S(1)} %pad_add_fusion.at_ref, bf16[512,320]{1,0:T(8,128)(2,1)S(1)} %get-tuple-element.35.k_ref, bf16[512,320]{1,0:T(8,128)(2,1)S(1)} %get-tuple-element.36.d_ref, f32[2,320,640]{2,1,0:T(8,128)} %wg_ref.1, f32[2,320,640]{2,1,0:T(8,128)} %wu_ref.1, ...), custom_call_target="tpu_custom_call" | custom-call | tf_op jit(solution)/shard_map/near_grads/pallas_call | solution.py:176
  8.6 2.4 %far_grads.1 = f32[8,3,40,640]{3,2,1,0:T(8,128)S(1)} custom-call(f32[512,640]{1,0:T(8,128)S(1)} %collective-permute-done.came, bf16[3,320,640]{2,1,0:T(8,128)(2,1)S(1)} %get-tuple-element.42.b_ref, f32[3,320,640]{2,1,0:T(8,128)S(1)} %get-tuple-element.43.p_ref), custom_call_target="tpu_custom_call" | custom-call | tf_op jit(solution)/shard_map/far_grads/pallas_call | solution.py:36
  11.0 39.8 %all_to_all.10.a_ref = f32[8,3,40,640]{3,2,1,0:T(8,128)S(1)} all-to-all(f32[8,3,40,640]{3,2,1,0:T(8,128)S(1)} %far_grads.1), channel_id=1, replica_groups=mesh['yl'=2,'z'=4,'x'=4,'yh'=2,'core'=2] {'x','yh'}, dimensions={0} | all-to-all | bytes 4915200 | tf_op jit(solution)/shard_map/all_to_all | solution.py:327
  51.0 34.7 %all_to_all.11.g_ref = f32[8,3,40,640]{3,2,1,0:T(8,128)S(1)} all-to-all(f32[8,3,40,640]{3,2,1,0:T(8,128)S(1)} %sum_parts.1), channel_id=1, replica_groups=mesh['yl'=2,'z'=4,'x'=4,'yh'=2,'core'=2] {'x','yh'}, dimensions={0} | all-to-all | bytes 4915200 | tf_op jit(solution)/shard_map/all_to_all | solution.py:329
  85.7 19.5 %newton.1.v_ref = bf16[3,320,640]{2,1,0:T(8,128)(2,1)S(1)} custom-call(s32[3]{0:T(128)S(1)} %pad_add_fusion.at_ref, f32[8,3,40,640]{3,2,1,0:T(8,128)S(1)} %all_to_all.11.g_ref, f32[2,320,640]{2,1,0:T(8,128)} %wg_ref.1, f32[2,320,640]{2,1,0:T(8,128)} %wu_ref.1, f32[2,320,640]{2,1,0:T(8,128)} %wd_ref.1), custom_call_target="tpu_custom_call" | custom-call | tf_op jit(solution)/shard_map/newton/pallas_call | solution.py:254
  105.1 1.4 far_query.1
  107.1 1.3 near_query.1.o_ref
  110.2 0.8 collective-permute-start.3
  110.9 0.8 fusion.2
  111.8 2.0 %collective-permute-start.5 = (f32[64,2816]{1,0:T(8,128)S(1)}, f32[64,2816]{1,0:T(8,128)S(1)}, u32[]{:S(2)}, u32[]{:S(2)}) collective-permute-start(f32[64,2816]{1,0:T(8,128)S(1)} %get-tuple-element.76), channel_id=1, source_target_pairs={{0,16},{16,32},{32,48},{48,0},{1,17},{17,33},{33,49},{49,1},{2,18}... | collective-permute-start | bytes 2162696 | tf_op jit(solution)/shard_map/ppermute | solution.py:315
  113.8 2.2 %collective-permute-start.7 = (f32[64,2816]{1,0:T(8,128)S(1)}, f32[64,2816]{1,0:T(8,128)S(1)}, u32[]{:S(2)}, u32[]{:S(2)}) collective-permute-start(f32[64,2816]{1,0:T(8,128)S(1)} %get-tuple-element.75), channel_id=1, source_target_pairs={{0,48},{16,0},{32,16},{48,32},{1,49},{17,1},{33,17},{49,33},{2,50}... | collective-permute-start | bytes 2162696 | tf_op jit(solution)/shard_map/ppermute | solution.py:315
  116.0 0.9 fusion.10
  116.9 9.1 %collective-permute-done.3 = f32[64,2304]{1,0:T(8,128)S(1)} collective-permute-done((f32[64,2304]{1,0:T(8,128)S(1)}, f32[64,2304]{1,0:T(8,128)S(1)}, u32[]{:S(2)}, u32[]{:S(2)}) %collective-permute-start.3) | collective-permute-done | bytes 589856 | tf_op jit(solution)/shard_map/ppermute | solution.py:311
  126.5 1.0 collective-permute-start.4
  127.6 0.8 fusion.4
  128.4 0.8 fusion
  129.2 3.2 %collective-permute-done.5 = f32[64,2816]{1,0:T(8,128)S(1)} collective-permute-done((f32[64,2816]{1,0:T(8,128)S(1)}, f32[64,2816]{1,0:T(8,128)S(1)}, u32[]{:S(2)}, u32[]{:S(2)}) %collective-permute-start.5) | collective-permute-done | bytes 720928 | tf_op jit(solution)/shard_map/ppermute | solution.py:315
  132.9 1.1 collective-permute-start.6
  134.1 2.2 %collective-permute-start.8 = (f32[128,1408]{1,0:T(8,128)S(1)}, f32[128,1408]{1,0:T(8,128)S(1)}, u32[]{:S(2)}, u32[]{:S(2)}) collective-permute-start(f32[128,1408]{1,0:T(8,128)S(1)} %get-tuple-element.70), channel_id=1, source_target_pairs={{0,48},{16,0},{32,16},{48,32},{1,49},{17,1},{33,17},{49,33},{2,50}... | collective-permute-start | bytes 2162696 | tf_op jit(solution)/shard_map/ppermute | solution.py:315
  136.3 1.7 collective-permute-start.10
  138.4 0.9 fusion.8
  139.3 18.3 %collective-permute-done.10 = f32[32,2304]{1,0:T(8,128)S(1)} collective-permute-done((f32[32,2304]{1,0:T(8,128)S(1)}, f32[32,2304]{1,0:T(8,128)S(1)}, u32[]{:S(2)}, u32[]{:S(2)}) %collective-permute-start.10) | collective-permute-done | bytes 294944 | tf_op jit(solution)/shard_map/ppermute | solution.py:315
  159.0 2.5 %collective-permute-start.15 = (f32[128,1408]{1,0:T(8,128)S(1)}, f32[128,1408]{1,0:T(8,128)S(1)}, u32[]{:S(2)}, u32[]{:S(2)}) collective-permute-start(f32[128,1408]{1,0:T(8,128)S(1)} %get-tuple-element.64), channel_id=1, source_target_pairs={{0,48},{16,0},{32,16},{48,32},{1,49},{17,1},{33,17},{49,33},{2,50}... | collective-permute-start | bytes 2162696 | tf_op jit(solution)/shard_map/ppermute | solution.py:315
  162.1 5.0 %collective-permute-done.4 = f32[192,2304]{1,0:T(8,128)S(1)} collective-permute-done((f32[192,2304]{1,0:T(8,128)S(1)}, f32[192,2304]{1,0:T(8,128)S(1)}, u32[]{:S(2)}, u32[]{:S(2)}) %collective-permute-start.4) | collective-permute-done | bytes 1769504 | tf_op jit(solution)/shard_map/ppermute | solution.py:311
  167.5 2.0 %collective-permute-start.11 = (f32[64,2304]{1,0:T(8,128)S(1)}, f32[64,2304]{1,0:T(8,128)S(1)}, u32[]{:S(2)}, u32[]{:S(2)}) collective-permute-start(f32[64,2304]{1,0:T(8,128)S(1)} %pad_maximum_fusion.3), channel_id=1, source_target_pairs={{0,16},{16,32},{32,48},{48,0},{1,17},{17,33},{33,49},{49,1},{2,18}... | collective-permute-start | bytes 1769480 | tf_op jit(solution)/shard_map/ppermute | solution.py:315
  169.5 2.2 %collective-permute-start.12 = (f32[64,2304]{1,0:T(8,128)S(1)}, f32[64,2304]{1,0:T(8,128)S(1)}, u32[]{:S(2)}, u32[]{:S(2)}) collective-permute-start(f32[64,2304]{1,0:T(8,128)S(1)} %pad_maximum_fusion.4), channel_id=1, source_target_pairs={{0,48},{16,0},{32,16},{48,32},{1,49},{17,1},{33,17},{49,33},{2,50}... | collective-permute-start | bytes 1769480 | tf_op jit(solution)/shard_map/ppermute | solution.py:315
  172.9 5.6 %collective-permute-done.14 = f32[128,1408]{1,0:T(8,128)S(1)} collective-permute-done((f32[128,1408]{1,0:T(8,128)S(1)}, f32[128,1408]{1,0:T(8,128)S(1)}, u32[]{:S(2)}, u32[]{:S(2)}) %collective-permute-start.14) | collective-permute-done | bytes 720928 | tf_op jit(solution)/shard_map/ppermute | solution.py:315
  178.8 1.4 collective-permute-start.16
  180.2 2.9 %collective-permute-done.13 = f32[64,1408]{1,0:T(8,128)S(1)} collective-permute-done((f32[64,1408]{1,0:T(8,128)S(1)}, f32[64,1408]{1,0:T(8,128)S(1)}, u32[]{:S(2)}, u32[]{:S(2)}) %collective-permute-start.13) | collective-permute-done | bytes 360480 | tf_op jit(solution)/shard_map/ppermute | solution.py:311
  183.2 5.2 %collective-permute-done.16 = f32[64,1408]{1,0:T(8,128)S(1)} collective-permute-done((f32[64,1408]{1,0:T(8,128)S(1)}, f32[64,1408]{1,0:T(8,128)S(1)}, u32[]{:S(2)}, u32[]{:S(2)}) %collective-permute-start.16) | collective-permute-done | bytes 360480 | tf_op jit(solution)/shard_map/ppermute | solution.py:311
  189.1 0.9 pad_maximum_fusion.2
  (49 shorter events, 10.3 us)
Async XLA Ops:
  0.1 0.7 copy-start.1
  3.1 5.4 %collective-permute-start = (f32[512,640]{1,0:T(8,128)S(1)}, f32[512,640]{1,0:T(8,128)S(1)}, u32[]{:S(2)}, u32[]{:S(2)}) collective-permute-start(f32[512,640]{1,0:T(8,128)S(1)} %get-tuple-element.41), channel_id=1, source_target_pairs={{0,1},{1,0},{2,3},{3,2},{4,5},{5,4},{6,7},{7,6},{8,9},{9,8},{10,11... | collective-permute-start | bytes 3932168 | tf_op jit(solution)/shard_map/ppermute | solution.py:311
  3.2 4.6 %copy-start = (bf16[512,640]{1,0:T(8,128)(2,1)S(1)}, bf16[512,640]{1,0:T(8,128)(2,1)}, u32[]{:S(2)}) copy-start(bf16[512,640]{1,0:T(8,128)(2,1)} %q_ref) | copy-start | bytes 1966084
  50.9 58.6 %slice-start = ((s8[6553600]{0:T(1024)(128)(4,1)}), s8[4194304]{0:T(1024)(128)(4,1)S(1)}, s32[]{:S(2)}) async-start(s8[6553600]{0:T(1024)(128)(4,1)} %bitcast.34), calls=%async_computation.2 | async-start | bytes 8388608
  85.7 23.9 %slice-start.1 = ((s8[6553600]{0:T(1024)(128)(4,1)}), s8[2359296]{0:T(1024)(128)(4,1)S(1)}, s32[]{:S(2)}) async-start(s8[6553600]{0:T(1024)(128)(4,1)} %bitcast.34), calls=%async_computation.3 | async-start | bytes 4718592
  85.7 19.5 %collective-permute-start.1 = (f32[256,640]{1,0:T(8,128)S(1)}, f32[256,640]{1,0:T(8,128)S(1)}, u32[]{:S(2)}, u32[]{:S(2)}) collective-permute-start(f32[256,640]{1,0:T(8,128)S(1)} %get-tuple-element.47), channel_id=1, source_target_pairs={{0,1},{1,0},{2,3},{3,2},{4,5},{5,4},{6,7},{7,6},{8,9},{9,8},{10,11... | collective-permute-start | bytes 1966088 | tf_op jit(solution)/shard_map/ppermute | solution.py:311
  106.5 2.3 %collective-permute-start.2 = (f32[256,640]{1,0:T(8,128)S(1)}, f32[256,640]{1,0:T(8,128)S(1)}, u32[]{:S(2)}, u32[]{:S(2)}) collective-permute-start(f32[256,640]{1,0:T(8,128)S(1)} %far_query.1), channel_id=1, source_target_pairs={{0,1},{1,0},{2,3},{3,2},{4,5},{5,4},{6,7},{7,6},{8,9},{9,8},{10,11... | collective-permute-start | bytes 1966088 | tf_op jit(solution)/shard_map/ppermute | solution.py:311
  110.2 15.8 %collective-permute-start.3 = (f32[64,2304]{1,0:T(8,128)S(1)}, f32[64,2304]{1,0:T(8,128)S(1)}, u32[]{:S(2)}, u32[]{:S(2)}) collective-permute-start(f32[64,2304]{1,0:T(8,128)S(1)} %fusion.12), channel_id=1, source_target_pairs={{0,64},{64,0},{1,65},{65,1},{2,66},{66,2},{3,67},{67,3},{4,68},{68... | collective-permute-start | bytes 1769480 | tf_op jit(solution)/shard_map/ppermute | solution.py:311
  111.8 20.6 %collective-permute-start.5 = (f32[64,2816]{1,0:T(8,128)S(1)}, f32[64,2816]{1,0:T(8,128)S(1)}, u32[]{:S(2)}, u32[]{:S(2)}) collective-permute-start(f32[64,2816]{1,0:T(8,128)S(1)} %get-tuple-element.76), channel_id=1, source_target_pairs={{0,16},{16,32},{32,48},{48,0},{1,17},{17,33},{33,49},{49,1},{2,18}... | collective-permute-start | bytes 2162696 | tf_op jit(solution)/shard_map/ppermute | solution.py:315
  113.8 18.8 %collective-permute-start.7 = (f32[64,2816]{1,0:T(8,128)S(1)}, f32[64,2816]{1,0:T(8,128)S(1)}, u32[]{:S(2)}, u32[]{:S(2)}) collective-permute-start(f32[64,2816]{1,0:T(8,128)S(1)} %get-tuple-element.75), channel_id=1, source_target_pairs={{0,48},{16,0},{32,16},{48,32},{1,49},{17,1},{33,17},{49,33},{2,50}... | collective-permute-start | bytes 2162696 | tf_op jit(solution)/shard_map/ppermute | solution.py:315
  126.5 40.5 %collective-permute-start.4 = (f32[192,2304]{1,0:T(8,128)S(1)}, f32[192,2304]{1,0:T(8,128)S(1)}, u32[]{:S(2)}, u32[]{:S(2)}) collective-permute-start(f32[192,2304]{1,0:T(8,128)S(1)} %fusion.10), channel_id=1, source_target_pairs={{0,64},{64,0},{1,65},{65,1},{2,66},{66,2},{3,67},{67,3},{4,68},{68... | collective-permute-start | bytes 5308424 | tf_op jit(solution)/shard_map/ppermute | solution.py:311
  132.9 28.6 %collective-permute-start.6 = (f32[128,1408]{1,0:T(8,128)S(1)}, f32[128,1408]{1,0:T(8,128)S(1)}, u32[]{:S(2)}, u32[]{:S(2)}) collective-permute-start(f32[128,1408]{1,0:T(8,128)S(1)} %get-tuple-element.81), channel_id=1, source_target_pairs={{0,16},{16,32},{32,48},{48,0},{1,17},{17,33},{33,49},{49,1},{2,18}... | collective-permute-start | bytes 2162696 | tf_op jit(solution)/shard_map/ppermute | solution.py:315
  134.1 27.4 %collective-permute-start.8 = (f32[128,1408]{1,0:T(8,128)S(1)}, f32[128,1408]{1,0:T(8,128)S(1)}, u32[]{:S(2)}, u32[]{:S(2)}) collective-permute-start(f32[128,1408]{1,0:T(8,128)S(1)} %get-tuple-element.70), channel_id=1, source_target_pairs={{0,48},{16,0},{32,16},{48,32},{1,49},{17,1},{33,17},{49,33},{2,50}... | collective-permute-start | bytes 2162696 | tf_op jit(solution)/shard_map/ppermute | solution.py:315
  136.3 21.3 %collective-permute-start.10 = (f32[32,2304]{1,0:T(8,128)S(1)}, f32[32,2304]{1,0:T(8,128)S(1)}, u32[]{:S(2)}, u32[]{:S(2)}) collective-permute-start(f32[32,2304]{1,0:T(8,128)S(1)} %get-tuple-element.79), channel_id=1, source_target_pairs={{0,48},{16,0},{32,16},{48,32},{1,49},{17,1},{33,17},{49,33},{2,50}... | collective-permute-start | bytes 884744 | tf_op jit(solution)/shard_map/ppermute | solution.py:315
  138.0 20.3 %collective-permute-start.9 = (f32[32,2304]{1,0:T(8,128)S(1)}, f32[32,2304]{1,0:T(8,128)S(1)}, u32[]{:S(2)}, u32[]{:S(2)}) collective-permute-start(f32[32,2304]{1,0:T(8,128)S(1)} %get-tuple-element.80), channel_id=1, source_target_pairs={{0,16},{16,32},{32,48},{48,0},{1,17},{17,33},{33,49},{49,1},{2,18}... | collective-permute-start | bytes 884744 | tf_op jit(solution)/shard_map/ppermute | solution.py:315
  158.3 20.3 %collective-permute-start.14 = (f32[128,1408]{1,0:T(8,128)S(1)}, f32[128,1408]{1,0:T(8,128)S(1)}, u32[]{:S(2)}, u32[]{:S(2)}) collective-permute-start(f32[128,1408]{1,0:T(8,128)S(1)} %get-tuple-element.63), channel_id=1, source_target_pairs={{0,16},{16,32},{32,48},{48,0},{1,17},{17,33},{33,49},{49,1},{2,18}... | collective-permute-start | bytes 2162696 | tf_op jit(solution)/shard_map/ppermute | solution.py:315
  159.0 19.6 %collective-permute-start.15 = (f32[128,1408]{1,0:T(8,128)S(1)}, f32[128,1408]{1,0:T(8,128)S(1)}, u32[]{:S(2)}, u32[]{:S(2)}) collective-permute-start(f32[128,1408]{1,0:T(8,128)S(1)} %get-tuple-element.64), channel_id=1, source_target_pairs={{0,48},{16,0},{32,16},{48,32},{1,49},{17,1},{33,17},{49,33},{2,50}... | collective-permute-start | bytes 2162696 | tf_op jit(solution)/shard_map/ppermute | solution.py:315
  167.5 21.5 %collective-permute-start.11 = (f32[64,2304]{1,0:T(8,128)S(1)}, f32[64,2304]{1,0:T(8,128)S(1)}, u32[]{:S(2)}, u32[]{:S(2)}) collective-permute-start(f32[64,2304]{1,0:T(8,128)S(1)} %pad_maximum_fusion.3), channel_id=1, source_target_pairs={{0,16},{16,32},{32,48},{48,0},{1,17},{17,33},{33,49},{49,1},{2,18}... | collective-permute-start | bytes 1769480 | tf_op jit(solution)/shard_map/ppermute | solution.py:315
  169.5 19.5 %collective-permute-start.12 = (f32[64,2304]{1,0:T(8,128)S(1)}, f32[64,2304]{1,0:T(8,128)S(1)}, u32[]{:S(2)}, u32[]{:S(2)}) collective-permute-start(f32[64,2304]{1,0:T(8,128)S(1)} %pad_maximum_fusion.4), channel_id=1, source_target_pairs={{0,48},{16,0},{32,16},{48,32},{1,49},{17,1},{33,17},{49,33},{2,50}... | collective-permute-start | bytes 1769480 | tf_op jit(solution)/shard_map/ppermute | solution.py:315
  171.7 11.4 %collective-permute-start.13 = (f32[64,1408]{1,0:T(8,128)S(1)}, f32[64,1408]{1,0:T(8,128)S(1)}, u32[]{:S(2)}, u32[]{:S(2)}) collective-permute-start(f32[64,1408]{1,0:T(8,128)S(1)} %slice.139), channel_id=1, source_target_pairs={{0,64},{64,0},{1,65},{65,1},{2,66},{66,2},{3,67},{67,3},{4,68},{68... | collective-permute-start | bytes 1081352 | tf_op jit(solution)/shard_map/ppermute | solution.py:311
  178.8 9.6 %collective-permute-start.16 = (f32[64,1408]{1,0:T(8,128)S(1)}, f32[64,1408]{1,0:T(8,128)S(1)}, u32[]{:S(2)}, u32[]{:S(2)}) collective-permute-start(f32[64,1408]{1,0:T(8,128)S(1)} %slice.162), channel_id=1, source_target_pairs={{0,64},{64,0},{1,65},{65,1},{2,66},{66,2},{3,67},{67,3},{4,68},{68... | collective-permute-start | bytes 1081352 | tf_op jit(solution)/shard_map/ppermute | solution.py:311
